TPU v7x, 32 devices: a whole 2x2x4 slice. The times are simulated.
32 devices in a mesh: rep: 16 (over z, y, core), grp: 2 (over x).
Axes of the slice: x: 2, y: 2, z: 4, core: 2. Of those that a mesh axis runs over, the one named last changes fastest.
Arguments:
- tokens: bfloat16 [16, 1568, 1024], P('rep', 'grp'), may hold values from -6 to 6
- query_weight: bfloat16 [1024, 1024], P('grp'), may hold values from -0.1875 to 0.1875
- key_weight: bfloat16 [1024, 1024], P('grp'), may hold values from -0.1875 to 0.1875
- value_weight: bfloat16 [1024, 1024], P('grp'), may hold values from -0.1875 to 0.1875
- query_bias: float32 [1024], P('grp'), may hold values from -4 to 4
- value_bias: float32 [1024], P('grp'), may hold values from -0.75 to 0.75
- out_weight: bfloat16 [1024, 1024], P('grp'), may hold values from -4 to 4
- out_bias: float32 [1024], P('grp'), may hold values from -4 to 4
- first_gain: float32 [1024], P('grp'), may hold values from 0.5 to 1.5
- first_shift: float32 [1024], P('grp'), may hold values from -4 to 4
- second_gain: float32 [1024], P('grp'), may hold values from 0.5 to 1.5
- second_shift: float32 [1024], P('grp'), may hold values from -4 to 4
- up_weight: bfloat16 [1024, 4096], P('grp'), may hold values from -0.1875 to 0.1875
- up_bias: float32 [4096], P('grp'), may hold values from -4 to 4
- down_weight: bfloat16 [4096, 1024], P('grp'), may hold values from -0.09375 to 0.09375
- down_bias: float32 [1024], P('grp'), may hold values from -4 to 4
- cotangent: bfloat16 [16, 1568, 1024], P('rep', 'grp'), may hold values from -6 to 6
Outputs:
- layer_out: bfloat16 [16, 1568, 1024], P('rep', 'grp')
- tokens_grad: bfloat16 [16, 1568, 1024], P('rep', 'grp')
- query_weight_grad: float32 [1024, 1024], P('grp')
- key_weight_grad: float32 [1024, 1024], P('grp')
- value_weight_grad: float32 [1024, 1024], P('grp')
- query_bias_grad: float32 [1024], P('grp')
- value_bias_grad: float32 [1024], P('grp')
- out_weight_grad: float32 [1024, 1024], P('grp')
- out_bias_grad: float32 [1024], P('grp')
- first_gain_grad: float32 [1024], P('grp')
- first_shift_grad: float32 [1024], P('grp')
- second_gain_grad: float32 [1024], P('grp')
- second_shift_grad: float32 [1024], P('grp')
- up_weight_grad: float32 [1024, 4096], P('grp')
- up_bias_grad: float32 [4096], P('grp')
- down_weight_grad: float32 [4096, 1024], P('grp')
- down_bias_grad: float32 [1024], P('grp')
All inputs are finite; a program needn't handle non-finite values.
Results may differ from a plain program's by a relative error of at most 0.033.
Values may be sent and summed in bfloat16 or wider, within the bound.
No kernel may reach another device: no remote copies, remote signals or barrier semaphores. Data moves between devices by JAX's collectives and lax.ppermute only.
A program may use at most 448 MiB of HBM per device.

v0:
```python
from functools import partial

import jax
import jax.numpy as jnp
from jax import lax
from jax.sharding import PartitionSpec as P

HEAD_DIM = 64


EPS = 1e-06


def norm_parts(values, gain, shift):
    average = jnp.mean(values, axis=-1, keepdims=True)
    centred = values - average
    spread = jnp.mean(centred * centred, axis=-1, keepdims=True)
    inverse = lax.rsqrt(spread + EPS)
    normed = centred * inverse
    return (normed * gain + shift, normed, inverse)


def norm_back(grad, normed, inverse, gain):
    scaled = grad * gain
    first_term = jnp.mean(scaled, axis=-1, keepdims=True)
    second_term = jnp.mean(scaled * normed, axis=-1, keepdims=True)
    result = inverse * (scaled - first_term - normed * second_term)
    return (result, jnp.sum(grad * normed, axis=0), jnp.sum(grad, axis=0))


def matmul(left, right):
    return jnp.dot(left, right, preferred_element_type=jnp.float32)


def matmul_right_t(left, right):
    return lax.dot_general(
        left, right, (((1,), (1,)), ((), ())), preferred_element_type=jnp.float32
    )


def matmul_left_t(left, right):
    return lax.dot_general(
        left, right, (((0,), (0,)), ((), ())), preferred_element_type=jnp.float32
    )


def split_heads(values):
    return values.reshape(values.shape[0], values.shape[1] // HEAD_DIM, HEAD_DIM)


def attend_clip(operands):
    queries, keys, values = operands
    scale = HEAD_DIM ** (-0.5)
    scores = (
        jnp.einsum(
            "qhd,khd->hqk",
            split_heads(queries),
            split_heads(keys),
            preferred_element_type=jnp.float32,
        )
        * scale
    )
    highest = jnp.max(scores, axis=-1, keepdims=True)
    expon = jnp.exp(scores - highest)
    totals = jnp.sum(expon, axis=-1, keepdims=True)
    probs = (expon / totals).astype(jnp.bfloat16)
    mixed = jnp.einsum(
        "hqk,khd->qhd", probs, split_heads(values), preferred_element_type=jnp.float32
    )
    return (
        mixed.reshape(queries.shape[0], queries.shape[1]),
        highest[..., 0] + jnp.log(totals[..., 0]),
    )


def attend_back(operands):
    queries, keys, values, grad_mixed, log_total = operands
    scale = HEAD_DIM ** (-0.5)
    query_heads = split_heads(queries)
    key_heads = split_heads(keys)
    grad_heads = split_heads(grad_mixed)
    scores = (
        jnp.einsum("qhd,khd->hqk", query_heads, key_heads, preferred_element_type=jnp.float32)
        * scale
    )
    weights = jnp.exp(scores - log_total[..., None])
    probs = weights.astype(jnp.bfloat16)
    grad_probs = jnp.einsum(
        "qhd,khd->hqk", grad_heads, split_heads(values), preferred_element_type=jnp.float32
    )
    grad_values = jnp.einsum("hqk,qhd->khd", probs, grad_heads, preferred_element_type=jnp.float32)
    inner = jnp.sum(grad_probs * weights, axis=-1, keepdims=True)
    grad_scores = (weights * (grad_probs - inner)).astype(jnp.bfloat16)
    grad_queries = (
        jnp.einsum("hqk,khd->qhd", grad_scores, key_heads, preferred_element_type=jnp.float32)
        * scale
    )
    grad_keys = (
        jnp.einsum("hqk,qhd->khd", grad_scores, query_heads, preferred_element_type=jnp.float32)
        * scale
    )
    return (
        grad_queries.reshape(queries.shape[0], queries.shape[1]),
        grad_keys.reshape(keys.shape[0], keys.shape[1]),
        grad_values.reshape(keys.shape[0], keys.shape[1]),
    )


def body(
    tokens,
    query_weight,
    key_weight,
    value_weight,
    query_bias,
    value_bias,
    out_weight,
    out_bias,
    first_gain,
    first_shift,
    second_gain,
    second_shift,
    up_weight,
    up_bias,
    down_weight,
    down_bias,
    cotangent,
):
    clips, local_len, width = tokens.shape
    rows = clips * local_len
    attention_set = (
        lax.all_gather(query_weight, "grp", axis=0, tiled=True),
        lax.all_gather(key_weight, "grp", axis=0, tiled=True),
        lax.all_gather(value_weight, "grp", axis=0, tiled=True),
        lax.all_gather(query_bias.astype(jnp.bfloat16), "grp", axis=0, tiled=True).astype(
            query_bias.dtype
        ),
        lax.all_gather(value_bias.astype(jnp.bfloat16), "grp", axis=0, tiled=True).astype(
            value_bias.dtype
        ),
        lax.all_gather(out_weight, "grp", axis=0, tiled=True),
        lax.all_gather(out_bias.astype(jnp.bfloat16), "grp", axis=0, tiled=True).astype(
            out_bias.dtype
        ),
        lax.all_gather(first_gain.astype(jnp.bfloat16), "grp", axis=0, tiled=True).astype(
            first_gain.dtype
        ),
        lax.all_gather(first_shift.astype(jnp.bfloat16), "grp", axis=0, tiled=True).astype(
            first_shift.dtype
        ),
    )
    feed_set = (
        lax.all_gather(second_gain.astype(jnp.bfloat16), "grp", axis=0, tiled=True).astype(
            second_gain.dtype
        ),
        lax.all_gather(second_shift.astype(jnp.bfloat16), "grp", axis=0, tiled=True).astype(
            second_shift.dtype
        ),
        lax.all_gather(up_weight, "grp", axis=0, tiled=True),
        lax.all_gather(up_bias.astype(jnp.bfloat16), "grp", axis=0, tiled=True).astype(
            up_bias.dtype
        ),
        lax.all_gather(down_weight, "grp", axis=0, tiled=True),
        lax.all_gather(down_bias.astype(jnp.bfloat16), "grp", axis=0, tiled=True).astype(
            down_bias.dtype
        ),
    )
    (
        full_query,
        full_key,
        full_value,
        full_qbias,
        full_vbias,
        full_out,
        full_obias,
        full_gain_one,
        full_shift_one,
    ) = attention_set
    full_gain_two, full_shift_two, full_up, full_ubias, full_down, full_dbias = feed_set
    inputs = tokens.reshape(rows, width).astype(jnp.float32)
    first_norm, first_normed, first_inverse = norm_parts(inputs, full_gain_one, full_shift_one)
    first_low = first_norm.astype(jnp.bfloat16)
    query_low = (matmul(first_low, full_query) + full_qbias).astype(jnp.bfloat16)
    key_low = matmul(first_low, full_key).astype(jnp.bfloat16)
    value_low = (matmul(first_low, full_value) + full_vbias).astype(jnp.bfloat16)
    query_clips = query_low.reshape(clips, local_len, width)
    key_clips = key_low.reshape(clips, local_len, width)
    value_clips = value_low.reshape(clips, local_len, width)
    key_whole, value_whole = (
        lax.all_gather(key_clips, "grp", axis=1, tiled=True),
        lax.all_gather(value_clips, "grp", axis=1, tiled=True),
    )
    mixed, log_total = lax.map(attend_clip, (query_clips, key_whole, value_whole))
    mixed_low = mixed.reshape(rows, width).astype(jnp.bfloat16)
    middle = inputs + matmul(mixed_low, full_out) + full_obias
    second_norm, second_normed, second_inverse = norm_parts(middle, full_gain_two, full_shift_two)
    second_low = second_norm.astype(jnp.bfloat16)
    hidden_pre = matmul(second_low, full_up) + full_ubias
    hidden_low = jax.nn.gelu(hidden_pre, approximate=False).astype(jnp.bfloat16)
    result = middle + matmul(hidden_low, full_down) + full_dbias
    layer_out = result.astype(jnp.bfloat16).reshape(clips, local_len, width)
    attention_back = (
        lax.all_gather(query_weight, "grp", axis=0, tiled=True),
        lax.all_gather(key_weight, "grp", axis=0, tiled=True),
        lax.all_gather(value_weight, "grp", axis=0, tiled=True),
        lax.all_gather(query_bias.astype(jnp.bfloat16), "grp", axis=0, tiled=True).astype(
            query_bias.dtype
        ),
        lax.all_gather(value_bias.astype(jnp.bfloat16), "grp", axis=0, tiled=True).astype(
            value_bias.dtype
        ),
        lax.all_gather(out_weight, "grp", axis=0, tiled=True),
        lax.all_gather(out_bias.astype(jnp.bfloat16), "grp", axis=0, tiled=True).astype(
            out_bias.dtype
        ),
        lax.all_gather(first_gain.astype(jnp.bfloat16), "grp", axis=0, tiled=True).astype(
            first_gain.dtype
        ),
        lax.all_gather(first_shift.astype(jnp.bfloat16), "grp", axis=0, tiled=True).astype(
            first_shift.dtype
        ),
    )
    feed_back = (
        lax.all_gather(second_gain.astype(jnp.bfloat16), "grp", axis=0, tiled=True).astype(
            second_gain.dtype
        ),
        lax.all_gather(second_shift.astype(jnp.bfloat16), "grp", axis=0, tiled=True).astype(
            second_shift.dtype
        ),
        lax.all_gather(up_weight, "grp", axis=0, tiled=True),
        lax.all_gather(up_bias.astype(jnp.bfloat16), "grp", axis=0, tiled=True).astype(
            up_bias.dtype
        ),
        lax.all_gather(down_weight, "grp", axis=0, tiled=True),
        lax.all_gather(down_bias.astype(jnp.bfloat16), "grp", axis=0, tiled=True).astype(
            down_bias.dtype
        ),
    )
    (
        back_query,
        back_key,
        back_value,
        unused_qbias,
        unused_vbias,
        back_out,
        unused_obias,
        back_gain_one,
        unused_shift_one,
    ) = attention_back
    back_gain_two, unused_shift_two, back_up, unused_ubias, back_down, unused_dbias = feed_back
    grad_out = cotangent.reshape(rows, width)
    grad_out_wide = grad_out.astype(jnp.float32)
    grad_hidden = matmul_right_t(grad_out, back_down)
    grad_down_weight = matmul_left_t(hidden_low, grad_out)
    grad_down_bias = jnp.sum(grad_out_wide, axis=0)
    unused_value, gelu_pull = jax.vjp(partial(jax.nn.gelu, approximate=False), hidden_pre)
    grad_pre_low = gelu_pull(grad_hidden)[0].astype(jnp.bfloat16)
    grad_up_weight = matmul_left_t(second_low, grad_pre_low)
    grad_up_bias = jnp.sum(grad_pre_low.astype(jnp.float32), axis=0)
    grad_second, grad_gain_two, grad_shift_two = norm_back(
        matmul_right_t(grad_pre_low, back_up), second_normed, second_inverse, back_gain_two
    )
    grad_middle = grad_out_wide + grad_second
    grad_middle_low = grad_middle.astype(jnp.bfloat16)
    grad_out_weight = matmul_left_t(mixed_low, grad_middle_low)
    grad_out_bias = jnp.sum(grad_middle_low.astype(jnp.float32), axis=0)
    grad_mixed_low = matmul_right_t(grad_middle_low, back_out).astype(jnp.bfloat16)
    grad_mixed_clips = grad_mixed_low.reshape(clips, local_len, width)
    grad_queries, grad_keys, grad_values = lax.map(
        attend_back, (query_clips, key_whole, value_whole, grad_mixed_clips, log_total)
    )
    key_share, value_share = (
        lax.psum_scatter(
            grad_keys.astype(jnp.bfloat16), "grp", scatter_dimension=1, tiled=True
        ).astype(jnp.float32),
        lax.psum_scatter(
            grad_values.astype(jnp.bfloat16), "grp", scatter_dimension=1, tiled=True
        ).astype(jnp.float32),
    )
    query_grad_low = grad_queries.reshape(rows, width).astype(jnp.bfloat16)
    key_grad_low = key_share.reshape(rows, width).astype(jnp.bfloat16)
    value_grad_low = value_share.reshape(rows, width).astype(jnp.bfloat16)
    grad_query_weight = matmul_left_t(first_low, query_grad_low)
    grad_key_weight = matmul_left_t(first_low, key_grad_low)
    grad_value_weight = matmul_left_t(first_low, value_grad_low)
    grad_query_bias = jnp.sum(query_grad_low.astype(jnp.float32), axis=0)
    grad_value_bias = jnp.sum(value_grad_low.astype(jnp.float32), axis=0)
    grad_first_norm = (
        matmul_right_t(query_grad_low, back_query)
        + matmul_right_t(key_grad_low, back_key)
        + matmul_right_t(value_grad_low, back_value)
    )
    grad_first, grad_gain_one, grad_shift_one = norm_back(
        grad_first_norm, first_normed, first_inverse, back_gain_one
    )
    tokens_grad = (grad_middle + grad_first).astype(jnp.bfloat16).reshape(clips, local_len, width)
    shares = (
        lax.psum_scatter(
            grad_query_weight.astype(jnp.bfloat16), "grp", scatter_dimension=0, tiled=True
        ).astype(jnp.float32),
        lax.psum_scatter(
            grad_key_weight.astype(jnp.bfloat16), "grp", scatter_dimension=0, tiled=True
        ).astype(jnp.float32),
        lax.psum_scatter(
            grad_value_weight.astype(jnp.bfloat16), "grp", scatter_dimension=0, tiled=True
        ).astype(jnp.float32),
        lax.psum_scatter(
            grad_query_bias.astype(jnp.bfloat16), "grp", scatter_dimension=0, tiled=True
        ).astype(jnp.float32),
        lax.psum_scatter(
            grad_value_bias.astype(jnp.bfloat16), "grp", scatter_dimension=0, tiled=True
        ).astype(jnp.float32),
        lax.psum_scatter(
            grad_out_weight.astype(jnp.bfloat16), "grp", scatter_dimension=0, tiled=True
        ).astype(jnp.float32),
        lax.psum_scatter(
            grad_out_bias.astype(jnp.bfloat16), "grp", scatter_dimension=0, tiled=True
        ).astype(jnp.float32),
        lax.psum_scatter(
            grad_gain_one.astype(jnp.bfloat16), "grp", scatter_dimension=0, tiled=True
        ).astype(jnp.float32),
        lax.psum_scatter(
            grad_shift_one.astype(jnp.bfloat16), "grp", scatter_dimension=0, tiled=True
        ).astype(jnp.float32),
        lax.psum_scatter(
            grad_gain_two.astype(jnp.bfloat16), "grp", scatter_dimension=0, tiled=True
        ).astype(jnp.float32),
        lax.psum_scatter(
            grad_shift_two.astype(jnp.bfloat16), "grp", scatter_dimension=0, tiled=True
        ).astype(jnp.float32),
        lax.psum_scatter(
            grad_up_weight.astype(jnp.bfloat16), "grp", scatter_dimension=0, tiled=True
        ).astype(jnp.float32),
        lax.psum_scatter(
            grad_up_bias.astype(jnp.bfloat16), "grp", scatter_dimension=0, tiled=True
        ).astype(jnp.float32),
        lax.psum_scatter(
            grad_down_weight.astype(jnp.bfloat16), "grp", scatter_dimension=0, tiled=True
        ).astype(jnp.float32),
        lax.psum_scatter(
            grad_down_bias.astype(jnp.bfloat16), "grp", scatter_dimension=0, tiled=True
        ).astype(jnp.float32),
    )
    totals = (
        lax.psum(shares[0].astype(jnp.bfloat16), "rep").astype(jnp.float32),
        lax.psum(shares[1].astype(jnp.bfloat16), "rep").astype(jnp.float32),
        lax.psum(shares[2].astype(jnp.bfloat16), "rep").astype(jnp.float32),
        lax.psum(shares[3].astype(jnp.bfloat16), "rep").astype(jnp.float32),
        lax.psum(shares[4].astype(jnp.bfloat16), "rep").astype(jnp.float32),
        lax.psum(shares[5].astype(jnp.bfloat16), "rep").astype(jnp.float32),
        lax.psum(shares[6].astype(jnp.bfloat16), "rep").astype(jnp.float32),
        lax.psum(shares[7].astype(jnp.bfloat16), "rep").astype(jnp.float32),
        lax.psum(shares[8].astype(jnp.bfloat16), "rep").astype(jnp.float32),
        lax.psum(shares[9].astype(jnp.bfloat16), "rep").astype(jnp.float32),
        lax.psum(shares[10].astype(jnp.bfloat16), "rep").astype(jnp.float32),
        lax.psum(shares[11].astype(jnp.bfloat16), "rep").astype(jnp.float32),
        lax.psum(shares[12].astype(jnp.bfloat16), "rep").astype(jnp.float32),
        lax.psum(shares[13].astype(jnp.bfloat16), "rep").astype(jnp.float32),
        lax.psum(shares[14].astype(jnp.bfloat16), "rep").astype(jnp.float32),
    )
    return (
        layer_out,
        tokens_grad,
        totals[0],
        totals[1],
        totals[2],
        totals[3],
        totals[4],
        totals[5],
        totals[6],
        totals[7],
        totals[8],
        totals[9],
        totals[10],
        totals[11],
        totals[12],
        totals[13],
        totals[14],
    )


def solution(mesh):
    placed = (
        P("rep", "grp", None),
        P("grp", None),
        P("grp", None),
        P("grp", None),
        P("grp"),
        P("grp"),
        P("grp", None),
        P("grp"),
        P("grp"),
        P("grp"),
        P("grp"),
        P("grp"),
        P("grp", None),
        P("grp"),
        P("grp", None),
        P("grp"),
        P("rep", "grp", None),
    )
    return jax.shard_map(
        body,
        mesh=mesh,
        in_specs=placed,
        out_specs=(
            P("rep", "grp", None),
            P("rep", "grp", None),
            P("grp", None),
            P("grp", None),
            P("grp", None),
            P("grp"),
            P("grp"),
            P("grp", None),
            P("grp"),
            P("grp"),
            P("grp"),
            P("grp"),
            P("grp"),
            P("grp", None),
            P("grp"),
            P("grp", None),
            P("grp"),
        ),
        check_vma=False,
    )
```

profile of v0, /device:TPU:1, one launch (start us, length us, event | category | flops | bytes accessed | tf_op | source)
XLA Modules:
  0.0 1365.5 jit_solution(9006401191543345832)
XLA Ops:
  18.7 26.1 %all-gather.23.cloned.1.call-done = bf16[1024,1024]{1,0:T(8,128)(2,1)} async-done(((bf16[512,1024]{1,0:T(8,128)(2,1)}), bf16[1024,1024]{1,0:T(8,128)(2,1)}) %all-gather.23.cloned.1.call-update) | async-done | bytes 2097168 | tf_op jit(solution)/shard_map/all_gather | solution.py:132
  52.7 26.8 %all-gather.19.cloned.1.call-done = bf16[1024,1024]{1,0:T(8,128)(2,1)} async-done(((bf16[512,1024]{1,0:T(8,128)(2,1)}), bf16[1024,1024]{1,0:T(8,128)(2,1)}) %all-gather.19.cloned.1.call-update) | async-done | bytes 2097168 | tf_op jit(solution)/shard_map/all_gather | solution.py:133
  106.2 8.2 all-gather.21.cloned.1.call-done
  120.6 41.5 %all-gather.33.cloned.1.call-done = bf16[1568,1024]{1,0:T(8,128)(2,1)} async-done(((bf16[784,1024]{1,0:T(8,128)(2,1)}), bf16[1568,1024]{1,0:T(8,128)(2,1)}) %all-gather.33.cloned.1.call-update) | async-done | bytes 3211280 | tf_op jit(solution)/shard_map/all_gather | solution.py:189
  166.4 32.0 %multiply_reduce_fusion.1 = (f32[16,784]{1,0:T(8,128)S(1)}, f32[16,784,1568]{2,1,0:T(8,128)}) fusion(bf16[784,16,64]{0,2,1:T(8,128)(2,1)} %bitcast.148, bf16[1568,16,64]{0,2,1:T(8,128)(2,1)S(1)} %bitcast.144), kind=kOutput, calls=%fused_computation.6 | convolution fusion | flops 2556956416 | bytes 83543040 | tf_op jit(solution)/shard_map/while/body/eval_jaxpr/qhd,khd->hqk/dot_general | solution.py:55
  198.4 27.1 %fusion = f32[16,784]{1,0:T(8,128)S(1)} fusion(f32[16,784,1568]{2,1,0:T(8,128)} %get-tuple-element.101, f32[16,784]{1,0:T(8,128)S(1)} %get-tuple-element.100), kind=kLoop, calls=%fused_computation.5 | loop fusion | flops 58994432 | bytes 78776320 | tf_op jit(solution)/shard_map/while/body/eval_jaxpr/reduce_sum | solution.py:65
  231.5 36.8 %fusion.42 = bf16[16,64,784]{2,1,0:T(8,128)(2,1)} fusion(bf16[1568,16,64]{0,2,1:T(8,128)(2,1)} %bitcast.154, f32[16,784,1568]{2,1,0:T(8,128)} %get-tuple-element.101, f32[16,784]{1,0:T(8,128)S(1)} %fusion, f32[16,784]{1,0:T(8,128)S(1)} %get-tuple-element.100), kind=kOutput, calls=%fused_computation.84 | convolution fusion | flops 2597109760 | bytes 83593216 | tf_op jit(solution)/shard_map/while/body/eval_jaxpr/hqk,khd->qhd/dot_general | solution.py:67
  274.8 75.1 %all-gather.27.cloned.1.call-done = bf16[1024,4096]{1,0:T(8,128)(2,1)} async-done(((bf16[512,4096]{1,0:T(8,128)(2,1)}), bf16[1024,4096]{1,0:T(8,128)(2,1)}) %all-gather.27.cloned.1.call-update) | async-done | bytes 8388624 | tf_op jit(solution)/shard_map/all_gather | solution.py:158
  349.9 40.1 %multiply_convert_fusion.1 = (bf16[784,4096]{1,0:T(8,128)(2,1)}, f32[784,4096]{1,0:T(8,128)}, f32[784,4096]{1,0:T(8,128)}) fusion(f32[4096]{0:T(1024)S(1)} %copy-done.34, bf16[1024,4096]{1,0:T(8,128)(2,1)} %all-gather.27.cloned.1.call-done, f32[784,1024]{1,0:T(8,128)} %copy-done.7, f32[1024]{0:T(1024)S(1)} %bitcast.178, f32[1024]{0:T(1024)S(1)} %bitcast.168, ...), kind=kOutput, calls=%fused_computation.13 | convolution fusion | flops 6792626176 | bytes 43743360 | tf_op jit(solution)/shard_map/dot_general | solution.py:32
  390.0 65.5 %all-gather.29.cloned.1.call-done = bf16[4096,1024]{1,0:T(8,128)(2,1)} async-done(((bf16[2048,1024]{1,0:T(8,128)(2,1)}), bf16[4096,1024]{1,0:T(8,128)(2,1)}) %all-gather.29.cloned.1.call-update) | async-done | bytes 8388624 | tf_op jit(solution)/shard_map/all_gather | solution.py:162
  455.5 21.8 %fusion.65 = (bf16[4096]{0:T(1024)(128)(2,1)}, bf16[784,4096]{1,0:T(8,128)(2,1)}) fusion(f32[784,4096]{1,0:T(8,128)} %get-tuple-element.99, bf16[4096,1024]{1,0:T(8,128)(2,1)} %all-gather.29.cloned.1.call-done, bf16[1,784,1024]{2,1,0:T(8,128)(2,1)} %param.33, f32[784,4096]{1,0:T(8,128)} %get-tuple-element.104, f32[4096]{0:T(1024)S(1)} %copy-done.34), kind=kOutput, calls=%fused_computation.110 | convolution fusion | flops 6628044800 | bytes 42131456 | tf_op jit(solution)/shard_map/dot_general | solution.py:36
  477.3 12.7 multiply_reduce_fusion.2
  497.4 30.6 %fusion.19 = bf16[16,64,1568]{2,1,0:T(8,128)(2,1)} fusion(bf16[784,16,64]{0,2,1:T(8,128)(2,1)S(1)} %bitcast.150, f32[16,784,1568]{2,1,0:T(8,128)} %get-tuple-element.101, f32[16,784]{1,0:T(8,128)S(1)} %copy-done.11), kind=kOutput, calls=%fused_computation.41 | convolution fusion | flops 2578243584 | bytes 83543040 | tf_op jit(solution)/shard_map/while/body/eval_jaxpr/hqk,qhd->khd/dot_general | solution.py:91
  528.0 56.5 %multiply_reduce_fusion = (f32[16,784]{1,0:T(8,128)S(1)}, f32[16,784,1568]{2,1,0:T(8,128)}) fusion(f32[16,784,1568]{2,1,0:T(8,128)} %get-tuple-element.101, f32[16,784]{1,0:T(8,128)S(1)} %copy-done.11, bf16[784,16,64]{0,2,1:T(8,128)(2,1)S(1)} %bitcast.151, bf16[1568,16,64]{0,2,1:T(8,128)(2,1)} %bitcast.155), kind=kOutput, calls=%fused_computation.1 | convolution fusion | flops 2596294400 | bytes 162269184 | tf_op jit(solution)/shard_map/while/body/eval_jaxpr/qhd,khd->hqk/dot_general | solution.py:88
  584.5 16.1 %copy.52 = bf16[1,1568,1024]{2,0,1:T(2,128)(2,1)} copy(bf16[1,1568,1024]{1,2,0:T(8,128)(2,1)} %bitcast.152) | data formatting | bytes 6422528
  606.5 66.2 %multiply_convert_fusion = bf16[16,784,1568]{2,1,0:T(8,128)(2,1)} fusion(f32[16,784,1568]{2,1,0:T(8,128)} %get-tuple-element.107, f32[16,784,1568]{2,1,0:T(8,128)} %get-tuple-element.101, f32[16,784]{1,0:T(8,128)S(1)} %get-tuple-element.106, f32[16,784]{1,0:T(8,128)S(1)} %copy-done.11), kind=kLoop, calls=%fused_computation | loop fusion | flops 98344960 | bytes 196790272 | tf_op jit(solution)/shard_map/while/body/eval_jaxpr/convert_element_type | solution.py:93
  672.7 18.0 %multiply_convert_fusion.2 = bf16[16,64,1568]{2,1,0:T(8,128)(2,1)} fusion(bf16[784,16,64]{0,2,1:T(8,128)(2,1)S(1)} %bitcast.149, bf16[16,784,1568]{2,1,0:T(8,128)(2,1)} %multiply_convert_fusion), kind=kOutput, calls=%fused_computation.29 | convolution fusion | flops 2520842240 | bytes 44154880 | tf_op jit(solution)/shard_map/while/body/eval_jaxpr/hqk,qhd->khd/dot_general | solution.py:99
  690.8 16.1 %copy.50 = bf16[1,1568,1024]{2,0,1:T(2,128)(2,1)} copy(bf16[1,1568,1024]{1,2,0:T(8,128)(2,1)} %bitcast.153) | data formatting | bytes 6422528
  719.2 21.8 %bitcast_reduce_fusion = (bf16[16,64]{1,0:T(8,128)(2,1)S(1)}, bf16[16,64,784]{2,1,0:T(8,128)(2,1)}) fusion(bf16[1568,16,64]{0,2,1:T(8,128)(2,1)S(1)} %bitcast.145, bf16[16,784,1568]{2,1,0:T(8,128)(2,1)} %multiply_convert_fusion), kind=kOutput, calls=%fused_computation.83 | convolution fusion | flops 2520038400 | bytes 44156928 | tf_op jit(solution)/shard_map/while/body/eval_jaxpr/hqk,khd->qhd/dot_general | solution.py:95
  747.1 7.5 fusion.62
  754.7 8.2 copy.53
  772.0 7.9 copy.51
  784.1 14.7 %convolution_convert_fusion = bf16[1024,4096]{1,0:T(8,128)(2,1)} fusion(bf16[784,4096]{1,0:T(8,128)(2,1)} %get-tuple-element.112, f32[784,1024]{1,0:T(8,128)} %copy-done.7, f32[1024]{0:T(1024)S(1)} %bitcast.179, f32[1024]{0:T(1024)S(1)} %bitcast.171, f32[784]{0:T(1024)S(1)} %copy-done.33, f32[784]{0:T(1024)S(1)} %copy-done.25), kind=kOutput, calls=%fused_computation.27 | convolution fusion | flops 6584877056 | bytes 18036864 | tf_op jit(solution)/shard_map/dot_general | solution.py:42
  800.2 15.1 %convolution_convert_fusion.1 = bf16[4096,1024]{1,0:T(8,128)(2,1)} fusion(bf16[784,4096]{1,0:T(8,128)(2,1)} %get-tuple-element.98, bf16[1,784,1024]{2,1,0:T(8,128)(2,1)S(1)} %copy-done.10), kind=kOutput, calls=%fused_computation.28 | convolution fusion | flops 6580862976 | bytes 16416768 | tf_op jit(solution)/shard_map/dot_general | solution.py:42
  815.4 11.6 reduce-scatter.13.cloned.1.call-done
  827.0 34.7 %reduce-scatter.17.cloned.1.call-done = bf16[512,1024]{1,0:T(8,128)(2,1)} async-done(((bf16[1024,1024]{1,0:T(8,128)(2,1)}), bf16[512,1024]{1,0:T(8,128)(2,1)}) %reduce-scatter.17.cloned.1.call-update) | async-done | bytes 1048592 | tf_op jit(solution)/shard_map/reduce_scatter | solution.py:303
  861.7 34.6 %reduce-scatter.15.cloned.1.call-done = bf16[512,1024]{1,0:T(8,128)(2,1)} async-done(((bf16[1024,1024]{1,0:T(8,128)(2,1)}), bf16[512,1024]{1,0:T(8,128)(2,1)}) %reduce-scatter.15.cloned.1.call-update) | async-done | bytes 1048592 | tf_op jit(solution)/shard_map/reduce_scatter | solution.py:300
  896.3 102.0 %reduce-scatter.21.cloned.1.call-done = bf16[512,4096]{1,0:T(8,128)(2,1)} async-done(((bf16[1024,4096]{1,0:T(8,128)(2,1)}), bf16[512,4096]{1,0:T(8,128)(2,1)}) %reduce-scatter.21.cloned.1.call-update) | async-done | bytes 4194320 | tf_op jit(solution)/shard_map/reduce_scatter | solution.py:330
  998.3 102.1 %reduce-scatter.23.cloned.1.call-done = bf16[2048,1024]{1,0:T(8,128)(2,1)} async-done(((bf16[4096,1024]{1,0:T(8,128)(2,1)}), bf16[2048,1024]{1,0:T(8,128)(2,1)}) %reduce-scatter.23.cloned.1.call-update) | async-done | bytes 4194320 | tf_op jit(solution)/shard_map/reduce_scatter | solution.py:336
  1106.6 12.6 fusion.43
  1135.3 60.6 %all-reduce.9 = (bf16[512]{0:T(512)(128)(2,1)S(1)}, bf16[512]{0:T(512)(128)(2,1)S(1)}, bf16[512]{0:T(512)(128)(2,1)S(1)}, bf16[512]{0:T(512)(128)(2,1)S(1)}, bf1...) all-reduce(bf16[512]{0:T(512)(128)(2,1)S(1)} %dynamic-slice.4, ...), channel_id=1, replica_groups=mesh['rep'=16,'grp'=2] {'rep'}, use_global_device_ids=true, to_apply=%region_21.22 | all-reduce | flops 6144 | bytes 24576 | tf_op jit(solution)/shard_map/psum | solution.py:347
  1205.5 136.5 %all-reduce.14.cloned.1.call-done = (bf16[512,1024]{1,0:T(8,128)(2,1)}, bf16[512,1024]{1,0:T(8,128)(2,1)}, bf16[512,1024]{1,0:T(8,128)(2,1)}, bf16[512,1024]{1,0...) async-done(((bf16[512,1024]{1,0:T(8,128)(2,1)}, bf16[512,1024]{1,0:T(8,128)(2,1)}, bf16[512,1024]{1,0:T(8,128)(2,1)}, bf16[512,1024]{1,0:T(8,128)(2,1)}, ...) | async-done | bytes 12582928 | tf_op jit(solution)/shard_map/psum | solution.py:344
  (246 shorter events, 162.0 us)
Async XLA Ops:
  7.2 37.6 %all-gather.23.cloned.1.call-start = ((), (), s32[]{:S(2)}) async-start(), calls=%async_computation.10 | async-start | bytes 3145728 | tf_op jit(solution)/shard_map/all_gather | solution.py:132
  7.9 71.6 %all-gather.19.cloned.1.call-start = ((), (), s32[]{:S(2)}) async-start(), calls=%async_computation.8 | async-start | bytes 3145728 | tf_op jit(solution)/shard_map/all_gather | solution.py:133
  8.7 105.7 %all-gather.21.cloned.1.call-start = ((), (), s32[]{:S(2)}) async-start(), calls=%async_computation.9 | async-start | bytes 3145728 | tf_op jit(solution)/shard_map/all_gather | solution.py:131
  9.4 152.7 %all-gather.33.cloned.1.call-start = ((), (), s32[]{:S(2)}) async-start(), calls=%async_computation.21 | async-start | bytes 4816896 | tf_op jit(solution)/shard_map/all_gather | solution.py:189
  14.6 99.8 %copy-start.38 = (f32[2,1,512]{2,1,0:T(1,128)}, f32[2,1,512]{2,1,0:T(1,128)S(1)}, u32[]{:S(2)}) copy-start(f32[2,1,512]{2,1,0:T(1,128)S(1)} %convert_element_type.380) | copy-start | bytes 12292
  17.8 96.6 %copy-start.26 = (f32[2,1,512]{2,1,0:T(1,128)}, f32[2,1,512]{2,1,0:T(1,128)S(1)}, u32[]{:S(2)}) copy-start(f32[2,1,512]{2,1,0:T(1,128)S(1)} %convert_element_type.379) | copy-start | bytes 12292
  18.1 96.3 %copy-start.22 = (f32[784]{0:T(1024)}, f32[784]{0:T(1024)S(1)}, u32[]{:S(2)}) copy-start(f32[784]{0:T(1024)S(1)} %broadcast_multiply_fusion.5) | copy-start | bytes 9412
  18.7 95.7 %copy-start.28 = (f32[784]{0:T(1024)}, f32[784]{0:T(1024)S(1)}, u32[]{:S(2)}) copy-start(f32[784]{0:T(1024)S(1)} %add_rsqrt_fusion.1) | copy-start | bytes 9412
  49.5 176.7 %all-gather.31.cloned.1.call-start = ((), (), s32[]{:S(2)}) async-start(), calls=%async_computation.20 | async-start | bytes 4816896 | tf_op jit(solution)/shard_map/all_gather | solution.py:190
  84.1 184.1 %all-gather.25.cloned.1.call-start = ((), (), s32[]{:S(2)}) async-start(), calls=%async_computation.11 | async-start | bytes 3145728 | tf_op jit(solution)/shard_map/all_gather | solution.py:140
  84.8 265.1 %all-gather.27.cloned.1.call-start = ((), (), s32[]{:S(2)}) async-start(), calls=%async_computation.12 | async-start | bytes 12582912 | tf_op jit(solution)/shard_map/all_gather | solution.py:158
  85.5 370.0 %all-gather.29.cloned.1.call-start = ((), (), s32[]{:S(2)}) async-start(), calls=%async_computation.13 | async-start | bytes 12582912 | tf_op jit(solution)/shard_map/all_gather | solution.py:162
  86.3 660.8 %reduce-scatter.27.cloned.1.call-start = ((), (), s32[]{:S(2)}) async-start(), calls=%async_computation.23 | async-start | bytes 4816896
  166.4 32.0 %copy-start = (bf16[1568,1024]{0,1:T(8,128)(2,1)}, bf16[1568,1024]{0,1:T(8,128)(2,1)S(1)}, u32[]{:S(2)}) copy-start(bf16[1568,1024]{0,1:T(8,128)(2,1)S(1)} %copy.48) | copy-start | bytes 9633796
  231.5 36.8 %copy-start.4 = (bf16[1,784,1024]{2,1,0:T(8,128)(2,1)S(1)}, bf16[1,784,1024]{2,1,0:T(8,128)(2,1)}, u32[]{:S(2)}) copy-start(bf16[1,784,1024]{2,1,0:T(8,128)(2,1)} %param.17) | copy-start | bytes 4816900
  231.5 36.8 %copy-start.42 = (f32[2,1,512]{2,1,0:T(1,128)S(1)}, f32[2,1,512]{2,1,0:T(1,128)}, u32[]{:S(2)}) copy-start(f32[2,1,512]{2,1,0:T(1,128)} %convert_element_type.383) | copy-start | bytes 12292
  272.6 77.3 %copy-start.30 = (f32[2,1,512]{2,1,0:T(1,128)S(1)}, f32[2,1,512]{2,1,0:T(1,128)}, u32[]{:S(2)}) copy-start(f32[2,1,512]{2,1,0:T(1,128)} %convert_element_type.384) | copy-start | bytes 12292
  272.6 77.3 %copy-start.34 = (f32[4096]{0:T(1024)S(1)}, f32[4096]{0:T(1024)}, u32[]{:S(2)}) copy-start(f32[4096]{0:T(1024)} %convert_element_type.329) | copy-start | bytes 49156
  272.6 77.3 %copy-start.40 = (f32[2,1,512]{2,1,0:T(1,128)S(1)}, f32[2,1,512]{2,1,0:T(1,128)}, u32[]{:S(2)}) copy-start(f32[2,1,512]{2,1,0:T(1,128)} %convert_element_type.385) | copy-start | bytes 12292
  272.7 217.4 %copy-start.24 = (f32[784]{0:T(1024)}, f32[784]{0:T(1024)S(1)}, u32[]{:S(2)}) copy-start(f32[784]{0:T(1024)S(1)} %broadcast_multiply_fusion.4) | copy-start | bytes 9412
  274.8 215.3 %copy-start.32 = (f32[784]{0:T(1024)}, f32[784]{0:T(1024)S(1)}, u32[]{:S(2)}) copy-start(f32[784]{0:T(1024)S(1)} %add_rsqrt_fusion) | copy-start | bytes 9412
  606.4 160.6 %reduce-scatter.25.cloned.1.call-start = ((), (), s32[]{:S(2)}) async-start(), calls=%async_computation.22 | async-start | bytes 4816896
  606.5 66.2 %copy-start.2 = (bf16[784,1024]{0,1:T(8,128)(2,1)S(1)}, bf16[784,1024]{0,1:T(8,128)(2,1)}, u32[]{:S(2)}) copy-start(bf16[784,1024]{0,1:T(8,128)(2,1)} %copy.47) | copy-start | bytes 4816900
  712.7 102.7 %reduce-scatter.19.cloned.1.call-start = ((), (), s32[]{:S(2)}) async-start(), calls=%async_computation.17 | async-start | bytes 3145728 | tf_op jit(solution)/shard_map/reduce_scatter | solution.py:312
  719.1 21.9 %copy-start.23 = (f32[784]{0:T(1024)S(1)}, f32[784]{0:T(1024)}, u32[]{:S(2)}) copy-start(f32[784]{0:T(1024)} %copy-done.22) | copy-start | bytes 9412
  719.1 21.9 %copy-start.27 = (f32[2,1,512]{2,1,0:T(1,128)S(1)}, f32[2,1,512]{2,1,0:T(1,128)}, u32[]{:S(2)}) copy-start(f32[2,1,512]{2,1,0:T(1,128)} %copy-done.26) | copy-start | bytes 12292
  719.1 107.9 %reduce-scatter.13.cloned.1.call-start = ((), (), s32[]{:S(2)}) async-start(), calls=%async_computation.14 | async-start | bytes 3145728 | tf_op jit(solution)/shard_map/reduce_scatter | solution.py:297
  747.0 114.7 %reduce-scatter.17.cloned.1.call-start = ((), (), s32[]{:S(2)}) async-start(), calls=%async_computation.16 | async-start | bytes 3145728 | tf_op jit(solution)/shard_map/reduce_scatter | solution.py:303
  767.0 129.3 %reduce-scatter.15.cloned.1.call-start = ((), (), s32[]{:S(2)}) async-start(), calls=%async_computation.15 | async-start | bytes 3145728 | tf_op jit(solution)/shard_map/reduce_scatter | solution.py:300
  784.1 214.3 %reduce-scatter.21.cloned.1.call-start = ((), (), s32[]{:S(2)}) async-start(), calls=%async_computation.18 | async-start | bytes 12582912 | tf_op jit(solution)/shard_map/reduce_scatter | solution.py:330
  798.9 301.6 %reduce-scatter.23.cloned.1.call-start = ((), (), s32[]{:S(2)}) async-start(), calls=%async_computation.19 | async-start | bytes 12582912 | tf_op jit(solution)/shard_map/reduce_scatter | solution.py:336
  815.3 526.6 %all-reduce.14.cloned.1.call-start = ((), (), s32[]{:S(2)}) async-start(), calls=%async_computation.24 | async-start | bytes 25165824 | tf_op jit(solution)/shard_map/psum | solution.py:344
  (41 other events, 242.8 us)
Sparse Core Ops, SparseCore 0:
  9.6 35.1 all-gather.22
  46.3 33.1 all-gather.18
  81.1 33.3 all-gather.20
  116.4 45.6 all-gather.32
  164.1 45.6 all-gather.30
  211.2 33.1 all-gather.24
  245.9 103.9 all-gather.26
  351.5 103.9 all-gather.28
  606.6 44.0 reduce-scatter.26
  712.8 44.8 reduce-scatter.24
  760.6 31.8 reduce-scatter.18
  795.2 31.8 reduce-scatter.12
  829.8 31.8 reduce-scatter.16
  864.5 31.8 reduce-scatter.14
  899.0 99.2 reduce-scatter.20
  1001.1 99.2 reduce-scatter.22
  1105.4 236.5 all-reduce.13
where the time goes:
time: 1370 us
  waiting for transfers between devices  669 us (49%)
  matrix products  361 us (26%)
  other arithmetic  135 us (10%)
  blocking collectives  97.3 us (7%)
  local copies, waits for them, and re-layouts  85.9 us (6%)
  between operations  16.2 us (1%)
    psum x1, waiting for transfers between devices, body(): lax.psum(shares[0].astype(jnp.bfloat16), 'rep').astype(jnp.float32)  136 us
    reduce_scatter x1, waiting for transfers between devices, body(): lax.psum_scatter(grad_down_weight.astype(jnp.bfloat16), 'grp', scatter_di...  102 us
    reduce_scatter x1, waiting for transfers between devices, body(): lax.psum_scatter(grad_up_weight.astype(jnp.bfloat16), 'grp', scatter_dime...  102 us
    all_gather x1, waiting for transfers between devices, body(): lax.all_gather(up_weight, 'grp', axis=0, tiled=True)  75.1 us
    unnamed x137, local copies, waits for them, and re-layouts  71.9 us
    dot_general x6, matrix products, matmul(): return jnp.dot(left, right, preferred_element_type=jnp.float32)  69.7 us
    convert_element_type x1, other arithmetic, attend_back(): grad_scores = (weights * (grad_probs - inner)).astype(jnp.bfloat16)  66.2 us
    all_gather x1, waiting for transfers between devices, body(): lax.all_gather(down_weight, 'grp', axis=0, tiled=True)  65.5 us
  transfers between devices with their start and end apart: 17, of which 12 were waited for; matrix products, arithmetic and copies ran while one was open for 30% of the time, Pallas kernels for 0%

commit v1 on v0

v1 whole, which is shorter than its diff:
```python
import functools

import jax
import jax.numpy as jnp
from jax import lax
from jax.experimental import pallas as pl
from jax.experimental.pallas import tpu as pltpu
from jax.sharding import Mesh
from jax.sharding import PartitionSpec as P

HEAD_DIM = 64
PAIR = 2 * HEAD_DIM
EPS = 1e-06
LOG2E = 1.4426950408889634
F32 = jnp.float32
BF16 = jnp.bfloat16
SWAP = [(0, 1), (1, 0)]
VMEM_LIMIT = 62 << 20


def contract(left, right, left_dim, right_dim):
    return lax.dot_general(
        left, right, (((left_dim,), (right_dim,)), ((), ())), preferred_element_type=F32
    )


def attend_kernel(tile, rows, padded, qkv_ref, out_ref, lse_ref, q_t, v_t, out_t):
    scale = HEAD_DIM**-0.5 * LOG2E
    ones = jnp.ones((16, rows), BF16)
    q_t[:, :rows] = qkv_ref[:, :PAIR].T
    if padded > rows:
        q_t[:, rows:] = jnp.zeros((PAIR, padded - rows), BF16)
    values_t = qkv_ref[:, 2 * PAIR :].T
    step = HEAD_DIM + 16
    for head in range(2):
        v_t[head * step : head * step + HEAD_DIM, :] = values_t[
            head * HEAD_DIM : (head + 1) * HEAD_DIM, :
        ]
        v_t[head * step + HEAD_DIM : (head + 1) * step, :] = ones

    def block(index, carry):
        columns = pl.ds(pl.multiple_of(index * tile, tile), tile)
        empty = jnp.zeros((HEAD_DIM, tile), BF16)
        for head in range(2):
            lanes = slice(head * HEAD_DIM, (head + 1) * HEAD_DIM)
            query = q_t[lanes, columns]
            query = jnp.concatenate([query, empty] if head == 0 else [empty, query], axis=0)
            scores = contract(qkv_ref[:, PAIR : 2 * PAIR], query, 1, 0)
            highest = jnp.max(scores, axis=0, keepdims=True) * scale
            expon = jnp.exp2(scores * scale - highest).astype(BF16)
            mixed = contract(v_t[head * step : (head + 1) * step, :], expon, 1, 0)
            total = mixed[HEAD_DIM : HEAD_DIM + 1, :]
            out_t[lanes, columns] = mixed[:HEAD_DIM, :] / total
            lse_ref[head : head + 1, columns] = highest + jnp.log2(total)
        return carry

    lax.fori_loop(0, padded // tile, block, 0)
    out_ref[...] = out_t[...].T[:rows, :].astype(BF16)


def attend(qkv, tile=512):
    rows, width = qkv.shape
    pairs = width // (3 * PAIR)
    padded = -(-rows // tile) * tile
    return pl.pallas_call(
        functools.partial(attend_kernel, tile, rows, padded),
        grid=(pairs,),
        in_specs=[pl.BlockSpec((rows, 3 * PAIR), lambda i: (0, i))],
        out_specs=[
            pl.BlockSpec((rows, PAIR), lambda i: (0, i)),
            pl.BlockSpec((None, 2, padded), lambda i: (i, 0, 0)),
        ],
        out_shape=[
            jax.ShapeDtypeStruct((rows, pairs * PAIR), BF16),
            jax.ShapeDtypeStruct((pairs, 2, padded), F32),
        ],
        scratch_shapes=[
            pltpu.VMEM((PAIR, padded), BF16),
            pltpu.VMEM((PAIR + 32, rows), BF16),
            pltpu.VMEM((PAIR, padded), F32),
        ],
        compiler_params=pltpu.CompilerParams(vmem_limit_bytes=VMEM_LIMIT),
        cost_estimate=pl.CostEstimate(
            flops=16 * rows * rows * PAIR * pairs,
            bytes_accessed=8 * rows * PAIR * pairs,
            transcendentals=2 * rows * rows * pairs,
        ),
        name="attend",
    )(qkv)


def attend_back_kernel(
    tile, rows, padded, qkv_ref, grad_ref, out_ref, lse_ref, dqkv_ref, q_t, g_t, k_t, delta,
    dq_t, dk_t, dv_t,
):
    scale = HEAD_DIM**-0.5
    q_t[:, :rows] = qkv_ref[:, :PAIR].T
    g_t[:, :rows] = grad_ref[...].T
    if padded > rows:
        q_t[:, rows:] = jnp.zeros((PAIR, padded - rows), BF16)
        g_t[:, rows:] = jnp.zeros((PAIR, padded - rows), BF16)
        delta[:, rows:] = jnp.zeros((2, padded - rows), F32)
    k_t[...] = qkv_ref[:, PAIR : 2 * PAIR].T
    product = (grad_ref[...].astype(F32) * out_ref[...].astype(F32)).T
    delta[0:1, :rows] = jnp.sum(product[:HEAD_DIM, :], axis=0, keepdims=True)
    delta[1:2, :rows] = jnp.sum(product[HEAD_DIM:, :], axis=0, keepdims=True)
    dk_t[...] = jnp.zeros_like(dk_t)
    dv_t[...] = jnp.zeros_like(dv_t)

    def block(index, carry):
        columns = pl.ds(pl.multiple_of(index * tile, tile), tile)
        empty = jnp.zeros((HEAD_DIM, tile), BF16)
        for head in range(2):
            lanes = slice(head * HEAD_DIM, (head + 1) * HEAD_DIM)
            query = q_t[lanes, columns]
            grad = g_t[lanes, columns]
            query_pad = jnp.concatenate([query, empty] if head == 0 else [empty, query], axis=0)
            grad_pad = jnp.concatenate([grad, empty] if head == 0 else [empty, grad], axis=0)
            scores = contract(qkv_ref[:, PAIR : 2 * PAIR], query_pad, 1, 0)
            grad_probs = contract(qkv_ref[:, 2 * PAIR :], grad_pad, 1, 0)
            weights = jnp.exp2(scores * (scale * LOG2E) - lse_ref[head : head + 1, columns])
            grad_scores = (weights * (grad_probs - delta[head : head + 1, columns])).astype(BF16)
            dv_t[lanes, :] += contract(grad, weights.astype(BF16), 1, 1)
            dq_t[lanes, columns] = contract(k_t[lanes, :], grad_scores, 1, 0)
            dk_t[lanes, :] += contract(query, grad_scores, 1, 1)
        return carry

    lax.fori_loop(0, padded // tile, block, 0)
    dqkv_ref[:, :PAIR] = (dq_t[...].T[:rows, :] * scale).astype(BF16)
    dqkv_ref[:, PAIR : 2 * PAIR] = (dk_t[...].T * scale).astype(BF16)
    dqkv_ref[:, 2 * PAIR :] = dv_t[...].T.astype(BF16)


def attend_back(qkv, grad, out, lse, tile=256):
    rows, width = qkv.shape
    pairs = width // (3 * PAIR)
    padded = -(-rows // tile) * tile
    return pl.pallas_call(
        functools.partial(attend_back_kernel, tile, rows, padded),
        grid=(pairs,),
        in_specs=[
            pl.BlockSpec((rows, 3 * PAIR), lambda i: (0, i)),
            pl.BlockSpec((rows, PAIR), lambda i: (0, i)),
            pl.BlockSpec((rows, PAIR), lambda i: (0, i)),
            pl.BlockSpec((None, 2, lse.shape[2]), lambda i: (i, 0, 0)),
        ],
        out_specs=pl.BlockSpec((rows, 3 * PAIR), lambda i: (0, i)),
        out_shape=jax.ShapeDtypeStruct((rows, width), BF16),
        scratch_shapes=[
            pltpu.VMEM((PAIR, padded), BF16),
            pltpu.VMEM((PAIR, padded), BF16),
            pltpu.VMEM((PAIR, rows), BF16),
            pltpu.VMEM((2, padded), F32),
            pltpu.VMEM((PAIR, padded), F32),
            pltpu.VMEM((PAIR, rows), F32),
            pltpu.VMEM((PAIR, rows), F32),
        ],
        compiler_params=pltpu.CompilerParams(vmem_limit_bytes=VMEM_LIMIT),
        cost_estimate=pl.CostEstimate(
            flops=40 * rows * rows * PAIR * pairs,
            bytes_accessed=16 * rows * PAIR * pairs,
            transcendentals=2 * rows * rows * pairs,
        ),
        name="attend_back",
    )(qkv, grad, out, lse)


def feed_kernel(
    x_ref, dy_ref, up_ref, bias_ref, down_ref, out_ref, dx_ref, up_grad_ref, bias_grad_ref,
    down_grad_ref, x_t, out_sum, dx_sum, hidden, d_pre, *, chunk,
):
    index = pl.program_id(0)
    rows = x_ref.shape[0]

    @pl.when(index == 0)
    def _():
        x_t[...] = x_ref[...].T
        out_sum[...] = jnp.zeros_like(out_sum)
        dx_sum[...] = jnp.zeros_like(dx_sum)

    bias_grad = jnp.zeros(bias_grad_ref.shape, F32)
    for start in range(0, rows, chunk):
        part = slice(start, start + chunk)
        pre = contract(x_ref[part, :], up_ref[...], 1, 0) + bias_ref[...]
        d_hidden = contract(dy_ref[part, :], down_ref[...], 1, 1)
        share = 0.5 * (1.0 + lax.erf(pre * 0.7071067811865476))
        hidden[part, :] = (pre * share).astype(BF16)
        slope = share + pre * (jnp.exp(-0.5 * pre * pre) * 0.3989422804014327)
        d_low = (d_hidden * slope).astype(BF16)
        d_pre[part, :] = d_low
        bias_grad = bias_grad + jnp.sum(d_low.astype(F32), axis=0, keepdims=True)
        out_sum[part, :] += contract(hidden[part, :], down_ref[...], 1, 0)
        dx_sum[part, :] += contract(d_pre[part, :], up_ref[...], 1, 1)
    bias_grad_ref[...] = bias_grad
    up_grad_ref[...] = contract(x_t[...], d_pre[...], 1, 0).astype(BF16)
    down_grad_ref[...] = contract(hidden[...], dy_ref[...], 0, 0).astype(BF16)

    @pl.when(index == pl.num_programs(0) - 1)
    def _():
        out_ref[...] = out_sum[...].astype(BF16)
        dx_ref[...] = dx_sum[...].astype(BF16)


def feed(x, dy, up, bias, down, tile=512):
    rows, width = x.shape
    hidden = up.shape[1]
    chunk = rows // 2 if rows % 32 == 0 else rows
    whole = pl.BlockSpec((rows, width), lambda j: (0, 0), pipeline_mode=pl.Buffered(1))
    up_spec = pl.BlockSpec((width, tile), lambda j: (0, j))
    bias_spec = pl.BlockSpec((1, tile), lambda j: (0, j))
    down_spec = pl.BlockSpec((tile, width), lambda j: (j, 0))
    return pl.pallas_call(
        functools.partial(feed_kernel, chunk=chunk),
        grid=(hidden // tile,),
        in_specs=[whole, whole, up_spec, bias_spec, down_spec],
        out_specs=[whole, whole, up_spec, bias_spec, down_spec],
        out_shape=[
            jax.ShapeDtypeStruct((rows, width), BF16),
            jax.ShapeDtypeStruct((rows, width), BF16),
            jax.ShapeDtypeStruct((width, hidden), BF16),
            jax.ShapeDtypeStruct((1, hidden), F32),
            jax.ShapeDtypeStruct((hidden, width), BF16),
        ],
        scratch_shapes=[
            pltpu.VMEM((width, rows), BF16),
            pltpu.VMEM((rows, width), F32),
            pltpu.VMEM((rows, width), F32),
            pltpu.VMEM((rows, tile), BF16),
            pltpu.VMEM((rows, tile), BF16),
        ],
        compiler_params=pltpu.CompilerParams(vmem_limit_bytes=VMEM_LIMIT),
        cost_estimate=pl.CostEstimate(
            flops=12 * rows * width * hidden,
            bytes_accessed=8 * rows * width + 8 * width * hidden,
            transcendentals=2 * rows * hidden,
        ),
        name="feed",
    )(x, dy, up, bias, down)


def norm_parts(values, gain, shift):
    average = jnp.mean(values, axis=-1, keepdims=True)
    centred = values - average
    spread = jnp.mean(centred * centred, axis=-1, keepdims=True)
    inverse = lax.rsqrt(spread + EPS)
    normed = centred * inverse
    return (normed * gain + shift, normed, inverse)


def norm_back(grad, normed, inverse, gain):
    scaled = grad * gain
    first_term = jnp.mean(scaled, axis=-1, keepdims=True)
    second_term = jnp.mean(scaled * normed, axis=-1, keepdims=True)
    result = inverse * (scaled - first_term - normed * second_term)
    return (result, jnp.sum(grad * normed, axis=0), jnp.sum(grad, axis=0))


def pick(values, index, axis):
    return lax.dynamic_index_in_dim(values, index, axis, keepdims=False)


def join(own, other, index):
    return jnp.where(index == 0, jnp.stack([own, other]), jnp.stack([other, own]))


def body(
    grp, tokens, query_weight, key_weight, value_weight, query_bias, value_bias, out_weight,
    out_bias, first_gain, first_shift, second_gain, second_shift, up_weight, up_bias,
    down_weight, down_bias, cotangent,
):
    clips, local, width = tokens.shape
    assert clips == 1
    quarter = grp // 2
    core = lax.axis_index("core")
    half = lax.axis_index("half")
    own_rows = width // grp
    set_width = width // grp
    pairs = set_width // PAIR
    hidden = up_weight.shape[1]
    set_hidden = hidden // grp

    there = []
    for b in range(2):
        for h in range(2):
            for q in range(quarter):
                g = h * quarter + q
                source = (b * 2 + h) * quarter + q
                target = ((g % 2) * 2 + b) * quarter + g // 2
                there.append((source, target))
    back = [(target, source) for source, target in there]
    axes = ("core", "half", "gq")

    def swap_half(values):
        return lax.ppermute(values, "half", SWAP)

    def both_halves(values):
        return join(values, swap_half(values), half)

    def spread(values):
        if grp == 2:
            return jnp.concatenate([values, lax.ppermute(values, "core", SWAP)], axis=0)
        return lax.all_gather(values, ("gq", "core"), axis=0, tiled=True)

    def collect(values):
        if grp == 2:
            other = lax.ppermute(values[local:], "core", SWAP)
            return values[:local].astype(F32) + other.astype(F32)
        return lax.psum_scatter(
            values, ("gq", "core"), scatter_dimension=0, tiled=True
        ).astype(F32)

    def set_columns(values):
        parts = values.reshape(values.shape[0], 2, quarter, 2, -1)
        parts = pick(parts, core, 3)
        return parts.transpose(0, 2, 1, 3).reshape(values.shape[0], quarter, -1)

    def all_rows(values):
        if quarter > 1:
            values = lax.all_to_all(values, "gq", split_axis=1, concat_axis=0, tiled=True)
        values = both_halves(values.reshape(-1, values.shape[-1]))
        return values.reshape(-1, values.shape[-1])

    def set_rows(values):
        values = pick(values.reshape(2, -1, values.shape[-1]), core, 0)
        return both_halves(values).reshape(-1, values.shape[-1])

    def set_entries(values):
        parts = values.reshape(2, quarter, 2, -1)
        parts = pick(pick(parts, core, 2), lax.axis_index("gq"), 1)
        return parts.reshape(1, -1)

    vectors = jnp.concatenate(
        [query_bias, value_bias, out_bias, first_gain, first_shift, second_gain, second_shift,
         down_bias, up_bias]
    )
    if quarter > 1:
        vectors = lax.all_gather(vectors, "gq", axis=0)
    vectors = both_halves(vectors).reshape(grp, -1)
    (full_qbias, full_vbias, full_obias, gain_one, shift_one, gain_two, shift_two, full_dbias) = [
        vectors[:, i * own_rows : (i + 1) * own_rows].reshape(-1) for i in range(8)
    ]
    full_ubias = vectors[:, 8 * own_rows :].reshape(-1)

    clip_tokens = lax.ppermute(tokens.reshape(local, width), axes, there)

    parts = [
        set_columns(w).reshape(own_rows, quarter, pairs, PAIR)
        for w in (query_weight, key_weight, value_weight)
    ]
    qkv_weight = all_rows(jnp.stack(parts, axis=3).reshape(own_rows, quarter, 3 * set_width))
    out_set = set_rows(out_weight)
    up_set = all_rows(set_columns(up_weight))
    down_set = set_rows(down_weight)
    grad_out = lax.ppermute(cotangent.reshape(local, width), axes, there)

    zeros = jnp.zeros((1, set_width), F32)
    qkv_bias = jnp.stack(
        [b.reshape(pairs, PAIR) for b in (set_entries(full_qbias), zeros, set_entries(full_vbias))],
        axis=1,
    ).reshape(1, 3 * set_width)

    inputs = clip_tokens.astype(F32)
    first_norm, first_normed, first_inverse = norm_parts(inputs, gain_one, shift_one)
    first = spread(first_norm.astype(BF16))
    qkv = (contract(first, qkv_weight, 1, 0) + qkv_bias).astype(BF16)
    mixed, lse = attend(qkv)
    if grp == 2:
        other = contract(mixed[local:], out_set, 1, 0).astype(BF16)
        other = lax.ppermute(other, "core", SWAP)
        middle = inputs + contract(mixed[:local], out_set, 1, 0) + full_obias
        middle = middle + other.astype(F32)
    else:
        middle = inputs + collect(contract(mixed, out_set, 1, 0).astype(BF16)) + full_obias
    second_norm, second_normed, second_inverse = norm_parts(middle, gain_two, shift_two)
    second = spread(second_norm.astype(BF16))
    grad_all = spread(grad_out)
    feed_out, feed_back, up_grad, up_bias_grad, down_grad = feed(
        second, grad_all, up_set, set_entries(full_ubias), down_set
    )
    result = (middle + collect(feed_out) + full_dbias).astype(BF16)
    layer_out = lax.ppermute(result, axes, back).reshape(1, local, width)

    grad_wide = grad_out.astype(F32)
    grad_second, grad_gain_two, grad_shift_two = norm_back(
        collect(feed_back), second_normed, second_inverse, gain_two
    )
    grad_middle = grad_wide + grad_second
    grad_middle_low = grad_middle.astype(BF16)
    grad_middle_all = spread(grad_middle_low)
    grad_mixed = contract(grad_middle_all, out_set, 1, 1).astype(BF16)
    out_grad = contract(mixed, grad_middle_all, 0, 0).astype(BF16)
    dqkv = attend_back(qkv, grad_mixed, mixed, lse)
    qkv_grad = contract(first, dqkv, 0, 0).astype(BF16)
    grad_first_norm = collect(contract(dqkv, qkv_weight, 1, 1).astype(BF16))
    grad_first, grad_gain_one, grad_shift_one = norm_back(
        grad_first_norm, first_normed, first_inverse, gain_one
    )
    tokens_grad = lax.ppermute(
        (grad_middle + grad_first).astype(BF16), axes, back
    ).reshape(1, local, width)

    def scatter_half(values):
        values = values.reshape(2, -1, values.shape[-1])
        other = swap_half(pick(values, 1 - half, 0))
        return (pick(values, half, 0).astype(F32) + other.astype(F32)).astype(BF16)

    def both_cores(values):
        return join(values, lax.ppermute(values, "core", SWAP), core)

    def finish_columns(values):
        if quarter > 1:
            values = values.reshape(quarter, own_rows, 1, -1)
            values = lax.all_to_all(values, "gq", split_axis=0, concat_axis=2, tiled=True)
        values = values.reshape(own_rows, quarter, -1)
        return both_cores(values).transpose(1, 0, 2, 3)

    def natural_columns(values):
        values = values.reshape(own_rows, 2, quarter, 2, -1)
        return values.transpose(0, 3, 2, 1, 4).reshape(own_rows, -1).astype(F32)

    up_half = scatter_half(up_grad)
    down_half = scatter_half(down_grad)
    up_half, down_half = lax.psum((up_half, down_half), "rz")
    up_weight_grad = natural_columns(finish_columns(up_half))
    down_weight_grad = both_cores(down_half).reshape(-1, width).astype(F32)

    out_half = scatter_half(out_grad)
    qkv_half = scatter_half(qkv_grad)
    out_half, qkv_half, up_half = lax.optimization_barrier((out_half, qkv_half, up_half))
    out_half, qkv_half = lax.psum((out_half, qkv_half), "rz")
    out_weight_grad = both_cores(out_half).reshape(-1, width).astype(F32)
    columns = finish_columns(qkv_half).reshape(own_rows, 2, quarter, pairs, 3, PAIR)
    query_weight_grad, key_weight_grad, value_weight_grad = [
        natural_columns(columns[:, :, :, :, i]) for i in range(3)
    ]

    dqkv_sums = jnp.sum(dqkv.astype(F32), axis=0).reshape(pairs, 3, PAIR)

    def place_entries(values, size):
        parts = values.reshape(2, 1, 1, -1)
        empty = jnp.zeros((2, quarter, 2, size // (2 * grp)), F32)
        zero = jnp.zeros((), core.dtype)
        return lax.dynamic_update_slice(
            empty, parts, (zero, lax.axis_index("gq"), core, zero)
        ).reshape(-1)

    sums = [
        place_entries(dqkv_sums[:, 0], width),
        place_entries(dqkv_sums[:, 2], width),
        jnp.sum(grad_middle_low.astype(F32), axis=0),
        grad_gain_one, grad_shift_one, grad_gain_two, grad_shift_two,
        jnp.sum(grad_wide, axis=0),
    ]
    sums = jnp.concatenate(
        [s.reshape(grp, -1) for s in sums] + [place_entries(up_bias_grad, hidden).reshape(grp, -1)],
        axis=1,
    )
    sums = lax.psum(sums, ("rz", "core", "half", "gq"))
    sums = pick(sums, half * quarter + lax.axis_index("gq"), 0)
    small = [sums[i * own_rows : (i + 1) * own_rows] for i in range(8)]
    return (
        layer_out, tokens_grad, query_weight_grad, key_weight_grad, value_weight_grad,
        small[0], small[1], out_weight_grad, small[2], small[3], small[4], small[5], small[6],
        up_weight_grad, sums[8 * own_rows :], down_weight_grad, small[7],
    )


def solution(mesh):
    rep, grp = mesh.shape["rep"], mesh.shape["grp"]
    split = Mesh(
        mesh.devices.reshape(rep // 2, 2, 2, grp // 2), ("rz", "core", "half", "gq")
    )
    clip = P(("rz", "core"), ("half", "gq"), None)
    matrix = P(("half", "gq"), None)
    vector = P(("half", "gq"))
    return jax.shard_map(
        functools.partial(body, grp),
        mesh=split,
        in_specs=(
            clip, matrix, matrix, matrix, vector, vector, matrix, vector, vector, vector, vector,
            vector, matrix, vector, matrix, vector, clip,
        ),
        out_specs=(
            clip, clip, matrix, matrix, matrix, vector, vector, matrix, vector, vector, vector,
            vector, vector, matrix, vector, matrix, vector,
        ),
        check_vma=False,
    )
```

time: 1370 us -> 833 us (0.61)
  waiting for transfers between devices: 669 us -> 325 us
  matrix products: 361 us -> 41.1 us
  Pallas kernels: 0 us -> 167 us
  blocking collectives: 97.3 us -> 38.3 us
  other arithmetic: 135 us -> 84 us
  starting transfers between devices: 0.69 us -> 49.2 us
  local copies, waits for them, and re-layouts: 85.9 us -> 105 us
    dot_general x24 -> x7, matrix products: 361 us -> 41.1 us  [contract(): lax.dot_general(left, right, (((left_dim,), (right_dim,)), ((), ())), pre...]
    reduce_scatter x6 -> x0, waiting for transfers between devices: 285 us -> none  [the longest x1 102 us: body(): lax.psum_scatter(grad_down_weight.astype(jnp.bfloat16), 'grp', scatter_di...]
    all_gather x8 -> x0, waiting for transfers between devices: 243 us -> none  [the longest x1 75.1 us: body(): lax.all_gather(up_weight, 'grp', axis=0, tiled=True)]
    pallas_call x0 -> x3, Pallas kernels: none -> 167 us  [the longest x1 65.9 us: attend_back(): pl.pallas_call(functools.partial(attend_back_kernel, tile, rows, padded),...]
    ppermute x0 -> x25, waiting for transfers between devices: none -> 144 us  [the longest x9 143 us: swap_half(): return lax.ppermute(values, 'half', SWAP)]
    convert_element_type x34 -> x13, other arithmetic: 91.8 us -> 37.2 us  [the longest x4 12.3 us: scatter_half(): return (pick(values, half, 0).astype(F32) + other.astype(F32)).astype(BF16)]
    ppermute x0 -> x25, starting transfers between devices: none -> 49.1 us  [the longest x9 17.8 us: swap_half(): return lax.ppermute(values, 'half', SWAP)]
    psum x1 -> x2, waiting for transfers between devices: 136 us -> 180 us  [the longest x1 119 us: body(): out_half, qkv_half = lax.psum((out_half, qkv_half), 'rz')]
  transfers between devices with their start and end apart: 17 -> 27, of which waited for: 12 -> 9; matrix products, arithmetic and copies ran while one was open for 30% -> 25% of each run, Pallas kernels for 0% -> 14%
where the time goes in v1:
time: 833 us; the launch traced here: 825 us
  waiting for transfers between devices  325 us (39%)
  Pallas kernels  167 us (20%)
  local copies, waits for them, and re-layouts  105 us (13%)
  other arithmetic  84 us (10%)
  starting transfers between devices  49.2 us (6%)
  matrix products  41.1 us (5%)
  blocking collectives  38.3 us (5%)
  between operations  15.2 us (2%)
    ppermute x9, waiting for transfers between devices, swap_half(): return lax.ppermute(values, 'half', SWAP)  143 us
    psum x1, waiting for transfers between devices, body(): out_half, qkv_half = lax.psum((out_half, qkv_half), 'rz')  119 us
    pallas_call x1, Pallas kernels, attend_back(): pl.pallas_call(functools.partial(attend_back_kernel, tile, rows, padded),...  65.9 us
    psum x1, waiting for transfers between devices, body(): up_half, down_half = lax.psum((up_half, down_half), 'rz')  61.2 us
    pallas_call x1, Pallas kernels, feed(): pl.pallas_call(functools.partial(feed_kernel, chunk=chunk), grid=(hidden...  54 us
    pallas_call x1, Pallas kernels, attend(): pl.pallas_call(functools.partial(attend_kernel, tile, rows, padded), grid...  47.4 us
    dot_general x7, matrix products, contract(): lax.dot_general(left, right, (((left_dim,), (right_dim,)), ((), ())), pre...  41.1 us
    convert_element_type x6, local copies, waits for them, and re-layouts, natural_columns(): return values.transpose(0, 3, 2, 1, 4).reshape(own_rows, -1).astype(F32)  39.5 us
  transfers between devices with their start and end apart: 27, of which 9 were waited for; matrix products, arithmetic and copies ran while one was open for 25% of the time, Pallas kernels for 14%

profile of v1, /device:TPU:1, one launch (start us, length us, event | category | flops | bytes accessed | tf_op | source)
XLA Modules:
  0.0 824.9 jit_solution(1395427385697705286)
XLA Ops:
  7.3 4.6 collective-permute-start
  18.1 11.3 %collective-permute-start.1 = (f32[6144]{0:T(1024)S(1)}, f32[6144]{0:T(1024)S(1)}, u32[]{:S(2)}, u32[]{:S(2)}) collective-permute-start(f32[6144]{0:T(1024)S(1)} %constant_dynamic-update-slice_fusion.13), channel_id=1, source_target_pairs={{0,1},{1,0},{2,3},{3,2},{4,5},{5,4},{6,7},{7,6},{8,9},{9,8},{10,11... | collective-permute-start | bytes 73736 | tf_op jit(solution)/shard_map/ppermute | solution.py:294
  48.8 35.0 %collective-permute-done.4 = bf16[256,1024]{1,0:T(8,128)(2,1)} collective-permute-done((bf16[256,1024]{1,0:T(8,128)(2,1)}, bf16[256,1024]{1,0:T(8,128)(2,1)}, u32[]{:S(2)}, u32[]{:S(2)}) %collective-permute-start.4) | collective-permute-done | bytes 524320 | tf_op jit(solution)/shard_map/ppermute | solution.py:294
  88.9 4.6 copy.46
  93.6 9.2 %add_convert_fusion.qkv_ref = bf16[1568,1536]{1,0:T(8,128)(2,1)} fusion(bf16[1024,1536]{1,0:T(8,128)(2,1)} %bitcast.173, f32[1536]{0:T(1024)S(1)} %add.163, bf16[784,1024]{1,0:T(8,128)(2,1)} %collective-permute-done.2, bf16[784,1024]{1,0:T(8,128)(2,1)} %fusion.9), kind=kOutput, calls=%fused_computation.1 | convolution fusion | flops 4943740928 | bytes 11180032 | tf_op jit(solution)/shard_map/dot_general | solution.py:22
  102.8 47.4 %attend.1 = (bf16[1568,512]{1,0:T(8,128)(2,1)}, f32[4,2,2048]{2,1,0:T(2,128)}) custom-call(bf16[1568,1536]{1,0:T(8,128)(2,1)} %add_convert_fusion.qkv_ref), custom_call_target="tpu_custom_call" | custom-call | flops 20141047808 | bytes 6422528 | tf_op jit(solution)/shard_map/attend/pallas_call | solution.py:65
  153.5 6.4 copy.47
  171.8 36.7 %collective-permute-done.9 = bf16[512,2048]{0,1:T(8,128)(2,1)S(1)} collective-permute-done((bf16[512,2048]{0,1:T(8,128)(2,1)S(1)}, bf16[512,2048]{0,1:T(8,128)(2,1)S(1)}, u32[]{:S(2)}, u32[]{:S(2)}) %collective-permute-start.9) | collective-permute-done | bytes 2097184 | tf_op jit(solution)/shard_map/ppermute | solution.py:294
  210.9 6.3 copy.48
  217.2 36.4 %collective-permute-done.10 = bf16[1024,1024]{1,0:T(8,128)(2,1)} collective-permute-done((bf16[1024,1024]{1,0:T(8,128)(2,1)}, bf16[1024,1024]{1,0:T(8,128)(2,1)}, u32[]{:S(2)}, u32[]{:S(2)}) %collective-permute-start.10) | collective-permute-done | bytes 2097184 | tf_op jit(solution)/shard_map/ppermute | solution.py:294
  253.6 4.5 maximum_select_fusion.1
  265.9 54.0 %feed.1 = (bf16[1568,1024]{1,0:T(8,128)(2,1)}, bf16[1568,1024]{1,0:T(8,128)(2,1)}, bf16[1024,2048]{1,0:T(8,128)(2,1)}, f32[1,2048]{1,0:T(1,128)}, bf16[2048,1024]{1,0:T(8,128)(2,1)}) custom-call(bf16[1568,1024]{1,0:T(8,128)(2,1)} %pad_maximum_fusion.1.x_ref, bf16[1568,1024]{1,0:T(8,128)(2,1)} %pad_maximum_fusion.2.dy_ref, bf16[1024,2048]{1,0:T(8,128)(2,1)} %bitcast.168, ...), custom_call_target="tpu_custom_call" | custom-call | flops 39460012032 | bytes 29622272 | tf_op jit(solution)/shard_map/feed/pallas_call | solution.py:212
  328.4 5.0 convert_reduce_fusion.3
  340.0 4.4 convolution_convert_fusion.2.grad_ref
  344.4 65.9 %attend_back.1 = bf16[1568,1536]{1,0:T(8,128)(2,1)} custom-call(bf16[1568,1536]{1,0:T(8,128)(2,1)} %add_convert_fusion.qkv_ref, bf16[1568,512]{1,0:T(8,128)(2,1)} %convolution_convert_fusion.2.grad_ref, bf16[1568,512]{1,0:T(8,128)(2,1)} %get-tuple-element.26.out_ref, f32[4,2,2048]{2,1,0:T(2,128)} %get-tuple-element.29.lse_ref), custom_call_target="tpu_custom_call" | custom-call | flops 50352619520 | bytes 12845056 | tf_op jit(solution)/shard_map/attend_back/pallas_call | solution.py:138
  410.3 9.0 %convolution_convert_fusion = bf16[1024,1536]{1,0:T(8,128)(2,1)S(1)} fusion(bf16[1568,1536]{1,0:T(8,128)(2,1)} %attend_back.1, bf16[784,1024]{1,0:T(8,128)(2,1)} %collective-permute-done.2, bf16[784,1024]{1,0:T(8,128)(2,1)} %fusion.9), kind=kOutput, calls=%fused_computation.24 | convolution fusion | flops 4940496896 | bytes 11173888 | tf_op jit(solution)/shard_map/dot_general | solution.py:22
  423.4 5.7 collective-permute-done.19
  429.1 4.4 fusion.1
  433.6 4.1 fusion.27
  445.1 28.9 %collective-permute-done.17 = bf16[256,1024]{1,0:T(8,128)(2,1)S(1)} collective-permute-done((bf16[256,1024]{1,0:T(8,128)(2,1)}, bf16[256,1024]{1,0:T(8,128)(2,1)S(1)}, u32[]{:S(2)}, u32[]{:S(2)}) %collective-permute-start.17) | collective-permute-done | bytes 524320 | tf_op jit(solution)/shard_map/ppermute | solution.py:294
  477.9 61.2 %all-reduce.4.cloned.1.call-done = bf16[512,2048]{1,0:T(8,128)(2,1)} async-done(((bf16[512,2048]{1,0:T(8,128)(2,1)}), bf16[512,2048]{1,0:T(8,128)(2,1)}) %all-reduce.4.cloned.1.call-update) | async-done | bytes 2097168 | tf_op jit(solution)/shard_map/psum | solution.py:423
  539.2 8.3 %convolution_convert_fusion.1 = bf16[1568,1024]{1,0:T(8,128)(2,1)S(1)} fusion(bf16[1568,1536]{1,0:T(8,128)(2,1)} %attend_back.1, bf16[1024,1536]{1,0:T(8,128)(2,1)} %bitcast.174), kind=kOutput, calls=%fused_computation.25 | convolution fusion | flops 4934107136 | bytes 11173888 | tf_op jit(solution)/shard_map/dot_general | solution.py:22
  558.9 10.9 %collective-permute-start.22 = (bf16[512,1,2048]{2,0,1:T(8,128)(2,1)}, bf16[512,1,2048]{2,0,1:T(8,128)(2,1)}, u32[]{:S(2)}, u32[]{:S(2)}) collective-permute-start(bf16[512,1,2048]{2,0,1:T(8,128)(2,1)} %bitcast.179), channel_id=1, source_target_pairs={{0,2},{2,0},{1,3},{3,1},{4,6},{6,4},{5,7},{7,5},{8,10},{10,8},{9,1... | collective-permute-start | bytes 6291464 | tf_op jit(solution)/shard_map/ppermute | solution.py:408
  573.5 4.5 fusion.14
  581.5 119.2 %all-reduce.6.cloned.1.call-done = (bf16[512,1536]{0,1:T(8,128)(2,1)}, bf16[256,1024]{1,0:T(8,128)(2,1)}, bf16[1024,1024]{1,0:T(8,128)(2,1)}) async-done(((bf16[512,1536]{0,1:T(8,128)(2,1)}, bf16[256,1024]{1,0:T(8,128)(2,1)}, bf16[1024,1024]{1,0:T(8,128)(2,1)}), (bf16[512,1536]{0,1:T(8,128)(2,1)}, bf16[256,1024]{1,0:T(8,128)(2,1)}, bf16[1024,1024]{1,0:T(8,128)(2,1)})) %all-reduce.6.cloned.1.call-update) | async-done | bytes 4194320 | tf_op jit(solution)/shard_map/psum | solution.py:430
  701.4 38.3 %psum.37 = f32[2,6144]{1,0:T(2,128)S(1)} all-reduce(f32[2,6144]{1,0:T(2,128)S(1)} %constant_dynamic-update-slice_fusion.1), channel_id=1, replica_groups=mesh['rz'=8,'core'=2,'half'=2,'gq'=1] {'rz','core','half','gq'}, use_global_device_ids=true, to_apply=%region_17.18 | all-reduce | flops 12288 | bytes 98304 | tf_op jit(solution)/shard_map/psum | solution.py:458
  742.6 7.0 convert_bitcast_fusion
  749.6 11.7 %reshape.418 = f32[512,2,1,2,1024]{4,3,0,1,2:T(2,128)} reshape(f32[512,2,1,2048]{3,0,2,1:T(8,128)} %convert_bitcast_fusion) | data formatting | bytes 16777216 | tf_op jit(solution)/shard_map/convert_element_type | solution.py:419
  761.4 15.4 %copy.67 = f32[512,2,1,2,1024]{4,1,3,0,2:T(2,128)} copy(f32[512,2,1,2,1024]{4,3,0,1,2:T(2,128)} %reshape.418) | data formatting | bytes 16777216 | tf_op jit(solution)/shard_map/convert_element_type | solution.py:419
  776.7 11.8 %reshape.412 = f32[512,4096]{1,0:T(8,128)} reshape(f32[512,2,1,2,1024]{4,3,1,0,2:T(2,128)} %bitcast.152) | data formatting | bytes 16777216 | tf_op jit(solution)/shard_map/convert_element_type | solution.py:419
  804.5 4.4 maximum_select_fusion.3
  808.9 4.7 bitcast_convert_fusion
  (215 shorter events, 128.2 us)
Async XLA Ops:
  7.2 36.2 %copy-start = (bf16[512,1024]{1,0:T(8,128)(2,1)S(1)}, bf16[512,1024]{1,0:T(8,128)(2,1)}, u32[]{:S(2)}) copy-start(bf16[512,1024]{1,0:T(8,128)(2,1)} %param.23) | copy-start | bytes 3145732
  7.2 531.9 %all-reduce.4.cloned.1.call-start = ((), (), s32[]{:S(2)}) async-start(), calls=%async_computation | async-start | bytes 4194304 | tf_op jit(solution)/shard_map/psum | solution.py:423
  7.3 29.2 %collective-permute-start = (bf16[784,1024]{1,0:T(8,128)(2,1)}, bf16[784,1024]{1,0:T(8,128)(2,1)}, u32[]{:S(2)}, u32[]{:S(2)}) collective-permute-start(bf16[784,1024]{1,0:T(8,128)(2,1)} %bitcast.224), channel_id=1, source_target_pairs={{0,0},{1,2},{2,1},{3,3},{4,4},{5,6},{6,5},{7,7},{8,8},{9,10},{10,9... | collective-permute-start | bytes 4816904 | tf_op jit(solution)/shard_map/ppermute | solution.py:344
  18.1 18.2 %collective-permute-start.1 = (f32[6144]{0:T(1024)S(1)}, f32[6144]{0:T(1024)S(1)}, u32[]{:S(2)}, u32[]{:S(2)}) collective-permute-start(f32[6144]{0:T(1024)S(1)} %constant_dynamic-update-slice_fusion.13), channel_id=1, source_target_pairs={{0,1},{1,0},{2,3},{3,2},{4,5},{5,4},{6,7},{7,6},{8,9},{9,8},{10,11... | collective-permute-start | bytes 73736 | tf_op jit(solution)/shard_map/ppermute | solution.py:294
  36.2 49.0 %collective-permute-start.3 = (bf16[512,1536]{0,1:T(8,128)(2,1)S(1)}, bf16[512,1536]{0,1:T(8,128)(2,1)}, u32[]{:S(2)}, u32[]{:S(2)}) collective-permute-start(bf16[512,1536]{0,1:T(8,128)(2,1)S(1)} %bitcast.160), channel_id=1, source_target_pairs={{0,1},{1,0},{2,3},{3,2},{4,5},{5,4},{6,7},{7,6},{8,9},{9,8},{10,11... | collective-permute-start | bytes 4718600 | tf_op jit(solution)/shard_map/ppermute | solution.py:294
  43.4 50.2 %collective-permute-start.2 = (bf16[784,1024]{1,0:T(8,128)(2,1)}, bf16[784,1024]{1,0:T(8,128)(2,1)}, u32[]{:S(2)}, u32[]{:S(2)}) collective-permute-start(bf16[784,1024]{1,0:T(8,128)(2,1)} %fusion.9), channel_id=1, source_target_pairs={{0,2},{2,0},{1,3},{3,1},{4,6},{6,4},{5,7},{7,5},{8,10},{10,8},{9,1... | collective-permute-start | bytes 4816904 | tf_op jit(solution)/shard_map/ppermute | solution.py:301
  44.3 39.5 %collective-permute-start.4 = (bf16[256,1024]{1,0:T(8,128)(2,1)}, bf16[256,1024]{1,0:T(8,128)(2,1)}, u32[]{:S(2)}, u32[]{:S(2)}) collective-permute-start(bf16[256,1024]{1,0:T(8,128)(2,1)} %fusion.47), channel_id=1, source_target_pairs={{0,1},{1,0},{2,3},{3,2},{4,5},{5,4},{6,7},{7,6},{8,9},{9,8},{10,11... | collective-permute-start | bytes 1572872 | tf_op jit(solution)/shard_map/ppermute | solution.py:294
  45.7 119.4 %collective-permute-start.7 = (bf16[784,1024]{1,0:T(8,128)(2,1)}, bf16[784,1024]{1,0:T(8,128)(2,1)}, u32[]{:S(2)}, u32[]{:S(2)}) collective-permute-start(bf16[784,1024]{1,0:T(8,128)(2,1)} %bitcast.19), channel_id=1, source_target_pairs={{0,0},{1,2},{2,1},{3,3},{4,4},{5,6},{6,5},{7,7},{8,8},{9,10},{10,9... | collective-permute-start | bytes 4816904 | tf_op jit(solution)/shard_map/ppermute | solution.py:354
  153.5 12.5 %collective-permute-start.5 = (bf16[784,1024]{1,0:T(8,128)(2,1)}, bf16[784,1024]{1,0:T(8,128)(2,1)S(1)}, u32[]{:S(2)}, u32[]{:S(2)}) collective-permute-start(bf16[784,1024]{1,0:T(8,128)(2,1)} %convolution_convert_fusion.3), channel_id=1, source_target_pairs={{0,2},{2,0},{1,3},{3,1},{4,6},{6,4},{5,7},{7,5},{8,10},{10,8},{9,1... | collective-permute-start | bytes 4816904 | tf_op jit(solution)/shard_map/ppermute | solution.py:369
  161.8 46.8 %collective-permute-start.9 = (bf16[512,2048]{0,1:T(8,128)(2,1)S(1)}, bf16[512,2048]{0,1:T(8,128)(2,1)S(1)}, u32[]{:S(2)}, u32[]{:S(2)}) collective-permute-start(bf16[512,2048]{0,1:T(8,128)(2,1)S(1)} %bitcast.158), channel_id=1, source_target_pairs={{0,1},{1,0},{2,3},{3,2},{4,5},{5,4},{6,7},{7,6},{8,9},{9,8},{10,11... | collective-permute-start | bytes 6291464 | tf_op jit(solution)/shard_map/ppermute | solution.py:294
  164.2 89.4 %collective-permute-start.10 = (bf16[1024,1024]{1,0:T(8,128)(2,1)}, bf16[1024,1024]{1,0:T(8,128)(2,1)}, u32[]{:S(2)}, u32[]{:S(2)}) collective-permute-start(bf16[1024,1024]{1,0:T(8,128)(2,1)} %fusion.46), channel_id=1, source_target_pairs={{0,1},{1,0},{2,3},{3,2},{4,5},{5,4},{6,7},{7,6},{8,9},{9,8},{10,11... | collective-permute-start | bytes 6291464 | tf_op jit(solution)/shard_map/ppermute | solution.py:294
  165.0 93.0 %collective-permute-start.8 = (bf16[784,1024]{1,0:T(8,128)(2,1)}, bf16[784,1024]{1,0:T(8,128)(2,1)}, u32[]{:S(2)}, u32[]{:S(2)}) collective-permute-start(bf16[784,1024]{1,0:T(8,128)(2,1)} %collective-permute-done.7), channel_id=1, source_target_pairs={{0,2},{2,0},{1,3},{3,1},{4,6},{6,4},{5,7},{7,5},{8,10},{10,8},{9,1... | collective-permute-start | bytes 4816904 | tf_op jit(solution)/shard_map/ppermute | solution.py:301
  170.9 91.0 %collective-permute-start.6 = (bf16[784,1024]{1,0:T(8,128)(2,1)}, bf16[784,1024]{1,0:T(8,128)(2,1)}, u32[]{:S(2)}, u32[]{:S(2)}) collective-permute-start(bf16[784,1024]{1,0:T(8,128)(2,1)} %add_convert_fusion.2), channel_id=1, source_target_pairs={{0,2},{2,0},{1,3},{3,1},{4,6},{6,4},{5,7},{7,5},{8,10},{10,8},{9,1... | collective-permute-start | bytes 4816904 | tf_op jit(solution)/shard_map/ppermute | solution.py:301
  321.5 4.5 collective-permute-start.13
  324.5 3.8 collective-permute-start.11
  333.3 6.6 collective-permute-start.14
  337.0 102.4 %collective-permute-start.23 = (bf16[1024,1024]{1,0:T(8,128)(2,1)}, bf16[1024,1024]{1,0:T(8,128)(2,1)}, u32[]{:S(2)}, u32[]{:S(2)}) collective-permute-start(bf16[1024,1024]{1,0:T(8,128)(2,1)} %dynamic-slice_bitcast_fusion), channel_id=1, source_target_pairs={{0,1},{1,0},{2,3},{3,2},{4,5},{5,4},{6,7},{7,6},{8,9},{9,8},{10,11... | collective-permute-start | bytes 6291464 | tf_op jit(solution)/shard_map/ppermute | solution.py:294
  339.3 89.8 %collective-permute-start.19 = (bf16[512,2048]{1,0:T(8,128)(2,1)}, bf16[512,2048]{1,0:T(8,128)(2,1)}, u32[]{:S(2)}, u32[]{:S(2)}) collective-permute-start(bf16[512,2048]{1,0:T(8,128)(2,1)} %dynamic-slice_bitcast_fusion.1), channel_id=1, source_target_pairs={{0,1},{1,0},{2,3},{3,2},{4,5},{5,4},{6,7},{7,6},{8,9},{9,8},{10,11... | collective-permute-start | bytes 6291464 | tf_op jit(solution)/shard_map/ppermute | solution.py:294
  422.5 52.5 %collective-permute-start.18 = (bf16[512,1536]{0,1:T(8,128)(2,1)}, bf16[512,1536]{0,1:T(8,128)(2,1)}, u32[]{:S(2)}, u32[]{:S(2)}) collective-permute-start(bf16[512,1536]{0,1:T(8,128)(2,1)} %bitcast.186), channel_id=1, source_target_pairs={{0,1},{1,0},{2,3},{3,2},{4,5},{5,4},{6,7},{7,6},{8,9},{9,8},{10,11... | collective-permute-start | bytes 4718600 | tf_op jit(solution)/shard_map/ppermute | solution.py:294
  433.6 267.1 %all-reduce.6.cloned.1.call-start = ((), (), s32[]{:S(2)}) async-start(), calls=%async_computation.1 | async-start | bytes 8388608 | tf_op jit(solution)/shard_map/psum | solution.py:430
  438.6 35.3 %collective-permute-start.17 = (bf16[256,1024]{1,0:T(8,128)(2,1)}, bf16[256,1024]{1,0:T(8,128)(2,1)S(1)}, u32[]{:S(2)}, u32[]{:S(2)}) collective-permute-start(bf16[256,1024]{1,0:T(8,128)(2,1)} %dynamic-slice_bitcast_fusion.2), channel_id=1, source_target_pairs={{0,1},{1,0},{2,3},{3,2},{4,5},{5,4},{6,7},{7,6},{8,9},{9,8},{10,11... | collective-permute-start | bytes 1572872 | tf_op jit(solution)/shard_map/ppermute | solution.py:294
  550.4 19.4 %copy-start.18 = (f32[784]{0:T(1024)S(1)}, f32[784]{0:T(1024)}, u32[]{:S(2)}) copy-start(f32[784]{0:T(1024)} %copy-done.17) | copy-start | bytes 9412
  550.4 19.4 %copy-start.20 = (f32[1,4,2,128]{3,1,2,0:T(4,128)S(1)}, f32[1,4,2,128]{3,1,2,0:T(4,128)}, u32[]{:S(2)}) copy-start(f32[1,4,2,128]{3,1,2,0:T(4,128)} %copy-done.19) | copy-start | bytes 12292
  550.4 19.4 %copy-start.22 = (f32[784]{0:T(1024)S(1)}, f32[784]{0:T(1024)}, u32[]{:S(2)}) copy-start(f32[784]{0:T(1024)} %copy-done.21) | copy-start | bytes 9412
  550.4 19.4 %collective-permute-start.15 = (bf16[784,1024]{1,0:T(8,128)(2,1)}, bf16[784,1024]{1,0:T(8,128)(2,1)S(1)}, u32[]{:S(2)}, u32[]{:S(2)}) collective-permute-start(bf16[784,1024]{1,0:T(8,128)(2,1)} %slice.170), channel_id=1, source_target_pairs={{0,2},{2,0},{1,3},{3,1},{4,6},{6,4},{5,7},{7,5},{8,10},{10,8},{9,1... | collective-permute-start | bytes 4816904 | tf_op jit(solution)/shard_map/ppermute | solution.py:306
  552.7 28.8 %collective-permute-start.12 = (bf16[784,1024]{1,0:T(8,128)(2,1)}, bf16[784,1024]{1,0:T(8,128)(2,1)}, u32[]{:S(2)}, u32[]{:S(2)}) collective-permute-start(bf16[784,1024]{1,0:T(8,128)(2,1)} %get-tuple-element.68), channel_id=1, source_target_pairs={{0,0},{2,1},{1,2},{3,3},{4,4},{6,5},{5,6},{7,7},{8,8},{10,9},{9,10... | collective-permute-start | bytes 4816904 | tf_op jit(solution)/shard_map/ppermute | solution.py:381
  558.9 183.7 %collective-permute-start.22 = (bf16[512,1,2048]{2,0,1:T(8,128)(2,1)}, bf16[512,1,2048]{2,0,1:T(8,128)(2,1)}, u32[]{:S(2)}, u32[]{:S(2)}) collective-permute-start(bf16[512,1,2048]{2,0,1:T(8,128)(2,1)} %bitcast.179), channel_id=1, source_target_pairs={{0,2},{2,0},{1,3},{3,1},{4,6},{6,4},{5,7},{7,5},{8,10},{10,8},{9,1... | collective-permute-start | bytes 6291464 | tf_op jit(solution)/shard_map/ppermute | solution.py:408
  578.0 210.6 %collective-permute-start.16 = (bf16[784,1024]{1,0:T(8,128)(2,1)}, bf16[784,1024]{1,0:T(8,128)(2,1)S(1)}, u32[]{:S(2)}, u32[]{:S(2)}) collective-permute-start(bf16[784,1024]{1,0:T(8,128)(2,1)} %fusion.14), channel_id=1, source_target_pairs={{0,0},{2,1},{1,2},{3,3},{4,4},{6,5},{5,6},{7,7},{8,8},{10,9},{9,10... | collective-permute-start | bytes 4816904 | tf_op jit(solution)/shard_map/ppermute | solution.py:398
  700.7 92.1 %collective-permute-start.20 = (bf16[512,1,1536]{0,2,1:T(8,128)(2,1)}, bf16[512,1,1536]{0,2,1:T(8,128)(2,1)}, u32[]{:S(2)}, u32[]{:S(2)}) collective-permute-start(bf16[512,1,1536]{0,2,1:T(8,128)(2,1)} %bitcast.187), channel_id=1, source_target_pairs={{0,2},{2,0},{1,3},{3,1},{4,6},{6,4},{5,7},{7,5},{8,10},{10,8},{9,1... | collective-permute-start | bytes 4718600 | tf_op jit(solution)/shard_map/ppermute | solution.py:408
  740.5 48.2 %collective-permute-start.21 = (bf16[256,1024]{1,0:T(8,128)(2,1)}, bf16[256,1024]{1,0:T(8,128)(2,1)S(1)}, u32[]{:S(2)}, u32[]{:S(2)}) collective-permute-start(bf16[256,1024]{1,0:T(8,128)(2,1)} %get-tuple-element.63), channel_id=1, source_target_pairs={{0,2},{2,0},{1,3},{3,1},{4,6},{6,4},{5,7},{7,5},{8,10},{10,8},{9,1... | collective-permute-start | bytes 1572872 | tf_op jit(solution)/shard_map/ppermute | solution.py:408
  776.7 12.7 %copy-start.15 = (bf16[256,1024]{1,0:T(8,128)(2,1)S(1)}, bf16[256,1024]{1,0:T(8,128)(2,1)}, u32[]{:S(2)}) copy-start(bf16[256,1024]{1,0:T(8,128)(2,1)} %get-tuple-element.63) | copy-start | bytes 1572868
  788.6 16.0 %collective-permute-start.24 = (bf16[1024,1024]{1,0:T(8,128)(2,1)}, bf16[1024,1024]{1,0:T(8,128)(2,1)}, u32[]{:S(2)}, u32[]{:S(2)}) collective-permute-start(bf16[1024,1024]{1,0:T(8,128)(2,1)} %get-tuple-element.64), channel_id=1, source_target_pairs={{0,2},{2,0},{1,3},{3,1},{4,6},{6,4},{5,7},{7,5},{8,10},{10,8},{9,1... | collective-permute-start | bytes 6291464 | tf_op jit(solution)/shard_map/ppermute | solution.py:408
  (20 other events, 103.3 us)
Sparse Core Ops, SparseCore 0:
  433.7 105.4 all-reduce.3
  543.7 156.9 all-reduce.5

commit v2 on v1

v2 whole, which is shorter than its diff:
```python
import functools

import jax
import jax.numpy as jnp
from jax import lax
from jax.experimental import pallas as pl
from jax.experimental.pallas import tpu as pltpu
from jax.sharding import Mesh
from jax.sharding import PartitionSpec as P

HEAD_DIM = 64
PAIR = 2 * HEAD_DIM
EPS = 1e-06
LOG2E = 1.4426950408889634
F32 = jnp.float32
BF16 = jnp.bfloat16
SWAP = [(0, 1), (1, 0)]
VMEM_LIMIT = 62 << 20


def contract(left, right, left_dim, right_dim):
    return lax.dot_general(
        left, right, (((left_dim,), (right_dim,)), ((), ())), preferred_element_type=F32
    )


def attend_kernel(tile, rows, padded, qkv_ref, out_ref, lse_ref, q_t, v_t, out_t):
    scale = HEAD_DIM**-0.5 * LOG2E
    ones = jnp.ones((16, rows), BF16)
    q_t[:, :rows] = qkv_ref[:, :PAIR].T
    if padded > rows:
        q_t[:, rows:] = jnp.zeros((PAIR, padded - rows), BF16)
    values_t = qkv_ref[:, 2 * PAIR :].T
    step = HEAD_DIM + 16
    for head in range(2):
        v_t[head * step : head * step + HEAD_DIM, :] = values_t[
            head * HEAD_DIM : (head + 1) * HEAD_DIM, :
        ]
        v_t[head * step + HEAD_DIM : (head + 1) * step, :] = ones

    def block(index, carry):
        columns = pl.ds(pl.multiple_of(index * tile, tile), tile)
        empty = jnp.zeros((HEAD_DIM, tile), BF16)
        for head in range(2):
            lanes = slice(head * HEAD_DIM, (head + 1) * HEAD_DIM)
            query = q_t[lanes, columns]
            query = jnp.concatenate([query, empty] if head == 0 else [empty, query], axis=0)
            scores = contract(qkv_ref[:, PAIR : 2 * PAIR], query, 1, 0)
            highest = jnp.max(scores, axis=0, keepdims=True) * scale
            expon = jnp.exp2(scores * scale - highest).astype(BF16)
            mixed = contract(v_t[head * step : (head + 1) * step, :], expon, 1, 0)
            total = mixed[HEAD_DIM : HEAD_DIM + 1, :]
            out_t[lanes, columns] = mixed[:HEAD_DIM, :] / total
            lse_ref[head : head + 1, columns] = highest + jnp.log2(total)
        return carry

    lax.fori_loop(0, padded // tile, block, 0)
    out_ref[...] = out_t[...].T[:rows, :].astype(BF16)


def attend(qkv, first_pair, last_pair, kept=None, tile=512):
    rows, width = qkv.shape
    pairs = width // (3 * PAIR)
    padded = -(-rows // tile) * tile
    count = last_pair - first_pair
    kernel = functools.partial(attend_kernel, tile, rows, padded)
    anywhere = pl.BlockSpec(memory_space=pl.ANY)
    return pl.pallas_call(
        kernel if kept is None else lambda ref, a, b, *rest: kernel(ref, *rest),
        grid=(count,),
        in_specs=[pl.BlockSpec((rows, 3 * PAIR), lambda i: (0, i + first_pair))]
        + ([] if kept is None else [anywhere] * 2),
        out_specs=[
            pl.BlockSpec((rows, PAIR), lambda i: (0, i + first_pair)),
            pl.BlockSpec((None, 2, padded), lambda i: (i + first_pair, 0, 0)),
        ],
        out_shape=[
            jax.ShapeDtypeStruct((rows, pairs * PAIR), BF16),
            jax.ShapeDtypeStruct((pairs, 2, padded), F32),
        ],
        scratch_shapes=[
            pltpu.VMEM((PAIR, padded), BF16),
            pltpu.VMEM((PAIR + 32, rows), BF16),
            pltpu.VMEM((PAIR, padded), F32),
        ],
        input_output_aliases={} if kept is None else {1: 0, 2: 1},
        compiler_params=pltpu.CompilerParams(vmem_limit_bytes=VMEM_LIMIT),
        cost_estimate=pl.CostEstimate(
            flops=64 * rows * rows * PAIR * count,
            bytes_accessed=8 * rows * PAIR * count,
            transcendentals=2 * rows * rows * count,
        ),
        name="attend",
    )(qkv, *(() if kept is None else kept))


def attend_back_kernel(
    tile, rows, padded, qkv_ref, grad_ref, out_ref, lse_ref, dqkv_ref, q_t, g_t, k_t, delta,
    dq_t, dk_t, dv_t,
):
    scale = HEAD_DIM**-0.5
    q_t[:, :rows] = qkv_ref[:, :PAIR].T
    g_t[:, :rows] = grad_ref[...].T
    if padded > rows:
        q_t[:, rows:] = jnp.zeros((PAIR, padded - rows), BF16)
        g_t[:, rows:] = jnp.zeros((PAIR, padded - rows), BF16)
        delta[:, rows:] = jnp.zeros((2, padded - rows), F32)
    k_t[...] = qkv_ref[:, PAIR : 2 * PAIR].T
    product = (grad_ref[...].astype(F32) * out_ref[...].astype(F32)).T
    delta[0:1, :rows] = jnp.sum(product[:HEAD_DIM, :], axis=0, keepdims=True)
    delta[1:2, :rows] = jnp.sum(product[HEAD_DIM:, :], axis=0, keepdims=True)
    dk_t[...] = jnp.zeros_like(dk_t)
    dv_t[...] = jnp.zeros_like(dv_t)

    def block(index, carry):
        columns = pl.ds(pl.multiple_of(index * tile, tile), tile)
        empty = jnp.zeros((HEAD_DIM, tile), BF16)
        for head in range(2):
            lanes = slice(head * HEAD_DIM, (head + 1) * HEAD_DIM)
            query = q_t[lanes, columns]
            grad = g_t[lanes, columns]
            query_pad = jnp.concatenate([query, empty] if head == 0 else [empty, query], axis=0)
            grad_pad = jnp.concatenate([grad, empty] if head == 0 else [empty, grad], axis=0)
            scores = contract(qkv_ref[:, PAIR : 2 * PAIR], query_pad, 1, 0)
            grad_probs = contract(qkv_ref[:, 2 * PAIR :], grad_pad, 1, 0)
            weights = jnp.exp2(scores * (scale * LOG2E) - lse_ref[head : head + 1, columns])
            grad_scores = (weights * (grad_probs - delta[head : head + 1, columns])).astype(BF16)
            dv_t[lanes, :] += contract(grad, weights.astype(BF16), 1, 1)
            dq_t[lanes, columns] = contract(k_t[lanes, :], grad_scores, 1, 0)
            dk_t[lanes, :] += contract(query, grad_scores, 1, 1)
        return carry

    lax.fori_loop(0, padded // tile, block, 0)
    dqkv_ref[:, :PAIR] = (dq_t[...].T[:rows, :] * scale).astype(BF16)
    dqkv_ref[:, PAIR : 2 * PAIR] = (dk_t[...].T * scale).astype(BF16)
    dqkv_ref[:, 2 * PAIR :] = dv_t[...].T.astype(BF16)


def attend_back(qkv, grad, out, lse, first_pair, last_pair, tile=256):
    rows, width = qkv.shape
    padded = -(-rows // tile) * tile
    count = last_pair - first_pair
    return pl.pallas_call(
        functools.partial(attend_back_kernel, tile, rows, padded),
        grid=(count,),
        in_specs=[
            pl.BlockSpec((rows, 3 * PAIR), lambda i: (0, i + first_pair)),
            pl.BlockSpec((rows, PAIR), lambda i: (0, i + first_pair)),
            pl.BlockSpec((rows, PAIR), lambda i: (0, i + first_pair)),
            pl.BlockSpec((None, 2, lse.shape[2]), lambda i: (i + first_pair, 0, 0)),
        ],
        out_specs=pl.BlockSpec((rows, 3 * PAIR), lambda i: (0, i)),
        out_shape=jax.ShapeDtypeStruct((rows, 3 * PAIR * count), BF16),
        scratch_shapes=[
            pltpu.VMEM((PAIR, padded), BF16),
            pltpu.VMEM((PAIR, padded), BF16),
            pltpu.VMEM((PAIR, rows), BF16),
            pltpu.VMEM((2, padded), F32),
            pltpu.VMEM((PAIR, padded), F32),
            pltpu.VMEM((PAIR, rows), F32),
            pltpu.VMEM((PAIR, rows), F32),
        ],
        compiler_params=pltpu.CompilerParams(vmem_limit_bytes=VMEM_LIMIT),
        cost_estimate=pl.CostEstimate(
            flops=160 * rows * rows * PAIR * count,
            bytes_accessed=16 * rows * PAIR * count,
            transcendentals=2 * rows * rows * count,
        ),
        name="attend_back",
    )(qkv, grad, out, lse)


def feed_kernel(
    half_ref, *refs, parts, make, chunk,
):
    xs, refs = refs[:parts], refs[parts:]
    dys, refs = refs[:parts], refs[parts:]
    if not make:
        x_t, refs = refs[0], refs[1:]
    up_ref, bias_ref, down_ref, *refs = refs
    hidden_ref, d_pre_ref, up_send, up_keep, down_send, down_keep, bias_grad_ref, *refs = refs
    if make:
        x_t, refs = refs[0], refs[1:]
    x, dy, sems = refs
    index = pl.program_id(0)
    half = half_ref[0]
    rows, width = x.shape
    block = rows // parts
    own = width // 2
    tile = up_ref.shape[1]

    @pl.when(index == 0)
    def _():
        copies = []
        for i in range(parts):
            part = pl.ds(i * block, block)
            copies.append(pltpu.make_async_copy(xs[i], x.at[part], sems.at[i]))
            copies.append(pltpu.make_async_copy(dys[i], dy.at[part], sems.at[parts + i]))
        for copy in copies:
            copy.start()
        for copy in copies:
            copy.wait()
        if make:
            x_t[...] = x[...].T

    bias_grad = jnp.zeros(bias_grad_ref.shape, F32)
    for start in range(0, rows, chunk):
        part = slice(start, start + chunk)
        pre = contract(x[part, :], up_ref[...], 1, 0) + bias_ref[...]
        d_hidden = contract(dy[part, :], down_ref[...], 1, 1)
        share = 0.5 * (1.0 + lax.erf(pre * 0.7071067811865476))
        hidden_ref[part, :] = (pre * share).astype(BF16)
        slope = share + pre * (jnp.exp(-0.5 * pre * pre) * 0.3989422804014327)
        d_low = (d_hidden * slope).astype(BF16)
        d_pre_ref[part, :] = d_low
        bias_grad = bias_grad + jnp.sum(d_low.astype(F32), axis=0, keepdims=True)
    bias_grad_ref[...] = bias_grad
    columns = pl.ds(pl.multiple_of(index * tile, tile), tile)
    mine = pl.ds(pl.multiple_of(half * own, own), own)
    theirs = pl.ds(pl.multiple_of((1 - half) * own, own), own)
    up_keep[:, columns] = contract(x_t[mine, :], d_pre_ref[...], 1, 0).astype(BF16)
    up_send[:, columns] = contract(x_t[theirs, :], d_pre_ref[...], 1, 0).astype(BF16)
    down_grad = contract(hidden_ref[...], dy[...], 0, 0).astype(BF16)

    @pl.when(index == half)
    def _():
        down_keep[...] = down_grad

    @pl.when(index != half)
    def _():
        down_send[...] = down_grad


def feed(half, xs, dys, x_t, up, bias, down):
    parts = len(xs)
    width = xs[0].shape[1]
    rows = sum(part.shape[0] for part in xs)
    hidden = up.shape[1]
    tile = hidden // 2
    make = x_t is None
    chunk = rows // 2 if rows % 32 == 0 else rows
    anywhere = pl.BlockSpec(memory_space=pl.ANY)
    fixed = lambda shape: pl.BlockSpec(shape, lambda j, s: (0, 0), pipeline_mode=pl.Buffered(1))
    across = lambda size: pl.BlockSpec((size, tile), lambda j, s: (0, j))
    out_specs = [across(rows)] * 2 + [fixed((width // 2, hidden))] * 2
    out_specs += [fixed((tile, width))] * 2 + [across(1)]
    out_shape = [
        jax.ShapeDtypeStruct((rows, hidden), BF16),
        jax.ShapeDtypeStruct((rows, hidden), BF16),
        jax.ShapeDtypeStruct((width // 2, hidden), BF16),
        jax.ShapeDtypeStruct((width // 2, hidden), BF16),
        jax.ShapeDtypeStruct((tile, width), BF16),
        jax.ShapeDtypeStruct((tile, width), BF16),
        jax.ShapeDtypeStruct((1, hidden), F32),
    ]
    if make:
        out_specs.append(fixed((width, rows)))
        out_shape.append(jax.ShapeDtypeStruct((width, rows), BF16))
    return pl.pallas_call(
        functools.partial(feed_kernel, parts=parts, make=make, chunk=chunk),
        grid_spec=pltpu.PrefetchScalarGridSpec(
            num_scalar_prefetch=1,
            grid=(2,),
            in_specs=[anywhere] * (2 * parts)
            + ([] if make else [fixed((width, rows))])
            + [across(width), across(1), pl.BlockSpec((tile, width), lambda j, s: (j, 0))],
            out_specs=out_specs,
            scratch_shapes=[
                pltpu.VMEM((rows, width), BF16),
                pltpu.VMEM((rows, width), BF16),
                pltpu.SemaphoreType.DMA((2 * parts,)),
            ],
        ),
        out_shape=out_shape,
        compiler_params=pltpu.CompilerParams(vmem_limit_bytes=VMEM_LIMIT),
        cost_estimate=pl.CostEstimate(
            flops=8 * rows * width * hidden,
            bytes_accessed=8 * rows * width + 8 * width * hidden,
            transcendentals=2 * rows * hidden,
        ),
        name="feed",
    )(half.reshape(1), *xs, *dys, *(() if make else (x_t,)), up, bias, down)


def finish_feed_kernel(core_ref, *refs, ranges, tile):
    owns, refs = refs[: 2 * ranges], refs[2 * ranges :]
    others, (up_out, down_out) = refs[: 2 * ranges], refs[2 * ranges :]
    first = core_ref[0] == 0
    for j in range(ranges):
        for kind in range(2):
            own, other = owns[2 * j + kind][...], others[2 * j + kind][...]
            values = (jnp.where(first, own, other), jnp.where(first, other, own))
            for c in range(2):
                wide = values[c].astype(F32)
                if kind == 1:
                    down_out[c, j] = wide
                    continue
                for h in range(2):
                    start = ((h * 2 + c) * ranges + j) * tile
                    up_out[:, start : start + tile] = wide[:, h * tile : (h + 1) * tile]


def finish_feed(core, owns, others):
    ranges = len(owns) // 2
    rows, columns = owns[0].shape
    tile, width = owns[1].shape
    steps = 4
    up_spec = pl.BlockSpec((rows // steps, columns), lambda i, s: (i, 0))
    down_spec = pl.BlockSpec((tile // steps, width), lambda i, s: (i, 0))
    up, down = pl.pallas_call(
        functools.partial(finish_feed_kernel, ranges=ranges, tile=tile),
        grid_spec=pltpu.PrefetchScalarGridSpec(
            num_scalar_prefetch=1,
            grid=(steps,),
            in_specs=[up_spec, down_spec] * (2 * ranges),
            out_specs=[
                pl.BlockSpec((rows // steps, 2 * ranges * columns), lambda i, s: (i, 0)),
                pl.BlockSpec((2, ranges, tile // steps, width), lambda i, s: (0, 0, i, 0)),
            ],
        ),
        out_shape=[
            jax.ShapeDtypeStruct((rows, 2 * ranges * columns), F32),
            jax.ShapeDtypeStruct((2, ranges, tile, width), F32),
        ],
        compiler_params=pltpu.CompilerParams(vmem_limit_bytes=VMEM_LIMIT),
        name="finish_feed",
    )(core.reshape(1), *owns, *others)
    return up, down.reshape(2 * ranges * tile, width)


def finish_qkv_kernel(core_ref, *refs, pairs):
    owns, others, outs = refs[:2], refs[2:4], refs[4:]
    first = core_ref[0] == 0
    for h in range(2):
        own, other = owns[h][...], others[h][...]
        values = (jnp.where(first, own, other), jnp.where(first, other, own))
        for c in range(2):
            for p in range(pairs):
                for i in range(3):
                    start = (p * 3 + i) * PAIR
                    goal = ((h * 2 + c) * pairs + p) * PAIR
                    outs[i][:, goal : goal + PAIR] = values[c][:, start : start + PAIR].astype(F32)


def finish_qkv(core, owns, others):
    rows, columns = owns[0].shape
    pairs = columns // (3 * PAIR)
    steps = 4
    spec = pl.BlockSpec((rows // steps, columns), lambda i, s: (i, 0))
    return pl.pallas_call(
        functools.partial(finish_qkv_kernel, pairs=pairs),
        grid_spec=pltpu.PrefetchScalarGridSpec(
            num_scalar_prefetch=1,
            grid=(steps,),
            in_specs=[spec] * 4,
            out_specs=[pl.BlockSpec((rows // steps, 4 * pairs * PAIR), lambda i, s: (i, 0))] * 3,
        ),
        out_shape=[jax.ShapeDtypeStruct((rows, 4 * pairs * PAIR), F32)] * 3,
        compiler_params=pltpu.CompilerParams(vmem_limit_bytes=VMEM_LIMIT),
        name="finish_qkv",
    )(core.reshape(1), *owns, *others)


def norm_parts(values, gain, shift):
    average = jnp.mean(values, axis=-1, keepdims=True)
    centred = values - average
    spread = jnp.mean(centred * centred, axis=-1, keepdims=True)
    inverse = lax.rsqrt(spread + EPS)
    normed = centred * inverse
    return (normed * gain + shift, normed, inverse)


def norm_back(grad, normed, inverse, gain):
    scaled = grad * gain
    first_term = jnp.mean(scaled, axis=-1, keepdims=True)
    second_term = jnp.mean(scaled * normed, axis=-1, keepdims=True)
    result = inverse * (scaled - first_term - normed * second_term)
    return (result, jnp.sum(grad * normed, axis=0), jnp.sum(grad, axis=0))


def pick(values, index, axis):
    return lax.dynamic_index_in_dim(values, index, axis, keepdims=False)


def join(own, other, index):
    return jnp.where(index == 0, jnp.stack([own, other]), jnp.stack([other, own]))


def after(values, *earlier):
    return lax.optimization_barrier((values,) + earlier)[0]


def body(
    rep, grp, tokens, query_weight, key_weight, value_weight, query_bias, value_bias, out_weight,
    out_bias, first_gain, first_shift, second_gain, second_shift, up_weight, up_bias,
    down_weight, down_bias, cotangent,
):
    clips, local, width = tokens.shape
    assert clips == 1
    quarter = grp // 2
    ring = rep // 2
    deep = ring // 2
    core = lax.axis_index("core")
    half = lax.axis_index("half")
    gq = lax.axis_index("gq")
    place = lax.axis_index("rz")
    low = place % 2
    high = place // 2
    own_rows = width // grp
    pairs = own_rows // PAIR
    hidden = up_weight.shape[1]
    set_hidden = hidden // grp
    ranges = max(1, set_hidden // width)
    tile = set_hidden // (2 * ranges)

    there = []
    for b in range(2):
        for h in range(2):
            for q in range(quarter):
                g = h * quarter + q
                source = (b * 2 + h) * quarter + q
                target = ((g % 2) * 2 + b) * quarter + g // 2
                if source != target:
                    there.append((source, target))
    back = [(target, source) for source, target in there]
    block = half * quarter + gq
    stays = (block % 2 == core) & (block // 2 == gq) & (half == core)
    axes = ("core", "half", "gq")
    beside = [(i, i ^ 1) for i in range(ring)]

    def move(values, route):
        return jnp.where(stays, values, lax.ppermute(values, axes, route))

    def swap_half(values):
        return lax.ppermute(values, "half", SWAP)

    def swap_core(values):
        return lax.ppermute(values, "core", SWAP)

    def spread(values):
        if grp == 2:
            return [values, swap_core(values)]
        return [lax.all_gather(values, ("gq", "core"), axis=0, tiled=True)]

    def collect(values):
        if grp == 2:
            other = swap_core(values(slice(local, None)).astype(BF16))
            return values(slice(None, local)) + other.astype(F32)
        return lax.psum_scatter(
            values(slice(None)).astype(BF16), ("gq", "core"), scatter_dimension=0, tiled=True
        ).astype(F32)

    def other_half(pieces):
        mine = pick(jnp.stack(pieces), low, 0)
        first = swap_half(mine)
        second = lax.ppermute(first, "rz", beside)
        return first, jnp.where(low == 0, first, second), jnp.where(low == 0, second, first)

    def by_half(own, other):
        return join(own, other, half).reshape(-1, own.shape[-1])

    def set_columns(values, inner=1):
        parts = values.reshape(values.shape[0], 2, quarter, 2, inner, -1)
        return pick(parts, core, 3).transpose(0, 2, 3, 1, 4)

    def gather_rows(values):
        if quarter > 1:
            values = lax.all_to_all(values, "gq", split_axis=1, concat_axis=0, tiled=True)
        return values.reshape(-1, values.shape[-1])

    def set_entries(values, inner=1):
        parts = values.reshape(2, quarter, 2, inner, -1)
        return pick(pick(parts, core, 2), gq, 1).transpose(1, 0, 2).reshape(inner, 1, -1)

    clip_tokens = move(tokens.reshape(local, width), there)
    vectors = jnp.concatenate(
        [query_bias, value_bias, out_bias, first_gain, first_shift, second_gain, second_shift,
         down_bias, up_bias]
    )
    if quarter > 1:
        vectors = lax.all_gather(vectors, "gq", axis=0)
    vectors = join(vectors, swap_half(vectors), half).reshape(grp, -1)
    (full_qbias, full_vbias, full_obias, gain_one, shift_one, gain_two, shift_two, full_dbias) = [
        vectors[:, i * own_rows : (i + 1) * own_rows].reshape(-1) for i in range(8)
    ]
    bias_sets = set_entries(vectors[:, 8 * own_rows :].reshape(-1), ranges)

    parts = [
        set_columns(w).reshape(own_rows, quarter, pairs, PAIR)
        for w in (query_weight, key_weight, value_weight)
    ]
    own_qkv = gather_rows(jnp.stack(parts, axis=3).reshape(own_rows, quarter, 3 * own_rows))
    own_qkv = own_qkv.reshape(2, -1, 3 * own_rows)
    qkv_x, low_rows, high_rows = other_half([own_qkv[0], own_qkv[1]])
    qkv_weight = by_half(
        own_qkv.reshape(-1, 3 * own_rows), jnp.concatenate([low_rows, high_rows], axis=0)
    )
    own_out = pick(out_weight.reshape(2, -1, width), core, 0)
    out_x, low_rows, high_rows = other_half(
        [after(own_out, qkv_x)[: own_rows // 4], own_out[own_rows // 4 :]]
    )
    out_set = by_half(own_out, jnp.concatenate([low_rows, high_rows], axis=0))

    own_up = set_columns(up_weight, ranges)
    own_down = pick(down_weight.reshape(2, ranges, tile, width), core, 0)
    up_sets, down_sets, stages = [], [], [out_x]
    for j in range(ranges):
        up_part = gather_rows(own_up[:, :, j].reshape(own_rows, quarter, 2 * tile))
        down_part = own_down[j]
        if up_part.shape == down_part.shape:
            stage, other_up, other_down = other_half([after(up_part, stages[-1]), down_part])
        else:
            stage, other_up = swap_half(after(up_part, stages[-1])), None
            other_up, other_down = stage, swap_half(down_part)
        stages.append(stage)
        up_sets.append(by_half(up_part, other_up))
        down_sets.append(by_half(down_part, other_down))
    grad_out = move(after(cotangent.reshape(local, width), stages[1]), there)

    zeros = jnp.zeros((1, own_rows), F32)
    qkv_bias = jnp.stack(
        [
            b.reshape(pairs, PAIR)
            for b in (set_entries(full_qbias), zeros, set_entries(full_vbias))
        ],
        axis=1,
    ).reshape(1, 3 * own_rows)

    inputs = clip_tokens.astype(F32)
    first_norm, first_normed, first_inverse = norm_parts(inputs, gain_one, shift_one)
    first = jnp.concatenate(spread(first_norm.astype(BF16)), axis=0)
    qkv = (contract(first, qkv_weight, 1, 0) + qkv_bias).astype(BF16)
    if pairs > 1:
        kept = attend(qkv, 0, pairs // 2)
        mixed, lse = attend(qkv, pairs // 2, pairs, kept)
    else:
        mixed, lse = attend(qkv, 0, pairs)
    middle = collect(lambda rows: contract(mixed[rows], out_set, 1, 0)) + inputs + full_obias
    second_norm, second_normed, second_inverse = norm_parts(middle, gain_two, shift_two)
    seconds = spread(second_norm.astype(BF16))
    grads_out = spread(grad_out)
    x_t = None
    feeds = []
    for j in range(ranges):
        outs = feed(
            half, seconds, grads_out, x_t, up_sets[j],
            bias_sets[j] if j == 0 else after(bias_sets[j], feeds[-1][6]), down_sets[j],
        )
        x_t = outs[7] if j == 0 else x_t
        feeds.append(outs)

    def reduce_ring(pair):
        send, keep = pair
        total = keep.astype(F32) + lax.ppermute(send, "rz", beside).astype(F32)
        total = total.astype(BF16).reshape(deep, -1, keep.shape[-1])
        shifts = range(1, deep)

        def route(shift):
            return [(i, (i + 2 * shift) % ring) for i in range(ring)]

        pieces = [
            lax.ppermute(pick(total, (high + s) % deep, 0), "rz", route(s)) for s in shifts
        ]
        piece = pick(total, high, 0).astype(F32)
        for other in pieces:
            piece = piece + other.astype(F32)
        piece = piece.astype(BF16)
        gathered = [piece] + [lax.ppermute(piece, "rz", route(s)) for s in shifts]
        whole = jnp.stack(
            [
                functools.reduce(
                    lambda rest, s: jnp.where((high - s) % deep == i, gathered[s], rest),
                    shifts,
                    piece,
                )
                for i in range(deep)
            ]
        ).reshape(keep.shape)
        return whole, lax.ppermute(whole, "rz", beside)

    def reduce_parts(parts):
        stacked = jnp.stack(parts)
        own, other = reduce_ring((pick(stacked, 1 - low, 0), pick(stacked, low, 0)))
        return jnp.where(low == 0, own, other), jnp.where(low == 0, other, own)

    def add_half(keep, send):
        return (keep.astype(F32) + swap_half(send).astype(F32)).astype(BF16)

    def reduce_rows(values):
        size = values.shape[0]
        if size % (16 * ring):
            return lax.psum(values, "rz")
        return jnp.concatenate(reduce_parts([values[: size // 2], values[size // 2 :]]), axis=0)

    def scatter_half(values):
        values = values.reshape(2, -1, values.shape[-1])
        return add_half(pick(values, half, 0), pick(values, 1 - half, 0))

    sums_feed = []
    for outs in feeds:
        up_part, down_part = add_half(outs[3], outs[2]), add_half(outs[5], outs[4])
        if up_part.shape == down_part.shape:
            sums_feed.extend(reduce_parts([up_part, down_part]))
        else:
            sums_feed.extend([reduce_rows(up_part), reduce_rows(down_part)])

    grad_wide = grad_out.astype(F32)
    grad_second = collect(
        lambda rows: functools.reduce(
            jnp.add, [contract(feeds[j][1][rows], up_sets[j], 1, 1) for j in range(ranges)]
        )
    )
    grad_second, grad_gain_two, grad_shift_two = norm_back(
        grad_second, second_normed, second_inverse, gain_two
    )
    grad_middle = grad_wide + grad_second
    grad_middle_low = grad_middle.astype(BF16)
    grad_middle_all = jnp.concatenate(spread(grad_middle_low), axis=0)
    grad_mixed = contract(grad_middle_all, out_set, 1, 1).astype(BF16)
    out_half = reduce_rows(scatter_half(contract(mixed, grad_middle_all, 0, 0).astype(BF16)))
    spans = [(0, pairs // 2), (pairs // 2, pairs)] if pairs > 1 else [(0, pairs)]
    dqkvs, qkv_halves = [], []
    for begin, end in spans:
        gate = lse if not dqkvs else after(lse, qkv_halves[-1])
        dqkvs.append(attend_back(qkv, grad_mixed, mixed, gate, begin, end))
        qkv_halves.append(contract(first, dqkvs[-1], 0, 0).astype(BF16))
    qkv_halves = [reduce_rows(scatter_half(values)) for values in qkv_halves]

    result = collect(
        lambda rows: functools.reduce(
            jnp.add, [contract(feeds[j][0][rows], down_sets[j], 1, 0) for j in range(ranges)]
        )
    )
    result = (middle + result + full_dbias).astype(BF16)
    layer_out = move(result, back).reshape(1, local, width)

    def weight_of(span):
        return qkv_weight[:, span[0] * 3 * PAIR : span[1] * 3 * PAIR]

    grad_first_norm = collect(
        lambda rows: functools.reduce(
            jnp.add,
            [contract(d[rows], weight_of(span), 1, 1) for d, span in zip(dqkvs, spans)],
        )
    )
    grad_first, grad_gain_one, grad_shift_one = norm_back(
        grad_first_norm, first_normed, first_inverse, gain_one
    )
    tokens_grad = move((grad_middle + grad_first).astype(BF16), back).reshape(1, local, width)

    out_weight_grad = join(out_half, swap_core(out_half), core).reshape(-1, width).astype(F32)
    if grp == 2:
        up_weight_grad, down_weight_grad = finish_feed(
            core, sums_feed, [swap_core(values) for values in sums_feed]
        )
        query_weight_grad, key_weight_grad, value_weight_grad = finish_qkv(
            core, qkv_halves, [swap_core(values) for values in qkv_halves]
        )
    else:

        def finish_columns(values):
            values = values.reshape(quarter, own_rows, 1, -1)
            values = lax.all_to_all(values, "gq", split_axis=0, concat_axis=2, tiled=True)
            values = values.reshape(own_rows, quarter, -1)
            return join(values, swap_core(values), core).transpose(1, 0, 2, 3)

        def natural_columns(values, inner=1):
            values = values.reshape(own_rows, 2, quarter, inner, 2, -1)
            return values.transpose(0, 4, 2, 1, 3, 5).reshape(own_rows, -1).astype(F32)

        ups = jnp.stack([finish_columns(values) for values in sums_feed[::2]], axis=3)
        up_weight_grad = natural_columns(ups, ranges)
        downs = jnp.stack(sums_feed[1::2])
        down_weight_grad = join(downs, swap_core(downs), core).reshape(-1, width).astype(F32)
        columns = jnp.concatenate([finish_columns(values) for values in qkv_halves], axis=3)
        columns = columns.reshape(own_rows, 2, quarter, pairs, 3, PAIR)
        query_weight_grad, key_weight_grad, value_weight_grad = [
            natural_columns(columns[:, :, :, :, i]) for i in range(3)
        ]

    def place_entries(values, inner=1):
        values = values.reshape(inner, 2, 1, 1, -1).transpose(1, 2, 3, 0, 4)
        shape = (2, quarter, 2) + values.shape[3:]
        zero = jnp.zeros((), core.dtype)
        return lax.dynamic_update_slice(
            jnp.zeros(shape, F32), values, (zero, gq, core, zero, zero)
        ).reshape(grp, -1)

    dqkv_sums = jnp.concatenate([jnp.sum(d.astype(F32), axis=0) for d in dqkvs])
    dqkv_sums = dqkv_sums.reshape(pairs, 3, PAIR)
    sums = [
        place_entries(dqkv_sums[:, 0]),
        place_entries(dqkv_sums[:, 2]),
        jnp.sum(grad_middle_low.astype(F32), axis=0),
        grad_gain_one, grad_shift_one, grad_gain_two, grad_shift_two,
        jnp.sum(grad_wide, axis=0),
        place_entries(jnp.stack([outs[6] for outs in feeds]), ranges),
    ]
    sums = jnp.concatenate([s.reshape(grp, -1) for s in sums], axis=1)
    if grp == 2 and ring & (ring - 1) == 0:
        sums = sums + swap_core(sums)
        sums = pick(sums, half, 0) + swap_half(pick(sums, 1 - half, 0))
        step = 1
        while step < ring:
            sums = sums + lax.ppermute(sums, "rz", [(i, i ^ step) for i in range(ring)])
            step *= 2
    else:
        sums = lax.psum(sums, ("rz", "core", "half", "gq"))
        sums = pick(sums, half * quarter + gq, 0)
    small = [sums[i * own_rows : (i + 1) * own_rows] for i in range(8)]
    return (
        layer_out, tokens_grad, query_weight_grad, key_weight_grad, value_weight_grad,
        small[0], small[1], out_weight_grad, small[2], small[3], small[4], small[5], small[6],
        up_weight_grad, sums[8 * own_rows :], down_weight_grad, small[7],
    )


def solution(mesh):
    rep, grp = mesh.shape["rep"], mesh.shape["grp"]
    split = Mesh(
        mesh.devices.reshape(rep // 2, 2, 2, grp // 2), ("rz", "core", "half", "gq")
    )
    clip = P(("rz", "core"), ("half", "gq"), None)
    matrix = P(("half", "gq"), None)
    vector = P(("half", "gq"))
    return jax.shard_map(
        functools.partial(body, rep, grp),
        mesh=split,
        in_specs=(
            clip, matrix, matrix, matrix, vector, vector, matrix, vector, vector, vector, vector,
            vector, matrix, vector, matrix, vector, clip,
        ),
        out_specs=(
            clip, clip, matrix, matrix, matrix, vector, vector, matrix, vector, vector, vector,
            vector, vector, matrix, vector, matrix, vector,
        ),
        check_vma=False,
    )
```

time: 833 us -> 761 us (0.914)
  waiting for transfers between devices: 325 us -> 218 us
  starting transfers between devices: 49.2 us -> 131 us
  blocking collectives: 38.3 us -> 0 us
  local copies, waits for them, and re-layouts: 105 us -> 69.3 us
  matrix products: 41.1 us -> 66.2 us
  Pallas kernels: 167 us -> 185 us
  between operations: 15.2 us -> 3.08 us
    psum x2 -> x0, waiting for transfers between devices: 180 us -> none  [the longest x1 119 us: body(): out_half, qkv_half = lax.psum((out_half, qkv_half), 'rz')]
    ppermute x16 -> x67, waiting for transfers between devices: 1.59 us -> 102 us  [the longest x15 29.1 us: reduce_ring(): lax.ppermute(pick(total, (high + s) % deep, 0), 'rz', route(s))]
    ppermute x16 -> x67, starting transfers between devices: 31.3 us -> 116 us  [the longest x15 42.3 us: reduce_ring(): gathered = [piece] + [lax.ppermute(piece, 'rz', route(s)) for s in shifts]]
    convert_element_type x6 -> x0, local copies, waits for them, and re-layouts: 39.5 us -> none  [natural_columns(): return values.transpose(0, 3, 2, 1, 4).reshape(own_rows, -1).astype(F32)]
    psum x1 -> x0, blocking collectives: 38.3 us -> none  [body(): sums = lax.psum(sums, ('rz', 'core', 'half', 'gq'))]
    ppermute x9 -> x13, waiting for transfers between devices: 143 us -> 116 us  [swap_half(): return lax.ppermute(values, 'half', SWAP)]
    dot_general x7 -> x19, matrix products: 41.1 us -> 66.2 us  [contract(): lax.dot_general(left, right, (((left_dim,), (right_dim,)), ((), ())), pre...]
    convert_element_type x12 -> x16, other arithmetic: 32.7 us -> 12.7 us  [the longest x5 4.52 us: reduce_ring(): total = total.astype(BF16).reshape(deep, -1, keep.shape[-1])]
  transfers between devices with their start and end apart: 27 -> 80, of which waited for: 9 -> 31; matrix products, arithmetic and copies ran while one was open for 25% -> 25% of each run, Pallas kernels for 14% -> 18%
where the time goes in v2:
time: 761 us; the launch traced here: 748 us
  waiting for transfers between devices  218 us (29%)
  Pallas kernels  185 us (24%)
  starting transfers between devices  131 us (17%)
  other arithmetic  76.1 us (10%)
  local copies, waits for them, and re-layouts  69.3 us (9%)
  matrix products  66.2 us (9%)
    ppermute x13, waiting for transfers between devices, swap_half(): return lax.ppermute(values, 'half', SWAP)  116 us
    pallas_call x2, Pallas kernels, attend_back(): pl.pallas_call(functools.partial(attend_back_kernel, tile, rows, padded),...  68.9 us
    dot_general x19, matrix products, contract(): lax.dot_general(left, right, (((left_dim,), (right_dim,)), ((), ())), pre...  66.2 us
    pallas_call x2, Pallas kernels, feed(): pl.pallas_call(functools.partial(feed_kernel, parts=parts, make=make, chu...  51.4 us
    pallas_call x2, Pallas kernels, attend(): pl.pallas_call(kernel if kept is None else lambda ref, a, b, *rest: kerne...  49.4 us
    ppermute x15, starting transfers between devices, reduce_ring(): gathered = [piece] + [lax.ppermute(piece, 'rz', route(s)) for s in shifts]  42.3 us
    ppermute x15, waiting for transfers between devices, reduce_ring(): lax.ppermute(pick(total, (high + s) % deep, 0), 'rz', route(s))  29.1 us
    unnamed x170, local copies, waits for them, and re-layouts  23 us
  transfers between devices with their start and end apart: 80, of which 31 were waited for; matrix products, arithmetic and copies ran while one was open for 25% of the time, Pallas kernels for 18%

profile of v2, /device:TPU:1, one launch (start us, length us, event | category | flops | bytes accessed | tf_op | source)
XLA Modules:
  0.0 748.4 jit_solution(3144983153193365190)
XLA Ops:
  24.3 7.8 %reshape.286 = bf16[512,2,1,2,2,512]{5,4,3,1,0,2:T(2,128)(2,1)} reshape(bf16[512,4096]{1,0:T(8,128)(2,1)} %param.29) | data formatting | bytes 8388608 | tf_op jit(solution)/shard_map/reshape | solution.py:463
  65.0 9.5 %collective-permute-done.6 = bf16[128,1024]{1,0:T(8,128)(2,1)S(1)} collective-permute-done((bf16[128,1024]{1,0:T(8,128)(2,1)S(1)}, bf16[128,1024]{1,0:T(8,128)(2,1)S(1)}, u32[]{:S(2)}, u32[]{:S(2)}) %collective-permute-start.6) | collective-permute-done | bytes 262176 | tf_op jit(solution)/shard_map/ppermute | solution.py:456
  88.3 9.2 %add_convert_fusion.qkv_ref.ref = bf16[1568,1536]{1,0:T(8,128)(2,1)} fusion(bf16[1024,1536]{1,0:T(8,128)(2,1)} %bitcast.347, f32[1536]{0:T(1024)S(1)} %add.430, bf16[784,1024]{1,0:T(8,128)(2,1)} %collective-permute-done.2, bf16[784,1024]{1,0:T(8,128)(2,1)} %fusion.7), kind=kOutput, calls=%fused_computation | convolution fusion | flops 4943740928 | bytes 11180032 | tf_op jit(solution)/shard_map/dot_general | solution.py:22
  97.5 24.7 %attend.2 = (bf16[1568,512]{1,0:T(8,128)(2,1)}, f32[4,2,2048]{2,1,0:T(2,128)}) custom-call(bf16[1568,1536]{1,0:T(8,128)(2,1)} %add_convert_fusion.qkv_ref.ref), custom_call_target="tpu_custom_call" | custom-call | flops 40282095616 | bytes 3211264 | tf_op jit(solution)/shard_map/attend/pallas_call | solution.py:68
  122.2 24.7 %attend.3 = (bf16[1568,512]{1,0:T(8,128)(2,1)}, f32[4,2,2048]{2,1,0:T(2,128)}) custom-call(bf16[1568,1536]{1,0:T(8,128)(2,1)} %add_convert_fusion.qkv_ref.ref, bf16[1568,512]{1,0:T(8,128)(2,1)} %get-tuple-element.47.a, f32[4,2,2048]{2,1,0:T(2,128)} %get-tuple-element.48.b), custom_call_target="tpu_custom_call", output_to_operand_aliasing={{0}: (1, {}), {1}: (2, {})} | custom-call | flops 40282095616 | bytes 3211264 | tf_op jit(solution)/shard_map/attend/pallas_call | solution.py:68
  160.6 17.8 %collective-permute-done.13 = bf16[512,1024]{1,0:T(8,128)(2,1)} collective-permute-done((bf16[512,1024]{1,0:T(8,128)(2,1)}, bf16[512,1024]{1,0:T(8,128)(2,1)}, u32[]{:S(2)}, u32[]{:S(2)}) %collective-permute-start.13) | collective-permute-done | bytes 1048608 | tf_op jit(solution)/shard_map/ppermute | solution.py:435
  194.1 11.3 %collective-permute-done.14 = bf16[512,1024]{1,0:T(8,128)(2,1)S(1)} collective-permute-done((bf16[512,1024]{1,0:T(8,128)(2,1)}, bf16[512,1024]{1,0:T(8,128)(2,1)S(1)}, u32[]{:S(2)}, u32[]{:S(2)}) %collective-permute-start.14) | collective-permute-done | bytes 1048608 | tf_op jit(solution)/shard_map/ppermute | solution.py:456
  212.5 26.0 %feed.2 = (bf16[1568,1024]{1,0:T(8,128)(2,1)}, bf16[1568,1024]{1,0:T(8,128)(2,1)}, bf16[512,1024]{1,0:T(8,128)(2,1)}, bf16[512,1024]{1,0:T(8,128)(2,1)}, bf16[51...) custom-call(s32[1]{0:T(128)} %bitcast.23.half_ref, ...), custom_call_target="tpu_custom_call" | custom-call | flops 13153337344 | bytes 21233664 | tf_op jit(solution)/shard_map/feed/pallas_call | solution.py:259
  238.5 25.4 %feed.3 = (bf16[1568,1024]{1,0:T(8,128)(2,1)}, bf16[1568,1024]{1,0:T(8,128)(2,1)}, bf16[512,1024]{1,0:T(8,128)(2,1)}, bf16[512,1024]{1,0:T(8,128)(2,1)}, bf16[51...) custom-call(s32[1]{0:T(128)} %bitcast.23.half_ref, bf16[784,1024]{1,0:T(8,128)(2,1)} %copy-done.31, ...), custom_call_target="tpu_custom_call" | custom-call | flops 13153337344 | bytes 21233664 | tf_op jit(solution)/shard_map/feed/pallas_call | solution.py:259
  288.6 11.2 %collective-permute-done.56 = bf16[512,1024]{1,0:T(8,128)(2,1)S(1)} collective-permute-done((bf16[512,1024]{1,0:T(8,128)(2,1)S(1)}, bf16[512,1024]{1,0:T(8,128)(2,1)S(1)}, u32[]{:S(2)}, u32[]{:S(2)}) %collective-permute-start.56) | collective-permute-done | bytes 1048608 | tf_op jit(solution)/shard_map/ppermute | solution.py:435
  302.0 42.8 %collective-permute-done.57 = bf16[512,1024]{1,0:T(8,128)(2,1)S(1)} collective-permute-done((bf16[512,1024]{1,0:T(8,128)(2,1)S(1)}, bf16[512,1024]{1,0:T(8,128)(2,1)S(1)}, u32[]{:S(2)}, u32[]{:S(2)}) %collective-permute-start.57) | collective-permute-done | bytes 1048608 | tf_op jit(solution)/shard_map/ppermute | solution.py:435
  348.4 18.9 %collective-permute-done.67 = bf16[512,1024]{1,0:T(8,128)(2,1)S(1)} collective-permute-done((bf16[512,1024]{1,0:T(8,128)(2,1)S(1)}, bf16[512,1024]{1,0:T(8,128)(2,1)S(1)}, u32[]{:S(2)}, u32[]{:S(2)}) %collective-permute-start.67) | collective-permute-done | bytes 1048608 | tf_op jit(solution)/shard_map/ppermute | solution.py:435
  386.7 6.1 collective-permute-done.68
  399.7 9.1 %collective-permute-done.60 = bf16[128,1024]{1,0:T(8,128)(2,1)} collective-permute-done((bf16[128,1024]{1,0:T(8,128)(2,1)}, bf16[128,1024]{1,0:T(8,128)(2,1)}, u32[]{:S(2)}, u32[]{:S(2)}) %collective-permute-start.60) | collective-permute-done | bytes 262176 | tf_op jit(solution)/shard_map/ppermute | solution.py:562
  413.7 11.3 %collective-permute-start.63 = (bf16[128,1024]{1,0:T(8,128)(2,1)S(1)}, bf16[128,1024]{1,0:T(8,128)(2,1)S(1)}, u32[]{:S(2)}, u32[]{:S(2)}) collective-permute-start(bf16[128,1024]{1,0:T(8,128)(2,1)S(1)} %fusion.79), channel_id=1, source_target_pairs={{0,16},{4,20},{8,24},{12,28},{16,0},{20,4},{24,8},{28,12},{1,17},{... | collective-permute-start | bytes 786440 | tf_op jit(solution)/shard_map/ppermute | solution.py:568
  425.0 8.0 %collective-permute-done.70 = bf16[128,1024]{1,0:T(8,128)(2,1)S(1)} collective-permute-done((bf16[128,1024]{1,0:T(8,128)(2,1)}, bf16[128,1024]{1,0:T(8,128)(2,1)S(1)}, u32[]{:S(2)}, u32[]{:S(2)}) %collective-permute-start.70) | collective-permute-done | bytes 262176 | tf_op jit(solution)/shard_map/ppermute | solution.py:562
  448.6 5.2 collective-permute-done.63
  455.2 11.1 %collective-permute-start.74 = (bf16[128,1024]{1,0:T(8,128)(2,1)S(1)}, bf16[128,1024]{1,0:T(8,128)(2,1)S(1)}, u32[]{:S(2)}, u32[]{:S(2)}) collective-permute-start(bf16[128,1024]{1,0:T(8,128)(2,1)S(1)} %fusion.76), channel_id=1, source_target_pairs={{0,8},{4,12},{8,16},{12,20},{16,24},{20,28},{24,0},{28,4},{1,9},{5... | collective-permute-start | bytes 786440 | tf_op jit(solution)/shard_map/ppermute | solution.py:568
  468.8 7.5 collective-permute-done.73
  482.7 34.5 %attend_back.2 = bf16[1568,768]{1,0:T(8,128)(2,1)} custom-call(bf16[1568,1536]{1,0:T(8,128)(2,1)} %add_convert_fusion.qkv_ref.ref, bf16[1568,512]{1,0:T(8,128)(2,1)} %convolution_convert_fusion.grad_ref, bf16[1568,512]{1,0:T(8,128)(2,1)} %get-tuple-element.49.out_ref, f32[4,2,2048]{2,1,0:T(2,128)} %get-tuple-element.62.lse_ref), custom_call_target="tpu_custom_call" | custom-call | flops 100705239040 | bytes 6422528 | tf_op jit(solution)/shard_map/attend_back/pallas_call | solution.py:143
  517.1 5.1 fusion.40
  522.6 6.2 convolution_convert_fusion.3
  528.8 34.5 %attend_back.3 = bf16[1568,768]{1,0:T(8,128)(2,1)} custom-call(bf16[1568,1536]{1,0:T(8,128)(2,1)} %add_convert_fusion.qkv_ref.ref, bf16[1568,512]{1,0:T(8,128)(2,1)} %convolution_convert_fusion.grad_ref, bf16[1568,512]{1,0:T(8,128)(2,1)} %get-tuple-element.49.out_ref, f32[4,2,2048]{2,1,0:T(2,128)} %get-tuple-element.62.lse_ref), custom_call_target="tpu_custom_call" | custom-call | flops 100705239040 | bytes 6422528 | tf_op jit(solution)/shard_map/attend_back/pallas_call | solution.py:143
  569.0 5.0 convolution_convert_fusion.2
  592.0 19.8 %collective-permute-done.46 = bf16[256,1024]{1,0:T(8,128)(2,1)S(1)} collective-permute-done((bf16[256,1024]{1,0:T(8,128)(2,1)S(1)}, bf16[256,1024]{1,0:T(8,128)(2,1)S(1)}, u32[]{:S(2)}, u32[]{:S(2)}) %collective-permute-start.46) | collective-permute-done | bytes 524320 | tf_op jit(solution)/shard_map/ppermute | solution.py:435
  631.3 7.7 %collective-permute-start.19 = (bf16[784,1024]{1,0:T(8,128)(2,1)S(1)}, bf16[784,1024]{1,0:T(8,128)(2,1)S(1)}, u32[]{:S(2)}, u32[]{:S(2)}) collective-permute-start(bf16[784,1024]{1,0:T(8,128)(2,1)S(1)} %add_convert_fusion.1), channel_id=1, source_target_pairs={{0,2},{2,0},{1,3},{3,1},{4,6},{6,4},{5,7},{7,5},{8,10},{10,8},{9,1... | collective-permute-start | bytes 4816904 | tf_op jit(solution)/shard_map/ppermute | solution.py:438
  642.9 11.0 %collective-permute-done.54 = bf16[128,1024]{1,0:T(8,128)(2,1)S(1)} collective-permute-done((bf16[128,1024]{1,0:T(8,128)(2,1)S(1)}, bf16[128,1024]{1,0:T(8,128)(2,1)S(1)}, u32[]{:S(2)}, u32[]{:S(2)}) %collective-permute-start.54) | collective-permute-done | bytes 262176 | tf_op jit(solution)/shard_map/ppermute | solution.py:579
  666.7 5.1 collective-permute-done.33
  675.2 6.5 collective-permute-done.27
  706.3 6.2 collective-permute-done.38
  722.6 9.5 %finish_feed.1 = (f32[512,4096]{1,0:T(8,128)}, f32[2,2,512,1024]{3,2,1,0:T(8,128)}) custom-call(s32[1]{0:T(128)} %bitcast.49.core_ref, bf16[512,1024]{1,0:T(8,128)(2,1)} %get-tuple-element.99.refs_0_, bf16[512,1024]{1,0:T(8,128)(2,1)} %copy-done.15, bf16[512,1024]{1,0:T(8,128)(2,1)} %get-tuple-element.97.refs_2_, ...), custom_call_target="tpu_custom_call" | custom-call | tf_op jit(solution)/shard_map/finish_feed/pallas_call | solution.py:310
  739.9 5.4 finish_qkv.1
  (471 shorter events, 301.4 us)
Async XLA Ops:
  7.0 38.4 %collective-permute-start.1 = (f32[6144]{0:T(1024)S(1)}, f32[6144]{0:T(1024)S(1)}, u32[]{:S(2)}, u32[]{:S(2)}) collective-permute-start(f32[6144]{0:T(1024)S(1)} %constant_dynamic-update-slice_fusion.13), channel_id=1, source_target_pairs={{0,1},{1,0},{2,3},{3,2},{4,5},{5,4},{6,7},{7,6},{8,9},{9,8},{10,11... | collective-permute-start | bytes 73736 | tf_op jit(solution)/shard_map/ppermute | solution.py:435
  9.0 51.6 %collective-permute-start = (bf16[784,1024]{1,0:T(8,128)(2,1)}, bf16[784,1024]{1,0:T(8,128)(2,1)}, u32[]{:S(2)}, u32[]{:S(2)}) collective-permute-start(bf16[784,1024]{1,0:T(8,128)(2,1)} %bitcast.370), channel_id=1, source_target_pairs={{1,2},{2,1},{5,6},{6,5},{9,10},{10,9},{13,14},{14,13},{17,18},{18,... | collective-permute-start | bytes 4816904 | tf_op jit(solution)/shard_map/ppermute | solution.py:432
  49.5 26.3 %collective-permute-start.4 = (bf16[256,1536]{0,1:T(8,128)(2,1)}, bf16[256,1536]{0,1:T(8,128)(2,1)S(1)}, u32[]{:S(2)}, u32[]{:S(2)}) collective-permute-start(bf16[256,1536]{0,1:T(8,128)(2,1)} %collective-permute-done.3), channel_id=1, source_target_pairs={{0,4},{4,0},{8,12},{12,8},{16,20},{20,16},{24,28},{28,24},{1,5},{5... | collective-permute-start | bytes 2359304 | tf_op jit(solution)/shard_map/ppermute | solution.py:456
  56.0 29.1 %collective-permute-start.9 = (bf16[512,1024]{1,0:T(8,128)(2,1)}, bf16[512,1024]{1,0:T(8,128)(2,1)}, u32[]{:S(2)}, u32[]{:S(2)}) collective-permute-start(bf16[512,1024]{1,0:T(8,128)(2,1)} %fusion.55), channel_id=1, source_target_pairs={{0,1},{1,0},{2,3},{3,2},{4,5},{5,4},{6,7},{7,6},{8,9},{9,8},{10,11... | collective-permute-start | bytes 3145736 | tf_op jit(solution)/shard_map/ppermute | solution.py:435
  85.1 94.7 %collective-permute-start.10 = (bf16[784,1024]{1,0:T(8,128)(2,1)}, bf16[784,1024]{1,0:T(8,128)(2,1)}, u32[]{:S(2)}, u32[]{:S(2)}) collective-permute-start(bf16[784,1024]{1,0:T(8,128)(2,1)} %bitcast.371), channel_id=1, source_target_pairs={{1,2},{2,1},{5,6},{6,5},{9,10},{10,9},{13,14},{14,13},{17,18},{18,... | collective-permute-start | bytes 4816904 | tf_op jit(solution)/shard_map/ppermute | solution.py:432
  150.7 32.5 %collective-permute-start.7 = (bf16[784,1024]{1,0:T(8,128)(2,1)}, bf16[784,1024]{1,0:T(8,128)(2,1)}, u32[]{:S(2)}, u32[]{:S(2)}) collective-permute-start(bf16[784,1024]{1,0:T(8,128)(2,1)} %convolution_convert_fusion.1), channel_id=1, source_target_pairs={{0,2},{2,0},{1,3},{3,1},{4,6},{6,4},{5,7},{7,5},{8,10},{10,8},{9,1... | collective-permute-start | bytes 4816904 | tf_op jit(solution)/shard_map/ppermute | solution.py:438
  153.2 25.1 %collective-permute-start.13 = (bf16[512,1024]{1,0:T(8,128)(2,1)}, bf16[512,1024]{1,0:T(8,128)(2,1)}, u32[]{:S(2)}, u32[]{:S(2)}) collective-permute-start(bf16[512,1024]{1,0:T(8,128)(2,1)} %fusion.53), channel_id=1, source_target_pairs={{0,1},{1,0},{2,3},{3,2},{4,5},{5,4},{6,7},{7,6},{8,9},{9,8},{10,11... | collective-permute-start | bytes 3145736 | tf_op jit(solution)/shard_map/ppermute | solution.py:435
  158.9 30.4 %collective-permute-start.12 = (bf16[512,1024]{1,0:T(8,128)(2,1)}, bf16[512,1024]{1,0:T(8,128)(2,1)S(1)}, u32[]{:S(2)}, u32[]{:S(2)}) collective-permute-start(bf16[512,1024]{1,0:T(8,128)(2,1)} %collective-permute-done.9), channel_id=1, source_target_pairs={{0,4},{4,0},{8,12},{12,8},{16,20},{20,16},{24,28},{28,24},{1,5},{5... | collective-permute-start | bytes 3145736 | tf_op jit(solution)/shard_map/ppermute | solution.py:456
  178.4 27.1 %collective-permute-start.14 = (bf16[512,1024]{1,0:T(8,128)(2,1)}, bf16[512,1024]{1,0:T(8,128)(2,1)S(1)}, u32[]{:S(2)}, u32[]{:S(2)}) collective-permute-start(bf16[512,1024]{1,0:T(8,128)(2,1)} %collective-permute-done.13), channel_id=1, source_target_pairs={{0,4},{4,0},{8,12},{12,8},{16,20},{20,16},{24,28},{28,24},{1,5},{5... | collective-permute-start | bytes 3145736 | tf_op jit(solution)/shard_map/ppermute | solution.py:456
  182.0 28.1 %collective-permute-start.11 = (bf16[784,1024]{1,0:T(8,128)(2,1)S(1)}, bf16[784,1024]{1,0:T(8,128)(2,1)S(1)}, u32[]{:S(2)}, u32[]{:S(2)}) collective-permute-start(bf16[784,1024]{1,0:T(8,128)(2,1)S(1)} %get-tuple-element.86.refs_2_), channel_id=1, source_target_pairs={{0,2},{2,0},{1,3},{3,1},{4,6},{6,4},{5,7},{7,5},{8,10},{10,8},{9,1... | collective-permute-start | bytes 4816904 | tf_op jit(solution)/shard_map/ppermute | solution.py:438
  271.8 98.8 %collective-permute-start.17 = (bf16[784,1024]{1,0:T(8,128)(2,1)S(1)}, bf16[784,1024]{1,0:T(8,128)(2,1)}, u32[]{:S(2)}, u32[]{:S(2)}) collective-permute-start(bf16[784,1024]{1,0:T(8,128)(2,1)S(1)} %add_convert_fusion.2), channel_id=1, source_target_pairs={{0,2},{2,0},{1,3},{3,1},{4,6},{6,4},{5,7},{7,5},{8,10},{10,8},{9,1... | collective-permute-start | bytes 4816904 | tf_op jit(solution)/shard_map/ppermute | solution.py:438
  277.1 71.0 %collective-permute-start.66 = (bf16[512,1024]{1,0:T(8,128)(2,1)S(1)}, bf16[512,1024]{1,0:T(8,128)(2,1)S(1)}, u32[]{:S(2)}, u32[]{:S(2)}) collective-permute-start(bf16[512,1024]{1,0:T(8,128)(2,1)S(1)} %copy-done.59), channel_id=1, source_target_pairs={{0,1},{1,0},{2,3},{3,2},{4,5},{5,4},{6,7},{7,6},{8,9},{9,8},{10,11... | collective-permute-start | bytes 3145736 | tf_op jit(solution)/shard_map/ppermute | solution.py:435
  282.0 62.7 %collective-permute-start.57 = (bf16[512,1024]{1,0:T(8,128)(2,1)S(1)}, bf16[512,1024]{1,0:T(8,128)(2,1)S(1)}, u32[]{:S(2)}, u32[]{:S(2)}) collective-permute-start(bf16[512,1024]{1,0:T(8,128)(2,1)S(1)} %copy-done.60), channel_id=1, source_target_pairs={{0,1},{1,0},{2,3},{3,2},{4,5},{5,4},{6,7},{7,6},{8,9},{9,8},{10,11... | collective-permute-start | bytes 3145736 | tf_op jit(solution)/shard_map/ppermute | solution.py:435
  287.1 86.6 %collective-permute-start.15 = (bf16[784,1024]{1,0:T(8,128)(2,1)}, bf16[784,1024]{1,0:T(8,128)(2,1)}, u32[]{:S(2)}, u32[]{:S(2)}) collective-permute-start(bf16[784,1024]{1,0:T(8,128)(2,1)} %add_convert_fusion.4), channel_id=1, source_target_pairs={{0,2},{2,0},{1,3},{3,1},{4,6},{6,4},{5,7},{7,5},{8,10},{10,8},{9,1... | collective-permute-start | bytes 4816904 | tf_op jit(solution)/shard_map/ppermute | solution.py:438
  299.8 67.5 %collective-permute-start.67 = (bf16[512,1024]{1,0:T(8,128)(2,1)S(1)}, bf16[512,1024]{1,0:T(8,128)(2,1)S(1)}, u32[]{:S(2)}, u32[]{:S(2)}) collective-permute-start(bf16[512,1024]{1,0:T(8,128)(2,1)S(1)} %copy-done.58), channel_id=1, source_target_pairs={{0,1},{1,0},{2,3},{3,2},{4,5},{5,4},{6,7},{7,6},{8,9},{9,8},{10,11... | collective-permute-start | bytes 3145736 | tf_op jit(solution)/shard_map/ppermute | solution.py:435
  346.6 33.6 %collective-permute-start.58 = (bf16[512,1024]{1,0:T(8,128)(2,1)}, bf16[512,1024]{1,0:T(8,128)(2,1)}, u32[]{:S(2)}, u32[]{:S(2)}) collective-permute-start(bf16[512,1024]{1,0:T(8,128)(2,1)} %fusion.61), channel_id=1, source_target_pairs={{0,4},{4,0},{8,12},{12,8},{16,20},{20,16},{24,28},{28,24},{1,5},{5... | collective-permute-start | bytes 3145736 | tf_op jit(solution)/shard_map/ppermute | solution.py:554
  378.6 99.2 %collective-permute-start.18 = (bf16[784,1024]{1,0:T(8,128)(2,1)}, bf16[784,1024]{1,0:T(8,128)(2,1)}, u32[]{:S(2)}, u32[]{:S(2)}) collective-permute-start(bf16[784,1024]{1,0:T(8,128)(2,1)} %get-tuple-element.88), channel_id=1, source_target_pairs={{0,2},{2,0},{1,3},{3,1},{4,6},{6,4},{5,7},{7,5},{8,10},{10,8},{9,1... | collective-permute-start | bytes 4816904 | tf_op jit(solution)/shard_map/ppermute | solution.py:438
  399.1 33.9 %collective-permute-start.70 = (bf16[128,1024]{1,0:T(8,128)(2,1)}, bf16[128,1024]{1,0:T(8,128)(2,1)S(1)}, u32[]{:S(2)}, u32[]{:S(2)}) collective-permute-start(bf16[128,1024]{1,0:T(8,128)(2,1)} %get-tuple-element.116), channel_id=1, source_target_pairs={{0,16},{4,20},{8,24},{12,28},{16,0},{20,4},{24,8},{28,12},{1,17},{... | collective-permute-start | bytes 786440 | tf_op jit(solution)/shard_map/ppermute | solution.py:562
  408.9 31.1 %collective-permute-start.69 = (bf16[128,1024]{1,0:T(8,128)(2,1)S(1)}, bf16[128,1024]{1,0:T(8,128)(2,1)}, u32[]{:S(2)}, u32[]{:S(2)}) collective-permute-start(bf16[128,1024]{1,0:T(8,128)(2,1)S(1)} %get-tuple-element.114), channel_id=1, source_target_pairs={{0,8},{4,12},{8,16},{12,20},{16,24},{20,28},{24,0},{28,4},{1,9},{5... | collective-permute-start | bytes 786440 | tf_op jit(solution)/shard_map/ppermute | solution.py:562
  410.1 36.0 %collective-permute-start.62 = (bf16[128,1024]{1,0:T(8,128)(2,1)S(1)}, bf16[128,1024]{1,0:T(8,128)(2,1)S(1)}, u32[]{:S(2)}, u32[]{:S(2)}) collective-permute-start(bf16[128,1024]{1,0:T(8,128)(2,1)S(1)} %fusion.79), channel_id=1, source_target_pairs={{0,24},{4,28},{8,0},{12,4},{16,8},{20,12},{24,16},{28,20},{1,25},{... | collective-permute-start | bytes 786440 | tf_op jit(solution)/shard_map/ppermute | solution.py:568
  413.7 40.1 %collective-permute-start.63 = (bf16[128,1024]{1,0:T(8,128)(2,1)S(1)}, bf16[128,1024]{1,0:T(8,128)(2,1)S(1)}, u32[]{:S(2)}, u32[]{:S(2)}) collective-permute-start(bf16[128,1024]{1,0:T(8,128)(2,1)S(1)} %fusion.79), channel_id=1, source_target_pairs={{0,16},{4,20},{8,24},{12,28},{16,0},{20,4},{24,8},{28,12},{1,17},{... | collective-permute-start | bytes 786440 | tf_op jit(solution)/shard_map/ppermute | solution.py:568
  440.0 258.9 %collective-permute-start.16 = (bf16[784,1024]{1,0:T(8,128)(2,1)}, bf16[784,1024]{1,0:T(8,128)(2,1)}, u32[]{:S(2)}, u32[]{:S(2)}) collective-permute-start(bf16[784,1024]{1,0:T(8,128)(2,1)} %get-tuple-element.95), channel_id=1, source_target_pairs={{2,1},{1,2},{6,5},{5,6},{10,9},{9,10},{14,13},{13,14},{18,17},{17,... | collective-permute-start | bytes 4816904 | tf_op jit(solution)/shard_map/ppermute | solution.py:432
  468.6 115.8 %collective-permute-start.65 = (bf16[512,1024]{1,0:T(8,128)(2,1)}, bf16[512,1024]{1,0:T(8,128)(2,1)}, u32[]{:S(2)}, u32[]{:S(2)}) collective-permute-start(bf16[512,1024]{1,0:T(8,128)(2,1)} %bitcast.124), channel_id=1, source_target_pairs={{0,4},{4,0},{8,12},{12,8},{16,20},{20,16},{24,28},{28,24},{1,5},{5... | collective-permute-start | bytes 3145736 | tf_op jit(solution)/shard_map/ppermute | solution.py:579
  477.5 110.9 %collective-permute-start.75 = (bf16[512,1024]{1,0:T(8,128)(2,1)}, bf16[512,1024]{1,0:T(8,128)(2,1)}, u32[]{:S(2)}, u32[]{:S(2)}) collective-permute-start(bf16[512,1024]{1,0:T(8,128)(2,1)} %bitcast.138), channel_id=1, source_target_pairs={{0,4},{4,0},{8,12},{12,8},{16,20},{20,16},{24,28},{28,24},{1,5},{5... | collective-permute-start | bytes 3145736 | tf_op jit(solution)/shard_map/ppermute | solution.py:579
  565.5 47.9 %collective-permute-start.21 = (bf16[512,768]{1,0:T(8,128)(2,1)}, bf16[512,768]{1,0:T(8,128)(2,1)}, u32[]{:S(2)}, u32[]{:S(2)}) collective-permute-start(bf16[512,768]{1,0:T(8,128)(2,1)} %dynamic-slice_bitcast_fusion.3), channel_id=1, source_target_pairs={{0,1},{1,0},{2,3},{3,2},{4,5},{5,4},{6,7},{7,6},{8,9},{9,8},{10,11... | collective-permute-start | bytes 2359304 | tf_op jit(solution)/shard_map/ppermute | solution.py:435
  576.0 47.1 %collective-permute-start.30 = (bf16[512,768]{1,0:T(8,128)(2,1)}, bf16[512,768]{1,0:T(8,128)(2,1)S(1)}, u32[]{:S(2)}, u32[]{:S(2)}) collective-permute-start(bf16[512,768]{1,0:T(8,128)(2,1)} %dynamic-slice_bitcast_fusion.2), channel_id=1, source_target_pairs={{0,1},{1,0},{2,3},{3,2},{4,5},{5,4},{6,7},{7,6},{8,9},{9,8},{10,11... | collective-permute-start | bytes 2359304 | tf_op jit(solution)/shard_map/ppermute | solution.py:435
  584.3 27.4 %collective-permute-start.46 = (bf16[256,1024]{1,0:T(8,128)(2,1)S(1)}, bf16[256,1024]{1,0:T(8,128)(2,1)S(1)}, u32[]{:S(2)}, u32[]{:S(2)}) collective-permute-start(bf16[256,1024]{1,0:T(8,128)(2,1)S(1)} %dynamic-slice_bitcast_fusion.4), channel_id=1, source_target_pairs={{0,1},{1,0},{2,3},{3,2},{4,5},{5,4},{6,7},{7,6},{8,9},{9,8},{10,11... | collective-permute-start | bytes 1572872 | tf_op jit(solution)/shard_map/ppermute | solution.py:435
  615.0 25.7 %collective-permute-start.22 = (bf16[256,768]{1,0:T(8,128)(2,1)S(1)}, bf16[256,768]{1,0:T(8,128)(2,1)S(1)}, u32[]{:S(2)}, u32[]{:S(2)}) collective-permute-start(bf16[256,768]{1,0:T(8,128)(2,1)S(1)} %fusion.86), channel_id=1, source_target_pairs={{0,4},{4,0},{8,12},{12,8},{16,20},{20,16},{24,28},{28,24},{1,5},{5... | collective-permute-start | bytes 1179656 | tf_op jit(solution)/shard_map/ppermute | solution.py:554
  631.3 59.7 %collective-permute-start.19 = (bf16[784,1024]{1,0:T(8,128)(2,1)S(1)}, bf16[784,1024]{1,0:T(8,128)(2,1)S(1)}, u32[]{:S(2)}, u32[]{:S(2)}) collective-permute-start(bf16[784,1024]{1,0:T(8,128)(2,1)S(1)} %add_convert_fusion.1), channel_id=1, source_target_pairs={{0,2},{2,0},{1,3},{3,1},{4,6},{6,4},{5,7},{7,5},{8,10},{10,8},{9,1... | collective-permute-start | bytes 4816904 | tf_op jit(solution)/shard_map/ppermute | solution.py:438
  682.2 35.4 %collective-permute-start.76 = (bf16[512,1024]{1,0:T(8,128)(2,1)}, bf16[512,1024]{1,0:T(8,128)(2,1)}, u32[]{:S(2)}, u32[]{:S(2)}) collective-permute-start(bf16[512,1024]{1,0:T(8,128)(2,1)} %get-tuple-element.99.refs_0_), channel_id=1, source_target_pairs={{0,2},{2,0},{1,3},{3,1},{4,6},{6,4},{5,7},{7,5},{8,10},{10,8},{9,1... | collective-permute-start | bytes 3145736 | tf_op jit(solution)/shard_map/ppermute | solution.py:438
  687.9 30.9 %collective-permute-start.77 = (bf16[512,1024]{1,0:T(8,128)(2,1)S(1)}, bf16[512,1024]{1,0:T(8,128)(2,1)}, u32[]{:S(2)}, u32[]{:S(2)}) collective-permute-start(bf16[512,1024]{1,0:T(8,128)(2,1)S(1)} %get-tuple-element.98.refs_1_), channel_id=1, source_target_pairs={{0,2},{2,0},{1,3},{3,1},{4,6},{6,4},{5,7},{7,5},{8,10},{10,8},{9,1... | collective-permute-start | bytes 3145736 | tf_op jit(solution)/shard_map/ppermute | solution.py:438
  712.4 32.8 %collective-permute-start.20 = (bf16[784,1024]{1,0:T(8,128)(2,1)}, bf16[784,1024]{1,0:T(8,128)(2,1)}, u32[]{:S(2)}, u32[]{:S(2)}) collective-permute-start(bf16[784,1024]{1,0:T(8,128)(2,1)} %fusion.12), channel_id=1, source_target_pairs={{2,1},{1,2},{6,5},{5,6},{10,9},{9,10},{14,13},{13,14},{18,17},{17,... | collective-permute-start | bytes 4816904 | tf_op jit(solution)/shard_map/ppermute | solution.py:432
  (116 other events, 1527.8 us)

commit v3 on v2

--- a/solution.py
+++ b/solution.py
@@ -95,8 +95,8 @@
 
 
 def attend_back_kernel(
-    tile, rows, padded, qkv_ref, grad_ref, out_ref, lse_ref, dqkv_ref, q_t, g_t, k_t, delta,
-    dq_t, dk_t, dv_t,
+    tile, rows, padded, s_ref, qkv_ref, grad_ref, out_ref, lse_ref, first_ref, dqkv_ref, send_ref,
+    keep_ref, sums_ref, q_t, g_t, k_t, delta, dq_t, dk_t, dv_t, all_t,
 ):
     scale = HEAD_DIM**-0.5
     q_t[:, :rows] = qkv_ref[:, :PAIR].T
@@ -131,34 +131,65 @@
         return carry
 
     lax.fori_loop(0, padded // tile, block, 0)
-    dqkv_ref[:, :PAIR] = (dq_t[...].T[:rows, :] * scale).astype(BF16)
-    dqkv_ref[:, PAIR : 2 * PAIR] = (dk_t[...].T * scale).astype(BF16)
-    dqkv_ref[:, 2 * PAIR :] = dv_t[...].T.astype(BF16)
-
-
-def attend_back(qkv, grad, out, lse, first_pair, last_pair, tile=256):
-    rows, width = qkv.shape
+    all_t[:PAIR, :] = (dq_t[:, :rows] * scale).astype(BF16)
+    all_t[PAIR : 2 * PAIR, :] = (dk_t[...] * scale).astype(BF16)
+    all_t[2 * PAIR :, :] = dv_t[...].astype(BF16)
+    for part in range(3):
+        lanes = slice(part * PAIR, (part + 1) * PAIR)
+        dqkv_ref[:, lanes] = all_t[lanes, :].T
+    sums_ref[...] = contract(jnp.ones((8, rows), BF16), all_t[...], 1, 1)
+    own = first_ref.shape[1] // 2
+    for h in range(2):
+        grad = contract(all_t[...], first_ref[:, h * own : (h + 1) * own], 1, 0).astype(BF16)
+
+        @pl.when(s_ref[0] == h)
+        def _():
+            keep_ref[...] = grad
+
+        @pl.when(s_ref[0] != h)
+        def _():
+            send_ref[...] = grad
+
+
+def attend_back(scal, qkv, grad, out, lse, first, first_pair, last_pair, tile=256):
+    rows, full = qkv.shape
+    width = first.shape[1]
     padded = -(-rows // tile) * tile
     count = last_pair - first_pair
     return pl.pallas_call(
         functools.partial(attend_back_kernel, tile, rows, padded),
-        grid=(count,),
-        in_specs=[
-            pl.BlockSpec((rows, 3 * PAIR), lambda i: (0, i + first_pair)),
-            pl.BlockSpec((rows, PAIR), lambda i: (0, i + first_pair)),
-            pl.BlockSpec((rows, PAIR), lambda i: (0, i + first_pair)),
-            pl.BlockSpec((None, 2, lse.shape[2]), lambda i: (i + first_pair, 0, 0)),
-        ],
-        out_specs=pl.BlockSpec((rows, 3 * PAIR), lambda i: (0, i)),
-        out_shape=jax.ShapeDtypeStruct((rows, 3 * PAIR * count), BF16),
-        scratch_shapes=[
-            pltpu.VMEM((PAIR, padded), BF16),
-            pltpu.VMEM((PAIR, padded), BF16),
-            pltpu.VMEM((PAIR, rows), BF16),
-            pltpu.VMEM((2, padded), F32),
-            pltpu.VMEM((PAIR, padded), F32),
-            pltpu.VMEM((PAIR, rows), F32),
-            pltpu.VMEM((PAIR, rows), F32),
+        grid_spec=pltpu.PrefetchScalarGridSpec(
+            num_scalar_prefetch=1,
+            grid=(count,),
+            in_specs=[
+                pl.BlockSpec((rows, 3 * PAIR), lambda i, s: (0, i + first_pair)),
+                pl.BlockSpec((rows, PAIR), lambda i, s: (0, i + first_pair)),
+                pl.BlockSpec((rows, PAIR), lambda i, s: (0, i + first_pair)),
+                pl.BlockSpec((None, 2, lse.shape[2]), lambda i, s: (i + first_pair, 0, 0)),
+                pl.BlockSpec((rows, width), lambda i, s: (0, 0), pipeline_mode=pl.Buffered(1)),
+            ],
+            out_specs=[
+                pl.BlockSpec((rows, 3 * PAIR), lambda i, s: (0, i)),
+                pl.BlockSpec((3 * PAIR, width // 2), lambda i, s: (i, 0)),
+                pl.BlockSpec((3 * PAIR, width // 2), lambda i, s: (i, 0)),
+                pl.BlockSpec((8, 3 * PAIR), lambda i, s: (0, i)),
+            ],
+            scratch_shapes=[
+                pltpu.VMEM((PAIR, padded), BF16),
+                pltpu.VMEM((PAIR, padded), BF16),
+                pltpu.VMEM((PAIR, rows), BF16),
+                pltpu.VMEM((2, padded), F32),
+                pltpu.VMEM((PAIR, padded), F32),
+                pltpu.VMEM((PAIR, rows), F32),
+                pltpu.VMEM((PAIR, rows), F32),
+                pltpu.VMEM((3 * PAIR, rows), BF16),
+            ],
+        ),
+        out_shape=[
+            jax.ShapeDtypeStruct((rows, 3 * PAIR * count), BF16),
+            jax.ShapeDtypeStruct((3 * PAIR * count, width // 2), BF16),
+            jax.ShapeDtypeStruct((3 * PAIR * count, width // 2), BF16),
+            jax.ShapeDtypeStruct((8, 3 * PAIR * count), F32),
         ],
         compiler_params=pltpu.CompilerParams(vmem_limit_bytes=VMEM_LIMIT),
         cost_estimate=pl.CostEstimate(
@@ -167,35 +198,40 @@
             transcendentals=2 * rows * rows * count,
         ),
         name="attend_back",
-    )(qkv, grad, out, lse)
+    )(scal, qkv, grad, out, lse, first)
 
 
 def feed_kernel(
-    half_ref, *refs, parts, make, chunk,
+    s_ref, x_own, x_other, dy_own, dy_other, *refs, make,
 ):
-    xs, refs = refs[:parts], refs[parts:]
-    dys, refs = refs[:parts], refs[parts:]
     if not make:
         x_t, refs = refs[0], refs[1:]
-    up_ref, bias_ref, down_ref, *refs = refs
+    up_ref, down_ref, piece, beside, bias_ref, *refs = refs
     hidden_ref, d_pre_ref, up_send, up_keep, down_send, down_keep, bias_grad_ref, *refs = refs
+    up_full, down_full, *refs = refs
     if make:
         x_t, refs = refs[0], refs[1:]
     x, dy, sems = refs
     index = pl.program_id(0)
-    half = half_ref[0]
+    half = s_ref[0]
+    even = s_ref[1] == 0
     rows, width = x.shape
-    block = rows // parts
+    block = rows // 2
     own = width // 2
     tile = up_ref.shape[1]
+    columns = pl.ds(pl.multiple_of(index * tile, tile), tile)
+    mine = pl.ds(pl.multiple_of(half * own, own), own)
+    theirs = pl.ds(pl.multiple_of((1 - half) * own, own), own)
 
     @pl.when(index == 0)
     def _():
         copies = []
-        for i in range(parts):
-            part = pl.ds(i * block, block)
-            copies.append(pltpu.make_async_copy(xs[i], x.at[part], sems.at[i]))
-            copies.append(pltpu.make_async_copy(dys[i], dy.at[part], sems.at[parts + i]))
+        for i, ref in enumerate((x_own, x_other)):
+            copies.append(pltpu.make_async_copy(ref, x.at[pl.ds(i * block, block)], sems.at[i]))
+        for i, ref in enumerate((dy_own, dy_other)):
+            copies.append(
+                pltpu.make_async_copy(ref, dy.at[pl.ds(i * block, block)], sems.at[2 + i])
+            )
         for copy in copies:
             copy.start()
         for copy in copies:
@@ -203,11 +239,30 @@
         if make:
             x_t[...] = x[...].T
 
+    up_full[mine, :] = up_ref[...]
+    down_full[...] = down_ref[...]
+
+    @pl.when(even)
+    def _():
+        up_full[theirs, :] = piece[:, columns]
+
+    @pl.when(jnp.logical_not(even))
+    def _():
+        up_full[theirs, :] = beside[:, columns]
+
+    @pl.when((index != half) & even)
+    def _():
+        down_full[...] = beside[...]
+
+    @pl.when((index != half) & jnp.logical_not(even))
+    def _():
+        down_full[...] = piece[...]
+
     bias_grad = jnp.zeros(bias_grad_ref.shape, F32)
-    for start in range(0, rows, chunk):
-        part = slice(start, start + chunk)
-        pre = contract(x[part, :], up_ref[...], 1, 0) + bias_ref[...]
-        d_hidden = contract(dy[part, :], down_ref[...], 1, 1)
+    for start in range(0, rows, block):
+        part = slice(start, start + block)
+        pre = contract(x[part, :], up_full[...], 1, 0) + bias_ref[...]
+        d_hidden = contract(dy[part, :], down_full[...], 1, 1)
         share = 0.5 * (1.0 + lax.erf(pre * 0.7071067811865476))
         hidden_ref[part, :] = (pre * share).astype(BF16)
         slope = share + pre * (jnp.exp(-0.5 * pre * pre) * 0.3989422804014327)
@@ -215,9 +270,6 @@
         d_pre_ref[part, :] = d_low
         bias_grad = bias_grad + jnp.sum(d_low.astype(F32), axis=0, keepdims=True)
     bias_grad_ref[...] = bias_grad
-    columns = pl.ds(pl.multiple_of(index * tile, tile), tile)
-    mine = pl.ds(pl.multiple_of(half * own, own), own)
-    theirs = pl.ds(pl.multiple_of((1 - half) * own, own), own)
     up_keep[:, columns] = contract(x_t[mine, :], d_pre_ref[...], 1, 0).astype(BF16)
     up_send[:, columns] = contract(x_t[theirs, :], d_pre_ref[...], 1, 0).astype(BF16)
     down_grad = contract(hidden_ref[...], dy[...], 0, 0).astype(BF16)
@@ -231,55 +283,475 @@
         down_send[...] = down_grad
 
 
-def feed(half, xs, dys, x_t, up, bias, down):
-    parts = len(xs)
-    width = xs[0].shape[1]
-    rows = sum(part.shape[0] for part in xs)
-    hidden = up.shape[1]
-    tile = hidden // 2
+def feed(scal, seconds, grads, x_t, up, down, piece, beside, bias, j, ranges):
+    local, width = seconds[0].shape
+    rows = 2 * local
+    tile = down.shape[0] // (2 * ranges)
+    hidden = 2 * tile
     make = x_t is None
-    chunk = rows // 2 if rows % 32 == 0 else rows
     anywhere = pl.BlockSpec(memory_space=pl.ANY)
-    fixed = lambda shape: pl.BlockSpec(shape, lambda j, s: (0, 0), pipeline_mode=pl.Buffered(1))
-    across = lambda size: pl.BlockSpec((size, tile), lambda j, s: (0, j))
-    out_specs = [across(rows)] * 2 + [fixed((width // 2, hidden))] * 2
-    out_specs += [fixed((tile, width))] * 2 + [across(1)]
-    out_shape = [
-        jax.ShapeDtypeStruct((rows, hidden), BF16),
-        jax.ShapeDtypeStruct((rows, hidden), BF16),
-        jax.ShapeDtypeStruct((width // 2, hidden), BF16),
-        jax.ShapeDtypeStruct((width // 2, hidden), BF16),
-        jax.ShapeDtypeStruct((tile, width), BF16),
-        jax.ShapeDtypeStruct((tile, width), BF16),
-        jax.ShapeDtypeStruct((1, hidden), F32),
-    ]
+
+    def fixed(*shape):
+        return pl.BlockSpec(shape, lambda t, s: (0, 0), pipeline_mode=pl.Buffered(1))
+
+    def across(size):
+        return pl.BlockSpec((size, tile), lambda t, s: (0, t))
+
+    shape = jax.ShapeDtypeStruct
+    out_specs = [across(rows)] * 2 + [fixed(width // 2, hidden)] * 2 + [fixed(tile, width)] * 2
+    out_specs += [across(1), across(width), pl.BlockSpec((tile, width), lambda t, s: (t, 0))]
+    out_shape = [shape((rows, hidden), BF16)] * 2 + [shape((width // 2, hidden), BF16)] * 2
+    out_shape += [shape((tile, width), BF16)] * 2
+    out_shape += [shape((1, hidden), F32), shape((width, hidden), BF16), shape((hidden, width), BF16)]
     if make:
-        out_specs.append(fixed((width, rows)))
-        out_shape.append(jax.ShapeDtypeStruct((width, rows), BF16))
+        out_specs.append(fixed(width, rows))
+        out_shape.append(shape((width, rows), BF16))
     return pl.pallas_call(
-        functools.partial(feed_kernel, parts=parts, make=make, chunk=chunk),
+        functools.partial(feed_kernel, make=make),
         grid_spec=pltpu.PrefetchScalarGridSpec(
             num_scalar_prefetch=1,
             grid=(2,),
-            in_specs=[anywhere] * (2 * parts)
-            + ([] if make else [fixed((width, rows))])
-            + [across(width), across(1), pl.BlockSpec((tile, width), lambda j, s: (j, 0))],
+            in_specs=[anywhere] * 4
+            + ([] if make else [fixed(width, rows)])
+            + [
+                pl.BlockSpec((width // 2, tile), lambda t, s: (0, (t * 2 + s[2]) * ranges + j)),
+                pl.BlockSpec((tile, width), lambda t, s: (s[2] * ranges + j, 0)),
+                fixed(width // 2, hidden),
+                fixed(tile, width),
+                across(1),
+            ],
             out_specs=out_specs,
             scratch_shapes=[
                 pltpu.VMEM((rows, width), BF16),
                 pltpu.VMEM((rows, width), BF16),
-                pltpu.SemaphoreType.DMA((2 * parts,)),
+                pltpu.SemaphoreType.DMA((4,)),
             ],
         ),
         out_shape=out_shape,
         compiler_params=pltpu.CompilerParams(vmem_limit_bytes=VMEM_LIMIT),
         cost_estimate=pl.CostEstimate(
-            flops=8 * rows * width * hidden,
+            flops=16 * rows * width * hidden,
             bytes_accessed=8 * rows * width + 8 * width * hidden,
             transcendentals=2 * rows * hidden,
         ),
         name="feed",
-    )(half.reshape(1), *xs, *dys, *(() if make else (x_t,)), up, bias, down)
+    )(scal, *seconds, *grads, *(() if make else (x_t,)), up, down, piece, beside, bias)
+
+
+def run(kernel, name, scal, grid, in_specs, out_specs, out_shape, args, flops=0, scratch=()):
+    moved = sum(a.size * a.dtype.itemsize for a in args)
+    return pl.pallas_call(
+        kernel,
+        grid_spec=pltpu.PrefetchScalarGridSpec(
+            num_scalar_prefetch=1,
+            grid=grid,
+            in_specs=in_specs,
+            out_specs=out_specs,
+            scratch_shapes=scratch,
+        ),
+        out_shape=out_shape,
+        compiler_params=pltpu.CompilerParams(vmem_limit_bytes=VMEM_LIMIT),
+        cost_estimate=pl.CostEstimate(flops=flops, bytes_accessed=2 * moved, transcendentals=0),
+        name=name,
+    )(scal, *args)
+
+
+def spec(shape, index):
+    return pl.BlockSpec(shape, index)
+
+
+def held(*shape):
+    return pl.BlockSpec(shape, lambda i, s: (0,) * len(shape), pipeline_mode=pl.Buffered(1))
+
+
+def struct(*shape, dtype=BF16):
+    return jax.ShapeDtypeStruct(shape, dtype)
+
+
+def pack_qkv(scal, weights):
+    rows, width = weights[0].shape
+    pairs = width // (2 * PAIR)
+    per = pairs // 2
+
+    def kernel(s_ref, q_ref, k_ref, v_ref, own_ref, mine_ref):
+        for i, ref in enumerate((q_ref, k_ref, v_ref)):
+            own_ref[:, i * PAIR : (i + 1) * PAIR] = ref[...]
+        start = pl.multiple_of(s_ref[1] * (rows // 2), rows // 2)
+        mine_ref[...] = own_ref[pl.ds(start, rows // 2), :]
+
+    block = spec((rows, PAIR), lambda p, s: (0, ((p // per) * 2 + s[2]) * per + p % per))
+    return run(
+        kernel, "pack_qkv", scal, (pairs,), [block] * 3,
+        [
+            spec((rows, 3 * PAIR), lambda p, s: (0, p)),
+            spec((rows // 2, 3 * PAIR), lambda p, s: (0, p)),
+        ],
+        [struct(rows, 3 * PAIR * pairs), struct(rows // 2, 3 * PAIR * pairs)],
+        weights,
+    )
+
+
+def pack_feed(scal, up, down, j, ranges):
+    rows, hidden = up.shape
+    tile = hidden // (4 * ranges)
+    columns = down.shape[1] // 2
+
+    def kernel(s_ref, up_ref, down_ref, out_ref):
+        out_ref[...] = jnp.where(s_ref[1] == 0, up_ref[...], down_ref[...])
+
+    return run(
+        kernel, "pack_feed", scal, (2,),
+        [
+            spec((rows, tile), lambda t, s: (0, (t * 2 + s[2]) * ranges + j)),
+            spec((tile, columns), lambda t, s: (s[2] * ranges + j, t)),
+        ],
+        spec((rows, tile), lambda t, s: (0, t)), struct(rows, 2 * tile), (up, down),
+    )
+
+
+def normalize(values):
+    centred = values - jnp.mean(values, axis=-1, keepdims=True)
+    spread = jnp.mean(centred * centred, axis=-1, keepdims=True)
+    inverse = lax.rsqrt(spread + EPS)
+    return centred * inverse, inverse
+
+
+def first_norm(scal, tokens, received, gain, shift):
+    rows, width = tokens.shape
+    step = rows // 2
+
+    def kernel(s_ref, t_ref, r_ref, gain_ref, shift_ref, x_ref, first_ref):
+        x = jnp.where(s_ref[3] == 1, t_ref[...], r_ref[...])
+        x_ref[...] = x
+        normed, _ = normalize(x.astype(F32))
+        first_ref[...] = (normed * gain_ref[...] + shift_ref[...]).astype(BF16)
+
+    block = spec((step, width), lambda i, s: (i, 0))
+    return run(
+        kernel, "first_norm", scal, (2,), [block, block, held(1, width), held(1, width)],
+        [block, block], [struct(rows, width)] * 2, (tokens, received, gain, shift),
+    )
+
+
+def project(scal, firsts, own, piece, beside, bias):
+    local, width = firsts[0].shape
+    rows, total = 2 * local, own.shape[1]
+    block = 3 * PAIR
+    half_rows, quarter_rows = width // 2, width // 4
+
+    def kernel(
+        s_ref, mine_ref, theirs_ref, own_ref, piece_ref, beside_ref, bias_ref, qkv_ref, w_ref,
+        all_ref, sems,
+    ):
+        @pl.when(pl.program_id(0) == 0)
+        def _():
+            copies = [
+                pltpu.make_async_copy(ref, all_ref.at[pl.ds(i * local, local)], sems.at[i])
+                for i, ref in enumerate((mine_ref, theirs_ref))
+            ]
+            for copy in copies:
+                copy.start()
+            for copy in copies:
+                copy.wait()
+
+        half, low = s_ref[0], s_ref[1]
+        other = (1 - half) * half_rows
+        w_ref[pl.ds(pl.multiple_of(half * half_rows, half_rows), half_rows), :] = own_ref[...]
+        start = pl.multiple_of(other + low * quarter_rows, quarter_rows)
+        w_ref[pl.ds(start, quarter_rows), :] = piece_ref[...]
+        start = pl.multiple_of(other + (1 - low) * quarter_rows, quarter_rows)
+        w_ref[pl.ds(start, quarter_rows), :] = beside_ref[...]
+        qkv_ref[...] = (contract(all_ref[...], w_ref[...], 1, 0) + bias_ref[...]).astype(BF16)
+
+    def columns(size):
+        return spec((size, block), lambda p, s: (0, p))
+
+    anywhere = pl.BlockSpec(memory_space=pl.ANY)
+    return run(
+        kernel, "project", scal, (total // block,),
+        [anywhere] * 2
+        + [columns(half_rows), columns(quarter_rows), columns(quarter_rows), columns(1)],
+        [columns(rows), columns(width), held(rows, width)],
+        [struct(rows, total), struct(width, total), struct(rows, width)],
+        (*firsts, own, piece, beside, bias), flops=2 * rows * width * total,
+        scratch=[pltpu.SemaphoreType.DMA((2,))],
+    )
+
+
+def out_other(scal, mixed, weight, piece, beside):
+    rows, set_width = mixed.shape
+    local, width = rows // 2, weight.shape[1]
+    block, small = set_width // 2, set_width // 4
+
+    def kernel(s_ref, mixed_ref, own_ref, piece_ref, beside_ref, out_ref, set_ref):
+        half, low = s_ref[0], s_ref[1]
+        other = (1 - half) * block
+        set_ref[pl.ds(pl.multiple_of(half * block, block), block), :] = own_ref[...]
+        set_ref[pl.ds(pl.multiple_of(other + low * small, small), small), :] = piece_ref[...]
+        start = pl.multiple_of(other + (1 - low) * small, small)
+        set_ref[pl.ds(start, small), :] = beside_ref[...]
+        out_ref[...] = contract(mixed_ref[...], set_ref[...], 1, 0).astype(BF16)
+
+    return run(
+        kernel, "out_other", scal, (1,),
+        [
+            spec((local, set_width), lambda i, s: (1, 0)),
+            spec((block, width), lambda i, s: (s[2], 0)),
+            held(small, width), held(small, width),
+        ],
+        [held(local, width), held(set_width, width)],
+        [struct(local, width), struct(set_width, width)],
+        (mixed, weight, piece, beside), flops=2 * local * set_width * width,
+    )
+
+
+def second_norm(scal, mixed, out_set, x, received, bias, gain, shift):
+    rows, set_width = mixed.shape
+    local, width = x.shape
+    step = local // 2
+
+    def kernel(
+        s_ref, mixed_ref, w_ref, x_ref, r_ref, bias_ref, gain_ref, shift_ref, mid_ref, second_ref
+    ):
+        middle = contract(mixed_ref[...], w_ref[...], 1, 0) + r_ref[...].astype(F32)
+        middle = middle + x_ref[...].astype(F32) + bias_ref[...]
+        mid_ref[...] = middle
+        normed, _ = normalize(middle)
+        second_ref[...] = (normed * gain_ref[...] + shift_ref[...]).astype(BF16)
+
+    block = spec((step, width), lambda i, s: (i, 0))
+    return run(
+        kernel, "second_norm", scal, (2,),
+        [spec((step, set_width), lambda i, s: (i, 0)), held(set_width, width), block, block]
+        + [held(1, width)] * 3,
+        [block, block], [struct(local, width, dtype=F32), struct(local, width)],
+        (mixed, out_set, x, received, bias, gain, shift), flops=2 * local * set_width * width,
+    )
+
+
+def other_rows(scal, lefts, rights, name):
+    rows = lefts[0].shape[0]
+    width = rights[0].shape[0]
+    local = rows // 2
+    count = len(lefts)
+    step = width // 4
+
+    def kernel(s_ref, *refs):
+        total = contract(refs[0][...], refs[count][...], 1, 1)
+        for j in range(1, count):
+            total = total + contract(refs[j][...], refs[count + j][...], 1, 1)
+        refs[-1][...] = total.astype(BF16)
+
+    def fixed(size):
+        return pl.BlockSpec((local, size), lambda i, s: (1, 0), pipeline_mode=pl.Buffered(1))
+
+    return run(
+        kernel, name, scal, (4,),
+        [fixed(a.shape[1]) for a in lefts]
+        + [spec((step, a.shape[1]), lambda i, s: (i, 0)) for a in rights],
+        spec((local, step), lambda i, s: (0, i)), struct(local, width), (*lefts, *rights),
+        flops=sum(2 * local * a.shape[1] * width for a in lefts),
+    )
+
+
+def norm_back_rows(grad, normed, inverse, gain):
+    scaled = grad * gain
+    first_term = jnp.mean(scaled, axis=-1, keepdims=True)
+    second_term = jnp.mean(scaled * normed, axis=-1, keepdims=True)
+    return inverse * (scaled - first_term - normed * second_term)
+
+
+def column_sums(refs, values):
+    @pl.when(pl.program_id(0) == 0)
+    def _():
+        refs[...] = jnp.zeros_like(refs)
+
+    for i, value in enumerate(values):
+        refs[i : i + 1, :] += jnp.sum(value, axis=0, keepdims=True)
+
+
+def second_back(scal, d_pres, ups, received, middle, dy, gain):
+    local, width = middle.shape
+    step = local // 2
+    count = len(d_pres)
+
+    def kernel(s_ref, *refs):
+        r_ref, mid_ref, dy_ref, gain_ref, wide_ref, low_ref, sums_ref = refs[2 * count :]
+        grad = r_ref[...].astype(F32)
+        for j in range(count):
+            grad = grad + contract(refs[j][...], refs[count + j][...], 1, 1)
+        normed, inverse = normalize(mid_ref[...])
+        dy_wide = dy_ref[...].astype(F32)
+        wide = dy_wide + norm_back_rows(grad, normed, inverse, gain_ref[...])
+        low = wide.astype(BF16)
+        wide_ref[...] = wide
+        low_ref[...] = low
+        column_sums(sums_ref, (grad * normed, grad, dy_wide, low.astype(F32)))
+
+    block = spec((step, width), lambda i, s: (i, 0))
+    return run(
+        kernel, "second_back", scal, (2,),
+        [spec((step, a.shape[1]), lambda i, s: (i, 0)) for a in d_pres]
+        + [held(*a.shape) for a in ups] + [block] * 3 + [held(1, width)],
+        [block, block, held(8, width)],
+        [struct(local, width, dtype=F32), struct(local, width), struct(8, width, dtype=F32)],
+        (*d_pres, *ups, received, middle, dy, gain),
+        flops=sum(2 * local * a.shape[1] * width for a in d_pres),
+    )
+
+
+def mixed_back(scal, lows, out_set, mixed):
+    local, width = lows[0].shape
+    rows, set_width = mixed.shape
+    block = set_width // 2
+
+    def kernel(
+        s_ref, mine_ref, theirs_ref, w_ref, mixed_ref, d_ref, send_ref, keep_ref, low, sems
+    ):
+        @pl.when(pl.program_id(0) == 0)
+        def _():
+            copies = [
+                pltpu.make_async_copy(ref, low.at[pl.ds(i * local, local)], sems.at[i])
+                for i, ref in enumerate((mine_ref, theirs_ref))
+            ]
+            for copy in copies:
+                copy.start()
+            for copy in copies:
+                copy.wait()
+
+        d_ref[...] = contract(low[...], w_ref[...], 1, 1).astype(BF16)
+        grad = contract(mixed_ref[...], low[...], 0, 0).astype(BF16)
+
+        @pl.when(pl.program_id(0) == s_ref[0])
+        def _():
+            keep_ref[...] = grad
+
+        @pl.when(pl.program_id(0) != s_ref[0])
+        def _():
+            send_ref[...] = grad
+
+    anywhere = pl.BlockSpec(memory_space=pl.ANY)
+    across = spec((rows, block), lambda t, s: (0, t))
+    return run(
+        kernel, "mixed_back", scal, (2,),
+        [anywhere] * 2 + [spec((block, width), lambda t, s: (t, 0)), across],
+        [across, held(block, width), held(block, width)],
+        [struct(rows, set_width), struct(block, width), struct(block, width)],
+        (*lows, out_set, mixed), flops=4 * rows * set_width * width,
+        scratch=[pltpu.VMEM((rows, width), BF16), pltpu.SemaphoreType.DMA((2,))],
+    )
+
+
+def first_back(scal, dqkvs, weights, received, x, wide, gain):
+    local, width = x.shape
+    step = local // 2
+    count = len(dqkvs)
+
+    def kernel(s_ref, *refs):
+        r_ref, x_ref, wide_ref, gain_ref, out_ref, sums_ref = refs[2 * count :]
+        grad = r_ref[...].astype(F32)
+        for j in range(count):
+            grad = grad + contract(refs[j][...], refs[count + j][...], 1, 1)
+        normed, inverse = normalize(x_ref[...].astype(F32))
+        total = wide_ref[...] + norm_back_rows(grad, normed, inverse, gain_ref[...])
+        out_ref[...] = total.astype(BF16)
+        column_sums(sums_ref, (grad * normed, grad))
+
+    block = spec((step, width), lambda i, s: (i, 0))
+    return run(
+        kernel, "first_back", scal, (2,),
+        [spec((step, a.shape[1]), lambda i, s: (i, 0)) for a in dqkvs]
+        + [
+            pl.BlockSpec((width, a.shape[1]), functools.partial(lambda j, i, s: (0, j), j),
+                         pipeline_mode=pl.Buffered(1))
+            for j, a in enumerate(dqkvs)
+        ]
+        + [block] * 3 + [held(1, width)],
+        [block, held(8, width)],
+        [struct(local, width), struct(8, width, dtype=F32)],
+        (*dqkvs, *([weights] * count), received, x, wide, gain),
+        flops=sum(2 * local * a.shape[1] * width for a in dqkvs),
+    )
+
+
+def first_other(scal, dqkvs, weights):
+    rows = dqkvs[0].shape[0]
+    width = weights.shape[0]
+    local = rows // 2
+    count = len(dqkvs)
+    step = width // 4
+
+    def kernel(s_ref, *refs):
+        total = contract(refs[0][...], refs[count][...], 1, 1)
+        for j in range(1, count):
+            total = total + contract(refs[j][...], refs[count + j][...], 1, 1)
+        refs[-1][...] = total.astype(BF16)
+
+    return run(
+        kernel, "first_other", scal, (4,),
+        [
+            pl.BlockSpec((local, a.shape[1]), lambda i, s: (1, 0), pipeline_mode=pl.Buffered(1))
+            for a in dqkvs
+        ]
+        + [
+            pl.BlockSpec((step, a.shape[1]), functools.partial(lambda j, i, s: (i, j), j))
+            for j, a in enumerate(dqkvs)
+        ],
+        spec((local, step), lambda i, s: (0, i)), struct(local, width),
+        (*dqkvs, *([weights] * count)),
+        flops=sum(2 * local * a.shape[1] * width for a in dqkvs),
+    )
+
+
+def layer_other(scal, hiddens, downs):
+    rows = hiddens[0].shape[0]
+    width = downs[0].shape[1]
+    local = rows // 2
+    count = len(hiddens)
+    step = width // 4
+
+    def kernel(s_ref, *refs):
+        total = contract(refs[0][...], refs[count][...], 1, 0)
+        for j in range(1, count):
+            total = total + contract(refs[j][...], refs[count + j][...], 1, 0)
+        refs[-1][...] = total.astype(BF16)
+
+    return run(
+        kernel, "layer_other", scal, (4,),
+        [
+            pl.BlockSpec((local, a.shape[1]), lambda i, s: (1, 0), pipeline_mode=pl.Buffered(1))
+            for a in hiddens
+        ]
+        + [spec((a.shape[0], step), lambda i, s: (0, i)) for a in downs],
+        spec((local, step), lambda i, s: (0, i)), struct(local, width), (*hiddens, *downs),
+        flops=sum(2 * local * a.shape[1] * width for a in hiddens),
+    )
+
+
+def layer_own(scal, hiddens, downs, received, middle, bias):
+    local, width = middle.shape
+    count = len(hiddens)
+    step = width // 4
+
+    def kernel(s_ref, *refs):
+        r_ref, mid_ref, bias_ref, out_ref = refs[2 * count :]
+        total = mid_ref[...] + r_ref[...].astype(F32) + bias_ref[...]
+        for j in range(count):
+            total = total + contract(refs[j][...], refs[count + j][...], 1, 0)
+        out_ref[...] = total.astype(BF16)
+
+    across = spec((local, step), lambda i, s: (0, i))
+    return run(
+        kernel, "layer_own", scal, (4,),
+        [
+            pl.BlockSpec((local, a.shape[1]), lambda i, s: (0, 0), pipeline_mode=pl.Buffered(1))
+            for a in hiddens
+        ]
+        + [spec((a.shape[0], step), lambda i, s: (0, i)) for a in downs]
+        + [across, across, spec((1, step), lambda i, s: (0, i))],
+        across, struct(local, width), (*hiddens, *downs, received, middle, bias),
+        flops=sum(2 * local * a.shape[1] * width for a in hiddens),
+    )
 
 
 def finish_feed_kernel(core_ref, *refs, ranges, tile):
@@ -329,36 +801,231 @@
 
 
 def finish_qkv_kernel(core_ref, *refs, pairs):
-    owns, others, outs = refs[:2], refs[2:4], refs[4:]
+    outs = refs[-3:]
+    count = (len(refs) - 3) // 2
+    owns, others = refs[:count], refs[count : 2 * count]
     first = core_ref[0] == 0
-    for h in range(2):
-        own, other = owns[h][...], others[h][...]
+    per = pairs // count
+    half_pairs = pairs // 2
+    for g in range(count):
+        own, other = owns[g][...], others[g][...]
         values = (jnp.where(first, own, other), jnp.where(first, other, own))
         for c in range(2):
-            for p in range(pairs):
+            wide = values[c].astype(F32).T
+            for q in range(per):
+                pair = g * per + q
+                h, p = pair // half_pairs, pair % half_pairs
+                goal = ((h * 2 + c) * half_pairs + p) * PAIR
                 for i in range(3):
-                    start = (p * 3 + i) * PAIR
-                    goal = ((h * 2 + c) * pairs + p) * PAIR
-                    outs[i][:, goal : goal + PAIR] = values[c][:, start : start + PAIR].astype(F32)
+                    start = (q * 3 + i) * PAIR
+                    outs[i][:, goal : goal + PAIR] = wide[:, start : start + PAIR]
 
 
 def finish_qkv(core, owns, others):
-    rows, columns = owns[0].shape
-    pairs = columns // (3 * PAIR)
+    columns, rows = owns[0].shape
+    pairs = len(owns) * columns // (3 * PAIR)
     steps = 4
-    spec = pl.BlockSpec((rows // steps, columns), lambda i, s: (i, 0))
+    block = pl.BlockSpec((columns, rows // steps), lambda i, s: (0, i))
     return pl.pallas_call(
         functools.partial(finish_qkv_kernel, pairs=pairs),
         grid_spec=pltpu.PrefetchScalarGridSpec(
             num_scalar_prefetch=1,
             grid=(steps,),
-            in_specs=[spec] * 4,
-            out_specs=[pl.BlockSpec((rows // steps, 4 * pairs * PAIR), lambda i, s: (i, 0))] * 3,
+            in_specs=[block] * (2 * len(owns)),
+            out_specs=[pl.BlockSpec((rows // steps, 2 * pairs * PAIR), lambda i, s: (i, 0))] * 3,
         ),
-        out_shape=[jax.ShapeDtypeStruct((rows, 4 * pairs * PAIR), F32)] * 3,
+        out_shape=[jax.ShapeDtypeStruct((rows, 2 * pairs * PAIR), F32)] * 3,
         compiler_params=pltpu.CompilerParams(vmem_limit_bytes=VMEM_LIMIT),
         name="finish_qkv",
     )(core.reshape(1), *owns, *others)
+
+
+def wide_back_kernel(
+    tile, rows, padded, qkv_ref, grad_ref, out_ref, lse_ref, dqkv_ref, q_t, g_t, k_t, delta,
+    dq_t, dk_t, dv_t,
+):
+    scale = HEAD_DIM**-0.5
+    q_t[:, :rows] = qkv_ref[:, :PAIR].T
+    g_t[:, :rows] = grad_ref[...].T
+    if padded > rows:
+        q_t[:, rows:] = jnp.zeros((PAIR, padded - rows), BF16)
+        g_t[:, rows:] = jnp.zeros((PAIR, padded - rows), BF16)
+        delta[:, rows:] = jnp.zeros((2, padded - rows), F32)
+    k_t[...] = qkv_ref[:, PAIR : 2 * PAIR].T
+    product = (grad_ref[...].astype(F32) * out_ref[...].astype(F32)).T
+    delta[0:1, :rows] = jnp.sum(product[:HEAD_DIM, :], axis=0, keepdims=True)
+    delta[1:2, :rows] = jnp.sum(product[HEAD_DIM:, :], axis=0, keepdims=True)
+    dk_t[...] = jnp.zeros_like(dk_t)
+    dv_t[...] = jnp.zeros_like(dv_t)
+
+    def block(index, carry):
+        columns = pl.ds(pl.multiple_of(index * tile, tile), tile)
+        empty = jnp.zeros((HEAD_DIM, tile), BF16)
+        for head in range(2):
+            lanes = slice(head * HEAD_DIM, (head + 1) * HEAD_DIM)
+            query = q_t[lanes, columns]
+            grad = g_t[lanes, columns]
+            query_pad = jnp.concatenate([query, empty] if head == 0 else [empty, query], axis=0)
+            grad_pad = jnp.concatenate([grad, empty] if head == 0 else [empty, grad], axis=0)
+            scores = contract(qkv_ref[:, PAIR : 2 * PAIR], query_pad, 1, 0)
+            grad_probs = contract(qkv_ref[:, 2 * PAIR :], grad_pad, 1, 0)
+            weights = jnp.exp2(scores * (scale * LOG2E) - lse_ref[head : head + 1, columns])
+            grad_scores = (weights * (grad_probs - delta[head : head + 1, columns])).astype(BF16)
+            dv_t[lanes, :] += contract(grad, weights.astype(BF16), 1, 1)
+            dq_t[lanes, columns] = contract(k_t[lanes, :], grad_scores, 1, 0)
+            dk_t[lanes, :] += contract(query, grad_scores, 1, 1)
+        return carry
+
+    lax.fori_loop(0, padded // tile, block, 0)
+    dqkv_ref[:, :PAIR] = (dq_t[...].T[:rows, :] * scale).astype(BF16)
+    dqkv_ref[:, PAIR : 2 * PAIR] = (dk_t[...].T * scale).astype(BF16)
+    dqkv_ref[:, 2 * PAIR :] = dv_t[...].T.astype(BF16)
+
+
+def wide_back(qkv, grad, out, lse, first_pair, last_pair, tile=256):
+    rows, width = qkv.shape
+    padded = -(-rows // tile) * tile
+    count = last_pair - first_pair
+    return pl.pallas_call(
+        functools.partial(wide_back_kernel, tile, rows, padded),
+        grid=(count,),
+        in_specs=[
+            pl.BlockSpec((rows, 3 * PAIR), lambda i: (0, i + first_pair)),
+            pl.BlockSpec((rows, PAIR), lambda i: (0, i + first_pair)),
+            pl.BlockSpec((rows, PAIR), lambda i: (0, i + first_pair)),
+            pl.BlockSpec((None, 2, lse.shape[2]), lambda i: (i + first_pair, 0, 0)),
+        ],
+        out_specs=pl.BlockSpec((rows, 3 * PAIR), lambda i: (0, i)),
+        out_shape=jax.ShapeDtypeStruct((rows, 3 * PAIR * count), BF16),
+        scratch_shapes=[
+            pltpu.VMEM((PAIR, padded), BF16),
+            pltpu.VMEM((PAIR, padded), BF16),
+            pltpu.VMEM((PAIR, rows), BF16),
+            pltpu.VMEM((2, padded), F32),
+            pltpu.VMEM((PAIR, padded), F32),
+            pltpu.VMEM((PAIR, rows), F32),
+            pltpu.VMEM((PAIR, rows), F32),
+        ],
+        compiler_params=pltpu.CompilerParams(vmem_limit_bytes=VMEM_LIMIT),
+        cost_estimate=pl.CostEstimate(
+            flops=160 * rows * rows * PAIR * count,
+            bytes_accessed=16 * rows * PAIR * count,
+            transcendentals=2 * rows * rows * count,
+        ),
+        name="wide_back",
+    )(qkv, grad, out, lse)
+
+
+def wide_feed_kernel(
+    half_ref, *refs, parts, make, chunk,
+):
+    xs, refs = refs[:parts], refs[parts:]
+    dys, refs = refs[:parts], refs[parts:]
+    if not make:
+        x_t, refs = refs[0], refs[1:]
+    up_ref, bias_ref, down_ref, *refs = refs
+    hidden_ref, d_pre_ref, up_send, up_keep, down_send, down_keep, bias_grad_ref, *refs = refs
+    if make:
+        x_t, refs = refs[0], refs[1:]
+    x, dy, sems = refs
+    index = pl.program_id(0)
+    half = half_ref[0]
+    rows, width = x.shape
+    block = rows // parts
+    own = width // 2
+    tile = up_ref.shape[1]
+
+    @pl.when(index == 0)
+    def _():
+        copies = []
+        for i in range(parts):
+            part = pl.ds(i * block, block)
+            copies.append(pltpu.make_async_copy(xs[i], x.at[part], sems.at[i]))
+            copies.append(pltpu.make_async_copy(dys[i], dy.at[part], sems.at[parts + i]))
+        for copy in copies:
+            copy.start()
+        for copy in copies:
+            copy.wait()
+        if make:
+            x_t[...] = x[...].T
+
+    bias_grad = jnp.zeros(bias_grad_ref.shape, F32)
+    for start in range(0, rows, chunk):
+        part = slice(start, start + chunk)
+        pre = contract(x[part, :], up_ref[...], 1, 0) + bias_ref[...]
+        d_hidden = contract(dy[part, :], down_ref[...], 1, 1)
+        share = 0.5 * (1.0 + lax.erf(pre * 0.7071067811865476))
+        hidden_ref[part, :] = (pre * share).astype(BF16)
+        slope = share + pre * (jnp.exp(-0.5 * pre * pre) * 0.3989422804014327)
+        d_low = (d_hidden * slope).astype(BF16)
+        d_pre_ref[part, :] = d_low
+        bias_grad = bias_grad + jnp.sum(d_low.astype(F32), axis=0, keepdims=True)
+    bias_grad_ref[...] = bias_grad
+    columns = pl.ds(pl.multiple_of(index * tile, tile), tile)
+    mine = pl.ds(pl.multiple_of(half * own, own), own)
+    theirs = pl.ds(pl.multiple_of((1 - half) * own, own), own)
+    up_keep[:, columns] = contract(x_t[mine, :], d_pre_ref[...], 1, 0).astype(BF16)
+    up_send[:, columns] = contract(x_t[theirs, :], d_pre_ref[...], 1, 0).astype(BF16)
+    down_grad = contract(hidden_ref[...], dy[...], 0, 0).astype(BF16)
+
+    @pl.when(index == half)
+    def _():
+        down_keep[...] = down_grad
+
+    @pl.when(index != half)
+    def _():
+        down_send[...] = down_grad
+
+
+def wide_feed(half, xs, dys, x_t, up, bias, down):
+    parts = len(xs)
+    width = xs[0].shape[1]
+    rows = sum(part.shape[0] for part in xs)
+    hidden = up.shape[1]
+    tile = hidden // 2
+    make = x_t is None
+    chunk = rows // 2 if rows % 32 == 0 else rows
+    anywhere = pl.BlockSpec(memory_space=pl.ANY)
+    fixed = lambda shape: pl.BlockSpec(shape, lambda j, s: (0, 0), pipeline_mode=pl.Buffered(1))
+    across = lambda size: pl.BlockSpec((size, tile), lambda j, s: (0, j))
+    out_specs = [across(rows)] * 2 + [fixed((width // 2, hidden))] * 2
+    out_specs += [fixed((tile, width))] * 2 + [across(1)]
+    out_shape = [
+        jax.ShapeDtypeStruct((rows, hidden), BF16),
+        jax.ShapeDtypeStruct((rows, hidden), BF16),
+        jax.ShapeDtypeStruct((width // 2, hidden), BF16),
+        jax.ShapeDtypeStruct((width // 2, hidden), BF16),
+        jax.ShapeDtypeStruct((tile, width), BF16),
+        jax.ShapeDtypeStruct((tile, width), BF16),
+        jax.ShapeDtypeStruct((1, hidden), F32),
+    ]
+    if make:
+        out_specs.append(fixed((width, rows)))
+        out_shape.append(jax.ShapeDtypeStruct((width, rows), BF16))
+    return pl.pallas_call(
+        functools.partial(wide_feed_kernel, parts=parts, make=make, chunk=chunk),
+        grid_spec=pltpu.PrefetchScalarGridSpec(
+            num_scalar_prefetch=1,
+            grid=(2,),
+            in_specs=[anywhere] * (2 * parts)
+            + ([] if make else [fixed((width, rows))])
+            + [across(width), across(1), pl.BlockSpec((tile, width), lambda j, s: (j, 0))],
+            out_specs=out_specs,
+            scratch_shapes=[
+                pltpu.VMEM((rows, width), BF16),
+                pltpu.VMEM((rows, width), BF16),
+                pltpu.SemaphoreType.DMA((2 * parts,)),
+            ],
+        ),
+        out_shape=out_shape,
+        compiler_params=pltpu.CompilerParams(vmem_limit_bytes=VMEM_LIMIT),
+        cost_estimate=pl.CostEstimate(
+            flops=8 * rows * width * hidden,
+            bytes_accessed=8 * rows * width + 8 * width * hidden,
+            transcendentals=2 * rows * hidden,
+        ),
+        name="wide_feed",
+    )(half.reshape(1), *xs, *dys, *(() if make else (x_t,)), up, bias, down)
 
 
 def norm_parts(values, gain, shift):
@@ -390,7 +1057,7 @@
     return lax.optimization_barrier((values,) + earlier)[0]
 
 
-def body(
+def wide_body(
     rep, grp, tokens, query_weight, key_weight, value_weight, query_bias, value_bias, out_weight,
     out_bias, first_gain, first_shift, second_gain, second_shift, up_weight, up_bias,
     down_weight, down_bias, cotangent,
@@ -542,7 +1209,7 @@
     x_t = None
     feeds = []
     for j in range(ranges):
-        outs = feed(
+        outs = wide_feed(
             half, seconds, grads_out, x_t, up_sets[j],
             bias_sets[j] if j == 0 else after(bias_sets[j], feeds[-1][6]), down_sets[j],
         )
@@ -622,7 +1289,7 @@
     dqkvs, qkv_halves = [], []
     for begin, end in spans:
         gate = lse if not dqkvs else after(lse, qkv_halves[-1])
-        dqkvs.append(attend_back(qkv, grad_mixed, mixed, gate, begin, end))
+        dqkvs.append(wide_back(qkv, grad_mixed, mixed, gate, begin, end))
         qkv_halves.append(contract(first, dqkvs[-1], 0, 0).astype(BF16))
     qkv_halves = [reduce_rows(scatter_half(values)) for values in qkv_halves]
 
@@ -649,14 +1316,7 @@
     tokens_grad = move((grad_middle + grad_first).astype(BF16), back).reshape(1, local, width)
 
     out_weight_grad = join(out_half, swap_core(out_half), core).reshape(-1, width).astype(F32)
-    if grp == 2:
-        up_weight_grad, down_weight_grad = finish_feed(
-            core, sums_feed, [swap_core(values) for values in sums_feed]
-        )
-        query_weight_grad, key_weight_grad, value_weight_grad = finish_qkv(
-            core, qkv_halves, [swap_core(values) for values in qkv_halves]
-        )
-    else:
+    if True:
 
         def finish_columns(values):
             values = values.reshape(quarter, own_rows, 1, -1)
@@ -715,6 +1375,300 @@
     )
 
 
+class RingSum:
+    def __init__(self, place, ring, sends, keeps):
+        self.low, self.high = place % 2, place // 2
+        self.ring, self.deep = ring, ring // 2
+        self.beside = [(i, i ^ 1) for i in range(ring)]
+        self.keeps = keeps
+        self.sends = sends
+        self.received = [lax.ppermute(send, "half", SWAP) for send in sends]
+
+    def route(self, shift):
+        return [(i, (i + 2 * shift) % self.ring) for i in range(self.ring)]
+
+    def to_neighbour(self, *gates):
+        received = list(after_all(self.received, *gates))
+        totals = [
+            (keep.astype(F32) + other.astype(F32)).astype(BF16)
+            for keep, other in zip(self.keeps, received)
+        ]
+        if len(totals) == 1:
+            size = totals[0].shape[0] // 2
+            totals = [totals[0][:size], totals[0][size:]]
+        even = self.low == 0
+        self.keep = jnp.where(even, totals[0], totals[1])
+        self.sent = jnp.where(even, totals[1], totals[0])
+        self.received = [lax.ppermute(self.sent, "rz", self.beside)]
+        return self.sent
+
+    def along(self, *gates):
+        (received,) = after_all(self.received, *gates)
+        total = (self.keep.astype(F32) + received.astype(F32)).astype(BF16)
+        self.shape = total.shape
+        total = total.reshape(self.deep, -1, total.shape[-1])
+        self.keep = pick(total, self.high, 0)
+        shifts = range(1, self.deep)
+        sent = [pick(total, (self.high + s) % self.deep, 0) for s in shifts]
+        self.received = [lax.ppermute(p, "rz", self.route(s)) for p, s in zip(sent, shifts)]
+        return sent[0]
+
+    def spread(self, *gates):
+        piece = self.keep.astype(F32)
+        for other in after_all(self.received, *gates):
+            piece = piece + other.astype(F32)
+        self.piece = piece.astype(BF16)
+        self.received = [
+            lax.ppermute(self.piece, "rz", self.route(s)) for s in range(1, self.deep)
+        ]
+        return self.piece
+
+    def back_to_neighbour(self, *gates):
+        gathered = [self.piece] + list(after_all(self.received, *gates))
+        deep = self.deep
+        self.whole = jnp.stack(
+            [
+                functools.reduce(
+                    lambda rest, s: jnp.where((self.high - s) % deep == i, gathered[s], rest),
+                    range(1, deep),
+                    gathered[0],
+                )
+                for i in range(deep)
+            ]
+        ).reshape(self.shape)
+        self.received = [
+            lax.ppermute(self.whole, "rz", self.beside),
+            lax.ppermute(self.whole, "core", SWAP),
+        ]
+        return self.whole
+
+    def to_core(self, *gates):
+        neighbour, whole = after_all(self.received, *gates)
+        crossed = lax.ppermute(neighbour, "core", SWAP)
+        even = self.low == 0
+        self.own = (jnp.where(even, self.whole, neighbour), jnp.where(even, neighbour, self.whole))
+        self.other = (jnp.where(even, whole, crossed), jnp.where(even, crossed, whole))
+        return neighbour
+
+
+def after_all(values, *gates):
+    if not gates:
+        return tuple(values)
+    return lax.optimization_barrier(tuple(values) + gates)[: len(values)]
+
+
+def pair_body(
+    rep, grp, tokens, query_weight, key_weight, value_weight, query_bias, value_bias, out_weight,
+    out_bias, first_gain, first_shift, second_gain, second_shift, up_weight, up_bias,
+    down_weight, down_bias, cotangent,
+):
+    clips, local, width = tokens.shape
+    assert clips == 1
+    ring = rep // 2
+    core, half, place = lax.axis_index("core"), lax.axis_index("half"), lax.axis_index("rz")
+    low = place % 2
+    own_rows = width // 2
+    pairs = own_rows // PAIR
+    hidden = up_weight.shape[1]
+    ranges = hidden // (2 * width)
+    tile = hidden // (4 * ranges)
+    stays = core == half
+    scal = jnp.stack([half, low, core, stays.astype(jnp.int32)]).astype(jnp.int32)
+    cross = [(1, 2), (2, 1)]
+    beside = [(i, i ^ 1) for i in range(ring)]
+
+    def swap_half(values):
+        return lax.ppermute(values, "half", SWAP)
+
+    def swap_core(values):
+        return lax.ppermute(values, "core", SWAP)
+
+    def swap_low(values):
+        return lax.ppermute(values, "rz", beside)
+
+    def cross_over(values):
+        return lax.ppermute(values, ("core", "half"), cross)
+
+    tokens, cotangent = tokens.reshape(local, width), cotangent.reshape(local, width)
+
+    tokens_in = cross_over(tokens)
+    own_qkv, mine = pack_qkv(scal, (query_weight, key_weight, value_weight))
+    qkv_x = swap_half(mine)
+    vectors = jnp.concatenate(
+        [query_bias, value_bias, out_bias, first_gain, first_shift, second_gain, second_shift,
+         down_bias, up_bias]
+    )
+    vectors = join(vectors, swap_half(vectors), half)
+    (full_qbias, full_vbias, full_obias, gain_one, shift_one, gain_two, shift_two, full_dbias) = [
+        vectors[:, i * own_rows : (i + 1) * own_rows].reshape(1, width) for i in range(8)
+    ]
+
+    def set_entries(values, inner=1):
+        return pick(values.reshape(2, 2, inner, -1), core, 1).transpose(1, 0, 2).reshape(inner, -1)
+
+    bias_sets = set_entries(vectors[:, 8 * own_rows :], ranges)
+    packed_feed = [pack_feed(scal, up_weight, down_weight, j, ranges) for j in range(ranges)]
+    quarter = own_rows // 4
+    out_mine = lax.dynamic_slice(
+        out_weight, (core * (own_rows // 2) + low * quarter, 0 * core), (quarter, width)
+    )
+
+    x, first = first_norm(scal, tokens, tokens_in, gain_one, shift_one)
+    first_in = swap_core(first)
+    qkv_x, out_mine, *packed_feed = lax.optimization_barrier((qkv_x, out_mine, *packed_feed))
+    qkv_y = swap_low(qkv_x)
+    out_x = swap_half(out_mine)
+    feed_x = [swap_half(packed_feed[0])]
+    cotangent_in = cross_over(after(cotangent, qkv_x))
+    zeros = jnp.zeros((pairs, PAIR), F32)
+    qkv_bias = jnp.stack(
+        [set_entries(full_qbias).reshape(pairs, PAIR), zeros,
+         set_entries(full_vbias).reshape(pairs, PAIR)],
+        axis=1,
+    ).reshape(1, 3 * own_rows)
+    qkv, qkv_weight, first_all = project(
+        scal, (first, first_in), own_qkv, qkv_x, qkv_y, qkv_bias
+    )
+
+    kept = attend(qkv, 0, pairs // 2)
+    out_x, feed_x[0], lse = lax.optimization_barrier((out_x, feed_x[0], kept[1]))
+    out_y = swap_low(out_x)
+    feed_y = [swap_low(feed_x[0])]
+    for j in range(1, ranges):
+        feed_x.append(swap_half(after(packed_feed[j], lse)))
+    mixed, lse = attend(qkv, pairs // 2, pairs, (kept[0], lse))
+    for j in range(1, ranges):
+        feed_x[j], lse = lax.optimization_barrier((feed_x[j], lse))
+        feed_y.append(swap_low(feed_x[j]))
+    out_part, out_set = out_other(scal, mixed, out_weight, out_x, out_y)
+    out_in = swap_core(out_part)
+    grad_out = jnp.where(stays, cotangent, cotangent_in)
+    grad_out_in = swap_core(grad_out)
+    middle, second = second_norm(
+        scal, mixed, out_set, x, out_in, full_obias, gain_two, shift_two
+    )
+    second_in = swap_core(second)
+
+    feeds, sums = [], []
+    x_t = None
+    for j in range(ranges):
+        bias = bias_sets[j : j + 1]
+        if feeds:
+            bias = after(bias, feeds[-1][6], feeds[-1][2])
+        outs = feed(
+            scal, (second, second_in), (grad_out, grad_out_in), x_t, up_weight, down_weight,
+            feed_x[j], feed_y[j], bias, j, ranges,
+        )
+        x_t = outs[9] if j == 0 else x_t
+        feeds.append(outs)
+        sums.append(RingSum(place, ring, [outs[2], outs[4]], [outs[3], outs[5]]))
+    hiddens, d_pres = [f[0] for f in feeds], [f[1] for f in feeds]
+    ups, downs = [f[7] for f in feeds], [f[8] for f in feeds]
+    grad_part = other_rows(scal, d_pres, ups, "feed_other")
+    grad_in = swap_core(grad_part)
+    layer_part = layer_other(scal, hiddens, downs)
+    grad_wide, grad_low, sums_two = second_back(
+        scal, d_pres, ups, grad_in, middle, grad_out, gain_two
+    )
+    grad_low_in = swap_core(grad_low)
+    grad_mixed, out_send, out_keep = mixed_back(scal, (grad_low, grad_low_in), out_set, mixed)
+
+    first_sum, last_sum = sums[0], sums[-1]
+    issued = [first_sum.to_neighbour(grad_mixed)]
+    out_sum = None
+    backs, qkv_sums = [], []
+    groups = 2
+    per = pairs // groups
+    for pair in range(pairs):
+        gate = after(lse, *issued)
+        outs = attend_back(scal, qkv, grad_mixed, mixed, gate, first_all, pair, pair + 1)
+        backs.append(outs)
+        done = outs[3]
+        issued = [done]
+        if pair == 0:
+            issued.append(first_sum.along(done))
+        elif pair == 1:
+            issued.append(first_sum.spread(done))
+            issued.append(last_sum.to_neighbour(done))
+            out_sum = RingSum(place, ring, [after(out_send, done)], [out_keep])
+        elif pair == 2:
+            issued.append(first_sum.back_to_neighbour(done))
+            issued.append(last_sum.along(done))
+            issued.append(out_sum.to_neighbour(done))
+    qkv_sums = [RingSum(place, ring, [b[1]], [b[2]]) for b in backs]
+    done = backs[-1][3]
+    grad_part = first_other(scal, [b[0] for b in backs], qkv_weight)
+    grad_in = swap_core(grad_part)
+    first_sum.to_core(done)
+    last_sum.spread(done)
+    out_sum.along(done)
+    layer_in = swap_core(layer_part)
+    layer_out = layer_own(scal, hiddens, downs, layer_in, middle, full_dbias)
+    layer_out = jnp.where(stays, layer_out, cross_over(layer_out))
+    tokens_grad, sums_one = first_back(
+        scal, [b[0] for b in backs], qkv_weight, grad_in, x, grad_wide, gain_one
+    )
+    tokens_grad = jnp.where(stays, tokens_grad, cross_over(tokens_grad))
+    for item in qkv_sums:
+        item.to_neighbour()
+    last_sum.back_to_neighbour()
+    out_sum.spread()
+    for item in qkv_sums:
+        item.along()
+    out_sum.back_to_neighbour()
+    last_sum.to_core()
+    for item in qkv_sums:
+        item.spread()
+    out_sum.to_core()
+    for item in qkv_sums:
+        item.back_to_neighbour()
+    for item in qkv_sums:
+        item.to_core()
+
+    up_weight_grad, down_weight_grad = finish_feed(
+        core,
+        [v for item in sums for v in item.own],
+        [v for item in sums for v in item.other],
+    )
+    query_weight_grad, key_weight_grad, value_weight_grad = finish_qkv(
+        core,
+        [jnp.concatenate(item.own, axis=0) for item in qkv_sums],
+        [jnp.concatenate(item.other, axis=0) for item in qkv_sums],
+    )
+    out_own = jnp.concatenate(out_sum.own, axis=0)
+    out_other_core = jnp.concatenate(out_sum.other, axis=0)
+    out_weight_grad = join(out_own, out_other_core, core).reshape(own_rows, width).astype(F32)
+
+    def place_entries(values, inner=1):
+        values = values.reshape(inner, 2, 1, -1).transpose(1, 2, 0, 3)
+        empty = jnp.zeros_like(values)
+        return join(values[:, 0], empty[:, 0], core).transpose(1, 0, 2, 3).reshape(2, -1)
+
+    parts = jnp.concatenate([b[3][0] for b in backs]).reshape(pairs, 3, PAIR)
+    entries = [
+        place_entries(parts[:, 0]), place_entries(parts[:, 2]), sums_two[3], sums_one[0],
+        sums_one[1], sums_two[0], sums_two[1], sums_two[2],
+        place_entries(jnp.stack([f[6] for f in feeds]), ranges),
+    ]
+    entries = jnp.concatenate([e.reshape(2, -1) for e in entries], axis=1)
+    entries = entries + swap_core(entries)
+    entries = pick(entries, half, 0) + swap_half(pick(entries, 1 - half, 0))
+    step = 1
+    while step < ring:
+        if ring & (ring - 1):
+            entries = lax.psum(entries, "rz")
+            break
+        entries = entries + lax.ppermute(entries, "rz", [(i, i ^ step) for i in range(ring)])
+        step *= 2
+    small = [entries[i * own_rows : (i + 1) * own_rows] for i in range(8)]
+    return (
+        layer_out.reshape(1, local, width), tokens_grad.reshape(1, local, width),
+        query_weight_grad, key_weight_grad, value_weight_grad, small[0], small[1],
+        out_weight_grad, small[2], small[3], small[4], small[5], small[6], up_weight_grad,
+        entries[8 * own_rows :], down_weight_grad, small[7],
+    )
+
+
 def solution(mesh):
     rep, grp = mesh.shape["rep"], mesh.shape["grp"]
     split = Mesh(
@@ -724,7 +1678,7 @@
     matrix = P(("half", "gq"), None)
     vector = P(("half", "gq"))
     return jax.shard_map(
-        functools.partial(body, rep, grp),
+        functools.partial(pair_body if grp == 2 and rep % 4 == 0 else wide_body, rep, grp),
         mesh=split,
         in_specs=(
             clip, matrix, matrix, matrix, vector, vector, matrix, vector, vector, vector, vector,

time: 761 us -> 784 us (1.030)
  Pallas kernels: 185 us -> 313 us
  matrix products: 66.2 us -> 0 us
  local copies, waits for them, and re-layouts: 69.3 us -> 37.6 us
  other arithmetic: 76.1 us -> 57.9 us
  waiting for transfers between devices: 218 us -> 235 us
    pallas_call x2 -> x16, Pallas kernels: 51.4 us -> 160 us  [the longest x14 105 us: run(): pl.pallas_call(kernel, grid_spec=pltpu.PrefetchScalarGridSpec(num_scalar_...]
    dot_general x19 -> x0, matrix products: 66.2 us -> none  [contract(): lax.dot_general(left, right, (((left_dim,), (right_dim,)), ((), ())), pre...]
    ppermute x51 -> x90, waiting for transfers between devices: 101 us -> 168 us  [the longest x7 43.3 us: back_to_neighbour(): lax.ppermute(self.whole, 'rz', self.beside)]
    ppermute x13 -> x6, waiting for transfers between devices: 116 us -> 63.8 us  [swap_half(): return lax.ppermute(values, 'half', SWAP)]
    ppermute x51 -> x90, starting transfers between devices: 93.2 us -> 114 us  [the longest x21 23.4 us: along(): lax.ppermute(p, 'rz', self.route(s))]
    pallas_call x2 -> x4, Pallas kernels: 68.9 us -> 87.8 us  [attend_back(): pl.pallas_call(functools.partial(attend_back_kernel, tile, rows, padded),...]
    select_n x7 -> x22, other arithmetic: 8.75 us -> 26.1 us  [the longest x7 7.87 us: to_neighbour(): self.sent = jnp.where(even, totals[1], totals[0])]
    reduce_sum x8 -> x0, other arithmetic: 15.7 us -> none  [the longest x1 4.84 us: body(): jnp.sum(grad_middle_low.astype(F32), axis=0)]
  transfers between devices with their start and end apart: 80 -> 105, of which waited for: 31 -> 41; matrix products, arithmetic and copies ran while one was open for 25% -> 12% of each run, Pallas kernels for 18% -> 34%
where the time goes in v3:
time: 784 us; the launch traced here: 772 us
  Pallas kernels  313 us (40%)
  waiting for transfers between devices  235 us (30%)
  starting transfers between devices  127 us (16%)
  other arithmetic  57.9 us (7%)
  local copies, waits for them, and re-layouts  37.6 us (5%)
    pallas_call x14, Pallas kernels, run(): pl.pallas_call(kernel, grid_spec=pltpu.PrefetchScalarGridSpec(num_scalar_...  105 us
    pallas_call x4, Pallas kernels, attend_back(): pl.pallas_call(functools.partial(attend_back_kernel, tile, rows, padded),...  87.8 us
    ppermute x6, waiting for transfers between devices, swap_half(): return lax.ppermute(values, 'half', SWAP)  63.8 us
    pallas_call x2, Pallas kernels, feed(): pl.pallas_call(functools.partial(feed_kernel, make=make), grid_spec=pltpu...  55.5 us
    pallas_call x2, Pallas kernels, attend(): pl.pallas_call(kernel if kept is None else lambda ref, a, b, *rest: kerne...  49.4 us
    ppermute x7, waiting for transfers between devices, back_to_neighbour(): lax.ppermute(self.whole, 'rz', self.beside)  43.3 us
    ppermute x21, waiting for transfers between devices, spread(): lax.ppermute(self.piece, 'rz', self.route(s))  33.2 us
    ppermute x9, waiting for transfers between devices, __init__(): self.received = [lax.ppermute(send, 'half', SWAP) for send in sends]  27.3 us
  transfers between devices with their start and end apart: 105, of which 41 were waited for; matrix products, arithmetic and copies ran while one was open for 12% of the time, Pallas kernels for 34%

profile of v3, /device:TPU:1, one launch (start us, length us, event | category | flops | bytes accessed | tf_op | source)
XLA Modules:
  0.0 771.6 jit_solution(14955840611013816171)
XLA Ops:
  12.0 11.6 %collective-permute-done.1 = f32[6144]{0:T(1024)S(1)} collective-permute-done((f32[6144]{0:T(1024)S(1)}, f32[6144]{0:T(1024)S(1)}, u32[]{:S(2)}, u32[]{:S(2)}) %collective-permute-start.1) | collective-permute-done | bytes 24608 | tf_op jit(solution)/shard_map/ppermute | solution.py:1481
  44.5 11.8 %collective-permute-done.3.piece_ref = bf16[256,1536]{1,0:T(8,128)(2,1)} collective-permute-done((bf16[256,1536]{1,0:T(8,128)(2,1)}, bf16[256,1536]{1,0:T(8,128)(2,1)}, u32[]{:S(2)}, u32[]{:S(2)}) %collective-permute-start.3) | collective-permute-done | bytes 786464 | tf_op jit(solution)/shard_map/ppermute | solution.py:1481
  63.7 11.2 %collective-permute-done.4.beside_ref = bf16[256,1536]{1,0:T(8,128)(2,1)} collective-permute-done((bf16[256,1536]{1,0:T(8,128)(2,1)}, bf16[256,1536]{1,0:T(8,128)(2,1)}, u32[]{:S(2)}, u32[]{:S(2)}) %collective-permute-start.4) | collective-permute-done | bytes 786464 | tf_op jit(solution)/shard_map/ppermute | solution.py:1487
  74.9 12.6 %project.1 = (bf16[1568,1536]{1,0:T(8,128)(2,1)}, bf16[1024,1536]{1,0:T(8,128)(2,1)}, bf16[1568,1024]{1,0:T(8,128)(2,1)}) custom-call(s32[4]{0:T(128)} %pad_add_fusion.s_ref, bf16[784,1024]{1,0:T(8,128)(2,1)} %get-tuple-element.116.mine_ref, bf16[784,1024]{1,0:T(8,128)(2,1)} %collective-permute-done.2.theirs_ref, ...), custom_call_target="tpu_custom_call" | custom-call | flops 4932501504 | bytes 12726272 | tf_op jit(solution)/shard_map/project/pallas_call | solution.py:343
  87.5 24.7 %attend.2 = (bf16[1568,512]{1,0:T(8,128)(2,1)}, f32[4,2,2048]{2,1,0:T(2,128)}) custom-call(bf16[1568,1536]{1,0:T(8,128)(2,1)} %get-tuple-element.120.qkv_ref.ref), custom_call_target="tpu_custom_call" | custom-call | flops 40282095616 | bytes 3211264 | tf_op jit(solution)/shard_map/attend/pallas_call | solution.py:68
  113.5 24.7 %attend.3 = (bf16[1568,512]{1,0:T(8,128)(2,1)}, f32[4,2,2048]{2,1,0:T(2,128)}) custom-call(bf16[1568,1536]{1,0:T(8,128)(2,1)} %get-tuple-element.120.qkv_ref.ref, bf16[1568,512]{1,0:T(8,128)(2,1)} %get-tuple-element.121.a, f32[4,2,2048]{2,1,0:T(2,128)} %get-tuple-element.125.b), custom_call_target="tpu_custom_call", output_to_operand_aliasing={{0}: (1, {}), {1}: (2, {})} | custom-call | flops 40282095616 | bytes 3211264 | tf_op jit(solution)/shard_map/attend/pallas_call | solution.py:68
  149.2 6.2 second_norm.1
  157.4 23.6 %collective-permute-done.13.refs_3_ = bf16[512,1024]{1,0:T(8,128)(2,1)} collective-permute-done((bf16[512,1024]{1,0:T(8,128)(2,1)}, bf16[512,1024]{1,0:T(8,128)(2,1)}, u32[]{:S(2)}, u32[]{:S(2)}) %collective-permute-start.13) | collective-permute-done | bytes 1048608 | tf_op jit(solution)/shard_map/ppermute | solution.py:1481
  181.2 28.3 %feed.2 = (bf16[1568,1024]{1,0:T(8,128)(2,1)}, bf16[1568,1024]{1,0:T(8,128)(2,1)}, bf16[512,1024]{1,0:T(8,128)(2,1)}, bf16[512,1024]{1,0:T(8,128)(2,1)}, bf16[51...) custom-call(s32[4]{0:T(128)} %pad_add_fusion.s_ref, ...), custom_call_target="tpu_custom_call" | custom-call | flops 26306674688 | bytes 21233664 | tf_op jit(solution)/shard_map/feed/pallas_call | solution.py:309
  209.5 27.3 %feed.3 = (bf16[1568,1024]{1,0:T(8,128)(2,1)}, bf16[1568,1024]{1,0:T(8,128)(2,1)}, bf16[512,1024]{1,0:T(8,128)(2,1)}, bf16[512,1024]{1,0:T(8,128)(2,1)}, bf16[51...) custom-call(s32[4]{0:T(128)} %pad_add_fusion.s_ref, ...), custom_call_target="tpu_custom_call" | custom-call | flops 26306674688 | bytes 21233664 | tf_op jit(solution)/shard_map/feed/pallas_call | solution.py:309
  236.7 8.2 %feed_other.1 = bf16[784,1024]{1,0:T(8,128)(2,1)} custom-call(s32[4]{0:T(128)} %pad_add_fusion.s_ref, bf16[1568,1024]{1,0:T(8,128)(2,1)} %get-tuple-element.147.refs_0_, bf16[1568,1024]{1,0:T(8,128)(2,1)} %get-tuple-element.148.refs_1_, bf16[1024,1024]{1,0:T(8,128)(2,1)} %get-tuple-element.149.refs_2_, bf16[1024,1024]{1,0:T(8,128)(2,1)} %get-tuple-element.150.refs_3_), custom_call_target="tpu_custom_call" | custom-call | flops 3288334336 | bytes 21233664 | tf_op jit(solution)/shard_map/feed_other/pallas_call | solution.py:343
  250.5 12.3 %second_back.1 = (f32[784,1024]{1,0:T(8,128)}, bf16[784,1024]{1,0:T(8,128)(2,1)}, f32[8,1024]{1,0:T(8,128)}) custom-call(s32[4]{0:T(128)} %pad_add_fusion.s_ref, bf16[1568,1024]{1,0:T(8,128)(2,1)} %get-tuple-element.147.refs_0_, bf16[1568,1024]{1,0:T(8,128)(2,1)} %get-tuple-element.148.refs_1_, bf16[1024,1024]{1,0:T(8,128)(2,1)} %get-tuple-element.149.refs_2_, ...), custom_call_target="tpu_custom_call" | custom-call | flops 3288334336 | bytes 34086912 | tf_op jit(solution)/shard_map/second_back/pallas_call | solution.py:343
  264.7 8.2 %layer_other.1 = bf16[784,1024]{1,0:T(8,128)(2,1)} custom-call(s32[4]{0:T(128)} %pad_add_fusion.s_ref, bf16[1568,1024]{1,0:T(8,128)(2,1)} %get-tuple-element.134.refs_0_, bf16[1568,1024]{1,0:T(8,128)(2,1)} %get-tuple-element.143.refs_1_, bf16[1024,1024]{1,0:T(8,128)(2,1)} %get-tuple-element.144.refs_2_, bf16[1024,1024]{1,0:T(8,128)(2,1)} %get-tuple-element.145.refs_3_), custom_call_target="tpu_custom_call" | custom-call | flops 3288334336 | bytes 21233664 | tf_op jit(solution)/shard_map/layer_other/pallas_call | solution.py:343
  273.6 9.7 %mixed_back.1 = (bf16[1568,512]{1,0:T(8,128)(2,1)}, bf16[256,1024]{1,0:T(8,128)(2,1)}, bf16[256,1024]{1,0:T(8,128)(2,1)}) custom-call(s32[4]{0:T(128)} %pad_add_fusion.s_ref, bf16[784,1024]{1,0:T(8,128)(2,1)} %get-tuple-element.151.mine_ref, bf16[784,1024]{1,0:T(8,128)(2,1)} %collective-permute-done.18.theirs_ref, ...), custom_call_target="tpu_custom_call" | custom-call | flops 3288334336 | bytes 11730944 | tf_op jit(solution)/shard_map/mixed_back/pallas_call | solution.py:343
  288.2 22.5 %collective-permute-done.20 = bf16[512,1024]{1,0:T(8,128)(2,1)} collective-permute-done((bf16[512,1024]{1,0:T(8,128)(2,1)}, bf16[512,1024]{1,0:T(8,128)(2,1)}, u32[]{:S(2)}, u32[]{:S(2)}) %collective-permute-start.20) | collective-permute-done | bytes 1048608 | tf_op jit(solution)/shard_map/ppermute | solution.py:1385
  314.4 22.0 %attend_back.4 = (bf16[1568,384]{1,0:T(8,128)(2,1)}, bf16[384,512]{1,0:T(8,128)(2,1)}, bf16[384,512]{1,0:T(8,128)(2,1)}, f32[8,384]{1,0:T(8,128)}) custom-call(s32[4]{0:T(128)} %pad_add_fusion.s_ref, bf16[1568,1536]{1,0:T(8,128)(2,1)} %get-tuple-element.120.qkv_ref.ref, bf16[1568,512]{1,0:T(8,128)(2,1)} %get-tuple-element.152.grad_ref, ...), custom_call_target="tpu_custom_call" | custom-call | flops 50352619520 | bytes 3211264 | tf_op jit(solution)/shard_map/attend_back/pallas_call | solution.py:159
  338.0 9.7 %layer_own.1 = bf16[784,1024]{1,0:T(8,128)(2,1)} custom-call(s32[4]{0:T(128)} %pad_add_fusion.s_ref, bf16[1568,1024]{1,0:T(8,128)(2,1)} %get-tuple-element.134.refs_0_, bf16[1568,1024]{1,0:T(8,128)(2,1)} %get-tuple-element.143.refs_1_, bf16[1024,1024]{1,0:T(8,128)(2,1)} %get-tuple-element.144.refs_2_, bf16[1024,1024]{1,0:T(8,128)(2,1)} %get-tuple-element.145.refs_3_, ...), custom_call_target="tpu_custom_call" | custom-call | flops 3288334336 | bytes 30875648 | tf_op jit(solution)/shard_map/layer_own/pallas_call | solution.py:343
  376.0 7.2 collective-permute-done.16
  387.2 13.0 %collective-permute-done.42 = bf16[192,512]{1,0:T(8,128)(2,1)} collective-permute-done((bf16[192,512]{1,0:T(8,128)(2,1)S(1)}, bf16[192,512]{1,0:T(8,128)(2,1)}, u32[]{:S(2)}, u32[]{:S(2)}) %collective-permute-start.42) | collective-permute-done | bytes 196640 | tf_op jit(solution)/shard_map/ppermute | solution.py:1440
  411.0 21.9 %attend_back.5 = (bf16[1568,384]{1,0:T(8,128)(2,1)}, bf16[384,512]{1,0:T(8,128)(2,1)}, bf16[384,512]{1,0:T(8,128)(2,1)}, f32[8,384]{1,0:T(8,128)}) custom-call(s32[4]{0:T(128)} %pad_add_fusion.s_ref, bf16[1568,1536]{1,0:T(8,128)(2,1)} %get-tuple-element.120.qkv_ref.ref, bf16[1568,512]{1,0:T(8,128)(2,1)} %get-tuple-element.152.grad_ref, ...), custom_call_target="tpu_custom_call" | custom-call | flops 50352619520 | bytes 3211264 | tf_op jit(solution)/shard_map/attend_back/pallas_call | solution.py:159
  455.6 21.9 %attend_back.6 = (bf16[1568,384]{1,0:T(8,128)(2,1)}, bf16[384,512]{1,0:T(8,128)(2,1)}, bf16[384,512]{1,0:T(8,128)(2,1)}, f32[8,384]{1,0:T(8,128)}) custom-call(s32[4]{0:T(128)} %pad_add_fusion.s_ref, bf16[1568,1536]{1,0:T(8,128)(2,1)} %get-tuple-element.120.qkv_ref.ref, bf16[1568,512]{1,0:T(8,128)(2,1)} %get-tuple-element.152.grad_ref, ...), custom_call_target="tpu_custom_call" | custom-call | flops 50352619520 | bytes 3211264 | tf_op jit(solution)/shard_map/attend_back/pallas_call | solution.py:159
  504.9 15.3 %collective-permute-done.53 = bf16[192,512]{1,0:T(8,128)(2,1)S(1)} collective-permute-done((bf16[192,512]{1,0:T(8,128)(2,1)S(1)}, bf16[192,512]{1,0:T(8,128)(2,1)S(1)}, u32[]{:S(2)}, u32[]{:S(2)}) %collective-permute-start.53) | collective-permute-done | bytes 196640 | tf_op jit(solution)/shard_map/ppermute | solution.py:1402
  531.2 7.8 %collective-permute-start.94 = (bf16[512,1024]{1,0:T(8,128)(2,1)}, bf16[512,1024]{1,0:T(8,128)(2,1)}, u32[]{:S(2)}, u32[]{:S(2)}) collective-permute-start(bf16[512,1024]{1,0:T(8,128)(2,1)} %bitcast.23), channel_id=1, source_target_pairs={{0,2},{2,0},{1,3},{3,1},{4,6},{6,4},{5,7},{7,5},{8,10},{10,8},{9,1... | collective-permute-start | bytes 3145736 | tf_op jit(solution)/shard_map/ppermute | solution.py:1441
  548.0 21.9 %attend_back.7 = (bf16[1568,384]{1,0:T(8,128)(2,1)}, bf16[384,512]{1,0:T(8,128)(2,1)}, bf16[384,512]{1,0:T(8,128)(2,1)}, f32[8,384]{1,0:T(8,128)}) custom-call(s32[4]{0:T(128)} %pad_add_fusion.s_ref, bf16[1568,1536]{1,0:T(8,128)(2,1)} %get-tuple-element.120.qkv_ref.ref, bf16[1568,512]{1,0:T(8,128)(2,1)} %get-tuple-element.152.grad_ref, ...), custom_call_target="tpu_custom_call" | custom-call | flops 50352619520 | bytes 3211264 | tf_op jit(solution)/shard_map/attend_back/pallas_call | solution.py:159
  575.1 7.9 %first_other.1 = bf16[784,1024]{1,0:T(8,128)(2,1)} custom-call(s32[4]{0:T(128)} %pad_add_fusion.s_ref, bf16[1568,384]{1,0:T(8,128)(2,1)} %get-tuple-element.161.refs_0_, bf16[1568,384]{1,0:T(8,128)(2,1)} %get-tuple-element.165.refs_1_, bf16[1568,384]{1,0:T(8,128)(2,1)} %get-tuple-element.177.refs_2_, bf16[1568,384]{1,0:T(8,128)(2,1)} %get-tuple-element.188.refs_3_, ...), custom_call_target="tpu_custom_call" | custom-call | flops 2466250752 | bytes 34799616 | tf_op jit(solution)/shard_map/first_other/pallas_call | solution.py:343
  603.5 6.5 collective-permute-start.74
  622.8 6.0 collective-permute-done.90
  645.2 11.3 %collective-permute-done.99 = bf16[128,1024]{1,0:T(8,128)(2,1)S(1)} collective-permute-done((bf16[128,1024]{1,0:T(8,128)(2,1)S(1)}, bf16[128,1024]{1,0:T(8,128)(2,1)S(1)}, u32[]{:S(2)}, u32[]{:S(2)}) %collective-permute-start.99) | collective-permute-done | bytes 262176 | tf_op jit(solution)/shard_map/ppermute | solution.py:1422
  676.4 19.7 %collective-permute-done.69 = bf16[192,512]{1,0:T(8,128)(2,1)S(1)} collective-permute-done((bf16[192,512]{1,0:T(8,128)(2,1)S(1)}, bf16[192,512]{1,0:T(8,128)(2,1)S(1)}, u32[]{:S(2)}, u32[]{:S(2)}) %collective-permute-start.69) | collective-permute-done | bytes 196640 | tf_op jit(solution)/shard_map/ppermute | solution.py:1440
  696.2 10.6 %first_back.1 = (bf16[784,1024]{1,0:T(8,128)(2,1)}, f32[8,1024]{1,0:T(8,128)}) custom-call(s32[4]{0:T(128)} %pad_add_fusion.s_ref, bf16[1568,384]{1,0:T(8,128)(2,1)} %get-tuple-element.161.refs_0_, bf16[1568,384]{1,0:T(8,128)(2,1)} %get-tuple-element.165.refs_1_, bf16[1568,384]{1,0:T(8,128)(2,1)} %get-tuple-element.177.refs_2_, ...), custom_call_target="tpu_custom_call" | custom-call | flops 2466250752 | bytes 47652864 | tf_op jit(solution)/shard_map/first_back/pallas_call | solution.py:343
  721.8 16.8 %collective-permute-done.79 = f32[6144]{0:T(1024)S(1)} collective-permute-done((f32[6144]{0:T(1024)S(1)}, f32[6144]{0:T(1024)S(1)}, u32[]{:S(2)}, u32[]{:S(2)}) %collective-permute-start.79) | collective-permute-done | bytes 24608 | tf_op jit(solution)/shard_map/ppermute | solution.py:1481
  758.8 9.5 %finish_feed.1 = (f32[512,4096]{1,0:T(8,128)}, f32[2,2,512,1024]{3,2,1,0:T(8,128)}) custom-call(s32[1]{0:T(128)} %bitcast.2.core_ref, bf16[512,1024]{1,0:T(8,128)(2,1)} %get-tuple-element.230.refs_0_, bf16[512,1024]{1,0:T(8,128)(2,1)} %get-tuple-element.229.refs_1_, bf16[512,1024]{1,0:T(8,128)(2,1)} %get-tuple-element.228.refs_2_, ...), custom_call_target="tpu_custom_call" | custom-call | tf_op jit(solution)/shard_map/finish_feed/pallas_call | solution.py:782
  (408 shorter events, 297.8 us)
Async XLA Ops:
  30.8 44.1 %collective-permute-start.2 = (bf16[784,1024]{1,0:T(8,128)(2,1)}, bf16[784,1024]{1,0:T(8,128)(2,1)}, u32[]{:S(2)}, u32[]{:S(2)}) collective-permute-start(bf16[784,1024]{1,0:T(8,128)(2,1)} %get-tuple-element.116.mine_ref), channel_id=1, source_target_pairs={{0,2},{2,0},{1,3},{3,1},{4,6},{6,4},{5,7},{7,5},{8,10},{10,8},{9,1... | collective-permute-start | bytes 4816904 | tf_op jit(solution)/shard_map/ppermute | solution.py:1484
  58.3 53.9 %collective-permute-start.6 = (bf16[512,1024]{1,0:T(8,128)(2,1)}, bf16[512,1024]{1,0:T(8,128)(2,1)}, u32[]{:S(2)}, u32[]{:S(2)}) collective-permute-start(bf16[512,1024]{1,0:T(8,128)(2,1)} %pack_feed.2), channel_id=1, source_target_pairs={{0,1},{1,0},{2,3},{3,2},{4,5},{5,4},{6,7},{7,6},{8,9},{9,8},{10,11... | collective-permute-start | bytes 3145736 | tf_op jit(solution)/shard_map/ppermute | solution.py:1481
  58.3 53.9 %collective-permute-start.5 = (bf16[128,1024]{1,0:T(8,128)(2,1)S(1)}, bf16[128,1024]{1,0:T(8,128)(2,1)}, u32[]{:S(2)}, u32[]{:S(2)}) collective-permute-start(bf16[128,1024]{1,0:T(8,128)(2,1)S(1)} %constant_dynamic-slice_fusion.5), channel_id=1, source_target_pairs={{0,1},{1,0},{2,3},{3,2},{4,5},{5,4},{6,7},{7,6},{8,9},{9,8},{10,11... | collective-permute-start | bytes 786440 | tf_op jit(solution)/shard_map/ppermute | solution.py:1481
  59.8 87.2 %collective-permute-start.10 = (bf16[784,1024]{1,0:T(8,128)(2,1)S(1)}, bf16[784,1024]{1,0:T(8,128)(2,1)}, u32[]{:S(2)}, u32[]{:S(2)}) collective-permute-start(bf16[784,1024]{1,0:T(8,128)(2,1)S(1)} %bitcast.235), channel_id=1, source_target_pairs={{1,2},{2,1},{5,6},{6,5},{9,10},{10,9},{13,14},{14,13},{17,18},{18,... | collective-permute-start | bytes 4816904 | tf_op jit(solution)/shard_map/ppermute | solution.py:1490
  149.1 32.1 %collective-permute-start.11 = (bf16[784,1024]{1,0:T(8,128)(2,1)S(1)}, bf16[784,1024]{1,0:T(8,128)(2,1)}, u32[]{:S(2)}, u32[]{:S(2)}) collective-permute-start(bf16[784,1024]{1,0:T(8,128)(2,1)S(1)} %broadcast_select_fusion.dy_own.refs_6_), channel_id=1, source_target_pairs={{0,2},{2,0},{1,3},{3,1},{4,6},{6,4},{5,7},{7,5},{8,10},{10,8},{9,1... | collective-permute-start | bytes 4816904 | tf_op jit(solution)/shard_map/ppermute | solution.py:1484
  180.9 28.5 %collective-permute-start.14 = (bf16[512,1024]{1,0:T(8,128)(2,1)}, bf16[512,1024]{1,0:T(8,128)(2,1)}, u32[]{:S(2)}, u32[]{:S(2)}) collective-permute-start(bf16[512,1024]{1,0:T(8,128)(2,1)} %collective-permute-done.13.refs_3_), channel_id=1, source_target_pairs={{0,4},{4,0},{8,12},{12,8},{16,20},{20,16},{24,28},{28,24},{1,5},{5... | collective-permute-start | bytes 3145736 | tf_op jit(solution)/shard_map/ppermute | solution.py:1487
  264.2 46.4 %collective-permute-start.20 = (bf16[512,1024]{1,0:T(8,128)(2,1)}, bf16[512,1024]{1,0:T(8,128)(2,1)}, u32[]{:S(2)}, u32[]{:S(2)}) collective-permute-start(bf16[512,1024]{1,0:T(8,128)(2,1)} %get-tuple-element.155), channel_id=1, source_target_pairs={{0,1},{1,0},{2,3},{3,2},{4,5},{5,4},{6,7},{7,6},{8,9},{9,8},{10,11... | collective-permute-start | bytes 3145736 | tf_op jit(solution)/shard_map/ppermute | solution.py:1385
  272.9 65.1 %collective-permute-start.15 = (bf16[784,1024]{1,0:T(8,128)(2,1)}, bf16[784,1024]{1,0:T(8,128)(2,1)}, u32[]{:S(2)}, u32[]{:S(2)}) collective-permute-start(bf16[784,1024]{1,0:T(8,128)(2,1)} %layer_other.1), channel_id=1, source_target_pairs={{0,2},{2,0},{1,3},{3,1},{4,6},{6,4},{5,7},{7,5},{8,10},{10,8},{9,1... | collective-permute-start | bytes 4816904 | tf_op jit(solution)/shard_map/ppermute | solution.py:1484
  347.7 35.5 %collective-permute-start.16 = (bf16[784,1024]{1,0:T(8,128)(2,1)}, bf16[784,1024]{1,0:T(8,128)(2,1)}, u32[]{:S(2)}, u32[]{:S(2)}) collective-permute-start(bf16[784,1024]{1,0:T(8,128)(2,1)} %layer_own.1), channel_id=1, source_target_pairs={{1,2},{2,1},{5,6},{6,5},{9,10},{10,9},{13,14},{14,13},{17,18},{18,... | collective-permute-start | bytes 4816904 | tf_op jit(solution)/shard_map/ppermute | solution.py:1490
  354.7 78.2 %collective-permute-start.25 = (bf16[512,1024]{1,0:T(8,128)(2,1)}, bf16[512,1024]{1,0:T(8,128)(2,1)}, u32[]{:S(2)}, u32[]{:S(2)}) collective-permute-start(bf16[512,1024]{1,0:T(8,128)(2,1)} %get-tuple-element.171), channel_id=1, source_target_pairs={{0,1},{1,0},{2,3},{3,2},{4,5},{5,4},{6,7},{7,6},{8,9},{9,8},{10,11... | collective-permute-start | bytes 3145736 | tf_op jit(solution)/shard_map/ppermute | solution.py:1385
  373.3 61.0 %collective-permute-start.26 = (bf16[512,1024]{1,0:T(8,128)(2,1)}, bf16[512,1024]{1,0:T(8,128)(2,1)}, u32[]{:S(2)}, u32[]{:S(2)}) collective-permute-start(bf16[512,1024]{1,0:T(8,128)(2,1)} %get-tuple-element.172), channel_id=1, source_target_pairs={{0,1},{1,0},{2,3},{3,2},{4,5},{5,4},{6,7},{7,6},{8,9},{9,8},{10,11... | collective-permute-start | bytes 3145736 | tf_op jit(solution)/shard_map/ppermute | solution.py:1385
  374.3 31.7 %collective-permute-start.21 = (bf16[512,1024]{1,0:T(8,128)(2,1)S(1)}, bf16[512,1024]{1,0:T(8,128)(2,1)S(1)}, u32[]{:S(2)}, u32[]{:S(2)}) collective-permute-start(bf16[512,1024]{1,0:T(8,128)(2,1)S(1)} %copy-done.12), channel_id=1, source_target_pairs={{0,4},{4,0},{8,12},{12,8},{16,20},{20,16},{24,28},{28,24},{1,5},{5... | collective-permute-start | bytes 3145736 | tf_op jit(solution)/shard_map/ppermute | solution.py:1402
  387.2 53.4 %collective-permute-start.70 = (bf16[192,512]{1,0:T(8,128)(2,1)S(1)}, bf16[192,512]{1,0:T(8,128)(2,1)}, u32[]{:S(2)}, u32[]{:S(2)}) collective-permute-start(bf16[192,512]{1,0:T(8,128)(2,1)S(1)} %bitcast.247), channel_id=1, source_target_pairs={{0,2},{2,0},{1,3},{3,1},{4,6},{6,4},{5,7},{7,5},{8,10},{10,8},{9,1... | collective-permute-start | bytes 589832 | tf_op jit(solution)/shard_map/ppermute | solution.py:1441
  400.2 41.5 %collective-permute-start.71 = (bf16[192,512]{1,0:T(8,128)(2,1)}, bf16[192,512]{1,0:T(8,128)(2,1)}, u32[]{:S(2)}, u32[]{:S(2)}) collective-permute-start(bf16[192,512]{1,0:T(8,128)(2,1)} %collective-permute-done.42), channel_id=1, source_target_pairs={{0,2},{2,0},{1,3},{3,1},{4,6},{6,4},{5,7},{7,5},{8,10},{10,8},{9,1... | collective-permute-start | bytes 589832 | tf_op jit(solution)/shard_map/ppermute | solution.py:1447
  409.5 34.1 %collective-permute-start.22 = (bf16[128,1024]{1,0:T(8,128)(2,1)}, bf16[128,1024]{1,0:T(8,128)(2,1)S(1)}, u32[]{:S(2)}, u32[]{:S(2)}) collective-permute-start(bf16[128,1024]{1,0:T(8,128)(2,1)} %get-tuple-element.244), channel_id=1, source_target_pairs={{0,8},{4,12},{8,16},{12,20},{16,24},{20,28},{24,0},{28,4},{1,9},{5... | collective-permute-start | bytes 786440 | tf_op jit(solution)/shard_map/ppermute | solution.py:1413
  432.9 48.1 %collective-permute-start.31 = (bf16[256,1024]{1,0:T(8,128)(2,1)}, bf16[256,1024]{1,0:T(8,128)(2,1)}, u32[]{:S(2)}, u32[]{:S(2)}) collective-permute-start(bf16[256,1024]{1,0:T(8,128)(2,1)} %get-tuple-element.185), channel_id=1, source_target_pairs={{0,1},{1,0},{2,3},{3,2},{4,5},{5,4},{6,7},{7,6},{8,9},{9,8},{10,11... | collective-permute-start | bytes 1572872 | tf_op jit(solution)/shard_map/ppermute | solution.py:1385
  441.8 102.1 %collective-permute-start.30 = (bf16[512,1024]{1,0:T(8,128)(2,1)}, bf16[512,1024]{1,0:T(8,128)(2,1)}, u32[]{:S(2)}, u32[]{:S(2)}) collective-permute-start(bf16[512,1024]{1,0:T(8,128)(2,1)} %broadcast_select_fusion.9), channel_id=1, source_target_pairs={{0,4},{4,0},{8,12},{12,8},{16,20},{20,16},{24,28},{28,24},{1,5},{5... | collective-permute-start | bytes 3145736 | tf_op jit(solution)/shard_map/ppermute | solution.py:1402
  443.6 35.2 %collective-permute-start.43 = (bf16[384,512]{1,0:T(8,128)(2,1)}, bf16[384,512]{1,0:T(8,128)(2,1)S(1)}, u32[]{:S(2)}, u32[]{:S(2)}) collective-permute-start(bf16[384,512]{1,0:T(8,128)(2,1)} %get-tuple-element.195), channel_id=1, source_target_pairs={{0,1},{1,0},{2,3},{3,2},{4,5},{5,4},{6,7},{7,6},{8,9},{9,8},{10,11... | collective-permute-start | bytes 1179656 | tf_op jit(solution)/shard_map/ppermute | solution.py:1385
  494.0 139.3 %collective-permute-start.93 = (bf16[512,1024]{1,0:T(8,128)(2,1)}, bf16[512,1024]{1,0:T(8,128)(2,1)}, u32[]{:S(2)}, u32[]{:S(2)}) collective-permute-start(bf16[512,1024]{1,0:T(8,128)(2,1)} %bitcast.23), channel_id=1, source_target_pairs={{0,4},{4,0},{8,12},{12,8},{16,20},{20,16},{24,28},{28,24},{1,5},{5... | collective-permute-start | bytes 3145736 | tf_op jit(solution)/shard_map/ppermute | solution.py:1440
  531.2 102.4 %collective-permute-start.94 = (bf16[512,1024]{1,0:T(8,128)(2,1)}, bf16[512,1024]{1,0:T(8,128)(2,1)}, u32[]{:S(2)}, u32[]{:S(2)}) collective-permute-start(bf16[512,1024]{1,0:T(8,128)(2,1)} %bitcast.23), channel_id=1, source_target_pairs={{0,2},{2,0},{1,3},{3,1},{4,6},{6,4},{5,7},{7,5},{8,10},{10,8},{9,1... | collective-permute-start | bytes 3145736 | tf_op jit(solution)/shard_map/ppermute | solution.py:1441
  539.0 31.6 %collective-permute-start.83 = (bf16[128,1024]{1,0:T(8,128)(2,1)S(1)}, bf16[128,1024]{1,0:T(8,128)(2,1)}, u32[]{:S(2)}, u32[]{:S(2)}) collective-permute-start(bf16[128,1024]{1,0:T(8,128)(2,1)S(1)} %broadcast_select_fusion.15), channel_id=1, source_target_pairs={{0,4},{4,0},{8,12},{12,8},{16,20},{20,16},{24,28},{28,24},{1,5},{5... | collective-permute-start | bytes 786440 | tf_op jit(solution)/shard_map/ppermute | solution.py:1402
  539.8 43.3 %collective-permute-start.72 = (bf16[192,512]{1,0:T(8,128)(2,1)}, bf16[192,512]{1,0:T(8,128)(2,1)}, u32[]{:S(2)}, u32[]{:S(2)}) collective-permute-start(bf16[192,512]{1,0:T(8,128)(2,1)} %bitcast.46), channel_id=1, source_target_pairs={{0,2},{2,0},{1,3},{3,1},{4,6},{6,4},{5,7},{7,5},{8,10},{10,8},{9,1... | collective-permute-start | bytes 589832 | tf_op jit(solution)/shard_map/ppermute | solution.py:1441
  543.9 39.7 %collective-permute-start.73 = (bf16[192,512]{1,0:T(8,128)(2,1)}, bf16[192,512]{1,0:T(8,128)(2,1)}, u32[]{:S(2)}, u32[]{:S(2)}) collective-permute-start(bf16[192,512]{1,0:T(8,128)(2,1)} %collective-permute-done.51), channel_id=1, source_target_pairs={{0,2},{2,0},{1,3},{3,1},{4,6},{6,4},{5,7},{7,5},{8,10},{10,8},{9,1... | collective-permute-start | bytes 589832 | tf_op jit(solution)/shard_map/ppermute | solution.py:1447
  621.6 44.6 %collective-permute-start.91 = (bf16[128,1024]{1,0:T(8,128)(2,1)S(1)}, bf16[128,1024]{1,0:T(8,128)(2,1)S(1)}, u32[]{:S(2)}, u32[]{:S(2)}) collective-permute-start(bf16[128,1024]{1,0:T(8,128)(2,1)S(1)} %bitcast.241), channel_id=1, source_target_pairs={{0,2},{2,0},{1,3},{3,1},{4,6},{6,4},{5,7},{7,5},{8,10},{10,8},{9,1... | collective-permute-start | bytes 786440 | tf_op jit(solution)/shard_map/ppermute | solution.py:1441
  638.9 27.4 %collective-permute-start.92 = (bf16[128,1024]{1,0:T(8,128)(2,1)S(1)}, bf16[128,1024]{1,0:T(8,128)(2,1)S(1)}, u32[]{:S(2)}, u32[]{:S(2)}) collective-permute-start(bf16[128,1024]{1,0:T(8,128)(2,1)S(1)} %collective-permute-done.90), channel_id=1, source_target_pairs={{0,2},{2,0},{1,3},{3,1},{4,6},{6,4},{5,7},{7,5},{8,10},{10,8},{9,1... | collective-permute-start | bytes 786440 | tf_op jit(solution)/shard_map/ppermute | solution.py:1447
  661.7 34.5 %collective-permute-start.32 = (bf16[784,1024]{1,0:T(8,128)(2,1)S(1)}, bf16[784,1024]{1,0:T(8,128)(2,1)}, u32[]{:S(2)}, u32[]{:S(2)}) collective-permute-start(bf16[784,1024]{1,0:T(8,128)(2,1)S(1)} %copy-done.10), channel_id=1, source_target_pairs={{0,2},{2,0},{1,3},{3,1},{4,6},{6,4},{5,7},{7,5},{8,10},{10,8},{9,1... | collective-permute-start | bytes 4816904 | tf_op jit(solution)/shard_map/ppermute | solution.py:1484
  663.7 87.8 %collective-permute-start.102 = (bf16[512,1024]{1,0:T(8,128)(2,1)}, bf16[512,1024]{1,0:T(8,128)(2,1)}, u32[]{:S(2)}, u32[]{:S(2)}) collective-permute-start(bf16[512,1024]{1,0:T(8,128)(2,1)} %collective-permute-done.93), channel_id=1, source_target_pairs={{0,2},{2,0},{1,3},{3,1},{4,6},{6,4},{5,7},{7,5},{8,10},{10,8},{9,1... | collective-permute-start | bytes 3145736 | tf_op jit(solution)/shard_map/ppermute | solution.py:1447
  668.2 52.9 %collective-permute-start.101 = (bf16[512,1024]{1,0:T(8,128)(2,1)S(1)}, bf16[512,1024]{1,0:T(8,128)(2,1)}, u32[]{:S(2)}, u32[]{:S(2)}) collective-permute-start(bf16[512,1024]{1,0:T(8,128)(2,1)S(1)} %bitcast.233), channel_id=1, source_target_pairs={{0,4},{4,0},{8,12},{12,8},{16,20},{20,16},{24,28},{28,24},{1,5},{5... | collective-permute-start | bytes 3145736 | tf_op jit(solution)/shard_map/ppermute | solution.py:1440
  674.4 46.6 %collective-permute-start.76 = (bf16[192,512]{1,0:T(8,128)(2,1)S(1)}, bf16[192,512]{1,0:T(8,128)(2,1)S(1)}, u32[]{:S(2)}, u32[]{:S(2)}) collective-permute-start(bf16[192,512]{1,0:T(8,128)(2,1)S(1)} %bitcast.245), channel_id=1, source_target_pairs={{0,2},{2,0},{1,3},{3,1},{4,6},{6,4},{5,7},{7,5},{8,10},{10,8},{9,1... | collective-permute-start | bytes 589832 | tf_op jit(solution)/shard_map/ppermute | solution.py:1441
  716.9 51.5 %collective-permute-start.33 = (bf16[784,1024]{1,0:T(8,128)(2,1)}, bf16[784,1024]{1,0:T(8,128)(2,1)}, u32[]{:S(2)}, u32[]{:S(2)}) collective-permute-start(bf16[784,1024]{1,0:T(8,128)(2,1)} %get-tuple-element.191), channel_id=1, source_target_pairs={{1,2},{2,1},{5,6},{6,5},{9,10},{10,9},{13,14},{14,13},{17,18},{18,... | collective-permute-start | bytes 4816904 | tf_op jit(solution)/shard_map/ppermute | solution.py:1490
  721.1 34.7 %collective-permute-start.103 = (bf16[512,1024]{1,0:T(8,128)(2,1)S(1)}, bf16[512,1024]{1,0:T(8,128)(2,1)}, u32[]{:S(2)}, u32[]{:S(2)}) collective-permute-start(bf16[512,1024]{1,0:T(8,128)(2,1)S(1)} %bitcast.234), channel_id=1, source_target_pairs={{0,2},{2,0},{1,3},{3,1},{4,6},{6,4},{5,7},{7,5},{8,10},{10,8},{9,1... | collective-permute-start | bytes 3145736 | tf_op jit(solution)/shard_map/ppermute | solution.py:1441
  721.1 34.6 %collective-permute-start.104 = (bf16[512,1024]{1,0:T(8,128)(2,1)}, bf16[512,1024]{1,0:T(8,128)(2,1)}, u32[]{:S(2)}, u32[]{:S(2)}) collective-permute-start(bf16[512,1024]{1,0:T(8,128)(2,1)} %collective-permute-done.101), channel_id=1, source_target_pairs={{0,2},{2,0},{1,3},{3,1},{4,6},{6,4},{5,7},{7,5},{8,10},{10,8},{9,1... | collective-permute-start | bytes 3145736 | tf_op jit(solution)/shard_map/ppermute | solution.py:1447
  (101 other events, 1332.2 us)

commit v4 on v3

--- a/solution.py
+++ b/solution.py
@@ -202,24 +202,20 @@
 
 
 def feed_kernel(
-    s_ref, x_own, x_other, dy_own, dy_other, *refs, make,
+    s_ref, x_own, x_other, dy_own, dy_other, up_ref, down_ref, x_piece, x_beside, z_piece, z_beside,
+    bias_ref, out_own, out_other, dx_own, dx_other, up_send, up_keep, down_send, down_keep,
+    low_send, low_keep, bias_grad_ref, x, dy, x_t, out_sum, dx_sum, up_full, down_full, hidden,
+    d_pre, sems,
 ):
-    if not make:
-        x_t, refs = refs[0], refs[1:]
-    up_ref, down_ref, piece, beside, bias_ref, *refs = refs
-    hidden_ref, d_pre_ref, up_send, up_keep, down_send, down_keep, bias_grad_ref, *refs = refs
-    up_full, down_full, *refs = refs
-    if make:
-        x_t, refs = refs[0], refs[1:]
-    x, dy, sems = refs
     index = pl.program_id(0)
     half = s_ref[0]
-    even = s_ref[1] == 0
     rows, width = x.shape
     block = rows // 2
     own = width // 2
     tile = up_ref.shape[1]
-    columns = pl.ds(pl.multiple_of(index * tile, tile), tile)
+    first_range = index < 2
+    side = index % 2
+    columns = pl.ds(pl.multiple_of(side * tile, tile), tile)
     mine = pl.ds(pl.multiple_of(half * own, own), own)
     theirs = pl.ds(pl.multiple_of((1 - half) * own, own), own)
 
@@ -236,27 +232,36 @@
             copy.start()
         for copy in copies:
             copy.wait()
-        if make:
-            x_t[...] = x[...].T
+        x_t[...] = x[...].T
+        out_sum[...] = jnp.zeros_like(out_sum)
+        dx_sum[...] = jnp.zeros_like(dx_sum)
 
     up_full[mine, :] = up_ref[...]
-    down_full[...] = down_ref[...]
-
-    @pl.when(even)
+
+    @pl.when(side == half)
     def _():
-        up_full[theirs, :] = piece[:, columns]
-
-    @pl.when(jnp.logical_not(even))
-    def _():
-        up_full[theirs, :] = beside[:, columns]
-
-    @pl.when((index != half) & even)
-    def _():
-        down_full[...] = beside[...]
-
-    @pl.when((index != half) & jnp.logical_not(even))
-    def _():
-        down_full[...] = piece[...]
+        down_full[...] = down_ref[...]
+
+    for chosen, place, piece, beside in (
+        (first_range, 1, x_piece, x_beside), (jnp.logical_not(first_range), 4, z_piece, z_beside)
+    ):
+        even = s_ref[place] == 0
+
+        @pl.when(chosen & even)
+        def _():
+            up_full[theirs, :] = piece[:, columns]
+
+        @pl.when(chosen & jnp.logical_not(even))
+        def _():
+            up_full[theirs, :] = beside[:, columns]
+
+        @pl.when(chosen & (side != half) & even)
+        def _():
+            down_full[...] = beside[...]
+
+        @pl.when(chosen & (side != half) & jnp.logical_not(even))
+        def _():
+            down_full[...] = piece[...]
 
     bias_grad = jnp.zeros(bias_grad_ref.shape, F32)
     for start in range(0, rows, block):
@@ -264,78 +269,96 @@
         pre = contract(x[part, :], up_full[...], 1, 0) + bias_ref[...]
         d_hidden = contract(dy[part, :], down_full[...], 1, 1)
         share = 0.5 * (1.0 + lax.erf(pre * 0.7071067811865476))
-        hidden_ref[part, :] = (pre * share).astype(BF16)
+        hidden[part, :] = (pre * share).astype(BF16)
         slope = share + pre * (jnp.exp(-0.5 * pre * pre) * 0.3989422804014327)
         d_low = (d_hidden * slope).astype(BF16)
-        d_pre_ref[part, :] = d_low
+        d_pre[part, :] = d_low
         bias_grad = bias_grad + jnp.sum(d_low.astype(F32), axis=0, keepdims=True)
+        out_sum[part, :] += contract(hidden[part, :], down_full[...], 1, 0)
+        dx_sum[part, :] += contract(d_pre[part, :], up_full[...], 1, 1)
     bias_grad_ref[...] = bias_grad
-    up_keep[:, columns] = contract(x_t[mine, :], d_pre_ref[...], 1, 0).astype(BF16)
-    up_send[:, columns] = contract(x_t[theirs, :], d_pre_ref[...], 1, 0).astype(BF16)
-    down_grad = contract(hidden_ref[...], dy[...], 0, 0).astype(BF16)
-
-    @pl.when(index == half)
+    down_grad = contract(hidden[...], dy[...], 0, 0).astype(BF16)
+    side_rows = pl.ds(pl.multiple_of(side * tile, tile), tile)
+
+    @pl.when(first_range)
+    def _():
+        up_keep[:, columns] = contract(x_t[mine, :], d_pre[...], 1, 0).astype(BF16)
+        up_send[:, columns] = contract(x_t[theirs, :], d_pre[...], 1, 0).astype(BF16)
+
+    @pl.when(first_range & (side == half))
     def _():
         down_keep[...] = down_grad
 
-    @pl.when(index != half)
+    @pl.when(first_range & (side != half))
     def _():
         down_send[...] = down_grad
 
-
-def feed(scal, seconds, grads, x_t, up, down, piece, beside, bias, j, ranges):
+    for even in (True, False):
+        up_goal, down_goal = (low_keep, low_send) if even else (low_send, low_keep)
+
+        @pl.when(jnp.logical_not(first_range) & ((s_ref[1] == 0) == even))
+        def _():
+            up_goal[:, columns] = contract(x_t[...], d_pre[...], 1, 0).astype(BF16)
+            down_goal[side_rows, :] = down_grad
+
+    @pl.when(index == pl.num_programs(0) - 1)
+    def _():
+        out_own[...] = out_sum[:block, :].astype(BF16)
+        out_other[...] = out_sum[block:, :].astype(BF16)
+        dx_own[...] = dx_sum[:block, :].astype(BF16)
+        dx_other[...] = dx_sum[block:, :].astype(BF16)
+
+
+def feed(scal, seconds, grads, up, down, pieces, bias):
     local, width = seconds[0].shape
     rows = 2 * local
-    tile = down.shape[0] // (2 * ranges)
-    hidden = 2 * tile
-    make = x_t is None
+    tile = down.shape[0] // 4
     anywhere = pl.BlockSpec(memory_space=pl.ANY)
 
     def fixed(*shape):
         return pl.BlockSpec(shape, lambda t, s: (0, 0), pipeline_mode=pl.Buffered(1))
 
-    def across(size):
-        return pl.BlockSpec((size, tile), lambda t, s: (0, t))
-
-    shape = jax.ShapeDtypeStruct
-    out_specs = [across(rows)] * 2 + [fixed(width // 2, hidden)] * 2 + [fixed(tile, width)] * 2
-    out_specs += [across(1), across(width), pl.BlockSpec((tile, width), lambda t, s: (t, 0))]
-    out_shape = [shape((rows, hidden), BF16)] * 2 + [shape((width // 2, hidden), BF16)] * 2
-    out_shape += [shape((tile, width), BF16)] * 2
-    out_shape += [shape((1, hidden), F32), shape((width, hidden), BF16), shape((hidden, width), BF16)]
-    if make:
-        out_specs.append(fixed(width, rows))
-        out_shape.append(shape((width, rows), BF16))
+    shapes = [(local, width)] * 4 + [(width // 2, 2 * tile)] * 2 + [(tile, width)] * 2
+    shapes += [(width, 2 * tile)] * 2
+    across = pl.BlockSpec((1, tile), lambda t, s: (0, t))
     return pl.pallas_call(
-        functools.partial(feed_kernel, make=make),
+        feed_kernel,
         grid_spec=pltpu.PrefetchScalarGridSpec(
             num_scalar_prefetch=1,
-            grid=(2,),
+            grid=(4,),
             in_specs=[anywhere] * 4
-            + ([] if make else [fixed(width, rows)])
             + [
-                pl.BlockSpec((width // 2, tile), lambda t, s: (0, (t * 2 + s[2]) * ranges + j)),
-                pl.BlockSpec((tile, width), lambda t, s: (s[2] * ranges + j, 0)),
-                fixed(width // 2, hidden),
-                fixed(tile, width),
-                across(1),
-            ],
-            out_specs=out_specs,
+                pl.BlockSpec(
+                    (width // 2, tile), lambda t, s: (0, ((t % 2) * 2 + s[2]) * 2 + t // 2)
+                ),
+                pl.BlockSpec((tile, width), lambda t, s: (s[2] * 2 + t // 2, 0)),
+            ]
+            + [fixed(width // 2, 2 * tile)] * 4
+            + [across],
+            out_specs=[fixed(*shape) for shape in shapes] + [across],
             scratch_shapes=[
                 pltpu.VMEM((rows, width), BF16),
                 pltpu.VMEM((rows, width), BF16),
+                pltpu.VMEM((width, rows), BF16),
+                pltpu.VMEM((rows, width), F32),
+                pltpu.VMEM((rows, width), F32),
+                pltpu.VMEM((width, tile), BF16),
+                pltpu.VMEM((tile, width), BF16),
+                pltpu.VMEM((rows, tile), BF16),
+                pltpu.VMEM((rows, tile), BF16),
                 pltpu.SemaphoreType.DMA((4,)),
             ],
         ),
-        out_shape=out_shape,
+        out_shape=[jax.ShapeDtypeStruct(shape, BF16) for shape in shapes]
+        + [jax.ShapeDtypeStruct((1, 4 * tile), F32)],
         compiler_params=pltpu.CompilerParams(vmem_limit_bytes=VMEM_LIMIT),
         cost_estimate=pl.CostEstimate(
-            flops=16 * rows * width * hidden,
-            bytes_accessed=8 * rows * width + 8 * width * hidden,
-            transcendentals=2 * rows * hidden,
+            flops=48 * rows * width * tile,
+            bytes_accessed=16 * rows * width,
+            transcendentals=8 * rows * tile,
         ),
         name="feed",
-    )(scal, *seconds, *grads, *(() if make else (x_t,)), up, down, piece, beside, bias)
+    )(scal, *seconds, *grads, up, down, *pieces, bias)
 
 
 def run(kernel, name, scal, grid, in_specs, out_specs, out_shape, args, flops=0, scratch=()):
@@ -391,13 +414,13 @@
     )
 
 
-def pack_feed(scal, up, down, j, ranges):
+def pack_feed(scal, up, down, j, ranges, bit):
     rows, hidden = up.shape
     tile = hidden // (4 * ranges)
     columns = down.shape[1] // 2
 
     def kernel(s_ref, up_ref, down_ref, out_ref):
-        out_ref[...] = jnp.where(s_ref[1] == 0, up_ref[...], down_ref[...])
+        out_ref[...] = jnp.where(s_ref[bit] == 0, up_ref[...], down_ref[...])
 
     return run(
         kernel, "pack_feed", scal, (2,),
@@ -529,31 +552,6 @@
     )
 
 
-def other_rows(scal, lefts, rights, name):
-    rows = lefts[0].shape[0]
-    width = rights[0].shape[0]
-    local = rows // 2
-    count = len(lefts)
-    step = width // 4
-
-    def kernel(s_ref, *refs):
-        total = contract(refs[0][...], refs[count][...], 1, 1)
-        for j in range(1, count):
-            total = total + contract(refs[j][...], refs[count + j][...], 1, 1)
-        refs[-1][...] = total.astype(BF16)
-
-    def fixed(size):
-        return pl.BlockSpec((local, size), lambda i, s: (1, 0), pipeline_mode=pl.Buffered(1))
-
-    return run(
-        kernel, name, scal, (4,),
-        [fixed(a.shape[1]) for a in lefts]
-        + [spec((step, a.shape[1]), lambda i, s: (i, 0)) for a in rights],
-        spec((local, step), lambda i, s: (0, i)), struct(local, width), (*lefts, *rights),
-        flops=sum(2 * local * a.shape[1] * width for a in lefts),
-    )
-
-
 def norm_back_rows(grad, normed, inverse, gain):
     scaled = grad * gain
     first_term = jnp.mean(scaled, axis=-1, keepdims=True)
@@ -570,33 +568,27 @@
         refs[i : i + 1, :] += jnp.sum(value, axis=0, keepdims=True)
 
 
-def second_back(scal, d_pres, ups, received, middle, dy, gain):
+def row_step(rows):
+    return rows // 7 if rows % 112 == 0 else rows
+
+
+def second_back(scal, grad, received, middle, dy, gain):
     local, width = middle.shape
-    step = local // 2
-    count = len(d_pres)
-
-    def kernel(s_ref, *refs):
-        r_ref, mid_ref, dy_ref, gain_ref, wide_ref, low_ref, sums_ref = refs[2 * count :]
-        grad = r_ref[...].astype(F32)
-        for j in range(count):
-            grad = grad + contract(refs[j][...], refs[count + j][...], 1, 1)
+    step = row_step(local)
+
+    def kernel(s_ref, g_ref, r_ref, mid_ref, dy_ref, gain_ref, low_ref, sums_ref):
+        grad = g_ref[...].astype(F32) + r_ref[...].astype(F32)
         normed, inverse = normalize(mid_ref[...])
         dy_wide = dy_ref[...].astype(F32)
-        wide = dy_wide + norm_back_rows(grad, normed, inverse, gain_ref[...])
-        low = wide.astype(BF16)
-        wide_ref[...] = wide
+        low = (dy_wide + norm_back_rows(grad, normed, inverse, gain_ref[...])).astype(BF16)
         low_ref[...] = low
         column_sums(sums_ref, (grad * normed, grad, dy_wide, low.astype(F32)))
 
     block = spec((step, width), lambda i, s: (i, 0))
     return run(
-        kernel, "second_back", scal, (2,),
-        [spec((step, a.shape[1]), lambda i, s: (i, 0)) for a in d_pres]
-        + [held(*a.shape) for a in ups] + [block] * 3 + [held(1, width)],
-        [block, block, held(8, width)],
-        [struct(local, width, dtype=F32), struct(local, width), struct(8, width, dtype=F32)],
-        (*d_pres, *ups, received, middle, dy, gain),
-        flops=sum(2 * local * a.shape[1] * width for a in d_pres),
+        kernel, "second_back", scal, (local // step,), [block] * 4 + [held(1, width)],
+        [block, held(8, width)], [struct(local, width), struct(8, width, dtype=F32)],
+        (grad, received, middle, dy, gain),
     )
 
 
@@ -620,61 +612,32 @@
                 copy.wait()
 
         d_ref[...] = contract(low[...], w_ref[...], 1, 1).astype(BF16)
-        grad = contract(mixed_ref[...], low[...], 0, 0).astype(BF16)
-
-        @pl.when(pl.program_id(0) == s_ref[0])
-        def _():
-            keep_ref[...] = grad
-
-        @pl.when(pl.program_id(0) != s_ref[0])
-        def _():
-            send_ref[...] = grad
+        for c in range(2):
+            columns = slice(c * (width // 2), (c + 1) * (width // 2))
+            part = slice(c * block, (c + 1) * block)
+            grad = contract(mixed_ref[...], low[:, columns], 0, 0).astype(BF16)
+
+            @pl.when(pl.program_id(0) == s_ref[0])
+            def _():
+                keep_ref[part, :] = grad
+
+            @pl.when(pl.program_id(0) != s_ref[0])
+            def _():
+                send_ref[part, :] = grad
 
     anywhere = pl.BlockSpec(memory_space=pl.ANY)
     across = spec((rows, block), lambda t, s: (0, t))
     return run(
         kernel, "mixed_back", scal, (2,),
         [anywhere] * 2 + [spec((block, width), lambda t, s: (t, 0)), across],
-        [across, held(block, width), held(block, width)],
-        [struct(rows, set_width), struct(block, width), struct(block, width)],
+        [across, held(2 * block, width // 2), held(2 * block, width // 2)],
+        [struct(rows, set_width)] + [struct(2 * block, width // 2)] * 2,
         (*lows, out_set, mixed), flops=4 * rows * set_width * width,
         scratch=[pltpu.VMEM((rows, width), BF16), pltpu.SemaphoreType.DMA((2,))],
     )
 
 
-def first_back(scal, dqkvs, weights, received, x, wide, gain):
-    local, width = x.shape
-    step = local // 2
-    count = len(dqkvs)
-
-    def kernel(s_ref, *refs):
-        r_ref, x_ref, wide_ref, gain_ref, out_ref, sums_ref = refs[2 * count :]
-        grad = r_ref[...].astype(F32)
-        for j in range(count):
-            grad = grad + contract(refs[j][...], refs[count + j][...], 1, 1)
-        normed, inverse = normalize(x_ref[...].astype(F32))
-        total = wide_ref[...] + norm_back_rows(grad, normed, inverse, gain_ref[...])
-        out_ref[...] = total.astype(BF16)
-        column_sums(sums_ref, (grad * normed, grad))
-
-    block = spec((step, width), lambda i, s: (i, 0))
-    return run(
-        kernel, "first_back", scal, (2,),
-        [spec((step, a.shape[1]), lambda i, s: (i, 0)) for a in dqkvs]
-        + [
-            pl.BlockSpec((width, a.shape[1]), functools.partial(lambda j, i, s: (0, j), j),
-                         pipeline_mode=pl.Buffered(1))
-            for j, a in enumerate(dqkvs)
-        ]
-        + [block] * 3 + [held(1, width)],
-        [block, held(8, width)],
-        [struct(local, width), struct(8, width, dtype=F32)],
-        (*dqkvs, *([weights] * count), received, x, wide, gain),
-        flops=sum(2 * local * a.shape[1] * width for a in dqkvs),
-    )
-
-
-def first_other(scal, dqkvs, weights):
+def first_grad(scal, dqkvs, weights):
     rows = dqkvs[0].shape[0]
     width = weights.shape[0]
     local = rows // 2
@@ -685,135 +648,109 @@
         total = contract(refs[0][...], refs[count][...], 1, 1)
         for j in range(1, count):
             total = total + contract(refs[j][...], refs[count + j][...], 1, 1)
-        refs[-1][...] = total.astype(BF16)
-
+        refs[-2][...] = total[:local].astype(BF16)
+        refs[-1][...] = total[local:].astype(BF16)
+
+    across = spec((local, step), lambda i, s: (0, i))
     return run(
-        kernel, "first_other", scal, (4,),
-        [
-            pl.BlockSpec((local, a.shape[1]), lambda i, s: (1, 0), pipeline_mode=pl.Buffered(1))
-            for a in dqkvs
-        ]
+        kernel, "first_grad", scal, (4,),
+        [held(*a.shape) for a in dqkvs]
         + [
             pl.BlockSpec((step, a.shape[1]), functools.partial(lambda j, i, s: (i, j), j))
             for j, a in enumerate(dqkvs)
         ],
-        spec((local, step), lambda i, s: (0, i)), struct(local, width),
-        (*dqkvs, *([weights] * count)),
-        flops=sum(2 * local * a.shape[1] * width for a in dqkvs),
-    )
-
-
-def layer_other(scal, hiddens, downs):
-    rows = hiddens[0].shape[0]
-    width = downs[0].shape[1]
-    local = rows // 2
-    count = len(hiddens)
-    step = width // 4
-
-    def kernel(s_ref, *refs):
-        total = contract(refs[0][...], refs[count][...], 1, 0)
-        for j in range(1, count):
-            total = total + contract(refs[j][...], refs[count + j][...], 1, 0)
-        refs[-1][...] = total.astype(BF16)
-
+        [across, across], [struct(local, width)] * 2, (*dqkvs, *([weights] * count)),
+        flops=sum(2 * rows * a.shape[1] * width for a in dqkvs),
+    )
+
+
+def first_back(scal, grad, received, x, wide, gain):
+    local, width = x.shape
+    step = row_step(local)
+
+    def kernel(s_ref, g_ref, r_ref, x_ref, wide_ref, gain_ref, out_ref, sums_ref):
+        grad = g_ref[...].astype(F32) + r_ref[...].astype(F32)
+        normed, inverse = normalize(x_ref[...].astype(F32))
+        total = wide_ref[...].astype(F32) + norm_back_rows(grad, normed, inverse, gain_ref[...])
+        out_ref[...] = total.astype(BF16)
+        column_sums(sums_ref, (grad * normed, grad))
+
+    block = spec((step, width), lambda i, s: (i, 0))
     return run(
-        kernel, "layer_other", scal, (4,),
-        [
-            pl.BlockSpec((local, a.shape[1]), lambda i, s: (1, 0), pipeline_mode=pl.Buffered(1))
-            for a in hiddens
-        ]
-        + [spec((a.shape[0], step), lambda i, s: (0, i)) for a in downs],
-        spec((local, step), lambda i, s: (0, i)), struct(local, width), (*hiddens, *downs),
-        flops=sum(2 * local * a.shape[1] * width for a in hiddens),
-    )
-
-
-def layer_own(scal, hiddens, downs, received, middle, bias):
+        kernel, "first_back", scal, (local // step,), [block] * 4 + [held(1, width)],
+        [block, held(8, width)], [struct(local, width), struct(8, width, dtype=F32)],
+        (grad, received, x, wide, gain),
+    )
+
+
+def layer_rows(scal, own, received, middle, bias):
     local, width = middle.shape
-    count = len(hiddens)
-    step = width // 4
-
-    def kernel(s_ref, *refs):
-        r_ref, mid_ref, bias_ref, out_ref = refs[2 * count :]
-        total = mid_ref[...] + r_ref[...].astype(F32) + bias_ref[...]
-        for j in range(count):
-            total = total + contract(refs[j][...], refs[count + j][...], 1, 0)
+    step = row_step(local)
+
+    def kernel(s_ref, o_ref, r_ref, mid_ref, bias_ref, out_ref):
+        total = mid_ref[...] + o_ref[...].astype(F32) + r_ref[...].astype(F32) + bias_ref[...]
         out_ref[...] = total.astype(BF16)
 
-    across = spec((local, step), lambda i, s: (0, i))
+    block = spec((step, width), lambda i, s: (i, 0))
     return run(
-        kernel, "layer_own", scal, (4,),
-        [
-            pl.BlockSpec((local, a.shape[1]), lambda i, s: (0, 0), pipeline_mode=pl.Buffered(1))
-            for a in hiddens
-        ]
-        + [spec((a.shape[0], step), lambda i, s: (0, i)) for a in downs]
-        + [across, across, spec((1, step), lambda i, s: (0, i))],
-        across, struct(local, width), (*hiddens, *downs, received, middle, bias),
-        flops=sum(2 * local * a.shape[1] * width for a in hiddens),
-    )
-
-
-def finish_feed_kernel(core_ref, *refs, ranges, tile):
-    owns, refs = refs[: 2 * ranges], refs[2 * ranges :]
-    others, (up_out, down_out) = refs[: 2 * ranges], refs[2 * ranges :]
-    first = core_ref[0] == 0
-    for j in range(ranges):
-        for kind in range(2):
-            own, other = owns[2 * j + kind][...], others[2 * j + kind][...]
-            values = (jnp.where(first, own, other), jnp.where(first, other, own))
+        kernel, "layer_rows", scal, (local // step,), [block] * 3 + [held(1, width)],
+        block, struct(local, width), (own, received, middle, bias),
+    )
+
+
+def finish_feed_kernel(s_ref, *refs, tile):
+    sums, (up_out, down_out) = refs[:8], refs[8:]
+    first = s_ref[2] == 0
+    even = s_ref[1] == 0
+    for j in range(2):
+        mine, beside, mine_across, beside_across = [ref[...] for ref in sums[4 * j : 4 * j + 4]]
+        if j == 1:
+            mine, beside = jnp.where(even, mine, beside), jnp.where(even, beside, mine)
+            mine_across, beside_across = (
+                jnp.where(even, mine_across, beside_across),
+                jnp.where(even, beside_across, mine_across),
+            )
+        for kind, own, other in ((0, mine, mine_across), (1, beside, beside_across)):
             for c in range(2):
-                wide = values[c].astype(F32)
+                wide = jnp.where(first == (c == 0), own, other).astype(F32)
                 if kind == 1:
                     down_out[c, j] = wide
                     continue
                 for h in range(2):
-                    start = ((h * 2 + c) * ranges + j) * tile
+                    start = ((h * 2 + c) * 2 + j) * tile
                     up_out[:, start : start + tile] = wide[:, h * tile : (h + 1) * tile]
 
 
-def finish_feed(core, owns, others):
-    ranges = len(owns) // 2
-    rows, columns = owns[0].shape
-    tile, width = owns[1].shape
+def finish_feed(scal, sums):
+    rows, width = sums[0].shape
+    tile = rows
     steps = 4
-    up_spec = pl.BlockSpec((rows // steps, columns), lambda i, s: (i, 0))
-    down_spec = pl.BlockSpec((tile // steps, width), lambda i, s: (i, 0))
-    up, down = pl.pallas_call(
-        functools.partial(finish_feed_kernel, ranges=ranges, tile=tile),
-        grid_spec=pltpu.PrefetchScalarGridSpec(
-            num_scalar_prefetch=1,
-            grid=(steps,),
-            in_specs=[up_spec, down_spec] * (2 * ranges),
-            out_specs=[
-                pl.BlockSpec((rows // steps, 2 * ranges * columns), lambda i, s: (i, 0)),
-                pl.BlockSpec((2, ranges, tile // steps, width), lambda i, s: (0, 0, i, 0)),
-            ],
-        ),
-        out_shape=[
-            jax.ShapeDtypeStruct((rows, 2 * ranges * columns), F32),
-            jax.ShapeDtypeStruct((2, ranges, tile, width), F32),
+    block = spec((rows // steps, width), lambda i, s: (i, 0))
+    up, down = run(
+        functools.partial(finish_feed_kernel, tile=tile), "finish_feed", scal, (steps,),
+        [block] * 8,
+        [
+            spec((rows // steps, 4 * width), lambda i, s: (i, 0)),
+            spec((2, 2, rows // steps, width), lambda i, s: (0, 0, i, 0)),
         ],
-        compiler_params=pltpu.CompilerParams(vmem_limit_bytes=VMEM_LIMIT),
-        name="finish_feed",
-    )(core.reshape(1), *owns, *others)
-    return up, down.reshape(2 * ranges * tile, width)
-
-
-def finish_qkv_kernel(core_ref, *refs, pairs):
+        [struct(rows, 4 * width, dtype=F32), struct(2, 2, rows, width, dtype=F32)],
+        sums,
+    )
+    return up, down.reshape(4 * rows, width)
+
+
+def finish_qkv_kernel(s_ref, *refs, pairs, spans):
     outs = refs[-3:]
-    count = (len(refs) - 3) // 2
+    count = len(spans)
     owns, others = refs[:count], refs[count : 2 * count]
-    first = core_ref[0] == 0
-    per = pairs // count
+    first = s_ref[2] == 0
     half_pairs = pairs // 2
-    for g in range(count):
+    for g, (begin, end) in enumerate(spans):
         own, other = owns[g][...], others[g][...]
-        values = (jnp.where(first, own, other), jnp.where(first, other, own))
         for c in range(2):
-            wide = values[c].astype(F32).T
-            for q in range(per):
-                pair = g * per + q
+            wide = jnp.where(first == (c == 0), own, other).astype(F32).T
+            for q in range(end - begin):
+                pair = begin + q
                 h, p = pair // half_pairs, pair % half_pairs
                 goal = ((h * 2 + c) * half_pairs + p) * PAIR
                 for i in range(3):
@@ -821,23 +758,19 @@
                     outs[i][:, goal : goal + PAIR] = wide[:, start : start + PAIR]
 
 
-def finish_qkv(core, owns, others):
-    columns, rows = owns[0].shape
-    pairs = len(owns) * columns // (3 * PAIR)
+def finish_qkv(scal, owns, others, spans):
+    rows = owns[0].shape[1]
+    pairs = spans[-1][1]
     steps = 4
-    block = pl.BlockSpec((columns, rows // steps), lambda i, s: (0, i))
-    return pl.pallas_call(
-        functools.partial(finish_qkv_kernel, pairs=pairs),
-        grid_spec=pltpu.PrefetchScalarGridSpec(
-            num_scalar_prefetch=1,
-            grid=(steps,),
-            in_specs=[block] * (2 * len(owns)),
-            out_specs=[pl.BlockSpec((rows // steps, 2 * pairs * PAIR), lambda i, s: (i, 0))] * 3,
-        ),
-        out_shape=[jax.ShapeDtypeStruct((rows, 2 * pairs * PAIR), F32)] * 3,
-        compiler_params=pltpu.CompilerParams(vmem_limit_bytes=VMEM_LIMIT),
-        name="finish_qkv",
-    )(core.reshape(1), *owns, *others)
+    blocks = [
+        spec((3 * PAIR * (end - begin), rows // steps), lambda i, s: (0, i)) for begin, end in spans
+    ]
+    return run(
+        functools.partial(finish_qkv_kernel, pairs=pairs, spans=spans), "finish_qkv", scal,
+        (steps,), blocks * 2,
+        [spec((rows // steps, 2 * pairs * PAIR), lambda i, s: (i, 0))] * 3,
+        [struct(rows, 2 * pairs * PAIR, dtype=F32)] * 3, (*owns, *others),
+    )
 
 
 def wide_back_kernel(
@@ -1375,46 +1308,23 @@
     )
 
 
-class RingSum:
-    def __init__(self, place, ring, sends, keeps):
-        self.low, self.high = place % 2, place // 2
-        self.ring, self.deep = ring, ring // 2
-        self.beside = [(i, i ^ 1) for i in range(ring)]
-        self.keeps = keeps
-        self.sends = sends
-        self.received = [lax.ppermute(send, "half", SWAP) for send in sends]
+class LineSum:
+    def __init__(self, place, ring, values):
+        self.high, self.ring, self.deep = place // 2, ring, ring // 2
+        self.shape = values.shape
+        pieces = values.reshape(self.deep, -1, values.shape[-1])
+        self.piece = pick(pieces, self.high, 0)
+        self.sent = [pick(pieces, (self.high + s) % self.deep, 0) for s in range(1, self.deep)]
+        self.received = [
+            lax.ppermute(piece, "rz", self.route(s))
+            for s, piece in enumerate(self.sent, start=1)
+        ]
 
     def route(self, shift):
         return [(i, (i + 2 * shift) % self.ring) for i in range(self.ring)]
 
-    def to_neighbour(self, *gates):
-        received = list(after_all(self.received, *gates))
-        totals = [
-            (keep.astype(F32) + other.astype(F32)).astype(BF16)
-            for keep, other in zip(self.keeps, received)
-        ]
-        if len(totals) == 1:
-            size = totals[0].shape[0] // 2
-            totals = [totals[0][:size], totals[0][size:]]
-        even = self.low == 0
-        self.keep = jnp.where(even, totals[0], totals[1])
-        self.sent = jnp.where(even, totals[1], totals[0])
-        self.received = [lax.ppermute(self.sent, "rz", self.beside)]
-        return self.sent
-
-    def along(self, *gates):
-        (received,) = after_all(self.received, *gates)
-        total = (self.keep.astype(F32) + received.astype(F32)).astype(BF16)
-        self.shape = total.shape
-        total = total.reshape(self.deep, -1, total.shape[-1])
-        self.keep = pick(total, self.high, 0)
-        shifts = range(1, self.deep)
-        sent = [pick(total, (self.high + s) % self.deep, 0) for s in shifts]
-        self.received = [lax.ppermute(p, "rz", self.route(s)) for p, s in zip(sent, shifts)]
-        return sent[0]
-
     def spread(self, *gates):
-        piece = self.keep.astype(F32)
+        piece = self.piece.astype(F32)
         for other in after_all(self.received, *gates):
             piece = piece + other.astype(F32)
         self.piece = piece.astype(BF16)
@@ -1423,32 +1333,23 @@
         ]
         return self.piece
 
-    def back_to_neighbour(self, *gates):
+    def whole(self, *gates):
         gathered = [self.piece] + list(after_all(self.received, *gates))
-        deep = self.deep
-        self.whole = jnp.stack(
+        return jnp.concatenate(
             [
                 functools.reduce(
-                    lambda rest, s: jnp.where((self.high - s) % deep == i, gathered[s], rest),
-                    range(1, deep),
+                    lambda rest, s: jnp.where((self.high - s) % self.deep == i, gathered[s], rest),
+                    range(1, self.deep),
                     gathered[0],
                 )
-                for i in range(deep)
-            ]
+                for i in range(self.deep)
+            ],
+            axis=0,
         ).reshape(self.shape)
-        self.received = [
-            lax.ppermute(self.whole, "rz", self.beside),
-            lax.ppermute(self.whole, "core", SWAP),
-        ]
-        return self.whole
-
-    def to_core(self, *gates):
-        neighbour, whole = after_all(self.received, *gates)
-        crossed = lax.ppermute(neighbour, "core", SWAP)
-        even = self.low == 0
-        self.own = (jnp.where(even, self.whole, neighbour), jnp.where(even, neighbour, self.whole))
-        self.other = (jnp.where(even, whole, crossed), jnp.where(even, crossed, whole))
-        return neighbour
+
+
+def add_low(left, right):
+    return (left.astype(F32) + right.astype(F32)).astype(BF16)
 
 
 def after_all(values, *gates):
@@ -1465,17 +1366,15 @@
     clips, local, width = tokens.shape
     assert clips == 1
     ring = rep // 2
+    deep = ring // 2
     core, half, place = lax.axis_index("core"), lax.axis_index("half"), lax.axis_index("rz")
-    low = place % 2
+    low, high = place % 2, (place // 2) % 2
     own_rows = width // 2
     pairs = own_rows // PAIR
     hidden = up_weight.shape[1]
-    ranges = hidden // (2 * width)
-    tile = hidden // (4 * ranges)
     stays = core == half
-    scal = jnp.stack([half, low, core, stays.astype(jnp.int32)]).astype(jnp.int32)
+    scal = jnp.stack([half, low, core, stays.astype(jnp.int32), high]).astype(jnp.int32)
     cross = [(1, 2), (2, 1)]
-    beside = [(i, i ^ 1) for i in range(ring)]
 
     def swap_half(values):
         return lax.ppermute(values, "half", SWAP)
@@ -1484,14 +1383,16 @@
         return lax.ppermute(values, "core", SWAP)
 
     def swap_low(values):
-        return lax.ppermute(values, "rz", beside)
+        return lax.ppermute(values, "rz", [(i, i ^ 1) for i in range(ring)])
+
+    def swap_high(values):
+        return lax.ppermute(values, "rz", [(i, i ^ 2) for i in range(ring)])
 
     def cross_over(values):
         return lax.ppermute(values, ("core", "half"), cross)
 
     tokens, cotangent = tokens.reshape(local, width), cotangent.reshape(local, width)
 
-    tokens_in = cross_over(tokens)
     own_qkv, mine = pack_qkv(scal, (query_weight, key_weight, value_weight))
     qkv_x = swap_half(mine)
     vectors = jnp.concatenate(
@@ -1506,20 +1407,22 @@
     def set_entries(values, inner=1):
         return pick(values.reshape(2, 2, inner, -1), core, 1).transpose(1, 0, 2).reshape(inner, -1)
 
-    bias_sets = set_entries(vectors[:, 8 * own_rows :], ranges)
-    packed_feed = [pack_feed(scal, up_weight, down_weight, j, ranges) for j in range(ranges)]
+    bias_set = set_entries(vectors[:, 8 * own_rows :], 2).reshape(1, -1)
+    packed = [pack_feed(scal, up_weight, down_weight, j, 2, (1, 4)[j]) for j in range(2)]
     quarter = own_rows // 4
     out_mine = lax.dynamic_slice(
         out_weight, (core * (own_rows // 2) + low * quarter, 0 * core), (quarter, width)
     )
-
+    tokens, qkv_x, *packed = lax.optimization_barrier((tokens, qkv_x, *packed))
+    qkv_y = swap_low(qkv_x)
+    tokens_in = cross_over(tokens)
     x, first = first_norm(scal, tokens, tokens_in, gain_one, shift_one)
     first_in = swap_core(first)
-    qkv_x, out_mine, *packed_feed = lax.optimization_barrier((qkv_x, out_mine, *packed_feed))
-    qkv_y = swap_low(qkv_x)
+    out_mine, packed[0], packed[1], x = lax.optimization_barrier(
+        (out_mine, packed[0], packed[1], x)
+    )
     out_x = swap_half(out_mine)
-    feed_x = [swap_half(packed_feed[0])]
-    cotangent_in = cross_over(after(cotangent, qkv_x))
+    feed_x = [swap_half(values) for values in packed]
     zeros = jnp.zeros((pairs, PAIR), F32)
     qkv_bias = jnp.stack(
         [set_entries(full_qbias).reshape(pairs, PAIR), zeros,
@@ -1530,114 +1433,127 @@
         scal, (first, first_in), own_qkv, qkv_x, qkv_y, qkv_bias
     )
 
-    kept = attend(qkv, 0, pairs // 2)
-    out_x, feed_x[0], lse = lax.optimization_barrier((out_x, feed_x[0], kept[1]))
+    mixed, lse = attend(qkv, 0, pairs // 2)
+    out_x, feed_x[0], feed_x[1], cotangent, lse = lax.optimization_barrier(
+        (out_x, feed_x[0], feed_x[1], cotangent, lse)
+    )
     out_y = swap_low(out_x)
-    feed_y = [swap_low(feed_x[0])]
-    for j in range(1, ranges):
-        feed_x.append(swap_half(after(packed_feed[j], lse)))
-    mixed, lse = attend(qkv, pairs // 2, pairs, (kept[0], lse))
-    for j in range(1, ranges):
-        feed_x[j], lse = lax.optimization_barrier((feed_x[j], lse))
-        feed_y.append(swap_low(feed_x[j]))
+    feed_y = [swap_low(feed_x[0]), swap_high(feed_x[1])]
+    cotangent_in = cross_over(cotangent)
+    mixed, lse = attend(qkv, pairs // 2, pairs, (mixed, lse))
     out_part, out_set = out_other(scal, mixed, out_weight, out_x, out_y)
     out_in = swap_core(out_part)
-    grad_out = jnp.where(stays, cotangent, cotangent_in)
+    grad_out = jnp.where(stays, cotangent, after(cotangent_in, lse))
     grad_out_in = swap_core(grad_out)
     middle, second = second_norm(
         scal, mixed, out_set, x, out_in, full_obias, gain_two, shift_two
     )
     second_in = swap_core(second)
 
-    feeds, sums = [], []
-    x_t = None
-    for j in range(ranges):
-        bias = bias_sets[j : j + 1]
-        if feeds:
-            bias = after(bias, feeds[-1][6], feeds[-1][2])
-        outs = feed(
-            scal, (second, second_in), (grad_out, grad_out_in), x_t, up_weight, down_weight,
-            feed_x[j], feed_y[j], bias, j, ranges,
-        )
-        x_t = outs[9] if j == 0 else x_t
-        feeds.append(outs)
-        sums.append(RingSum(place, ring, [outs[2], outs[4]], [outs[3], outs[5]]))
-    hiddens, d_pres = [f[0] for f in feeds], [f[1] for f in feeds]
-    ups, downs = [f[7] for f in feeds], [f[8] for f in feeds]
-    grad_part = other_rows(scal, d_pres, ups, "feed_other")
-    grad_in = swap_core(grad_part)
-    layer_part = layer_other(scal, hiddens, downs)
-    grad_wide, grad_low, sums_two = second_back(
-        scal, d_pres, ups, grad_in, middle, grad_out, gain_two
-    )
+    (
+        out_own, out_part, dx_own, dx_part, up_send, up_keep, down_send, down_keep, low_send,
+        low_keep, up_bias_grad,
+    ) = feed(
+        scal, (second, second_in), (grad_out, grad_out_in), up_weight, down_weight,
+        (feed_x[0], feed_y[0], feed_x[1], feed_y[1]), bias_set,
+    )
+    first_in_half = [swap_half(up_send), swap_half(down_send)]
+    second_in_low = swap_low(low_send)
+    dx_in = swap_core(dx_part)
+    grad_low, sums_two = second_back(scal, dx_own, dx_in, middle, grad_out, gain_two)
     grad_low_in = swap_core(grad_low)
     grad_mixed, out_send, out_keep = mixed_back(scal, (grad_low, grad_low_in), out_set, mixed)
 
-    first_sum, last_sum = sums[0], sums[-1]
-    issued = [first_sum.to_neighbour(grad_mixed)]
-    out_sum = None
-    backs, qkv_sums = [], []
-    groups = 2
-    per = pairs // groups
-    for pair in range(pairs):
-        gate = after(lse, *issued)
-        outs = attend_back(scal, qkv, grad_mixed, mixed, gate, first_all, pair, pair + 1)
-        backs.append(outs)
-        done = outs[3]
-        issued = [done]
-        if pair == 0:
-            issued.append(first_sum.along(done))
-        elif pair == 1:
-            issued.append(first_sum.spread(done))
-            issued.append(last_sum.to_neighbour(done))
-            out_sum = RingSum(place, ring, [after(out_send, done)], [out_keep])
-        elif pair == 2:
-            issued.append(first_sum.back_to_neighbour(done))
-            issued.append(last_sum.along(done))
-            issued.append(out_sum.to_neighbour(done))
-    qkv_sums = [RingSum(place, ring, [b[1]], [b[2]]) for b in backs]
-    done = backs[-1][3]
-    grad_part = first_other(scal, [b[0] for b in backs], qkv_weight)
-    grad_in = swap_core(grad_part)
-    first_sum.to_core(done)
-    last_sum.spread(done)
-    out_sum.along(done)
-    layer_in = swap_core(layer_part)
-    layer_out = layer_own(scal, hiddens, downs, layer_in, middle, full_dbias)
-    layer_out = jnp.where(stays, layer_out, cross_over(layer_out))
-    tokens_grad, sums_one = first_back(
-        scal, [b[0] for b in backs], qkv_weight, grad_in, x, grad_wide, gain_one
-    )
-    tokens_grad = jnp.where(stays, tokens_grad, cross_over(tokens_grad))
-    for item in qkv_sums:
-        item.to_neighbour()
-    last_sum.back_to_neighbour()
-    out_sum.spread()
-    for item in qkv_sums:
-        item.along()
-    out_sum.back_to_neighbour()
-    last_sum.to_core()
-    for item in qkv_sums:
-        item.spread()
-    out_sum.to_core()
-    for item in qkv_sums:
-        item.back_to_neighbour()
-    for item in qkv_sums:
-        item.to_core()
+    backs = []
+
+    def back(pair, *issued):
+        gate = after(lse, *issued) if issued else lse
+        backs.append(attend_back(scal, qkv, grad_mixed, mixed, gate, first_all, pair, pair + 1))
+        return backs[-1][3]
+
+    done = back(0)
+    up_in, down_in, low_in = after_all((*first_in_half, second_in_low), done)
+    up_sum, down_sum = add_low(up_keep, up_in), add_low(down_keep, down_in)
+    range_sum = add_low(low_keep, low_in).reshape(2, own_rows, width)
+    half_send, half_keep = pick(range_sum, 1 - half, 0), pick(range_sum, half, 0)
+    half_in = swap_half(half_send)
+    up_sum, down_sum = lax.psum((up_sum, down_sum), "rz")
+
+    done = back(1, half_send)
+    (half_in,) = after_all((half_in,), done)
+    line = LineSum(place, ring, add_low(half_keep, half_in))
+
+    done = back(2, *line.sent)
+    issued = line.spread(done)
+    split = 3 * PAIR * (pairs - 1)
+
+    def start_half(sends, keeps, *gates):
+        send, keep = jnp.concatenate(sends, axis=0), jnp.concatenate(keeps, axis=0)
+        send = after(send, *gates) if gates else send
+        return send, keep, swap_half(send)
+
+    most_send, most_keep, most_in = start_half(
+        [b[1] for b in backs] + [out_send], [b[2] for b in backs] + [out_keep]
+    )
+
+    done = back(3, issued, most_send)
+    last_send, last_keep, last_in = start_half([backs[3][1]], [backs[3][2]])
+
+    def halves(values):
+        parts = values.reshape(deep, 2, -1, values.shape[-1])
+        return (
+            pick(parts, low, 1).reshape(-1, values.shape[-1]),
+            pick(parts, 1 - low, 1).reshape(-1, values.shape[-1]),
+        )
+
+    def meet(own, other):
+        width_in = own.shape[-1]
+        return join(
+            own.reshape(deep, -1, width_in), other.reshape(deep, -1, width_in), low
+        ).transpose(1, 0, 2, 3).reshape(-1, width_in)
+
+    first_own, first_part = first_grad(scal, [b[0] for b in backs], qkv_weight)
+    first_part_in = swap_core(first_part)
+    range_whole = line.whole(done)
+    range_beside = swap_low(range_whole)
+    range_across = swap_core(range_whole)
+
+    most_in, last_in = after_all((most_in, last_in), first_own)
+    most_keep, most_send = halves(add_low(most_keep, most_in))
+    last_keep, last_send = halves(add_low(last_keep, last_in))
+    most_low, last_low = swap_low(most_send), swap_low(last_send)
+    tokens_out, sums_one = first_back(
+        scal, first_own, after(first_part_in, most_send, last_send), x, grad_low, gain_one
+    )
+    out_in = swap_core(out_part)
+    layer = layer_rows(scal, out_own, out_in, middle, full_dbias)
+    layer_out = jnp.where(stays, layer, cross_over(layer))
+    tokens_grad = jnp.where(stays, tokens_out, cross_over(tokens_out))
+
+    most_line = LineSum(place, ring, add_low(most_keep, most_low))
+    last_line = LineSum(place, ring, add_low(last_keep, last_low))
+    most_line.spread()
+    last_line.spread()
+    most_whole, last_whole = most_line.whole(), last_line.whole()
+    most_sum = meet(most_whole, swap_low(most_whole))
+    last_sum = meet(last_whole, swap_low(last_whole))
 
     up_weight_grad, down_weight_grad = finish_feed(
-        core,
-        [v for item in sums for v in item.own],
-        [v for item in sums for v in item.other],
-    )
+        scal,
+        (
+            up_sum, down_sum, swap_core(up_sum), swap_core(down_sum),
+            range_whole, range_beside, range_across, swap_core(range_beside),
+        ),
+    )
+    most_across, last_across = swap_core(most_sum), swap_core(last_sum)
     query_weight_grad, key_weight_grad, value_weight_grad = finish_qkv(
-        core,
-        [jnp.concatenate(item.own, axis=0) for item in qkv_sums],
-        [jnp.concatenate(item.other, axis=0) for item in qkv_sums],
-    )
-    out_own = jnp.concatenate(out_sum.own, axis=0)
-    out_other_core = jnp.concatenate(out_sum.other, axis=0)
-    out_weight_grad = join(out_own, out_other_core, core).reshape(own_rows, width).astype(F32)
+        scal, (most_sum, last_sum), (most_across, last_across),
+        ((0, pairs - 1), (pairs - 1, pairs)),
+    )
+    out_weight_grad = join(most_sum[split:], most_across[split:], core)
+    out_weight_grad = out_weight_grad.reshape(2, 2, own_rows // 2, own_rows)
+    out_weight_grad = jnp.concatenate([out_weight_grad[:, 0], out_weight_grad[:, 1]], axis=2)
+    out_weight_grad = out_weight_grad.reshape(own_rows, width).astype(F32)
 
     def place_entries(values, inner=1):
         values = values.reshape(inner, 2, 1, -1).transpose(1, 2, 0, 3)
@@ -1647,8 +1563,7 @@
     parts = jnp.concatenate([b[3][0] for b in backs]).reshape(pairs, 3, PAIR)
     entries = [
         place_entries(parts[:, 0]), place_entries(parts[:, 2]), sums_two[3], sums_one[0],
-        sums_one[1], sums_two[0], sums_two[1], sums_two[2],
-        place_entries(jnp.stack([f[6] for f in feeds]), ranges),
+        sums_one[1], sums_two[0], sums_two[1], sums_two[2], place_entries(up_bias_grad, 2),
     ]
     entries = jnp.concatenate([e.reshape(2, -1) for e in entries], axis=1)
     entries = entries + swap_core(entries)
@@ -1678,7 +1593,7 @@
     matrix = P(("half", "gq"), None)
     vector = P(("half", "gq"))
     return jax.shard_map(
-        functools.partial(pair_body if grp == 2 and rep % 4 == 0 else wide_body, rep, grp),
+        functools.partial(pair_body if grp == 2 and rep % 8 == 0 else wide_body, rep, grp),
         mesh=split,
         in_specs=(
             clip, matrix, matrix, matrix, vector, vector, matrix, vector, vector, vector, vector,

time: 784 us -> 643 us (0.82)
  waiting for transfers between devices: 235 us -> 162 us
  starting transfers between devices: 127 us -> 95.8 us
  other arithmetic: 57.9 us -> 30.8 us
  between operations: 2.02 us -> 15.2 us
  Pallas kernels: 313 us -> 301 us
    ppermute x62 -> x19, waiting for transfers between devices: 127 us -> 72.1 us  [the longest x9 52.8 us: swap_low(): return lax.ppermute(values, 'rz', [(i, i ^ 1) for i in range(ring)])]
    ppermute x62 -> x19, starting transfers between devices: 73.6 us -> 25.4 us  [the longest x9 12.9 us: swap_low(): return lax.ppermute(values, 'rz', [(i, i ^ 1) for i in range(ring)])]
    ppermute x3, waiting for transfers between devices: 0.01 us -> 32.8 us  [pair_body(): lax.ppermute(entries, 'rz', [(i, i ^ step) for i in range(ring)])]
    ppermute x6 -> x11, waiting for transfers between devices: 63.8 us -> 35 us  [swap_half(): return lax.ppermute(values, 'half', SWAP)]
    select_n x22 -> x4, other arithmetic: 26.1 us -> 2.97 us  [the longest x1 1.59 us: pair_body(): grad_out = jnp.where(stays, cotangent, after(cotangent_in, lse))]
    ppermute x21 -> x9, waiting for transfers between devices: 33.2 us -> 17.5 us  [spread(): lax.ppermute(self.piece, 'rz', self.route(s))]
    pallas_call x4 -> x1, Pallas kernels: 70.7 us -> 60.3 us  [feed(): pl.pallas_call(feed_kernel, grid_spec=pltpu.PrefetchScalarGridSpec(num_sc...]
    unnamed x82 -> x110, local copies, waits for them, and re-layouts: 22.1 us -> 13.1 us
  transfers between devices with their start and end apart: 105 -> 62, of which waited for: 41 -> 22; matrix products, arithmetic and copies ran while one was open for 12% -> 8% of each run, Pallas kernels for 34% -> 35%
where the time goes in v4:
time: 643 us; the launch traced here: 636 us
  Pallas kernels  301 us (47%)
  waiting for transfers between devices  162 us (25%)
  starting transfers between devices  95.8 us (15%)
  local copies, waits for them, and re-layouts  31.1 us (5%)
  other arithmetic  30.8 us (5%)
  between operations  15.2 us (2%)
    pallas_call x14, Pallas kernels, run(): pl.pallas_call(kernel, grid_spec=pltpu.PrefetchScalarGridSpec(num_scalar_...  102 us
    pallas_call x4, Pallas kernels, attend_back(): pl.pallas_call(functools.partial(attend_back_kernel, tile, rows, padded),...  88.6 us
    pallas_call x1, Pallas kernels, feed(): pl.pallas_call(feed_kernel, grid_spec=pltpu.PrefetchScalarGridSpec(num_sc...  60.3 us
    ppermute x9, waiting for transfers between devices, swap_low(): return lax.ppermute(values, 'rz', [(i, i ^ 1) for i in range(ring)])  52.8 us
    pallas_call x2, Pallas kernels, attend(): pl.pallas_call(kernel if kept is None else lambda ref, a, b, *rest: kerne...  49.6 us
    ppermute x11, waiting for transfers between devices, swap_half(): return lax.ppermute(values, 'half', SWAP)  35 us
    ppermute x3, waiting for transfers between devices, pair_body(): lax.ppermute(entries, 'rz', [(i, i ^ step) for i in range(ring)])  32.8 us
    ppermute x9, starting transfers between devices, spread(): lax.ppermute(self.piece, 'rz', self.route(s))  28.4 us
  transfers between devices with their start and end apart: 62, of which 22 were waited for; matrix products, arithmetic and copies ran while one was open for 8% of the time, Pallas kernels for 35%

profile of v4, /device:TPU:1, one launch (start us, length us, event | category | flops | bytes accessed | tf_op | source)
XLA Modules:
  0.0 635.6 jit_solution(6548846415750998913)
XLA Ops:
  8.0 4.5 pack_qkv.1
  20.9 11.2 %collective-permute-done.piece_ref = bf16[256,1536]{1,0:T(8,128)(2,1)} collective-permute-done((bf16[256,1536]{1,0:T(8,128)(2,1)}, bf16[256,1536]{1,0:T(8,128)(2,1)}, u32[]{:S(2)}, u32[]{:S(2)}) %collective-permute-start) | collective-permute-done | bytes 786464 | tf_op jit(solution)/shard_map/ppermute | solution.py:1380
  32.1 4.5 collective-permute-start.1
  36.8 18.0 %collective-permute-done.2 = f32[6144]{0:T(1024)S(1)} collective-permute-done((f32[6144]{0:T(1024)S(1)}, f32[6144]{0:T(1024)S(1)}, u32[]{:S(2)}, u32[]{:S(2)}) %collective-permute-start.2) | collective-permute-done | bytes 24608 | tf_op jit(solution)/shard_map/ppermute | solution.py:1380
  66.9 14.3 %collective-permute-done.4.beside_ref = bf16[256,1536]{1,0:T(8,128)(2,1)S(1)} collective-permute-done((bf16[256,1536]{1,0:T(8,128)(2,1)}, bf16[256,1536]{1,0:T(8,128)(2,1)S(1)}, u32[]{:S(2)}, u32[]{:S(2)}) %collective-permute-start.4) | collective-permute-done | bytes 786464 | tf_op jit(solution)/shard_map/ppermute | solution.py:1386
  83.2 12.6 %project.1 = (bf16[1568,1536]{1,0:T(8,128)(2,1)}, bf16[1024,1536]{1,0:T(8,128)(2,1)}, bf16[1568,1024]{1,0:T(8,128)(2,1)}) custom-call(s32[5]{0:T(128)} %stack.88.s_ref, bf16[784,1024]{1,0:T(8,128)(2,1)} %get-tuple-element.105.mine_ref, bf16[784,1024]{1,0:T(8,128)(2,1)} %copy-done.39, bf16[512,1536]{1,0:T(8,128)(2,1)} %get-tuple-element.106.own_ref, ...), custom_call_target="tpu_custom_call" | custom-call | flops 4932501504 | bytes 12726272 | tf_op jit(solution)/shard_map/project/pallas_call | solution.py:366
  95.8 24.8 %attend.2 = (bf16[1568,512]{1,0:T(8,128)(2,1)}, f32[4,2,2048]{2,1,0:T(2,128)}) custom-call(bf16[1568,1536]{1,0:T(8,128)(2,1)} %get-tuple-element.108.qkv_ref.ref), custom_call_target="tpu_custom_call" | custom-call | flops 40282095616 | bytes 3211264 | tf_op jit(solution)/shard_map/attend/pallas_call | solution.py:68
  125.9 24.8 %attend.3 = (bf16[1568,512]{1,0:T(8,128)(2,1)}, f32[4,2,2048]{2,1,0:T(2,128)}) custom-call(bf16[1568,1536]{1,0:T(8,128)(2,1)} %get-tuple-element.108.qkv_ref.ref, bf16[1568,512]{1,0:T(8,128)(2,1)} %get-tuple-element.109.a, f32[4,2,2048]{2,1,0:T(2,128)} %get-tuple-element.117.b), custom_call_target="tpu_custom_call", output_to_operand_aliasing={{0}: (1, {}), {1}: (2, {})} | custom-call | flops 40282095616 | bytes 3211264 | tf_op jit(solution)/shard_map/attend/pallas_call | solution.py:68
  151.4 4.3 out_other.1
  159.7 6.1 second_norm.1
  168.1 22.4 %collective-permute-done.13.x_beside = bf16[512,1024]{1,0:T(8,128)(2,1)S(1)} collective-permute-done((bf16[512,1024]{1,0:T(8,128)(2,1)}, bf16[512,1024]{1,0:T(8,128)(2,1)S(1)}, u32[]{:S(2)}, u32[]{:S(2)}) %collective-permute-start.13) | collective-permute-done | bytes 1048608 | tf_op jit(solution)/shard_map/ppermute | solution.py:1386
  191.6 60.3 %feed.1 = (bf16[784,1024]{1,0:T(8,128)(2,1)}, bf16[784,1024]{1,0:T(8,128)(2,1)}, bf16[784,1024]{1,0:T(8,128)(2,1)}, bf16[784,1024]{1,0:T(8,128)(2,1)}, bf16[512,...) custom-call(s32[5]{0:T(128)} %stack.88.s_ref, ...), custom_call_target="tpu_custom_call" | custom-call | flops 39460012032 | bytes 25690112 | tf_op jit(solution)/shard_map/feed/pallas_call | solution.py:324
  253.2 4.8 collective-permute-done.17.r_ref
  258.0 9.0 %second_back.1 = (bf16[784,1024]{1,0:T(8,128)(2,1)}, f32[8,1024]{1,0:T(8,128)}) custom-call(s32[5]{0:T(128)} %stack.88.s_ref, bf16[784,1024]{1,0:T(8,128)(2,1)} %get-tuple-element.132.g_ref, bf16[784,1024]{1,0:T(8,128)(2,1)} %collective-permute-done.17.r_ref, f32[784,1024]{1,0:T(8,128)} %get-tuple-element.131.mid_ref, bf16[784,1024]{1,0:T(8,128)(2,1)} %copy-done.3, ...), custom_call_target="tpu_custom_call" | custom-call | bytes 16064512 | tf_op jit(solution)/shard_map/second_back/pallas_call | solution.py:366
  276.3 7.0 %layer_rows.1 = bf16[784,1024]{1,0:T(8,128)(2,1)} custom-call(s32[5]{0:T(128)} %stack.88.s_ref, bf16[784,1024]{1,0:T(8,128)(2,1)} %get-tuple-element.129.o_ref, bf16[784,1024]{1,0:T(8,128)(2,1)} %copy-done.7, f32[784,1024]{1,0:T(8,128)} %get-tuple-element.131.mid_ref, f32[1,1024]{1,0:T(1,128)} %bitcast.163), custom_call_target="tpu_custom_call" | custom-call | bytes 12853248 | tf_op jit(solution)/shard_map/layer_rows/pallas_call | solution.py:366
  283.2 11.6 %mixed_back.1 = (bf16[1568,512]{1,0:T(8,128)(2,1)}, bf16[512,512]{1,0:T(8,128)(2,1)}, bf16[512,512]{1,0:T(8,128)(2,1)}) custom-call(s32[5]{0:T(128)} %stack.88.s_ref, bf16[784,1024]{1,0:T(8,128)(2,1)} %get-tuple-element.134.mine_ref.wide_ref, bf16[784,1024]{1,0:T(8,128)(2,1)} %collective-permute-done.18.theirs_ref, ...), custom_call_target="tpu_custom_call" | custom-call | flops 3288334336 | bytes 11730944 | tf_op jit(solution)/shard_map/mixed_back/pallas_call | solution.py:366
  294.8 21.9 %attend_back.4 = (bf16[1568,384]{1,0:T(8,128)(2,1)}, bf16[384,512]{1,0:T(8,128)(2,1)}, bf16[384,512]{1,0:T(8,128)(2,1)}, f32[8,384]{1,0:T(8,128)}) custom-call(s32[5]{0:T(128)} %stack.88.s_ref, bf16[1568,1536]{1,0:T(8,128)(2,1)} %get-tuple-element.108.qkv_ref.ref, bf16[1568,512]{1,0:T(8,128)(2,1)} %get-tuple-element.135.grad_ref, ...), custom_call_target="tpu_custom_call" | custom-call | flops 50352619520 | bytes 3211264 | tf_op jit(solution)/shard_map/attend_back/pallas_call | solution.py:159
  322.5 22.4 %attend_back.5 = (bf16[1568,384]{1,0:T(8,128)(2,1)}, bf16[384,512]{1,0:T(8,128)(2,1)}, bf16[384,512]{1,0:T(8,128)(2,1)}, f32[8,384]{1,0:T(8,128)}) custom-call(s32[5]{0:T(128)} %stack.88.s_ref, bf16[1568,1536]{1,0:T(8,128)(2,1)} %get-tuple-element.108.qkv_ref.ref, bf16[1568,512]{1,0:T(8,128)(2,1)} %get-tuple-element.135.grad_ref, ...), custom_call_target="tpu_custom_call" | custom-call | flops 50352619520 | bytes 3211264 | tf_op jit(solution)/shard_map/attend_back/pallas_call | solution.py:159
  360.4 21.9 %attend_back.6 = (bf16[1568,384]{1,0:T(8,128)(2,1)}, bf16[384,512]{1,0:T(8,128)(2,1)}, bf16[384,512]{1,0:T(8,128)(2,1)}, f32[8,384]{1,0:T(8,128)}) custom-call(s32[5]{0:T(128)} %stack.88.s_ref, bf16[1568,1536]{1,0:T(8,128)(2,1)} %get-tuple-element.108.qkv_ref.ref, bf16[1568,512]{1,0:T(8,128)(2,1)} %get-tuple-element.135.grad_ref, ...), custom_call_target="tpu_custom_call" | custom-call | flops 50352619520 | bytes 3211264 | tf_op jit(solution)/shard_map/attend_back/pallas_call | solution.py:159
  391.9 15.3 %collective-permute-start.55 = (bf16[128,1024]{1,0:T(8,128)(2,1)S(1)}, bf16[128,1024]{1,0:T(8,128)(2,1)S(1)}, u32[]{:S(2)}, u32[]{:S(2)}) collective-permute-start(bf16[128,1024]{1,0:T(8,128)(2,1)S(1)} %fusion.4), channel_id=1, source_target_pairs={{0,8},{4,12},{8,16},{12,20},{16,24},{20,28},{24,0},{28,4},{1,9},{5... | collective-permute-start | bytes 786440 | tf_op jit(solution)/shard_map/ppermute | solution.py:1332
  409.4 22.3 %attend_back.7 = (bf16[1568,384]{1,0:T(8,128)(2,1)}, bf16[384,512]{1,0:T(8,128)(2,1)}, bf16[384,512]{1,0:T(8,128)(2,1)}, f32[8,384]{1,0:T(8,128)}) custom-call(s32[5]{0:T(128)} %stack.88.s_ref, bf16[1568,1536]{1,0:T(8,128)(2,1)} %get-tuple-element.108.qkv_ref.ref, bf16[1568,512]{1,0:T(8,128)(2,1)} %get-tuple-element.135.grad_ref, ...), custom_call_target="tpu_custom_call" | custom-call | flops 50352619520 | bytes 3211264 | tf_op jit(solution)/shard_map/attend_back/pallas_call | solution.py:159
  431.7 12.0 %first_grad.1 = (bf16[784,1024]{1,0:T(8,128)(2,1)}, bf16[784,1024]{1,0:T(8,128)(2,1)}) custom-call(s32[5]{0:T(128)} %stack.88.s_ref, bf16[1568,384]{1,0:T(8,128)(2,1)} %get-tuple-element.137.refs_0_, bf16[1568,384]{1,0:T(8,128)(2,1)} %get-tuple-element.145.refs_1_, bf16[1568,384]{1,0:T(8,128)(2,1)} %get-tuple-element.149.refs_2_, ...), custom_call_target="tpu_custom_call" | custom-call | flops 4932501504 | bytes 34799616 | tf_op jit(solution)/shard_map/first_grad/pallas_call | solution.py:366
  450.6 5.8 collective-permute-done.28
  461.8 8.4 %first_back.1 = (bf16[784,1024]{1,0:T(8,128)(2,1)}, f32[8,1024]{1,0:T(8,128)}) custom-call(s32[5]{0:T(128)} %stack.88.s_ref, bf16[784,1024]{1,0:T(8,128)(2,1)} %get-tuple-element.161.g_ref, bf16[784,1024]{1,0:T(8,128)(2,1)} %collective-permute-done.26.r_ref, bf16[784,1024]{1,0:T(8,128)(2,1)} %get-tuple-element.121.x_ref, ...), custom_call_target="tpu_custom_call" | custom-call | bytes 12853248 | tf_op jit(solution)/shard_map/first_back/pallas_call | solution.py:366
  472.8 14.8 %collective-permute-done.30 = bf16[832,512]{1,0:T(8,128)(2,1)} collective-permute-done((bf16[832,512]{1,0:T(8,128)(2,1)}, bf16[832,512]{1,0:T(8,128)(2,1)}, u32[]{:S(2)}, u32[]{:S(2)}) %collective-permute-start.30) | collective-permute-done | bytes 852000 | tf_op jit(solution)/shard_map/ppermute | solution.py:1386
  494.2 13.0 %collective-permute-done.32 = bf16[208,512]{1,0:T(8,128)(2,1)S(1)} collective-permute-done((bf16[208,512]{1,0:T(8,128)(2,1)S(1)}, bf16[208,512]{1,0:T(8,128)(2,1)S(1)}, u32[]{:S(2)}, u32[]{:S(2)}) %collective-permute-start.32) | collective-permute-done | bytes 213024 | tf_op jit(solution)/shard_map/ppermute | solution.py:1319
  513.2 7.7 %collective-permute-done.35 = bf16[208,512]{1,0:T(8,128)(2,1)S(1)} collective-permute-done((bf16[208,512]{1,0:T(8,128)(2,1)S(1)}, bf16[208,512]{1,0:T(8,128)(2,1)S(1)}, u32[]{:S(2)}, u32[]{:S(2)}) %collective-permute-start.35) | collective-permute-done | bytes 213024 | tf_op jit(solution)/shard_map/ppermute | solution.py:1332
  522.6 7.3 %collective-permute-start.37 = (bf16[832,512]{1,0:T(8,128)(2,1)S(1)}, bf16[832,512]{1,0:T(8,128)(2,1)}, u32[]{:S(2)}, u32[]{:S(2)}) collective-permute-start(bf16[832,512]{1,0:T(8,128)(2,1)S(1)} %pad_maximum_fusion.1), channel_id=1, source_target_pairs={{0,4},{4,0},{8,12},{12,8},{16,20},{20,16},{24,28},{28,24},{1,5},{5... | collective-permute-start | bytes 2555912 | tf_op jit(solution)/shard_map/ppermute | solution.py:1386
  538.4 31.2 %collective-permute-done.50 = f32[6144]{0:T(1024)S(1)} collective-permute-done((f32[6144]{0:T(1024)S(1)}, f32[6144]{0:T(1024)S(1)}, u32[]{:S(2)}, u32[]{:S(2)}) %collective-permute-start.50) | collective-permute-done | bytes 24608 | tf_op jit(solution)/shard_map/ppermute | solution.py:1576
  584.2 7.6 %collective-permute-start.29 = (bf16[784,1024]{1,0:T(8,128)(2,1)}, bf16[784,1024]{1,0:T(8,128)(2,1)}, u32[]{:S(2)}, u32[]{:S(2)}) collective-permute-start(bf16[784,1024]{1,0:T(8,128)(2,1)} %get-tuple-element.172), channel_id=1, source_target_pairs={{1,2},{2,1},{5,6},{6,5},{9,10},{10,9},{13,14},{14,13},{17,18},{18,... | collective-permute-start | bytes 4816904 | tf_op jit(solution)/shard_map/ppermute | solution.py:1392
  606.6 10.1 %finish_feed.1 = (f32[512,4096]{1,0:T(8,128)}, f32[2,2,512,1024]{3,2,1,0:T(8,128)}) custom-call(s32[5]{0:T(128)} %stack.88.s_ref, bf16[512,1024]{1,0:T(8,128)(2,1)} %get-tuple-element.197.refs_0_, bf16[512,1024]{1,0:T(8,128)(2,1)} %get-tuple-element.198.refs_1_, bf16[512,1024]{1,0:T(8,128)(2,1)} %collective-permute-done.53.refs_2_, ...), custom_call_target="tpu_custom_call" | custom-call | bytes 16777216 | tf_op jit(solution)/shard_map/finish_feed/pallas_call | solution.py:366
  622.5 6.1 finish_qkv.1
  (304 shorter events, 152.6 us)
Async XLA Ops:
  7.2 589.4 %all-reduce.9.cloned.1.call-start = ((), (), s32[]{:S(2)}) async-start(), calls=%async_computation | async-start | bytes 4194304 | tf_op jit(solution)/shard_map/psum | solution.py:1480
  32.1 24.0 %collective-permute-start.1 = (bf16[784,1024]{1,0:T(8,128)(2,1)S(1)}, bf16[784,1024]{1,0:T(8,128)(2,1)}, u32[]{:S(2)}, u32[]{:S(2)}) collective-permute-start(bf16[784,1024]{1,0:T(8,128)(2,1)S(1)} %bitcast.146), channel_id=1, source_target_pairs={{1,2},{2,1},{5,6},{6,5},{9,10},{10,9},{13,14},{14,13},{17,18},{18,... | collective-permute-start | bytes 4816904 | tf_op jit(solution)/shard_map/ppermute | solution.py:1392
  64.8 55.9 %collective-permute-start.5 = (bf16[128,1024]{1,0:T(8,128)(2,1)S(1)}, bf16[128,1024]{1,0:T(8,128)(2,1)}, u32[]{:S(2)}, u32[]{:S(2)}) collective-permute-start(bf16[128,1024]{1,0:T(8,128)(2,1)S(1)} %constant_dynamic-slice_fusion.7), channel_id=1, source_target_pairs={{0,1},{1,0},{2,3},{3,2},{4,5},{5,4},{6,7},{7,6},{8,9},{9,8},{10,11... | collective-permute-start | bytes 786440 | tf_op jit(solution)/shard_map/ppermute | solution.py:1380
  65.4 55.2 %collective-permute-start.6 = (bf16[512,1024]{1,0:T(8,128)(2,1)}, bf16[512,1024]{1,0:T(8,128)(2,1)}, u32[]{:S(2)}, u32[]{:S(2)}) collective-permute-start(bf16[512,1024]{1,0:T(8,128)(2,1)} %pack_feed.2), channel_id=1, source_target_pairs={{0,1},{1,0},{2,3},{3,2},{4,5},{5,4},{6,7},{7,6},{8,9},{9,8},{10,11... | collective-permute-start | bytes 3145736 | tf_op jit(solution)/shard_map/ppermute | solution.py:1380
  66.2 54.4 %collective-permute-start.7 = (bf16[512,1024]{1,0:T(8,128)(2,1)}, bf16[512,1024]{1,0:T(8,128)(2,1)}, u32[]{:S(2)}, u32[]{:S(2)}) collective-permute-start(bf16[512,1024]{1,0:T(8,128)(2,1)} %pack_feed.3), channel_id=1, source_target_pairs={{0,1},{1,0},{2,3},{3,2},{4,5},{5,4},{6,7},{7,6},{8,9},{9,8},{10,11... | collective-permute-start | bytes 3145736 | tf_op jit(solution)/shard_map/ppermute | solution.py:1380
  120.7 30.0 %collective-permute-start.8 = (bf16[128,1024]{1,0:T(8,128)(2,1)}, bf16[128,1024]{1,0:T(8,128)(2,1)S(1)}, u32[]{:S(2)}, u32[]{:S(2)}) collective-permute-start(bf16[128,1024]{1,0:T(8,128)(2,1)} %collective-permute-done.5.piece_ref), channel_id=1, source_target_pairs={{0,4},{4,0},{8,12},{12,8},{16,20},{20,16},{24,28},{28,24},{1,5},{5... | collective-permute-start | bytes 786440 | tf_op jit(solution)/shard_map/ppermute | solution.py:1386
  122.0 35.5 %collective-permute-start.11 = (bf16[784,1024]{1,0:T(8,128)(2,1)S(1)}, bf16[784,1024]{1,0:T(8,128)(2,1)}, u32[]{:S(2)}, u32[]{:S(2)}) collective-permute-start(bf16[784,1024]{1,0:T(8,128)(2,1)S(1)} %bitcast.144), channel_id=1, source_target_pairs={{1,2},{2,1},{5,6},{6,5},{9,10},{10,9},{13,14},{14,13},{17,18},{18,... | collective-permute-start | bytes 4816904 | tf_op jit(solution)/shard_map/ppermute | solution.py:1392
  159.1 31.4 %collective-permute-start.12 = (bf16[784,1024]{1,0:T(8,128)(2,1)S(1)}, bf16[784,1024]{1,0:T(8,128)(2,1)}, u32[]{:S(2)}, u32[]{:S(2)}) collective-permute-start(bf16[784,1024]{1,0:T(8,128)(2,1)S(1)} %broadcast_select_fusion.dy_own.dy_ref), channel_id=1, source_target_pairs={{0,2},{2,0},{1,3},{3,1},{4,6},{6,4},{5,7},{7,5},{8,10},{10,8},{9,1... | collective-permute-start | bytes 4816904 | tf_op jit(solution)/shard_map/ppermute | solution.py:1383
  165.8 25.8 %collective-permute-start.10 = (bf16[784,1024]{1,0:T(8,128)(2,1)}, bf16[784,1024]{1,0:T(8,128)(2,1)}, u32[]{:S(2)}, u32[]{:S(2)}) collective-permute-start(bf16[784,1024]{1,0:T(8,128)(2,1)} %get-tuple-element.123.x_own), channel_id=1, source_target_pairs={{0,2},{2,0},{1,3},{3,1},{4,6},{6,4},{5,7},{7,5},{8,10},{10,8},{9,1... | collective-permute-start | bytes 4816904 | tf_op jit(solution)/shard_map/ppermute | solution.py:1383
  165.8 24.7 %collective-permute-start.13 = (bf16[512,1024]{1,0:T(8,128)(2,1)}, bf16[512,1024]{1,0:T(8,128)(2,1)S(1)}, u32[]{:S(2)}, u32[]{:S(2)}) collective-permute-start(bf16[512,1024]{1,0:T(8,128)(2,1)} %collective-permute-done.6.x_piece), channel_id=1, source_target_pairs={{0,4},{4,0},{8,12},{12,8},{16,20},{20,16},{24,28},{28,24},{1,5},{5... | collective-permute-start | bytes 3145736 | tf_op jit(solution)/shard_map/ppermute | solution.py:1386
  166.1 24.4 %collective-permute-start.14 = (bf16[512,1024]{1,0:T(8,128)(2,1)}, bf16[512,1024]{1,0:T(8,128)(2,1)}, u32[]{:S(2)}, u32[]{:S(2)}) collective-permute-start(bf16[512,1024]{1,0:T(8,128)(2,1)} %collective-permute-done.7.z_piece), channel_id=1, source_target_pairs={{0,8},{4,12},{8,0},{12,4},{16,24},{20,28},{24,16},{28,20},{1,9},{5... | collective-permute-start | bytes 3145736 | tf_op jit(solution)/shard_map/ppermute | solution.py:1389
  253.1 22.0 %collective-permute-start.15 = (bf16[784,1024]{1,0:T(8,128)(2,1)}, bf16[784,1024]{1,0:T(8,128)(2,1)S(1)}, u32[]{:S(2)}, u32[]{:S(2)}) collective-permute-start(bf16[784,1024]{1,0:T(8,128)(2,1)} %get-tuple-element.130), channel_id=1, source_target_pairs={{0,2},{2,0},{1,3},{3,1},{4,6},{6,4},{5,7},{7,5},{8,10},{10,8},{9,1... | collective-permute-start | bytes 4816904 | tf_op jit(solution)/shard_map/ppermute | solution.py:1383
  268.0 48.8 %collective-permute-start.19 = (bf16[512,1024]{1,0:T(8,128)(2,1)}, bf16[512,1024]{1,0:T(8,128)(2,1)}, u32[]{:S(2)}, u32[]{:S(2)}) collective-permute-start(bf16[512,1024]{1,0:T(8,128)(2,1)} %get-tuple-element.139), channel_id=1, source_target_pairs={{0,1},{1,0},{2,3},{3,2},{4,5},{5,4},{6,7},{7,6},{8,9},{9,8},{10,11... | collective-permute-start | bytes 3145736 | tf_op jit(solution)/shard_map/ppermute | solution.py:1380
  268.2 48.6 %collective-permute-start.20 = (bf16[512,1024]{1,0:T(8,128)(2,1)}, bf16[512,1024]{1,0:T(8,128)(2,1)}, u32[]{:S(2)}, u32[]{:S(2)}) collective-permute-start(bf16[512,1024]{1,0:T(8,128)(2,1)} %get-tuple-element.140), channel_id=1, source_target_pairs={{0,1},{1,0},{2,3},{3,2},{4,5},{5,4},{6,7},{7,6},{8,9},{9,8},{10,11... | collective-permute-start | bytes 3145736 | tf_op jit(solution)/shard_map/ppermute | solution.py:1380
  269.4 47.3 %collective-permute-start.21 = (bf16[1024,1024]{1,0:T(8,128)(2,1)}, bf16[1024,1024]{1,0:T(8,128)(2,1)}, u32[]{:S(2)}, u32[]{:S(2)}) collective-permute-start(bf16[1024,1024]{1,0:T(8,128)(2,1)} %get-tuple-element.141), channel_id=1, source_target_pairs={{0,4},{4,0},{8,12},{12,8},{16,20},{20,16},{24,28},{28,24},{1,5},{5... | collective-permute-start | bytes 6291464 | tf_op jit(solution)/shard_map/ppermute | solution.py:1386
  322.3 30.9 %collective-permute-start.22 = (bf16[512,1024]{1,0:T(8,128)(2,1)}, bf16[512,1024]{1,0:T(8,128)(2,1)}, u32[]{:S(2)}, u32[]{:S(2)}) collective-permute-start(bf16[512,1024]{1,0:T(8,128)(2,1)} %dynamic-slice_bitcast_fusion), channel_id=1, source_target_pairs={{0,1},{1,0},{2,3},{3,2},{4,5},{5,4},{6,7},{7,6},{8,9},{9,8},{10,11... | collective-permute-start | bytes 3145736 | tf_op jit(solution)/shard_map/ppermute | solution.py:1380
  355.7 31.1 %collective-permute-start.23 = (bf16[128,1024]{1,0:T(8,128)(2,1)}, bf16[128,1024]{1,0:T(8,128)(2,1)S(1)}, u32[]{:S(2)}, u32[]{:S(2)}) collective-permute-start(bf16[128,1024]{1,0:T(8,128)(2,1)} %get-tuple-element.209), channel_id=1, source_target_pairs={{0,8},{4,12},{8,16},{12,20},{16,24},{20,28},{24,0},{28,4},{1,9},{5... | collective-permute-start | bytes 786440 | tf_op jit(solution)/shard_map/ppermute | solution.py:1319
  357.0 33.7 %collective-permute-start.24 = (bf16[128,1024]{1,0:T(8,128)(2,1)}, bf16[128,1024]{1,0:T(8,128)(2,1)}, u32[]{:S(2)}, u32[]{:S(2)}) collective-permute-start(bf16[128,1024]{1,0:T(8,128)(2,1)} %get-tuple-element.208), channel_id=1, source_target_pairs={{0,16},{4,20},{8,24},{12,28},{16,0},{20,4},{24,8},{28,12},{1,17},{... | collective-permute-start | bytes 786440 | tf_op jit(solution)/shard_map/ppermute | solution.py:1319
  359.4 31.4 %collective-permute-start.25 = (bf16[128,1024]{1,0:T(8,128)(2,1)}, bf16[128,1024]{1,0:T(8,128)(2,1)}, u32[]{:S(2)}, u32[]{:S(2)}) collective-permute-start(bf16[128,1024]{1,0:T(8,128)(2,1)} %get-tuple-element.207), channel_id=1, source_target_pairs={{0,24},{4,28},{8,0},{12,4},{16,8},{20,12},{24,16},{28,20},{1,25},{... | collective-permute-start | bytes 786440 | tf_op jit(solution)/shard_map/ppermute | solution.py:1319
  385.0 71.4 %collective-permute-start.27 = (bf16[1664,512]{1,0:T(8,128)(2,1)}, bf16[1664,512]{1,0:T(8,128)(2,1)}, u32[]{:S(2)}, u32[]{:S(2)}) collective-permute-start(bf16[1664,512]{1,0:T(8,128)(2,1)} %constant_dynamic-update-slice_fusion.1), channel_id=1, source_target_pairs={{0,1},{1,0},{2,3},{3,2},{4,5},{5,4},{6,7},{7,6},{8,9},{9,8},{10,11... | collective-permute-start | bytes 5111816 | tf_op jit(solution)/shard_map/ppermute | solution.py:1380
  391.9 53.5 %collective-permute-start.55 = (bf16[128,1024]{1,0:T(8,128)(2,1)S(1)}, bf16[128,1024]{1,0:T(8,128)(2,1)S(1)}, u32[]{:S(2)}, u32[]{:S(2)}) collective-permute-start(bf16[128,1024]{1,0:T(8,128)(2,1)S(1)} %fusion.4), channel_id=1, source_target_pairs={{0,8},{4,12},{8,16},{12,20},{16,24},{20,28},{24,0},{28,4},{1,9},{5... | collective-permute-start | bytes 786440 | tf_op jit(solution)/shard_map/ppermute | solution.py:1332
  407.3 39.5 %collective-permute-start.56 = (bf16[128,1024]{1,0:T(8,128)(2,1)S(1)}, bf16[128,1024]{1,0:T(8,128)(2,1)S(1)}, u32[]{:S(2)}, u32[]{:S(2)}) collective-permute-start(bf16[128,1024]{1,0:T(8,128)(2,1)S(1)} %fusion.4), channel_id=1, source_target_pairs={{0,16},{4,20},{8,24},{12,28},{16,0},{20,4},{24,8},{28,12},{1,17},{... | collective-permute-start | bytes 786440 | tf_op jit(solution)/shard_map/ppermute | solution.py:1332
  407.8 41.5 %collective-permute-start.57 = (bf16[128,1024]{1,0:T(8,128)(2,1)S(1)}, bf16[128,1024]{1,0:T(8,128)(2,1)}, u32[]{:S(2)}, u32[]{:S(2)}) collective-permute-start(bf16[128,1024]{1,0:T(8,128)(2,1)S(1)} %fusion.4), channel_id=1, source_target_pairs={{0,24},{4,28},{8,0},{12,4},{16,8},{20,12},{24,16},{28,20},{1,25},{... | collective-permute-start | bytes 786440 | tf_op jit(solution)/shard_map/ppermute | solution.py:1332
  446.8 147.4 %collective-permute-start.16 = (bf16[784,1024]{1,0:T(8,128)(2,1)}, bf16[784,1024]{1,0:T(8,128)(2,1)}, u32[]{:S(2)}, u32[]{:S(2)}) collective-permute-start(bf16[784,1024]{1,0:T(8,128)(2,1)} %layer_rows.1), channel_id=1, source_target_pairs={{1,2},{2,1},{5,6},{6,5},{9,10},{10,9},{13,14},{14,13},{17,18},{18,... | collective-permute-start | bytes 4816904 | tf_op jit(solution)/shard_map/ppermute | solution.py:1392
  459.4 28.2 %collective-permute-start.30 = (bf16[832,512]{1,0:T(8,128)(2,1)}, bf16[832,512]{1,0:T(8,128)(2,1)}, u32[]{:S(2)}, u32[]{:S(2)}) collective-permute-start(bf16[832,512]{1,0:T(8,128)(2,1)} %bitcast.23), channel_id=1, source_target_pairs={{0,4},{4,0},{8,12},{12,8},{16,20},{20,16},{24,28},{28,24},{1,5},{5... | collective-permute-start | bytes 2555912 | tf_op jit(solution)/shard_map/ppermute | solution.py:1386
  461.3 30.4 %collective-permute-start.38 = (bf16[192,512]{1,0:T(8,128)(2,1)}, bf16[192,512]{1,0:T(8,128)(2,1)}, u32[]{:S(2)}, u32[]{:S(2)}) collective-permute-start(bf16[192,512]{1,0:T(8,128)(2,1)} %bitcast.25), channel_id=1, source_target_pairs={{0,4},{4,0},{8,12},{12,8},{16,20},{20,16},{24,28},{28,24},{1,5},{5... | collective-permute-start | bytes 589832 | tf_op jit(solution)/shard_map/ppermute | solution.py:1386
  522.6 69.2 %collective-permute-start.37 = (bf16[832,512]{1,0:T(8,128)(2,1)S(1)}, bf16[832,512]{1,0:T(8,128)(2,1)}, u32[]{:S(2)}, u32[]{:S(2)}) collective-permute-start(bf16[832,512]{1,0:T(8,128)(2,1)S(1)} %pad_maximum_fusion.1), channel_id=1, source_target_pairs={{0,4},{4,0},{8,12},{12,8},{16,20},{20,16},{24,28},{28,24},{1,5},{5... | collective-permute-start | bytes 2555912 | tf_op jit(solution)/shard_map/ppermute | solution.py:1386
  534.7 60.5 %collective-permute-start.58 = (bf16[512,1024]{1,0:T(8,128)(2,1)S(1)}, bf16[512,1024]{1,0:T(8,128)(2,1)}, u32[]{:S(2)}, u32[]{:S(2)}) collective-permute-start(bf16[512,1024]{1,0:T(8,128)(2,1)S(1)} %pad_maximum_fusion.refs_4_), channel_id=1, source_target_pairs={{0,4},{4,0},{8,12},{12,8},{16,20},{20,16},{24,28},{28,24},{1,5},{5... | collective-permute-start | bytes 3145736 | tf_op jit(solution)/shard_map/ppermute | solution.py:1386
  535.2 61.3 %collective-permute-start.59 = (bf16[512,1024]{1,0:T(8,128)(2,1)S(1)}, bf16[512,1024]{1,0:T(8,128)(2,1)}, u32[]{:S(2)}, u32[]{:S(2)}) collective-permute-start(bf16[512,1024]{1,0:T(8,128)(2,1)S(1)} %pad_maximum_fusion.refs_4_), channel_id=1, source_target_pairs={{0,2},{2,0},{1,3},{3,1},{4,6},{6,4},{5,7},{7,5},{8,10},{10,8},{9,1... | collective-permute-start | bytes 3145736 | tf_op jit(solution)/shard_map/ppermute | solution.py:1383
  538.4 31.2 %collective-permute-start.50 = (f32[6144]{0:T(1024)S(1)}, f32[6144]{0:T(1024)S(1)}, u32[]{:S(2)}, u32[]{:S(2)}) collective-permute-start(f32[6144]{0:T(1024)S(1)} %add.261), channel_id=1, source_target_pairs={{0,4},{4,0},{8,12},{12,8},{16,20},{20,16},{24,28},{28,24},{1,5},{5... | collective-permute-start | bytes 73736 | tf_op jit(solution)/shard_map/ppermute | solution.py:1576
  584.2 32.6 %collective-permute-start.29 = (bf16[784,1024]{1,0:T(8,128)(2,1)}, bf16[784,1024]{1,0:T(8,128)(2,1)}, u32[]{:S(2)}, u32[]{:S(2)}) collective-permute-start(bf16[784,1024]{1,0:T(8,128)(2,1)} %get-tuple-element.172), channel_id=1, source_target_pairs={{1,2},{2,1},{5,6},{6,5},{9,10},{10,9},{13,14},{14,13},{17,18},{18,... | collective-permute-start | bytes 4816904 | tf_op jit(solution)/shard_map/ppermute | solution.py:1392
  594.2 25.4 %collective-permute-start.46 = (bf16[1664,512]{1,0:T(8,128)(2,1)S(1)}, bf16[1664,512]{1,0:T(8,128)(2,1)}, u32[]{:S(2)}, u32[]{:S(2)}) collective-permute-start(bf16[1664,512]{1,0:T(8,128)(2,1)S(1)} %bitcast.128), channel_id=1, source_target_pairs={{0,2},{2,0},{1,3},{3,1},{4,6},{6,4},{5,7},{7,5},{8,10},{10,8},{9,1... | collective-permute-start | bytes 5111816 | tf_op jit(solution)/shard_map/ppermute | solution.py:1383
  (72 other events, 862.6 us)
Sparse Core Ops, SparseCore 0:
  350.4 139.7 all-reduce.8

commit v5 on v4

--- a/solution.py
+++ b/solution.py
@@ -459,7 +459,7 @@
 def project(scal, firsts, own, piece, beside, bias):
     local, width = firsts[0].shape
     rows, total = 2 * local, own.shape[1]
-    block = 3 * PAIR
+    block = 6 * PAIR
     half_rows, quarter_rows = width // 2, width // 4
 
     def kernel(
@@ -612,18 +612,23 @@
                 copy.wait()
 
         d_ref[...] = contract(low[...], w_ref[...], 1, 1).astype(BF16)
-        for c in range(2):
-            columns = slice(c * (width // 2), (c + 1) * (width // 2))
-            part = slice(c * block, (c + 1) * block)
-            grad = contract(mixed_ref[...], low[:, columns], 0, 0).astype(BF16)
-
-            @pl.when(pl.program_id(0) == s_ref[0])
-            def _():
-                keep_ref[part, :] = grad
-
-            @pl.when(pl.program_id(0) != s_ref[0])
-            def _():
-                send_ref[part, :] = grad
+        grad = contract(mixed_ref[...], low[...], 0, 0).astype(BF16)
+
+        def store(goal):
+            for c in range(2):
+                for i in range(width // (2 * PAIR)):
+                    start = (2 * i + c) * PAIR
+                    goal[c * block : (c + 1) * block, i * PAIR : (i + 1) * PAIR] = (
+                        grad[:, start : start + PAIR]
+                    )
+
+        @pl.when(pl.program_id(0) == s_ref[0])
+        def _():
+            store(keep_ref)
+
+        @pl.when(pl.program_id(0) != s_ref[0])
+        def _():
+            store(send_ref)
 
     anywhere = pl.BlockSpec(memory_space=pl.ANY)
     across = spec((rows, block), lambda t, s: (0, t))
@@ -645,21 +650,16 @@
     step = width // 4
 
     def kernel(s_ref, *refs):
-        total = contract(refs[0][...], refs[count][...], 1, 1)
-        for j in range(1, count):
-            total = total + contract(refs[j][...], refs[count + j][...], 1, 1)
+        left = jnp.concatenate([refs[j][...] for j in range(count)], axis=1)
+        total = contract(left, refs[count][...], 1, 1)
         refs[-2][...] = total[:local].astype(BF16)
         refs[-1][...] = total[local:].astype(BF16)
 
     across = spec((local, step), lambda i, s: (0, i))
     return run(
         kernel, "first_grad", scal, (4,),
-        [held(*a.shape) for a in dqkvs]
-        + [
-            pl.BlockSpec((step, a.shape[1]), functools.partial(lambda j, i, s: (i, j), j))
-            for j, a in enumerate(dqkvs)
-        ],
-        [across, across], [struct(local, width)] * 2, (*dqkvs, *([weights] * count)),
+        [held(*a.shape) for a in dqkvs] + [spec((step, weights.shape[1]), lambda i, s: (i, 0))],
+        [across, across], [struct(local, width)] * 2, (*dqkvs, weights),
         flops=sum(2 * rows * a.shape[1] * width for a in dqkvs),
     )
 
@@ -704,12 +704,11 @@
     even = s_ref[1] == 0
     for j in range(2):
         mine, beside, mine_across, beside_across = [ref[...] for ref in sums[4 * j : 4 * j + 4]]
-        if j == 1:
-            mine, beside = jnp.where(even, mine, beside), jnp.where(even, beside, mine)
-            mine_across, beside_across = (
-                jnp.where(even, mine_across, beside_across),
-                jnp.where(even, beside_across, mine_across),
-            )
+        mine, beside = jnp.where(even, mine, beside), jnp.where(even, beside, mine)
+        mine_across, beside_across = (
+            jnp.where(even, mine_across, beside_across),
+            jnp.where(even, beside_across, mine_across),
+        )
         for kind, own, other in ((0, mine, mine_across), (1, beside, beside_across)):
             for c in range(2):
                 wide = jnp.where(first == (c == 0), own, other).astype(F32)
@@ -739,37 +738,54 @@
     return up, down.reshape(4 * rows, width)
 
 
-def finish_qkv_kernel(s_ref, *refs, pairs, spans):
-    outs = refs[-3:]
-    count = len(spans)
-    owns, others = refs[:count], refs[count : 2 * count]
-    first = s_ref[2] == 0
+def finish_attention_kernel(s_ref, *refs, pairs, spans):
+    q_out, k_out, v_out, out_out = refs[-4:]
+    first, even = s_ref[2] == 0, s_ref[1] == 0
     half_pairs = pairs // 2
     for g, (begin, end) in enumerate(spans):
-        own, other = owns[g][...], others[g][...]
+        if g == 0:
+            mine, beside, mine_across, beside_across = [ref[...] for ref in refs[:4]]
+            own = jnp.concatenate(
+                [jnp.where(even, mine, beside), jnp.where(even, beside, mine)], axis=0
+            )
+            other = jnp.concatenate(
+                [
+                    jnp.where(even, mine_across, beside_across),
+                    jnp.where(even, beside_across, mine_across),
+                ],
+                axis=0,
+            )
+        else:
+            own, other = refs[2 * g + 2][...], refs[2 * g + 3][...]
         for c in range(2):
-            wide = jnp.where(first == (c == 0), own, other).astype(F32).T
+            total = jnp.where(first == (c == 0), own, other).astype(F32)
+            wide = total[: (end - begin) * 3 * PAIR].T
             for q in range(end - begin):
                 pair = begin + q
                 h, p = pair // half_pairs, pair % half_pairs
                 goal = ((h * 2 + c) * half_pairs + p) * PAIR
-                for i in range(3):
+                for i, out in enumerate((q_out, k_out, v_out)):
                     start = (q * 3 + i) * PAIR
-                    outs[i][:, goal : goal + PAIR] = wide[:, start : start + PAIR]
-
-
-def finish_qkv(scal, owns, others, spans):
-    rows = owns[0].shape[1]
+                    out[:, goal : goal + PAIR] = wide[:, start : start + PAIR]
+            if g == 0:
+                rest = total[(end - begin) * 3 * PAIR :]
+                rows = rest.shape[0] // 2
+                out_out[c * rows : (c + 1) * rows, :PAIR] = rest[:rows]
+                out_out[c * rows : (c + 1) * rows, PAIR:] = rest[rows:]
+
+
+def finish_attention(scal, sums, spans):
+    rows = sums[0].shape[1]
     pairs = spans[-1][1]
-    steps = 4
-    blocks = [
-        spec((3 * PAIR * (end - begin), rows // steps), lambda i, s: (0, i)) for begin, end in spans
-    ]
+    steps = rows // PAIR
     return run(
-        functools.partial(finish_qkv_kernel, pairs=pairs, spans=spans), "finish_qkv", scal,
-        (steps,), blocks * 2,
-        [spec((rows // steps, 2 * pairs * PAIR), lambda i, s: (i, 0))] * 3,
-        [struct(rows, 2 * pairs * PAIR, dtype=F32)] * 3, (*owns, *others),
+        functools.partial(finish_attention_kernel, pairs=pairs, spans=spans), "finish_attention",
+        scal, (steps,),
+        [spec((values.shape[0], PAIR), lambda i, s: (0, i)) for values in sums],
+        [spec((PAIR, 2 * pairs * PAIR), lambda i, s: (i, 0))] * 3
+        + [spec((rows, 2 * PAIR), lambda i, s: (0, i))],
+        [struct(rows, 2 * pairs * PAIR, dtype=F32)] * 3 + [struct(rows, 2 * rows, dtype=F32)],
+        sums,
     )
 
 
@@ -1308,44 +1324,110 @@
     )
 
 
+class Order:
+    def __init__(self):
+        self.before = ()
+
+    def pin(self, *values):
+        pinned = lax.optimization_barrier(values + self.before)[: len(values)]
+        self.before = tuple(pinned) + self.before
+        return pinned[0] if len(values) == 1 else list(pinned)
+
+    def fence(self, *values):
+        self.before = values
+
+
 class LineSum:
-    def __init__(self, place, ring, values):
-        self.high, self.ring, self.deep = place // 2, ring, ring // 2
+    def __init__(self, order, axes, size, values):
+        self.order, self.axes, self.size = order, axes, size
         self.shape = values.shape
-        pieces = values.reshape(self.deep, -1, values.shape[-1])
-        self.piece = pick(pieces, self.high, 0)
-        self.sent = [pick(pieces, (self.high + s) % self.deep, 0) for s in range(1, self.deep)]
-        self.received = [
-            lax.ppermute(piece, "rz", self.route(s))
-            for s, piece in enumerate(self.sent, start=1)
+        if axes == "line":
+            self.place = lax.axis_index("line")
+            pieces = values.reshape(size, -1, values.shape[-1])
+            sent = [pick(pieces, (self.place + s) % size, 0) for s in range(1, size)]
+            self.piece, *sent = order.pin(pick(pieces, self.place, 0), *sent)
+            self.received = [self.shift(values, s) for s, values in enumerate(sent, start=1)]
+            return
+        values = order.pin(values)
+        self.received = self.exchange(values.reshape(size, -1, values.shape[-1]))
+
+    def shift(self, values, s):
+        return lax.ppermute(values, "line", [(i, (i + s) % self.size) for i in range(self.size)])
+
+    def exchange(self, values):
+        return lax.all_to_all(values, self.axes, split_axis=0, concat_axis=0, tiled=True)
+
+    def spread(self):
+        if self.axes == "line":
+            piece = self.piece.astype(F32)
+            for other in self.order.pin(*self.received):
+                piece = piece + other.astype(F32)
+            self.piece = self.order.pin(piece.astype(BF16))
+            self.received = [self.shift(self.piece, s) for s in range(1, self.size)]
+            return
+        received = self.order.pin(self.received)
+        piece = received[0].astype(F32)
+        for i in range(1, self.size):
+            piece = piece + received[i].astype(F32)
+        piece = piece.astype(BF16)
+        copies = self.order.pin(jnp.broadcast_to(piece[None], (self.size,) + piece.shape))
+        self.received = self.exchange(copies)
+
+    def gather(self):
+        if self.axes != "line":
+            return self.order.pin(self.received).reshape(self.shape)
+        gathered = [self.piece] + list(self.order.pin(*self.received))
+        whole = [
+            functools.reduce(
+                lambda rest, s: jnp.where((self.place - s) % self.size == i, gathered[s], rest),
+                range(1, self.size),
+                gathered[0],
+            )
+            for i in range(self.size)
         ]
-
-    def route(self, shift):
-        return [(i, (i + 2 * shift) % self.ring) for i in range(self.ring)]
-
-    def spread(self, *gates):
-        piece = self.piece.astype(F32)
-        for other in after_all(self.received, *gates):
-            piece = piece + other.astype(F32)
-        self.piece = piece.astype(BF16)
-        self.received = [
-            lax.ppermute(self.piece, "rz", self.route(s)) for s in range(1, self.deep)
-        ]
-        return self.piece
-
-    def whole(self, *gates):
-        gathered = [self.piece] + list(after_all(self.received, *gates))
-        return jnp.concatenate(
-            [
-                functools.reduce(
-                    lambda rest, s: jnp.where((self.high - s) % self.deep == i, gathered[s], rest),
-                    range(1, self.deep),
-                    gathered[0],
-                )
-                for i in range(self.deep)
-            ],
-            axis=0,
-        ).reshape(self.shape)
+        return self.order.pin(jnp.concatenate(whole, axis=0))
+
+    def meet(self):
+        self.whole = self.gather()
+        if self.axes == "line":
+            self.beside = lax.ppermute(self.whole, "low", SWAP)
+        self.across = lax.ppermute(self.whole, "core", SWAP)
+
+    def cross(self):
+        if self.axes != "line":
+            return self.whole, self.order.pin(self.across)
+        self.beside = self.order.pin(self.beside)
+        self.beside_across = lax.ppermute(self.beside, "core", SWAP)
+        return self.whole, self.beside, self.across, self.beside_across
+
+
+class PlaneSum:
+    def __init__(self, order, low, deep, send, keep, both=False):
+        self.order, self.low, self.deep, self.both = order, low, deep, both
+        send, self.keep = order.pin(send, keep)
+        self.received = lax.ppermute(send, "half", SWAP)
+
+    def to_neighbour(self):
+        total = add_low(self.keep, self.order.pin(self.received))
+        if self.both:
+            self.line = LineSum(self.order, ("line", "low"), 2 * self.deep, total)
+            return
+        parts = total.reshape(2, -1, total.shape[-1])
+        send, self.keep = self.order.pin(pick(parts, 1 - self.low, 0), pick(parts, self.low, 0))
+        self.received = lax.ppermute(send, "low", SWAP)
+
+    def along(self):
+        received = self.order.pin(self.received)
+        self.line = LineSum(self.order, "line", self.deep, add_low(self.keep, received))
+
+    def spread(self):
+        self.line.spread()
+
+    def meet(self):
+        self.line.meet()
+
+    def cross(self):
+        return self.line.cross()
 
 
 def add_low(left, right):
@@ -1367,8 +1449,8 @@
     assert clips == 1
     ring = rep // 2
     deep = ring // 2
-    core, half, place = lax.axis_index("core"), lax.axis_index("half"), lax.axis_index("rz")
-    low, high = place % 2, (place // 2) % 2
+    core, half = lax.axis_index("core"), lax.axis_index("half")
+    low, high = lax.axis_index("low"), lax.axis_index("line") % 2
     own_rows = width // 2
     pairs = own_rows // PAIR
     hidden = up_weight.shape[1]
@@ -1383,10 +1465,10 @@
         return lax.ppermute(values, "core", SWAP)
 
     def swap_low(values):
-        return lax.ppermute(values, "rz", [(i, i ^ 1) for i in range(ring)])
+        return lax.ppermute(values, "low", SWAP)
 
     def swap_high(values):
-        return lax.ppermute(values, "rz", [(i, i ^ 2) for i in range(ring)])
+        return lax.ppermute(values, "line", [(i, i ^ 1) for i in range(deep)])
 
     def cross_over(values):
         return lax.ppermute(values, ("core", "half"), cross)
@@ -1413,15 +1495,19 @@
     out_mine = lax.dynamic_slice(
         out_weight, (core * (own_rows // 2) + low * quarter, 0 * core), (quarter, width)
     )
-    tokens, qkv_x, *packed = lax.optimization_barrier((tokens, qkv_x, *packed))
+    order = Order()
+    order.pin(*packed)
+    tokens, qkv_x = order.pin(tokens, qkv_x)
+    tokens_in = cross_over(tokens)
     qkv_y = swap_low(qkv_x)
-    tokens_in = cross_over(tokens)
+    out_mine = order.pin(out_mine)
+    tokens_in, qkv_y = order.pin(tokens_in, qkv_y)
+    out_x = swap_half(after(out_mine, tokens_in))
+    packed = after_all(packed, tokens_in)
     x, first = first_norm(scal, tokens, tokens_in, gain_one, shift_one)
+    x, first = order.pin(x, first)
+    order.fence(x)
     first_in = swap_core(first)
-    out_mine, packed[0], packed[1], x = lax.optimization_barrier(
-        (out_mine, packed[0], packed[1], x)
-    )
-    out_x = swap_half(out_mine)
     feed_x = [swap_half(values) for values in packed]
     zeros = jnp.zeros((pairs, PAIR), F32)
     qkv_bias = jnp.stack(
@@ -1429,27 +1515,33 @@
          set_entries(full_vbias).reshape(pairs, PAIR)],
         axis=1,
     ).reshape(1, 3 * own_rows)
+    first_in = order.pin(first_in)
     qkv, qkv_weight, first_all = project(
         scal, (first, first_in), own_qkv, qkv_x, qkv_y, qkv_bias
     )
 
-    mixed, lse = attend(qkv, 0, pairs // 2)
-    out_x, feed_x[0], feed_x[1], cotangent, lse = lax.optimization_barrier(
-        (out_x, feed_x[0], feed_x[1], cotangent, lse)
-    )
+    qkv, out_x = order.pin(qkv, out_x)
+    order.fence(qkv)
     out_y = swap_low(out_x)
+    mixed, lse = attend(qkv, 0, pairs - 1)
+    lse, out_y, *feed_x = order.pin(lse, out_y, *feed_x)
     feed_y = [swap_low(feed_x[0]), swap_high(feed_x[1])]
-    cotangent_in = cross_over(cotangent)
-    mixed, lse = attend(qkv, pairs // 2, pairs, (mixed, lse))
+    cotangent_in = cross_over(after(cotangent, lse))
+    mixed, lse = attend(qkv, pairs - 1, pairs, (mixed, lse))
+    mixed = order.pin(mixed)
     out_part, out_set = out_other(scal, mixed, out_weight, out_x, out_y)
+    out_part, cotangent_in, *feed_y = order.pin(out_part, cotangent_in, *feed_y)
     out_in = swap_core(out_part)
-    grad_out = jnp.where(stays, cotangent, after(cotangent_in, lse))
+    grad_out = order.pin(jnp.where(stays, cotangent, cotangent_in))
     grad_out_in = swap_core(grad_out)
     middle, second = second_norm(
-        scal, mixed, out_set, x, out_in, full_obias, gain_two, shift_two
-    )
+        scal, mixed, out_set, x, order.pin(out_in), full_obias, gain_two, shift_two
+    )
+    middle, second = order.pin(middle, second)
+    order.fence(second)
     second_in = swap_core(second)
 
+    second_in = order.pin(second_in)
     (
         out_own, out_part, dx_own, dx_part, up_send, up_keep, down_send, down_keep, low_send,
         low_keep, up_bias_grad,
@@ -1457,103 +1549,79 @@
         scal, (second, second_in), (grad_out, grad_out_in), up_weight, down_weight,
         (feed_x[0], feed_y[0], feed_x[1], feed_y[1]), bias_set,
     )
-    first_in_half = [swap_half(up_send), swap_half(down_send)]
-    second_in_low = swap_low(low_send)
+    dx_part, up_send, down_send, low_send, out_part = order.pin(
+        dx_part, up_send, down_send, low_send, out_part
+    )
+    order.fence(dx_part)
     dx_in = swap_core(dx_part)
-    grad_low, sums_two = second_back(scal, dx_own, dx_in, middle, grad_out, gain_two)
+    up_in, down_in, low_in = swap_half(up_send), swap_half(down_send), swap_low(low_send)
+    out_in = swap_core(out_part)
+    grad_low, sums_two = second_back(
+        scal, dx_own, order.pin(dx_in), middle, grad_out, gain_two
+    )
+    grad_low = order.pin(grad_low)
     grad_low_in = swap_core(grad_low)
+    layer = layer_rows(scal, out_own, order.pin(out_in), middle, full_dbias)
+    grad_low_in, layer = order.pin(grad_low_in, layer)
     grad_mixed, out_send, out_keep = mixed_back(scal, (grad_low, grad_low_in), out_set, mixed)
+    grad_mixed = order.pin(grad_mixed)
 
     backs = []
 
-    def back(pair, *issued):
-        gate = after(lse, *issued) if issued else lse
+    def back(pair):
+        gate = order.pin(lse)
         backs.append(attend_back(scal, qkv, grad_mixed, mixed, gate, first_all, pair, pair + 1))
-        return backs[-1][3]
-
-    done = back(0)
-    up_in, down_in, low_in = after_all((*first_in_half, second_in_low), done)
+        backs[-1] = order.pin(*backs[-1])
+        order.fence(backs[-1][3])
+
+    back(0)
+    up_in, down_in, low_in = order.pin(up_in, down_in, low_in)
     up_sum, down_sum = add_low(up_keep, up_in), add_low(down_keep, down_in)
+    even = low == 0
+    low_mine, low_other = order.pin(
+        jnp.where(even, up_sum, down_sum), jnp.where(even, down_sum, up_sum)
+    )
+    one_in = lax.ppermute(low_other, "low", SWAP)
     range_sum = add_low(low_keep, low_in).reshape(2, own_rows, width)
-    half_send, half_keep = pick(range_sum, 1 - half, 0), pick(range_sum, half, 0)
+    half_send, half_keep = order.pin(pick(range_sum, 1 - half, 0), pick(range_sum, half, 0))
     half_in = swap_half(half_send)
-    up_sum, down_sum = lax.psum((up_sum, down_sum), "rz")
-
-    done = back(1, half_send)
-    (half_in,) = after_all((half_in,), done)
-    line = LineSum(place, ring, add_low(half_keep, half_in))
-
-    done = back(2, *line.sent)
-    issued = line.spread(done)
-    split = 3 * PAIR * (pairs - 1)
-
-    def start_half(sends, keeps, *gates):
-        send, keep = jnp.concatenate(sends, axis=0), jnp.concatenate(keeps, axis=0)
-        send = after(send, *gates) if gates else send
-        return send, keep, swap_half(send)
-
-    most_send, most_keep, most_in = start_half(
-        [b[1] for b in backs] + [out_send], [b[2] for b in backs] + [out_keep]
-    )
-
-    done = back(3, issued, most_send)
-    last_send, last_keep, last_in = start_half([backs[3][1]], [backs[3][2]])
-
-    def halves(values):
-        parts = values.reshape(deep, 2, -1, values.shape[-1])
-        return (
-            pick(parts, low, 1).reshape(-1, values.shape[-1]),
-            pick(parts, 1 - low, 1).reshape(-1, values.shape[-1]),
-        )
-
-    def meet(own, other):
-        width_in = own.shape[-1]
-        return join(
-            own.reshape(deep, -1, width_in), other.reshape(deep, -1, width_in), low
-        ).transpose(1, 0, 2, 3).reshape(-1, width_in)
-
-    first_own, first_part = first_grad(scal, [b[0] for b in backs], qkv_weight)
+
+    back(1)
+    one = LineSum(order, "line", deep, add_low(low_mine, order.pin(one_in)))
+    early = PlaneSum(
+        order, low, deep,
+        jnp.concatenate([backs[0][1], backs[1][1], out_send], axis=0),
+        jnp.concatenate([backs[0][2], backs[1][2], out_keep], axis=0),
+    )
+
+    back(2)
+    one.spread()
+    two = LineSum(order, "line", deep, add_low(half_keep, order.pin(half_in)))
+    early.to_neighbour()
+
+    back(3)
+    one.meet()
+    late = PlaneSum(
+        order, low, deep,
+        jnp.concatenate([backs[2][1], backs[3][1]], axis=0),
+        jnp.concatenate([backs[2][2], backs[3][2]], axis=0), both=True,
+    )
+    early.along()
+    layer_in = cross_over(order.pin(layer))
+    first_own, first_part = first_grad(
+        scal, [order.pin(backs[0][0])] + [b[0] for b in backs[1:]], qkv_weight
+    )
+    first_own, first_part = order.pin(first_own, first_part)
+    order.fence(first_part)
     first_part_in = swap_core(first_part)
-    range_whole = line.whole(done)
-    range_beside = swap_low(range_whole)
-    range_across = swap_core(range_whole)
-
-    most_in, last_in = after_all((most_in, last_in), first_own)
-    most_keep, most_send = halves(add_low(most_keep, most_in))
-    last_keep, last_send = halves(add_low(last_keep, last_in))
-    most_low, last_low = swap_low(most_send), swap_low(last_send)
+    late.to_neighbour()
+    early.spread()
+    two.spread()
     tokens_out, sums_one = first_back(
-        scal, first_own, after(first_part_in, most_send, last_send), x, grad_low, gain_one
-    )
-    out_in = swap_core(out_part)
-    layer = layer_rows(scal, out_own, out_in, middle, full_dbias)
-    layer_out = jnp.where(stays, layer, cross_over(layer))
-    tokens_grad = jnp.where(stays, tokens_out, cross_over(tokens_out))
-
-    most_line = LineSum(place, ring, add_low(most_keep, most_low))
-    last_line = LineSum(place, ring, add_low(last_keep, last_low))
-    most_line.spread()
-    last_line.spread()
-    most_whole, last_whole = most_line.whole(), last_line.whole()
-    most_sum = meet(most_whole, swap_low(most_whole))
-    last_sum = meet(last_whole, swap_low(last_whole))
-
-    up_weight_grad, down_weight_grad = finish_feed(
-        scal,
-        (
-            up_sum, down_sum, swap_core(up_sum), swap_core(down_sum),
-            range_whole, range_beside, range_across, swap_core(range_beside),
-        ),
-    )
-    most_across, last_across = swap_core(most_sum), swap_core(last_sum)
-    query_weight_grad, key_weight_grad, value_weight_grad = finish_qkv(
-        scal, (most_sum, last_sum), (most_across, last_across),
-        ((0, pairs - 1), (pairs - 1, pairs)),
-    )
-    out_weight_grad = join(most_sum[split:], most_across[split:], core)
-    out_weight_grad = out_weight_grad.reshape(2, 2, own_rows // 2, own_rows)
-    out_weight_grad = jnp.concatenate([out_weight_grad[:, 0], out_weight_grad[:, 1]], axis=2)
-    out_weight_grad = out_weight_grad.reshape(own_rows, width).astype(F32)
+        scal, first_own, order.pin(first_part_in), x, grad_low, gain_one
+    )
+    tokens_out, sums_one = order.pin(tokens_out, sums_one)
+    order.fence(sums_one)
 
     def place_entries(values, inner=1):
         values = values.reshape(inner, 2, 1, -1).transpose(1, 2, 0, 3)
@@ -1565,16 +1633,39 @@
         place_entries(parts[:, 0]), place_entries(parts[:, 2]), sums_two[3], sums_one[0],
         sums_one[1], sums_two[0], sums_two[1], sums_two[2], place_entries(up_bias_grad, 2),
     ]
-    entries = jnp.concatenate([e.reshape(2, -1) for e in entries], axis=1)
-    entries = entries + swap_core(entries)
-    entries = pick(entries, half, 0) + swap_half(pick(entries, 1 - half, 0))
-    step = 1
-    while step < ring:
-        if ring & (ring - 1):
-            entries = lax.psum(entries, "rz")
-            break
-        entries = entries + lax.ppermute(entries, "rz", [(i, i ^ step) for i in range(ring)])
-        step *= 2
+    entries = order.pin(jnp.concatenate([e.reshape(2, -1) for e in entries], axis=1))
+    entries_in = swap_core(entries)
+    late.spread()
+    entries = entries + order.pin(entries_in)
+    keep, send = order.pin(pick(entries, half, 0), pick(entries, 1 - half, 0))
+    entries_in = swap_half(send)
+    tokens_in = cross_over(after(tokens_out, send))
+    early.meet()
+    one_parts = one.cross()
+    steps = [("line", 1 << bit, deep) for bit in range((deep - 1).bit_length())] + [("low", 1, 2)]
+
+    def exchange(axis, step, size):
+        return lax.ppermute(entries, axis, [(i, i ^ step) for i in range(size)])
+
+    entries = order.pin(keep + order.pin(entries_in))
+    entries_in = exchange(*steps[0])
+    two.meet()
+    for step in steps[1:]:
+        entries = order.pin(entries + order.pin(entries_in))
+        entries_in = exchange(*step)
+    late.meet()
+    early_parts = early.cross()
+    two_parts = two.cross()
+    up_weight_grad, down_weight_grad = finish_feed(
+        scal, order.pin(*one_parts, *two_parts)
+    )
+    entries = entries + entries_in
+    late_parts = late.cross()
+    query_weight_grad, key_weight_grad, value_weight_grad, out_weight_grad = finish_attention(
+        scal, (*early_parts, *late_parts), ((0, 2), (2, 4))
+    )
+    layer_out = jnp.where(stays, layer, layer_in)
+    tokens_grad = jnp.where(stays, tokens_out, tokens_in)
     small = [entries[i * own_rows : (i + 1) * own_rows] for i in range(8)]
     return (
         layer_out.reshape(1, local, width), tokens_grad.reshape(1, local, width),
@@ -1586,15 +1677,17 @@
 
 def solution(mesh):
     rep, grp = mesh.shape["rep"], mesh.shape["grp"]
-    split = Mesh(
-        mesh.devices.reshape(rep // 2, 2, 2, grp // 2), ("rz", "core", "half", "gq")
-    )
-    clip = P(("rz", "core"), ("half", "gq"), None)
-    matrix = P(("half", "gq"), None)
-    vector = P(("half", "gq"))
+    paired = grp == 2 and rep >= 8 and rep & (rep - 1) == 0
+    if paired:
+        sizes, names = (rep // 4, 2, 2, 2), ("line", "low", "core", "half")
+        reps, groups, body = ("line", "low", "core"), "half", pair_body
+    else:
+        sizes, names = (rep // 2, 2, 2, grp // 2), ("rz", "core", "half", "gq")
+        reps, groups, body = ("rz", "core"), ("half", "gq"), wide_body
+    clip, matrix, vector = P(reps, groups, None), P(groups, None), P(groups)
     return jax.shard_map(
-        functools.partial(pair_body if grp == 2 and rep % 8 == 0 else wide_body, rep, grp),
-        mesh=split,
+        functools.partial(body, rep, grp),
+        mesh=Mesh(mesh.devices.reshape(sizes), names),
         in_specs=(
             clip, matrix, matrix, matrix, vector, vector, matrix, vector, vector, vector, vector,
             vector, matrix, vector, matrix, vector, clip,

time: 643 us -> 575 us (0.89)
  waiting for transfers between devices: 162 us -> 98.7 us
  between operations: 15.2 us -> 1.97 us
  starting transfers between devices: 95.8 us -> 104 us
  other arithmetic: 30.8 us -> 37.4 us
    ppermute x31 -> x40, waiting for transfers between devices: 122 us -> 56.3 us  [the longest x2 14.3 us: __init__(): self.received = lax.ppermute(send, 'half', SWAP)]
    ppermute x31 -> x40, starting transfers between devices: 55.2 us -> 69.2 us  [the longest x18 39.6 us: shift(): lax.ppermute(values, 'line', [(i, (i + s) % self.size) for i in range(sel...]
    all_to_all x0 -> x2, starting transfers between devices: none -> 7.79 us  [exchange(): lax.all_to_all(values, self.axes, split_axis=0, concat_axis=0, tiled=True)]
    select_n x4 -> x5, other arithmetic: 2.97 us -> 10.2 us  [the longest x1 4.37 us: pair_body(): jnp.where(even, down_sum, up_sum)]
    convert_element_type x8 -> x6, other arithmetic: 14.6 us -> 9.82 us  [add_low(): return (left.astype(F32) + right.astype(F32)).astype(BF16)]
    unnamed x110 -> x108, local copies, waits for them, and re-layouts: 13.1 us -> 9.53 us
    ppermute x11 -> x9, waiting for transfers between devices: 35 us -> 32.8 us  [swap_half(): return lax.ppermute(values, 'half', SWAP)]
  transfers between devices with their start and end apart: 62 -> 64, of which waited for: 22 -> 19; matrix products, arithmetic and copies ran while one was open for 8% -> 9% of each run, Pallas kernels for 35% -> 36%
where the time goes in v5:
time: 575 us; the launch traced here: 566 us
  Pallas kernels  296 us (51%)
  starting transfers between devices  104 us (18%)
  waiting for transfers between devices  98.7 us (17%)
  other arithmetic  37.4 us (7%)
  local copies, waits for them, and re-layouts  28.1 us (5%)
    pallas_call x14, Pallas kernels, run(): pl.pallas_call(kernel, grid_spec=pltpu.PrefetchScalarGridSpec(num_scalar_...  97.5 us
    pallas_call x4, Pallas kernels, attend_back(): pl.pallas_call(functools.partial(attend_back_kernel, tile, rows, padded),...  88.4 us
    pallas_call x1, Pallas kernels, feed(): pl.pallas_call(feed_kernel, grid_spec=pltpu.PrefetchScalarGridSpec(num_sc...  60.5 us
    pallas_call x2, Pallas kernels, attend(): pl.pallas_call(kernel if kept is None else lambda ref, a, b, *rest: kerne...  49.4 us
    ppermute x18, starting transfers between devices, shift(): lax.ppermute(values, 'line', [(i, (i + s) % self.size) for i in range(sel...  39.6 us
    ppermute x9, waiting for transfers between devices, swap_half(): return lax.ppermute(values, 'half', SWAP)  32.8 us
    ppermute x2, waiting for transfers between devices, __init__(): self.received = lax.ppermute(send, 'half', SWAP)  14.3 us
    ppermute x4, starting transfers between devices, cross_over(): return lax.ppermute(values, ('core', 'half'), cross)  13.4 us
  transfers between devices with their start and end apart: 64, of which 19 were waited for; matrix products, arithmetic and copies ran while one was open for 9% of the time, Pallas kernels for 36%

profile of v5, /device:TPU:1, one launch (start us, length us, event | category | flops | bytes accessed | tf_op | source)
XLA Modules:
  0.0 566.5 jit_solution(14849935462218063552)
XLA Ops:
  1.3 4.5 pack_qkv.1
  14.3 11.2 %collective-permute-done.piece_ref = bf16[256,1536]{1,0:T(8,128)(2,1)} collective-permute-done((bf16[256,1536]{1,0:T(8,128)(2,1)}, bf16[256,1536]{1,0:T(8,128)(2,1)}, u32[]{:S(2)}, u32[]{:S(2)}) %collective-permute-start) | collective-permute-done | bytes 786464 | tf_op jit(solution)/shard_map/ppermute | solution.py:1462
  25.4 4.5 collective-permute-start.1
  32.4 15.7 %collective-permute-done.3 = f32[6144]{0:T(1024)S(1)} collective-permute-done((f32[6144]{0:T(1024)S(1)}, f32[6144]{0:T(1024)S(1)}, u32[]{:S(2)}, u32[]{:S(2)}) %collective-permute-start.3) | collective-permute-done | bytes 24608 | tf_op jit(solution)/shard_map/ppermute | solution.py:1462
  51.0 4.2 first_norm.1
  59.9 11.1 %project.1 = (bf16[1568,1536]{1,0:T(8,128)(2,1)}, bf16[1024,1536]{1,0:T(8,128)(2,1)}, bf16[1568,1024]{1,0:T(8,128)(2,1)}) custom-call(s32[5]{0:T(128)} %stack.62.s_ref, bf16[784,1024]{1,0:T(8,128)(2,1)} %get-tuple-element.233.mine_ref, bf16[784,1024]{1,0:T(8,128)(2,1)} %collective-permute-done.4.theirs_ref, bf16[512,1536]{1,0:T(8,128)(2,1)} %get-tuple-element.236.own_ref, ...), custom_call_target="tpu_custom_call" | custom-call | flops 4932501504 | bytes 12726272 | tf_op jit(solution)/shard_map/project/pallas_call | solution.py:366
  73.0 36.1 %attend.2 = (bf16[1568,512]{1,0:T(8,128)(2,1)}, f32[4,2,2048]{2,1,0:T(2,128)}) custom-call(bf16[1568,1536]{1,0:T(8,128)(2,1)} %get-tuple-element.239.qkv_ref.ref), custom_call_target="tpu_custom_call" | custom-call | flops 60423143424 | bytes 4816896 | tf_op jit(solution)/shard_map/attend/pallas_call | solution.py:68
  117.7 13.4 %attend.3 = (bf16[1568,512]{1,0:T(8,128)(2,1)}, f32[4,2,2048]{2,1,0:T(2,128)}) custom-call(bf16[1568,1536]{1,0:T(8,128)(2,1)} %get-tuple-element.239.qkv_ref.ref, bf16[1568,512]{1,0:T(8,128)(2,1)} %get-tuple-element.240.a, f32[4,2,2048]{2,1,0:T(2,128)} %copy.58.b), custom_call_target="tpu_custom_call", output_to_operand_aliasing={{0}: (1, {}), {1}: (2, {})} | custom-call | flops 20141047808 | bytes 1605632 | tf_op jit(solution)/shard_map/attend/pallas_call | solution.py:68
  131.1 4.3 out_other.1
  135.4 4.9 collective-permute-done.10.x_beside
  146.2 6.1 %second_norm.1 = (f32[784,1024]{1,0:T(8,128)}, bf16[784,1024]{1,0:T(8,128)(2,1)}) custom-call(s32[5]{0:T(128)} %stack.62.s_ref, bf16[1568,512]{1,0:T(8,128)(2,1)} %get-tuple-element.250.mixed_ref.out_ref, bf16[512,1024]{1,0:T(8,128)(2,1)} %get-tuple-element.251.w_ref, bf16[784,1024]{1,0:T(8,128)(2,1)} %get-tuple-element.234.x_ref, ...), custom_call_target="tpu_custom_call" | custom-call | flops 822083584 | bytes 11755520 | tf_op jit(solution)/shard_map/second_norm/pallas_call | solution.py:366
  158.2 60.5 %feed.1 = (bf16[784,1024]{1,0:T(8,128)(2,1)}, bf16[784,1024]{1,0:T(8,128)(2,1)}, bf16[784,1024]{1,0:T(8,128)(2,1)}, bf16[784,1024]{1,0:T(8,128)(2,1)}, bf16[512,...) custom-call(s32[5]{0:T(128)} %stack.62.s_ref, ...), custom_call_target="tpu_custom_call" | custom-call | flops 39460012032 | bytes 25690112 | tf_op jit(solution)/shard_map/feed/pallas_call | solution.py:324
  219.2 4.1 collective-permute-done.15.r_ref
  223.3 9.0 %second_back.1 = (bf16[784,1024]{1,0:T(8,128)(2,1)}, f32[8,1024]{1,0:T(8,128)}) custom-call(s32[5]{0:T(128)} %stack.62.s_ref, bf16[784,1024]{1,0:T(8,128)(2,1)} %get-tuple-element.264.g_ref, bf16[784,1024]{1,0:T(8,128)(2,1)} %collective-permute-done.15.r_ref, f32[784,1024]{1,0:T(8,128)} %get-tuple-element.272.mid_ref, bf16[784,1024]{1,0:T(8,128)(2,1)} %copy-done.1, ...), custom_call_target="tpu_custom_call" | custom-call | bytes 16064512 | tf_op jit(solution)/shard_map/second_back/pallas_call | solution.py:366
  239.9 7.0 %layer_rows.1 = bf16[784,1024]{1,0:T(8,128)(2,1)} custom-call(s32[5]{0:T(128)} %stack.62.s_ref, bf16[784,1024]{1,0:T(8,128)(2,1)} %get-tuple-element.275.o_ref, bf16[784,1024]{1,0:T(8,128)(2,1)} %copy-done.9, f32[784,1024]{1,0:T(8,128)} %get-tuple-element.272.mid_ref, f32[1,1024]{1,0:T(1,128)} %bitcast.131), custom_call_target="tpu_custom_call" | custom-call | bytes 12853248 | tf_op jit(solution)/shard_map/layer_rows/pallas_call | solution.py:366
  246.9 9.4 %mixed_back.1 = (bf16[1568,512]{1,0:T(8,128)(2,1)}, bf16[512,512]{1,0:T(8,128)(2,1)}, bf16[512,512]{1,0:T(8,128)(2,1)}) custom-call(s32[5]{0:T(128)} %stack.62.s_ref, bf16[784,1024]{1,0:T(8,128)(2,1)} %get-tuple-element.274.mine_ref.wide_ref, bf16[784,1024]{1,0:T(8,128)(2,1)} %collective-permute-done.16.theirs_ref, ...), custom_call_target="tpu_custom_call" | custom-call | flops 3288334336 | bytes 11730944 | tf_op jit(solution)/shard_map/mixed_back/pallas_call | solution.py:366
  256.3 22.1 %attend_back.4 = (bf16[1568,384]{1,0:T(8,128)(2,1)}, bf16[384,512]{1,0:T(8,128)(2,1)}, bf16[384,512]{1,0:T(8,128)(2,1)}, f32[8,384]{1,0:T(8,128)}) custom-call(s32[5]{0:T(128)} %stack.62.s_ref, bf16[1568,1536]{1,0:T(8,128)(2,1)} %get-tuple-element.239.qkv_ref.ref, bf16[1568,512]{1,0:T(8,128)(2,1)} %get-tuple-element.281.grad_ref, ...), custom_call_target="tpu_custom_call" | custom-call | flops 50352619520 | bytes 3211264 | tf_op jit(solution)/shard_map/attend_back/pallas_call | solution.py:159
  280.2 4.4 broadcast_select_fusion.1
  290.3 22.1 %attend_back.5 = (bf16[1568,384]{1,0:T(8,128)(2,1)}, bf16[384,512]{1,0:T(8,128)(2,1)}, bf16[384,512]{1,0:T(8,128)(2,1)}, f32[8,384]{1,0:T(8,128)}) custom-call(s32[5]{0:T(128)} %stack.62.s_ref, bf16[1568,1536]{1,0:T(8,128)(2,1)} %get-tuple-element.239.qkv_ref.ref, bf16[1568,512]{1,0:T(8,128)(2,1)} %get-tuple-element.281.grad_ref, ...), custom_call_target="tpu_custom_call" | custom-call | flops 50352619520 | bytes 3211264 | tf_op jit(solution)/shard_map/attend_back/pallas_call | solution.py:159
  324.7 21.9 %attend_back.6 = (bf16[1568,384]{1,0:T(8,128)(2,1)}, bf16[384,512]{1,0:T(8,128)(2,1)}, bf16[384,512]{1,0:T(8,128)(2,1)}, f32[8,384]{1,0:T(8,128)}) custom-call(s32[5]{0:T(128)} %stack.62.s_ref, bf16[1568,1536]{1,0:T(8,128)(2,1)} %get-tuple-element.239.qkv_ref.ref, bf16[1568,512]{1,0:T(8,128)(2,1)} %get-tuple-element.281.grad_ref, ...), custom_call_target="tpu_custom_call" | custom-call | flops 50352619520 | bytes 3211264 | tf_op jit(solution)/shard_map/attend_back/pallas_call | solution.py:159
  357.2 22.3 %attend_back.7 = (bf16[1568,384]{1,0:T(8,128)(2,1)}, bf16[384,512]{1,0:T(8,128)(2,1)}, bf16[384,512]{1,0:T(8,128)(2,1)}, f32[8,384]{1,0:T(8,128)}) custom-call(s32[5]{0:T(128)} %stack.62.s_ref, bf16[1568,1536]{1,0:T(8,128)(2,1)} %get-tuple-element.239.qkv_ref.ref, bf16[1568,512]{1,0:T(8,128)(2,1)} %get-tuple-element.281.grad_ref, ...), custom_call_target="tpu_custom_call" | custom-call | flops 50352619520 | bytes 3211264 | tf_op jit(solution)/shard_map/attend_back/pallas_call | solution.py:159
  385.1 10.1 %first_grad.1 = (bf16[784,1024]{1,0:T(8,128)(2,1)}, bf16[784,1024]{1,0:T(8,128)(2,1)}) custom-call(s32[5]{0:T(128)} %stack.62.s_ref, bf16[1568,384]{1,0:T(8,128)(2,1)} %get-tuple-element.363.refs_0_, bf16[1568,384]{1,0:T(8,128)(2,1)} %get-tuple-element.364.refs_1_, bf16[1568,384]{1,0:T(8,128)(2,1)} %get-tuple-element.365.refs_2_, ...), custom_call_target="tpu_custom_call" | custom-call | flops 4932501504 | bytes 15925248 | tf_op jit(solution)/shard_map/first_grad/pallas_call | solution.py:366
  405.0 14.3 %collective-permute-done.39 = bf16[768,512]{1,0:T(8,128)(2,1)S(1)} collective-permute-done((bf16[768,512]{1,0:T(8,128)(2,1)}, bf16[768,512]{1,0:T(8,128)(2,1)S(1)}, u32[]{:S(2)}, u32[]{:S(2)}) %collective-permute-start.39) | collective-permute-done | bytes 786464 | tf_op jit(solution)/shard_map/ppermute | solution.py:1408
  427.6 9.4 %collective-permute-done.38 = bf16[160,512]{1,0:T(8,128)(2,1)} collective-permute-done((bf16[160,512]{1,0:T(8,128)(2,1)}, bf16[160,512]{1,0:T(8,128)(2,1)}, u32[]{:S(2)}, u32[]{:S(2)}) %collective-permute-start.38) | collective-permute-done | bytes 163872 | tf_op jit(solution)/shard_map/ppermute | solution.py:1355
  440.3 18.6 %collective-permute-start.42 = (bf16[160,512]{1,0:T(8,128)(2,1)}, bf16[160,512]{1,0:T(8,128)(2,1)}, u32[]{:S(2)}, u32[]{:S(2)}) collective-permute-start(bf16[160,512]{1,0:T(8,128)(2,1)} %add_convert_fusion.10), channel_id=1, source_target_pairs={{0,8},{8,16},{16,24},{24,0},{1,9},{9,17},{17,25},{25,1},{2,10},{10... | collective-permute-start | bytes 491528 | tf_op jit(solution)/shard_map/ppermute | solution.py:1355
  462.8 8.4 %first_back.1 = (bf16[784,1024]{1,0:T(8,128)(2,1)}, f32[8,1024]{1,0:T(8,128)}) custom-call(s32[5]{0:T(128)} %stack.62.s_ref, bf16[784,1024]{1,0:T(8,128)(2,1)} %get-tuple-element.370.g_ref, bf16[784,1024]{1,0:T(8,128)(2,1)} %collective-permute-done.32.r_ref, bf16[784,1024]{1,0:T(8,128)(2,1)} %get-tuple-element.234.x_ref, ...), custom_call_target="tpu_custom_call" | custom-call | bytes 12853248 | tf_op jit(solution)/shard_map/first_back/pallas_call | solution.py:366
  487.2 4.1 all-to-all-start.1
  495.2 7.0 %collective-permute-start.48 = (f32[6144]{0:T(1024)S(1)}, f32[6144]{0:T(1024)S(1)}, u32[]{:S(2)}, u32[]{:S(2)}) collective-permute-start(f32[6144]{0:T(1024)S(1)} %add.285), channel_id=1, source_target_pairs={{0,8},{8,0},{16,24},{24,16},{1,9},{9,1},{17,25},{25,17},{2,10},{10... | collective-permute-start | bytes 73736 | tf_op jit(solution)/shard_map/ppermute | solution.py:1648
  509.9 8.7 %collective-permute-done.52 = f32[6144]{0:T(1024)S(1)} collective-permute-done((f32[6144]{0:T(1024)S(1)}, f32[6144]{0:T(1024)S(1)}, u32[]{:S(2)}, u32[]{:S(2)}) %collective-permute-start.52) | collective-permute-done | bytes 24608 | tf_op jit(solution)/shard_map/ppermute | solution.py:1648
  519.7 12.9 %collective-permute-done.58.refs_5_ = bf16[512,1024]{1,0:T(8,128)(2,1)} collective-permute-done((bf16[512,1024]{1,0:T(8,128)(2,1)}, bf16[512,1024]{1,0:T(8,128)(2,1)}, u32[]{:S(2)}, u32[]{:S(2)}) %collective-permute-start.58) | collective-permute-done | bytes 1048608 | tf_op jit(solution)/shard_map/ppermute | solution.py:1393
  548.7 10.1 %finish_feed.1 = (f32[512,4096]{1,0:T(8,128)}, f32[2,2,512,1024]{3,2,1,0:T(8,128)}) custom-call(s32[5]{0:T(128)} %stack.62.s_ref, bf16[512,1024]{1,0:T(8,128)(2,1)} %copy-done.4, bf16[512,1024]{1,0:T(8,128)(2,1)} %collective-permute-done.47.refs_1_, bf16[512,1024]{1,0:T(8,128)(2,1)} %collective-permute-done.56.refs_2_, ...), custom_call_target="tpu_custom_call" | custom-call | bytes 16777216 | tf_op jit(solution)/shard_map/finish_feed/pallas_call | solution.py:366
  558.9 7.2 %finish_attention.1 = (f32[512,1024]{1,0:T(8,128)}, f32[512,1024]{1,0:T(8,128)}, f32[512,1024]{1,0:T(8,128)}, f32[512,1024]{1,0:T(8,128)}) custom-call(s32[5]{0:T(128)} %stack.62.s_ref, bf16[640,512]{1,0:T(8,128)(2,1)} %pad_maximum_fusion.6.refs_0_, bf16[640,512]{1,0:T(8,128)(2,1)} %collective-permute-done.45.refs_1_, ...), custom_call_target="tpu_custom_call" | custom-call | bytes 8388608 | tf_op jit(solution)/shard_map/finish_attention/pallas_call | solution.py:366
  (301 shorter events, 155.2 us)
Async XLA Ops:
  25.4 24.7 %collective-permute-start.1 = (bf16[784,1024]{1,0:T(8,128)(2,1)S(1)}, bf16[784,1024]{1,0:T(8,128)(2,1)}, u32[]{:S(2)}, u32[]{:S(2)}) collective-permute-start(bf16[784,1024]{1,0:T(8,128)(2,1)S(1)} %bitcast.119), channel_id=1, source_target_pairs={{1,2},{2,1},{5,6},{6,5},{9,10},{10,9},{13,14},{14,13},{17,18},{18,... | collective-permute-start | bytes 4816904 | tf_op jit(solution)/shard_map/ppermute | solution.py:1474
  57.5 51.5 %collective-permute-start.7 = (bf16[512,1024]{1,0:T(8,128)(2,1)}, bf16[512,1024]{1,0:T(8,128)(2,1)}, u32[]{:S(2)}, u32[]{:S(2)}) collective-permute-start(bf16[512,1024]{1,0:T(8,128)(2,1)} %pack_feed.2), channel_id=1, source_target_pairs={{0,1},{1,0},{2,3},{3,2},{4,5},{5,4},{6,7},{7,6},{8,9},{9,8},{10,11... | collective-permute-start | bytes 3145736 | tf_op jit(solution)/shard_map/ppermute | solution.py:1462
  58.7 51.5 %collective-permute-start.8 = (bf16[512,1024]{1,0:T(8,128)(2,1)}, bf16[512,1024]{1,0:T(8,128)(2,1)}, u32[]{:S(2)}, u32[]{:S(2)}) collective-permute-start(bf16[512,1024]{1,0:T(8,128)(2,1)} %pack_feed.3), channel_id=1, source_target_pairs={{0,1},{1,0},{2,3},{3,2},{4,5},{5,4},{6,7},{7,6},{8,9},{9,8},{10,11... | collective-permute-start | bytes 3145736 | tf_op jit(solution)/shard_map/ppermute | solution.py:1462
  71.7 38.5 %collective-permute-start.6 = (bf16[128,1024]{1,0:T(8,128)(2,1)}, bf16[128,1024]{1,0:T(8,128)(2,1)S(1)}, u32[]{:S(2)}, u32[]{:S(2)}) collective-permute-start(bf16[128,1024]{1,0:T(8,128)(2,1)} %copy-done.24), channel_id=1, source_target_pairs={{0,4},{4,0},{1,5},{5,1},{2,6},{6,2},{3,7},{7,3},{8,12},{12,8},{9,1... | collective-permute-start | bytes 786440 | tf_op jit(solution)/shard_map/ppermute | solution.py:1468
  111.7 30.0 %collective-permute-start.9 = (bf16[784,1024]{1,0:T(8,128)(2,1)S(1)}, bf16[784,1024]{1,0:T(8,128)(2,1)}, u32[]{:S(2)}, u32[]{:S(2)}) collective-permute-start(bf16[784,1024]{1,0:T(8,128)(2,1)S(1)} %bitcast.117), channel_id=1, source_target_pairs={{1,2},{2,1},{5,6},{6,5},{9,10},{10,9},{13,14},{14,13},{17,18},{18,... | collective-permute-start | bytes 4816904 | tf_op jit(solution)/shard_map/ppermute | solution.py:1474
  114.8 25.5 %collective-permute-start.10 = (bf16[512,1024]{1,0:T(8,128)(2,1)}, bf16[512,1024]{1,0:T(8,128)(2,1)}, u32[]{:S(2)}, u32[]{:S(2)}) collective-permute-start(bf16[512,1024]{1,0:T(8,128)(2,1)} %collective-permute-done.7.x_piece), channel_id=1, source_target_pairs={{0,4},{4,0},{1,5},{5,1},{2,6},{6,2},{3,7},{7,3},{8,12},{12,8},{9,1... | collective-permute-start | bytes 3145736 | tf_op jit(solution)/shard_map/ppermute | solution.py:1468
  116.4 25.3 %collective-permute-start.11 = (bf16[512,1024]{1,0:T(8,128)(2,1)}, bf16[512,1024]{1,0:T(8,128)(2,1)}, u32[]{:S(2)}, u32[]{:S(2)}) collective-permute-start(bf16[512,1024]{1,0:T(8,128)(2,1)} %collective-permute-done.8.z_piece), channel_id=1, source_target_pairs={{0,8},{8,0},{16,24},{24,16},{1,9},{9,1},{17,25},{25,17},{2,10},{10... | collective-permute-start | bytes 3145736 | tf_op jit(solution)/shard_map/ppermute | solution.py:1471
  233.0 47.2 %collective-permute-start.20 = (bf16[1024,1024]{1,0:T(8,128)(2,1)}, bf16[1024,1024]{1,0:T(8,128)(2,1)}, u32[]{:S(2)}, u32[]{:S(2)}) collective-permute-start(bf16[1024,1024]{1,0:T(8,128)(2,1)} %get-tuple-element.293), channel_id=1, source_target_pairs={{0,4},{4,0},{1,5},{5,1},{2,6},{6,2},{3,7},{7,3},{8,12},{12,8},{9,1... | collective-permute-start | bytes 6291464 | tf_op jit(solution)/shard_map/ppermute | solution.py:1468
  233.3 45.1 %collective-permute-start.18 = (bf16[512,1024]{1,0:T(8,128)(2,1)}, bf16[512,1024]{1,0:T(8,128)(2,1)}, u32[]{:S(2)}, u32[]{:S(2)}) collective-permute-start(bf16[512,1024]{1,0:T(8,128)(2,1)} %get-tuple-element.291), channel_id=1, source_target_pairs={{0,1},{1,0},{2,3},{3,2},{4,5},{5,4},{6,7},{7,6},{8,9},{9,8},{10,11... | collective-permute-start | bytes 3145736 | tf_op jit(solution)/shard_map/ppermute | solution.py:1462
  233.3 46.8 %collective-permute-start.19 = (bf16[512,1024]{1,0:T(8,128)(2,1)}, bf16[512,1024]{1,0:T(8,128)(2,1)}, u32[]{:S(2)}, u32[]{:S(2)}) collective-permute-start(bf16[512,1024]{1,0:T(8,128)(2,1)} %get-tuple-element.292), channel_id=1, source_target_pairs={{0,1},{1,0},{2,3},{3,2},{4,5},{5,4},{6,7},{7,6},{8,9},{9,8},{10,11... | collective-permute-start | bytes 3145736 | tf_op jit(solution)/shard_map/ppermute | solution.py:1462
  287.1 28.5 %collective-permute-start.21 = (bf16[512,1024]{1,0:T(8,128)(2,1)}, bf16[512,1024]{1,0:T(8,128)(2,1)}, u32[]{:S(2)}, u32[]{:S(2)}) collective-permute-start(bf16[512,1024]{1,0:T(8,128)(2,1)} %get-tuple-element.301), channel_id=1, source_target_pairs={{0,4},{4,0},{1,5},{5,1},{2,6},{6,2},{3,7},{7,3},{8,12},{12,8},{9,1... | collective-permute-start | bytes 3145736 | tf_op jit(solution)/shard_map/ppermute | solution.py:1584
  289.9 61.4 %collective-permute-start.23 = (bf16[512,1024]{1,0:T(8,128)(2,1)}, bf16[512,1024]{1,0:T(8,128)(2,1)}, u32[]{:S(2)}, u32[]{:S(2)}) collective-permute-start(bf16[512,1024]{1,0:T(8,128)(2,1)} %get-tuple-element.302), channel_id=1, source_target_pairs={{0,1},{1,0},{2,3},{3,2},{4,5},{5,4},{6,7},{7,6},{8,9},{9,8},{10,11... | collective-permute-start | bytes 3145736 | tf_op jit(solution)/shard_map/ppermute | solution.py:1462
  318.6 28.0 %collective-permute-start.24 = (bf16[128,1024]{1,0:T(8,128)(2,1)}, bf16[128,1024]{1,0:T(8,128)(2,1)}, u32[]{:S(2)}, u32[]{:S(2)}) collective-permute-start(bf16[128,1024]{1,0:T(8,128)(2,1)} %get-tuple-element.317), channel_id=1, source_target_pairs={{0,8},{8,16},{16,24},{24,0},{1,9},{9,17},{17,25},{25,1},{2,10},{10... | collective-permute-start | bytes 786440 | tf_op jit(solution)/shard_map/ppermute | solution.py:1355
  319.9 26.7 %collective-permute-start.25 = (bf16[128,1024]{1,0:T(8,128)(2,1)}, bf16[128,1024]{1,0:T(8,128)(2,1)}, u32[]{:S(2)}, u32[]{:S(2)}) collective-permute-start(bf16[128,1024]{1,0:T(8,128)(2,1)} %get-tuple-element.318), channel_id=1, source_target_pairs={{0,16},{8,24},{16,0},{24,8},{1,17},{9,25},{17,1},{25,9},{2,18},{10... | collective-permute-start | bytes 786440 | tf_op jit(solution)/shard_map/ppermute | solution.py:1355
  322.3 24.3 %collective-permute-start.26 = (bf16[128,1024]{1,0:T(8,128)(2,1)S(1)}, bf16[128,1024]{1,0:T(8,128)(2,1)}, u32[]{:S(2)}, u32[]{:S(2)}) collective-permute-start(bf16[128,1024]{1,0:T(8,128)(2,1)S(1)} %get-tuple-element.319), channel_id=1, source_target_pairs={{0,24},{8,0},{16,8},{24,16},{1,25},{9,1},{17,9},{25,17},{2,26},{10... | collective-permute-start | bytes 786440 | tf_op jit(solution)/shard_map/ppermute | solution.py:1355
  323.5 30.5 %collective-permute-start.22 = (bf16[1280,512]{1,0:T(8,128)(2,1)}, bf16[1280,512]{1,0:T(8,128)(2,1)}, u32[]{:S(2)}, u32[]{:S(2)}) collective-permute-start(bf16[1280,512]{1,0:T(8,128)(2,1)} %pad_maximum_fusion), channel_id=1, source_target_pairs={{0,1},{1,0},{2,3},{3,2},{4,5},{5,4},{6,7},{7,6},{8,9},{9,8},{10,11... | collective-permute-start | bytes 3932168 | tf_op jit(solution)/shard_map/ppermute | solution.py:1408
  348.0 31.4 %collective-permute-start.28 = (bf16[128,1024]{1,0:T(8,128)(2,1)S(1)}, bf16[128,1024]{1,0:T(8,128)(2,1)S(1)}, u32[]{:S(2)}, u32[]{:S(2)}) collective-permute-start(bf16[128,1024]{1,0:T(8,128)(2,1)S(1)} %add_convert_fusion.9), channel_id=1, source_target_pairs={{0,8},{8,16},{16,24},{24,0},{1,9},{9,17},{17,25},{25,1},{2,10},{10... | collective-permute-start | bytes 786440 | tf_op jit(solution)/shard_map/ppermute | solution.py:1355
  348.3 31.1 %collective-permute-start.29 = (bf16[128,1024]{1,0:T(8,128)(2,1)S(1)}, bf16[128,1024]{1,0:T(8,128)(2,1)}, u32[]{:S(2)}, u32[]{:S(2)}) collective-permute-start(bf16[128,1024]{1,0:T(8,128)(2,1)S(1)} %add_convert_fusion.9), channel_id=1, source_target_pairs={{0,16},{8,24},{16,0},{24,8},{1,17},{9,25},{17,1},{25,9},{2,18},{10... | collective-permute-start | bytes 786440 | tf_op jit(solution)/shard_map/ppermute | solution.py:1355
  348.3 31.1 %collective-permute-start.30 = (bf16[128,1024]{1,0:T(8,128)(2,1)S(1)}, bf16[128,1024]{1,0:T(8,128)(2,1)}, u32[]{:S(2)}, u32[]{:S(2)}) collective-permute-start(bf16[128,1024]{1,0:T(8,128)(2,1)S(1)} %add_convert_fusion.9), channel_id=1, source_target_pairs={{0,24},{8,0},{16,8},{24,16},{1,25},{9,1},{17,9},{25,17},{2,26},{10... | collective-permute-start | bytes 786440 | tf_op jit(solution)/shard_map/ppermute | solution.py:1355
  356.9 26.1 %collective-permute-start.27 = (bf16[640,512]{1,0:T(8,128)(2,1)}, bf16[640,512]{1,0:T(8,128)(2,1)}, u32[]{:S(2)}, u32[]{:S(2)}) collective-permute-start(bf16[640,512]{1,0:T(8,128)(2,1)} %get-tuple-element.339), channel_id=1, source_target_pairs={{0,4},{4,0},{1,5},{5,1},{2,6},{6,2},{3,7},{7,3},{8,12},{12,8},{9,1... | collective-permute-start | bytes 1966088 | tf_op jit(solution)/shard_map/ppermute | solution.py:1417
  395.2 67.7 %collective-permute-start.32 = (bf16[784,1024]{1,0:T(8,128)(2,1)}, bf16[784,1024]{1,0:T(8,128)(2,1)}, u32[]{:S(2)}, u32[]{:S(2)}) collective-permute-start(bf16[784,1024]{1,0:T(8,128)(2,1)} %get-tuple-element.371), channel_id=1, source_target_pairs={{0,2},{2,0},{1,3},{3,1},{4,6},{6,4},{5,7},{7,5},{8,10},{10,8},{9,1... | collective-permute-start | bytes 4816904 | tf_op jit(solution)/shard_map/ppermute | solution.py:1465
  400.5 39.8 %collective-permute-start.33 = (bf16[128,1024]{1,0:T(8,128)(2,1)}, bf16[128,1024]{1,0:T(8,128)(2,1)S(1)}, u32[]{:S(2)}, u32[]{:S(2)}) collective-permute-start(bf16[128,1024]{1,0:T(8,128)(2,1)} %get-tuple-element.334), channel_id=1, source_target_pairs={{0,8},{8,16},{16,24},{24,0},{1,9},{9,17},{17,25},{25,1},{2,10},{10... | collective-permute-start | bytes 786440 | tf_op jit(solution)/shard_map/ppermute | solution.py:1355
  419.2 39.6 %collective-permute-start.34 = (bf16[128,1024]{1,0:T(8,128)(2,1)}, bf16[128,1024]{1,0:T(8,128)(2,1)S(1)}, u32[]{:S(2)}, u32[]{:S(2)}) collective-permute-start(bf16[128,1024]{1,0:T(8,128)(2,1)} %get-tuple-element.335), channel_id=1, source_target_pairs={{0,16},{8,24},{16,0},{24,8},{1,17},{9,25},{17,1},{25,9},{2,18},{10... | collective-permute-start | bytes 786440 | tf_op jit(solution)/shard_map/ppermute | solution.py:1355
  420.9 38.0 %collective-permute-start.35 = (bf16[128,1024]{1,0:T(8,128)(2,1)}, bf16[128,1024]{1,0:T(8,128)(2,1)}, u32[]{:S(2)}, u32[]{:S(2)}) collective-permute-start(bf16[128,1024]{1,0:T(8,128)(2,1)} %get-tuple-element.336), channel_id=1, source_target_pairs={{0,24},{8,0},{16,8},{24,16},{1,25},{9,1},{17,9},{25,17},{2,26},{10... | collective-permute-start | bytes 786440 | tf_op jit(solution)/shard_map/ppermute | solution.py:1355
  423.9 49.8 %all-to-all-start = ((bf16[8,96,512]{2,1,0:T(8,128)(2,1)}), bf16[8,96,512]{2,1,0:T(8,128)(2,1)S(1)}, u32[]{:S(2)}, u32[]{:S(2)}) async-start(bf16[8,96,512]{2,1,0:T(8,128)(2,1)} %bitcast.44), calls=%async_computation | async-start | bytes 1572864 | tf_op jit(solution)/shard_map/all_to_all | solution.py:1358
  437.0 43.4 %collective-permute-start.47 = (bf16[512,1024]{1,0:T(8,128)(2,1)S(1)}, bf16[512,1024]{1,0:T(8,128)(2,1)}, u32[]{:S(2)}, u32[]{:S(2)}) collective-permute-start(bf16[512,1024]{1,0:T(8,128)(2,1)S(1)} %pad_maximum_fusion.2.refs_0_), channel_id=1, source_target_pairs={{0,4},{4,0},{1,5},{5,1},{2,6},{6,2},{3,7},{7,3},{8,12},{12,8},{9,1... | collective-permute-start | bytes 3145736 | tf_op jit(solution)/shard_map/ppermute | solution.py:1393
  440.3 34.6 %collective-permute-start.42 = (bf16[160,512]{1,0:T(8,128)(2,1)}, bf16[160,512]{1,0:T(8,128)(2,1)}, u32[]{:S(2)}, u32[]{:S(2)}) collective-permute-start(bf16[160,512]{1,0:T(8,128)(2,1)} %add_convert_fusion.10), channel_id=1, source_target_pairs={{0,8},{8,16},{16,24},{24,0},{1,9},{9,17},{17,25},{25,1},{2,10},{10... | collective-permute-start | bytes 491528 | tf_op jit(solution)/shard_map/ppermute | solution.py:1355
  476.9 25.3 %collective-permute-start.51 = (bf16[128,1024]{1,0:T(8,128)(2,1)}, bf16[128,1024]{1,0:T(8,128)(2,1)}, u32[]{:S(2)}, u32[]{:S(2)}) collective-permute-start(bf16[128,1024]{1,0:T(8,128)(2,1)} %add_convert_fusion.8), channel_id=1, source_target_pairs={{0,24},{8,0},{16,8},{24,16},{1,25},{9,1},{17,9},{25,17},{2,26},{10... | collective-permute-start | bytes 786440 | tf_op jit(solution)/shard_map/ppermute | solution.py:1355
  480.4 39.2 %collective-permute-start.45 = (bf16[640,512]{1,0:T(8,128)(2,1)}, bf16[640,512]{1,0:T(8,128)(2,1)}, u32[]{:S(2)}, u32[]{:S(2)}) collective-permute-start(bf16[640,512]{1,0:T(8,128)(2,1)} %pad_maximum_fusion.6.refs_0_), channel_id=1, source_target_pairs={{0,4},{4,0},{1,5},{5,1},{2,6},{6,2},{3,7},{7,3},{8,12},{12,8},{9,1... | collective-permute-start | bytes 1966088 | tf_op jit(solution)/shard_map/ppermute | solution.py:1393
  483.5 52.2 %collective-permute-start.31 = (bf16[784,1024]{1,0:T(8,128)(2,1)S(1)}, bf16[784,1024]{1,0:T(8,128)(2,1)}, u32[]{:S(2)}, u32[]{:S(2)}) collective-permute-start(bf16[784,1024]{1,0:T(8,128)(2,1)S(1)} %copy-done), channel_id=1, source_target_pairs={{1,2},{2,1},{5,6},{6,5},{9,10},{10,9},{13,14},{14,13},{17,18},{18,... | collective-permute-start | bytes 4816904 | tf_op jit(solution)/shard_map/ppermute | solution.py:1474
  487.2 32.5 %all-to-all-start.1 = ((bf16[8,96,512]{2,1,0:T(8,128)(2,1)}), bf16[8,96,512]{2,1,0:T(8,128)(2,1)S(1)}, u32[]{:S(2)}, u32[]{:S(2)}) async-start(bf16[8,96,512]{2,1,0:T(8,128)(2,1)} %broadcast_in_dim.9), calls=%async_computation.1 | async-start | bytes 1572864 | tf_op jit(solution)/shard_map/all_to_all | solution.py:1358
  491.3 49.2 %collective-permute-start.41 = (bf16[784,1024]{1,0:T(8,128)(2,1)}, bf16[784,1024]{1,0:T(8,128)(2,1)}, u32[]{:S(2)}, u32[]{:S(2)}) collective-permute-start(bf16[784,1024]{1,0:T(8,128)(2,1)} %get-tuple-element.394), channel_id=1, source_target_pairs={{1,2},{2,1},{5,6},{6,5},{9,10},{10,9},{13,14},{14,13},{17,18},{18,... | collective-permute-start | bytes 4816904 | tf_op jit(solution)/shard_map/ppermute | solution.py:1474
  (74 other events, 1049.5 us)

commit v6 on v5

--- a/solution.py
+++ b/solution.py
@@ -24,7 +24,43 @@
     )
 
 
-def attend_kernel(tile, rows, padded, qkv_ref, out_ref, lse_ref, q_t, v_t, out_t):
+def padded_rows(rows, tile):
+    full = rows // tile
+    return full * tile + -(-(rows - full * tile) // PAIR) * PAIR
+
+
+def walk(rows, tile, start, finish):
+    full = rows // tile
+    rest = padded_rows(rows, tile) - full * tile
+    start(0, pl.ds(0, tile), tile)
+
+    def step(columns, size, following, following_size):
+        start(1, columns, size)
+        finish(0, columns, size)
+        if following is not None:
+            start(0, following, following_size)
+        finish(1, columns, size)
+
+    def block(index, carry):
+        first = pl.multiple_of(index * tile, tile)
+        following = pl.multiple_of(index * tile + tile, tile)
+        step(pl.ds(first, tile), tile, pl.ds(following, tile), tile)
+        return carry
+
+    lax.fori_loop(0, full - 1, block, 0)
+    last = pl.ds(full * tile, rest) if rest else None
+    step(pl.ds((full - 1) * tile, tile), tile, last, rest)
+    if rest:
+        step(last, rest, None, 0)
+
+
+def one_head(values_t, head, columns, size):
+    empty = jnp.zeros((HEAD_DIM, size), BF16)
+    values = values_t[head * HEAD_DIM : (head + 1) * HEAD_DIM, columns]
+    return jnp.concatenate([values, empty] if head == 0 else [empty, values], axis=0)
+
+
+def attend_kernel(tile, rows, padded, qkv_ref, out_ref, lse_ref, q_t, v_t, out_t, scores):
     scale = HEAD_DIM**-0.5 * LOG2E
     ones = jnp.ones((16, rows), BF16)
     q_t[:, :rows] = qkv_ref[:, :PAIR].T
@@ -38,30 +74,27 @@
         ]
         v_t[head * step + HEAD_DIM : (head + 1) * step, :] = ones
 
-    def block(index, carry):
-        columns = pl.ds(pl.multiple_of(index * tile, tile), tile)
-        empty = jnp.zeros((HEAD_DIM, tile), BF16)
-        for head in range(2):
-            lanes = slice(head * HEAD_DIM, (head + 1) * HEAD_DIM)
-            query = q_t[lanes, columns]
-            query = jnp.concatenate([query, empty] if head == 0 else [empty, query], axis=0)
-            scores = contract(qkv_ref[:, PAIR : 2 * PAIR], query, 1, 0)
-            highest = jnp.max(scores, axis=0, keepdims=True) * scale
-            expon = jnp.exp2(scores * scale - highest).astype(BF16)
-            mixed = contract(v_t[head * step : (head + 1) * step, :], expon, 1, 0)
-            total = mixed[HEAD_DIM : HEAD_DIM + 1, :]
-            out_t[lanes, columns] = mixed[:HEAD_DIM, :] / total
-            lse_ref[head : head + 1, columns] = highest + jnp.log2(total)
-        return carry
-
-    lax.fori_loop(0, padded // tile, block, 0)
+    def start(head, columns, size):
+        query = one_head(q_t, head, columns, size)
+        scores[head, :, :size] = contract(qkv_ref[:, PAIR : 2 * PAIR], query, 1, 0)
+
+    def finish(head, columns, size):
+        values = scores[head, :, :size]
+        highest = jnp.max(values, axis=0, keepdims=True) * scale
+        expon = jnp.exp2(values * scale - highest).astype(BF16)
+        mixed = contract(v_t[head * step : (head + 1) * step, :], expon, 1, 0)
+        total = mixed[HEAD_DIM : HEAD_DIM + 1, :]
+        out_t[head * HEAD_DIM : (head + 1) * HEAD_DIM, columns] = mixed[:HEAD_DIM, :] / total
+        lse_ref[head : head + 1, columns] = highest + jnp.log2(total)
+
+    walk(rows, tile, start, finish)
     out_ref[...] = out_t[...].T[:rows, :].astype(BF16)
 
 
 def attend(qkv, first_pair, last_pair, kept=None, tile=512):
     rows, width = qkv.shape
     pairs = width // (3 * PAIR)
-    padded = -(-rows // tile) * tile
+    padded = padded_rows(rows, tile)
     count = last_pair - first_pair
     kernel = functools.partial(attend_kernel, tile, rows, padded)
     anywhere = pl.BlockSpec(memory_space=pl.ANY)
@@ -82,6 +115,7 @@
             pltpu.VMEM((PAIR, padded), BF16),
             pltpu.VMEM((PAIR + 32, rows), BF16),
             pltpu.VMEM((PAIR, padded), F32),
+            pltpu.VMEM((2, rows, tile), F32),
         ],
         input_output_aliases={} if kept is None else {1: 0, 2: 1},
         compiler_params=pltpu.CompilerParams(vmem_limit_bytes=VMEM_LIMIT),
@@ -96,7 +130,7 @@
 
 def attend_back_kernel(
     tile, rows, padded, s_ref, qkv_ref, grad_ref, out_ref, lse_ref, first_ref, dqkv_ref, send_ref,
-    keep_ref, sums_ref, q_t, g_t, k_t, delta, dq_t, dk_t, dv_t, all_t,
+    keep_ref, sums_ref, q_t, g_t, k_t, delta, dq_t, dk_t, dv_t, all_t, scores, d_probs,
 ):
     scale = HEAD_DIM**-0.5
     q_t[:, :rows] = qkv_ref[:, :PAIR].T
@@ -112,25 +146,22 @@
     dk_t[...] = jnp.zeros_like(dk_t)
     dv_t[...] = jnp.zeros_like(dv_t)
 
-    def block(index, carry):
-        columns = pl.ds(pl.multiple_of(index * tile, tile), tile)
-        empty = jnp.zeros((HEAD_DIM, tile), BF16)
-        for head in range(2):
-            lanes = slice(head * HEAD_DIM, (head + 1) * HEAD_DIM)
-            query = q_t[lanes, columns]
-            grad = g_t[lanes, columns]
-            query_pad = jnp.concatenate([query, empty] if head == 0 else [empty, query], axis=0)
-            grad_pad = jnp.concatenate([grad, empty] if head == 0 else [empty, grad], axis=0)
-            scores = contract(qkv_ref[:, PAIR : 2 * PAIR], query_pad, 1, 0)
-            grad_probs = contract(qkv_ref[:, 2 * PAIR :], grad_pad, 1, 0)
-            weights = jnp.exp2(scores * (scale * LOG2E) - lse_ref[head : head + 1, columns])
-            grad_scores = (weights * (grad_probs - delta[head : head + 1, columns])).astype(BF16)
-            dv_t[lanes, :] += contract(grad, weights.astype(BF16), 1, 1)
-            dq_t[lanes, columns] = contract(k_t[lanes, :], grad_scores, 1, 0)
-            dk_t[lanes, :] += contract(query, grad_scores, 1, 1)
-        return carry
-
-    lax.fori_loop(0, padded // tile, block, 0)
+    def start(head, columns, size):
+        query, grad = one_head(q_t, head, columns, size), one_head(g_t, head, columns, size)
+        scores[head, :, :size] = contract(qkv_ref[:, PAIR : 2 * PAIR], query, 1, 0)
+        d_probs[head, :, :size] = contract(qkv_ref[:, 2 * PAIR :], grad, 1, 0)
+
+    def finish(head, columns, size):
+        lanes = slice(head * HEAD_DIM, (head + 1) * HEAD_DIM)
+        log_total = lse_ref[head : head + 1, columns]
+        weights = jnp.exp2(scores[head, :, :size] * (scale * LOG2E) - log_total)
+        inner = delta[head : head + 1, columns]
+        d_scores = (weights * (d_probs[head, :, :size] - inner)).astype(BF16)
+        dv_t[lanes, :] += contract(g_t[lanes, columns], weights.astype(BF16), 1, 1)
+        dq_t[lanes, columns] = contract(k_t[lanes, :], d_scores, 1, 0)
+        dk_t[lanes, :] += contract(q_t[lanes, columns], d_scores, 1, 1)
+
+    walk(rows, tile, start, finish)
     all_t[:PAIR, :] = (dq_t[:, :rows] * scale).astype(BF16)
     all_t[PAIR : 2 * PAIR, :] = (dk_t[...] * scale).astype(BF16)
     all_t[2 * PAIR :, :] = dv_t[...].astype(BF16)
@@ -154,7 +185,7 @@
 def attend_back(scal, qkv, grad, out, lse, first, first_pair, last_pair, tile=256):
     rows, full = qkv.shape
     width = first.shape[1]
-    padded = -(-rows // tile) * tile
+    padded = padded_rows(rows, tile)
     count = last_pair - first_pair
     return pl.pallas_call(
         functools.partial(attend_back_kernel, tile, rows, padded),
@@ -183,6 +214,8 @@
                 pltpu.VMEM((PAIR, rows), F32),
                 pltpu.VMEM((PAIR, rows), F32),
                 pltpu.VMEM((3 * PAIR, rows), BF16),
+                pltpu.VMEM((2, rows, tile), F32),
+                pltpu.VMEM((2, rows, tile), F32),
             ],
         ),
         out_shape=[
@@ -699,34 +732,37 @@
 
 
 def finish_feed_kernel(s_ref, *refs, tile):
-    sums, (up_out, down_out) = refs[:8], refs[8:]
+    up_out, down_out = refs[8:]
     first = s_ref[2] == 0
     even = s_ref[1] == 0
-    for j in range(2):
-        mine, beside, mine_across, beside_across = [ref[...] for ref in sums[4 * j : 4 * j + 4]]
-        mine, beside = jnp.where(even, mine, beside), jnp.where(even, beside, mine)
-        mine_across, beside_across = (
-            jnp.where(even, mine_across, beside_across),
-            jnp.where(even, beside_across, mine_across),
-        )
-        for kind, own, other in ((0, mine, mine_across), (1, beside, beside_across)):
-            for c in range(2):
-                wide = jnp.where(first == (c == 0), own, other).astype(F32)
-                if kind == 1:
-                    down_out[c, j] = wide
-                    continue
-                for h in range(2):
-                    start = ((h * 2 + c) * 2 + j) * tile
-                    up_out[:, start : start + tile] = wide[:, h * tile : (h + 1) * tile]
+    low_range = s_ref[4] == 0
+    cores = []
+    for refs_of in (refs[:4], refs[4:8]):
+        whole, beside, along, last = [ref[...] for ref in refs_of]
+        ranges = []
+        for j in range(2):
+            mine = jnp.where(low_range == (j == 0), whole, along)
+            theirs = jnp.where(low_range == (j == 0), beside, last)
+            ranges.append((jnp.where(even, mine, theirs), jnp.where(even, theirs, mine)))
+        cores.append(ranges)
+    for c in range(2):
+        for j in range(2):
+            up, down = [
+                jnp.where(first == (c == 0), cores[0][j][kind], cores[1][j][kind]).astype(F32)
+                for kind in range(2)
+            ]
+            down_out[c, j] = down
+            for h in range(2):
+                start = ((h * 2 + c) * 2 + j) * tile
+                up_out[:, start : start + tile] = up[:, h * tile : (h + 1) * tile]
 
 
 def finish_feed(scal, sums):
     rows, width = sums[0].shape
-    tile = rows
     steps = 4
     block = spec((rows // steps, width), lambda i, s: (i, 0))
     up, down = run(
-        functools.partial(finish_feed_kernel, tile=tile), "finish_feed", scal, (steps,),
+        functools.partial(finish_feed_kernel, tile=rows), "finish_feed", scal, (steps,),
         [block] * 8,
         [
             spec((rows // steps, 4 * width), lambda i, s: (i, 0)),
@@ -743,20 +779,17 @@
     first, even = s_ref[2] == 0, s_ref[1] == 0
     half_pairs = pairs // 2
     for g, (begin, end) in enumerate(spans):
-        if g == 0:
-            mine, beside, mine_across, beside_across = [ref[...] for ref in refs[:4]]
-            own = jnp.concatenate(
-                [jnp.where(even, mine, beside), jnp.where(even, beside, mine)], axis=0
-            )
-            other = jnp.concatenate(
-                [
-                    jnp.where(even, mine_across, beside_across),
-                    jnp.where(even, beside_across, mine_across),
-                ],
-                axis=0,
-            )
-        else:
-            own, other = refs[2 * g + 2][...], refs[2 * g + 3][...]
+        mine, beside, mine_across, beside_across = [ref[...] for ref in refs[4 * g : 4 * g + 4]]
+        own = jnp.concatenate(
+            [jnp.where(even, mine, beside), jnp.where(even, beside, mine)], axis=0
+        )
+        other = jnp.concatenate(
+            [
+                jnp.where(even, mine_across, beside_across),
+                jnp.where(even, beside_across, mine_across),
+            ],
+            axis=0,
+        )
         for c in range(2):
             total = jnp.where(first == (c == 0), own, other).astype(F32)
             wide = total[: (end - begin) * 3 * PAIR].T
@@ -834,6 +867,7 @@
 def wide_back(qkv, grad, out, lse, first_pair, last_pair, tile=256):
     rows, width = qkv.shape
     padded = -(-rows // tile) * tile
+    lse = jnp.pad(lse, ((0, 0), (0, 0), (0, padded - lse.shape[2])))
     count = last_pair - first_pair
     return pl.pallas_call(
         functools.partial(wide_back_kernel, tile, rows, padded),
@@ -1337,97 +1371,103 @@
         self.before = values
 
 
-class LineSum:
-    def __init__(self, order, axes, size, values):
-        self.order, self.axes, self.size = order, axes, size
-        self.shape = values.shape
-        if axes == "line":
-            self.place = lax.axis_index("line")
-            pieces = values.reshape(size, -1, values.shape[-1])
-            sent = [pick(pieces, (self.place + s) % size, 0) for s in range(1, size)]
-            self.piece, *sent = order.pin(pick(pieces, self.place, 0), *sent)
-            self.received = [self.shift(values, s) for s, values in enumerate(sent, start=1)]
-            return
-        values = order.pin(values)
-        self.received = self.exchange(values.reshape(size, -1, values.shape[-1]))
-
-    def shift(self, values, s):
-        return lax.ppermute(values, "line", [(i, (i + s) % self.size) for i in range(self.size)])
-
-    def exchange(self, values):
-        return lax.all_to_all(values, self.axes, split_axis=0, concat_axis=0, tiled=True)
-
-    def spread(self):
-        if self.axes == "line":
-            piece = self.piece.astype(F32)
-            for other in self.order.pin(*self.received):
-                piece = piece + other.astype(F32)
-            self.piece = self.order.pin(piece.astype(BF16))
-            self.received = [self.shift(self.piece, s) for s in range(1, self.size)]
-            return
-        received = self.order.pin(self.received)
-        piece = received[0].astype(F32)
-        for i in range(1, self.size):
-            piece = piece + received[i].astype(F32)
-        piece = piece.astype(BF16)
-        copies = self.order.pin(jnp.broadcast_to(piece[None], (self.size,) + piece.shape))
-        self.received = self.exchange(copies)
-
-    def gather(self):
-        if self.axes != "line":
-            return self.order.pin(self.received).reshape(self.shape)
-        gathered = [self.piece] + list(self.order.pin(*self.received))
-        whole = [
-            functools.reduce(
-                lambda rest, s: jnp.where((self.place - s) % self.size == i, gathered[s], rest),
-                range(1, self.size),
-                gathered[0],
-            )
-            for i in range(self.size)
-        ]
-        return self.order.pin(jnp.concatenate(whole, axis=0))
-
-    def meet(self):
-        self.whole = self.gather()
-        if self.axes == "line":
-            self.beside = lax.ppermute(self.whole, "low", SWAP)
-        self.across = lax.ppermute(self.whole, "core", SWAP)
-
-    def cross(self):
-        if self.axes != "line":
-            return self.whole, self.order.pin(self.across)
-        self.beside = self.order.pin(self.beside)
-        self.beside_across = lax.ppermute(self.beside, "core", SWAP)
-        return self.whole, self.beside, self.across, self.beside_across
-
-
-class PlaneSum:
-    def __init__(self, order, low, deep, send, keep, both=False):
-        self.order, self.low, self.deep, self.both = order, low, deep, both
-        send, self.keep = order.pin(send, keep)
-        self.received = lax.ppermute(send, "half", SWAP)
-
-    def to_neighbour(self):
-        total = add_low(self.keep, self.order.pin(self.received))
-        if self.both:
-            self.line = LineSum(self.order, ("line", "low"), 2 * self.deep, total)
-            return
-        parts = total.reshape(2, -1, total.shape[-1])
-        send, self.keep = self.order.pin(pick(parts, 1 - self.low, 0), pick(parts, self.low, 0))
-        self.received = lax.ppermute(send, "low", SWAP)
-
-    def along(self):
-        received = self.order.pin(self.received)
-        self.line = LineSum(self.order, "line", self.deep, add_low(self.keep, received))
-
-    def spread(self):
-        self.line.spread()
-
-    def meet(self):
-        self.line.meet()
-
-    def cross(self):
-        return self.line.cross()
+class Steps:
+    def __init__(self, steps):
+        self.steps = steps
+        self.waiting = next(steps)
+
+
+def advance(order, *chains):
+    pinned = order.pin(*[values for chain in chains for values in chain.waiting])
+    pinned = list(pinned) if isinstance(pinned, (list, tuple)) else [pinned]
+    for chain in chains:
+        count = len(chain.waiting)
+        values, pinned = pinned[:count], pinned[count:]
+        chain.waiting = chain.steps.send(values)
+
+
+def line_steps(order, deep, parts, result):
+    place = lax.axis_index("line")
+    bits = range((deep - 1).bit_length())
+
+    def exchange(values, bit):
+        return lax.ppermute(values, "line", [(i, i ^ (1 << bit)) for i in range(deep)])
+
+    for bit in bits:
+        even = (place >> bit) % 2 == 0
+        keep, send = order.pin(jnp.where(even, *parts), jnp.where(even, *parts[::-1]))
+        (other,) = yield [exchange(send, bit)]
+        total = add_low(keep, other)
+        size = total.shape[0] // 2
+        parts = (total[:size], total[size:])
+    for bit in reversed(bits):
+        total = order.pin(total)
+        (other,) = yield [exchange(total, bit)]
+        total = join(total, other, (place >> bit) % 2).reshape(-1, total.shape[-1])
+    whole = order.pin(total)
+    beside, across = yield [lax.ppermute(whole, "low", SWAP), lax.ppermute(whole, "core", SWAP)]
+    crossed = lax.ppermute(beside, "core", SWAP)
+    (crossed,) = yield [crossed]
+    result.extend([whole, beside, across, crossed])
+    yield []
+
+
+def range_steps(order, deep, parts, result):
+    place = lax.axis_index("line")
+    bits = range((deep - 1).bit_length())
+
+    def exchange(values, bit):
+        return lax.ppermute(values, "line", [(i, i ^ (1 << bit)) for i in range(deep)])
+
+    for bit in bits:
+        even = (place >> bit) % 2 == 0
+        keep, send = order.pin(jnp.where(even, *parts), jnp.where(even, *parts[::-1]))
+        (other,) = yield [exchange(send, bit)]
+        total = add_low(keep, other)
+        size = total.shape[0] // 2
+        parts = (total[:size], total[size:])
+    for bit in reversed(bits[1:]):
+        total = order.pin(total)
+        (other,) = yield [exchange(total, bit)]
+        total = join(total, other, (place >> bit) % 2).reshape(-1, total.shape[-1])
+    whole = order.pin(total)
+    beside, along = yield [lax.ppermute(whole, "low", SWAP), exchange(whole, 0)]
+    last, crossed = yield [lax.ppermute(along, "low", SWAP), lax.ppermute(whole, "core", SWAP)]
+    rest = yield [lax.ppermute(values, "core", SWAP) for values in (beside, along, last)]
+    result.extend([whole, beside, along, last, crossed, *rest])
+    yield []
+
+
+def plane_steps(order, low, deep, send, keep, result):
+    send, keep = order.pin(send, keep)
+    (other,) = yield [lax.ppermute(send, "half", SWAP)]
+    total = add_low(keep, other)
+    size = total.shape[0] // 2
+    parts = (total[:size], total[size:])
+    even = low == 0
+    keep, send = order.pin(jnp.where(even, *parts), jnp.where(even, *parts[::-1]))
+    (other,) = yield [lax.ppermute(send, "low", SWAP)]
+    total = add_low(keep, other)
+    size = total.shape[0] // 2
+    yield from line_steps(order, deep, (total[:size], total[size:]), result)
+
+
+def vector_steps(order, half, deep, entries, result):
+    def line(values, bit):
+        return lax.ppermute(values, "line", [(i, i ^ (1 << bit)) for i in range(deep)])
+
+    entries = order.pin(entries)
+    (other,) = yield [lax.ppermute(entries, "core", SWAP)]
+    entries = entries + other
+    keep, send = order.pin(pick(entries, half, 0), pick(entries, 1 - half, 0))
+    (other,) = yield [lax.ppermute(send, "half", SWAP)]
+    total = order.pin(keep + other)
+    for bit in range((deep - 1).bit_length()):
+        (other,) = yield [line(total, bit)]
+        total = order.pin(total + other)
+    (other,) = yield [lax.ppermute(total, "low", SWAP)]
+    result.append(total + other)
+    yield []
 
 
 def add_low(left, right):
@@ -1475,13 +1515,21 @@
 
     tokens, cotangent = tokens.reshape(local, width), cotangent.reshape(local, width)
 
+    tokens_in = cross_over(tokens)
     own_qkv, mine = pack_qkv(scal, (query_weight, key_weight, value_weight))
     qkv_x = swap_half(mine)
+    packed = [pack_feed(scal, up_weight, down_weight, j, 2, (1, 4)[j]) for j in range(2)]
     vectors = jnp.concatenate(
-        [query_bias, value_bias, out_bias, first_gain, first_shift, second_gain, second_shift,
-         down_bias, up_bias]
-    )
-    vectors = join(vectors, swap_half(vectors), half)
+        [after(query_bias, mine, *packed), value_bias, out_bias, first_gain, first_shift,
+         second_gain, second_shift, down_bias, up_bias]
+    )
+    order = Order()
+    tokens_in, qkv_x, vectors, vectors_in, *packed = order.pin(
+        tokens_in, qkv_x, vectors, swap_half(vectors), *packed
+    )
+    qkv_y = swap_low(qkv_x)
+    feed_x = [swap_half(packed[0])]
+    vectors = join(vectors, vectors_in, half)
     (full_qbias, full_vbias, full_obias, gain_one, shift_one, gain_two, shift_two, full_dbias) = [
         vectors[:, i * own_rows : (i + 1) * own_rows].reshape(1, width) for i in range(8)
     ]
@@ -1490,32 +1538,24 @@
         return pick(values.reshape(2, 2, inner, -1), core, 1).transpose(1, 0, 2).reshape(inner, -1)
 
     bias_set = set_entries(vectors[:, 8 * own_rows :], 2).reshape(1, -1)
-    packed = [pack_feed(scal, up_weight, down_weight, j, 2, (1, 4)[j]) for j in range(2)]
     quarter = own_rows // 4
     out_mine = lax.dynamic_slice(
         out_weight, (core * (own_rows // 2) + low * quarter, 0 * core), (quarter, width)
     )
-    order = Order()
-    order.pin(*packed)
-    tokens, qkv_x = order.pin(tokens, qkv_x)
-    tokens_in = cross_over(tokens)
-    qkv_y = swap_low(qkv_x)
-    out_mine = order.pin(out_mine)
-    tokens_in, qkv_y = order.pin(tokens_in, qkv_y)
-    out_x = swap_half(after(out_mine, tokens_in))
-    packed = after_all(packed, tokens_in)
     x, first = first_norm(scal, tokens, tokens_in, gain_one, shift_one)
     x, first = order.pin(x, first)
     order.fence(x)
-    first_in = swap_core(first)
-    feed_x = [swap_half(values) for values in packed]
+    first, qkv_y, feed_x[0] = order.pin(first, qkv_y, feed_x[0])
+    first_in = order.pin(swap_core(first))
+    feed_y = [swap_low(feed_x[0])]
+    out_x = swap_half(order.pin(out_mine))
+    feed_x.append(swap_half(order.pin(packed[1])))
     zeros = jnp.zeros((pairs, PAIR), F32)
     qkv_bias = jnp.stack(
         [set_entries(full_qbias).reshape(pairs, PAIR), zeros,
          set_entries(full_vbias).reshape(pairs, PAIR)],
         axis=1,
     ).reshape(1, 3 * own_rows)
-    first_in = order.pin(first_in)
     qkv, qkv_weight, first_all = project(
         scal, (first, first_in), own_qkv, qkv_x, qkv_y, qkv_bias
     )
@@ -1524,8 +1564,8 @@
     order.fence(qkv)
     out_y = swap_low(out_x)
     mixed, lse = attend(qkv, 0, pairs - 1)
-    lse, out_y, *feed_x = order.pin(lse, out_y, *feed_x)
-    feed_y = [swap_low(feed_x[0]), swap_high(feed_x[1])]
+    lse, out_y, feed_x[1] = order.pin(lse, out_y, feed_x[1])
+    feed_y.append(swap_high(feed_x[1]))
     cotangent_in = cross_over(after(cotangent, lse))
     mixed, lse = attend(qkv, pairs - 1, pairs, (mixed, lse))
     mixed = order.pin(mixed)
@@ -1587,41 +1627,48 @@
     half_in = swap_half(half_send)
 
     back(1)
-    one = LineSum(order, "line", deep, add_low(low_mine, order.pin(one_in)))
-    early = PlaneSum(
-        order, low, deep,
-        jnp.concatenate([backs[0][1], backs[1][1], out_send], axis=0),
-        jnp.concatenate([backs[0][2], backs[1][2], out_keep], axis=0),
+    one_in, half_in = order.pin(one_in, half_in)
+    feed_parts, early_parts, late_parts, vector_parts = [], [], [], []
+    ranges = Steps(
+        range_steps(
+            order, deep, (add_low(low_mine, one_in), add_low(half_keep, half_in)), feed_parts
+        )
+    )
+    early = Steps(
+        plane_steps(
+            order, low, deep,
+            jnp.concatenate([backs[0][1], backs[1][1], out_send], axis=0),
+            jnp.concatenate([backs[0][2], backs[1][2], out_keep], axis=0), early_parts,
+        )
     )
 
     back(2)
-    one.spread()
-    two = LineSum(order, "line", deep, add_low(half_keep, order.pin(half_in)))
-    early.to_neighbour()
+    advance(order, ranges, early)
+    layer_in = cross_over(order.pin(layer))
 
     back(3)
-    one.meet()
-    late = PlaneSum(
-        order, low, deep,
-        jnp.concatenate([backs[2][1], backs[3][1]], axis=0),
-        jnp.concatenate([backs[2][2], backs[3][2]], axis=0), both=True,
-    )
-    early.along()
-    layer_in = cross_over(order.pin(layer))
+    layer_in = order.pin(layer_in)
+    late = Steps(
+        plane_steps(
+            order, low, deep,
+            jnp.concatenate([backs[2][1], backs[3][1]], axis=0),
+            jnp.concatenate([backs[2][2], backs[3][2]], axis=0), late_parts,
+        )
+    )
+    advance(order, ranges, early)
     first_own, first_part = first_grad(
         scal, [order.pin(backs[0][0])] + [b[0] for b in backs[1:]], qkv_weight
     )
     first_own, first_part = order.pin(first_own, first_part)
     order.fence(first_part)
-    first_part_in = swap_core(first_part)
-    late.to_neighbour()
-    early.spread()
-    two.spread()
+    advance(order, late, early, ranges)
+    first_part_in = swap_core(order.pin(first_part))
     tokens_out, sums_one = first_back(
         scal, first_own, order.pin(first_part_in), x, grad_low, gain_one
     )
     tokens_out, sums_one = order.pin(tokens_out, sums_one)
     order.fence(sums_one)
+    advance(order, early, late, ranges)
 
     def place_entries(values, inner=1):
         values = values.reshape(inner, 2, 1, -1).transpose(1, 2, 0, 3)
@@ -1633,34 +1680,19 @@
         place_entries(parts[:, 0]), place_entries(parts[:, 2]), sums_two[3], sums_one[0],
         sums_one[1], sums_two[0], sums_two[1], sums_two[2], place_entries(up_bias_grad, 2),
     ]
-    entries = order.pin(jnp.concatenate([e.reshape(2, -1) for e in entries], axis=1))
-    entries_in = swap_core(entries)
-    late.spread()
-    entries = entries + order.pin(entries_in)
-    keep, send = order.pin(pick(entries, half, 0), pick(entries, 1 - half, 0))
-    entries_in = swap_half(send)
-    tokens_in = cross_over(after(tokens_out, send))
-    early.meet()
-    one_parts = one.cross()
-    steps = [("line", 1 << bit, deep) for bit in range((deep - 1).bit_length())] + [("low", 1, 2)]
-
-    def exchange(axis, step, size):
-        return lax.ppermute(entries, axis, [(i, i ^ step) for i in range(size)])
-
-    entries = order.pin(keep + order.pin(entries_in))
-    entries_in = exchange(*steps[0])
-    two.meet()
-    for step in steps[1:]:
-        entries = order.pin(entries + order.pin(entries_in))
-        entries_in = exchange(*step)
-    late.meet()
-    early_parts = early.cross()
-    two_parts = two.cross()
-    up_weight_grad, down_weight_grad = finish_feed(
-        scal, order.pin(*one_parts, *two_parts)
-    )
-    entries = entries + entries_in
-    late_parts = late.cross()
+    entries = jnp.concatenate([e.reshape(2, -1) for e in entries], axis=1)
+    vectors = Steps(vector_steps(order, half, deep, entries, vector_parts))
+    advance(order, vectors)
+    advance(order, vectors, early, late)
+    tokens_in = cross_over(order.pin(tokens_out))
+    advance(order, vectors, early, late)
+    advance(order, vectors, late)
+    advance(order, early, ranges, late)
+    advance(order, ranges, vectors, early)
+    up_weight_grad, down_weight_grad = finish_feed(scal, feed_parts)
+    advance(order, late)
+    advance(order, late)
+    (entries,) = vector_parts
     query_weight_grad, key_weight_grad, value_weight_grad, out_weight_grad = finish_attention(
         scal, (*early_parts, *late_parts), ((0, 2), (2, 4))
     )

time: 575 us -> 552 us (0.960)
  starting transfers between devices: 104 us -> 63.5 us
  waiting for transfers between devices: 98.7 us -> 135 us
  Pallas kernels: 296 us -> 272 us
    ppermute x34 -> x33, starting transfers between devices: 62.3 us -> 28.6 us  [the longest x12 10.8 us: exchange(): lax.ppermute(values, 'line', [(i, i ^ 1 << bit) for i in range(deep)])]
    ppermute x34 -> x33, waiting for transfers between devices: 49.2 us -> 70.1 us  [the longest x12 32.3 us: exchange(): lax.ppermute(values, 'line', [(i, i ^ 1 << bit) for i in range(deep)])]
    pallas_call x2, Pallas kernels: 49.4 us -> 30.6 us  [attend(): pl.pallas_call(kernel if kept is None else lambda ref, a, b, *rest: kerne...]
    ppermute x1, waiting for transfers between devices: 1.4 us -> 10.5 us  [swap_high(): return lax.ppermute(values, 'line', [(i, i ^ 1) for i in range(deep)])]
    all_to_all x2 -> x0, starting transfers between devices: 7.79 us -> none  [exchange(): lax.all_to_all(values, self.axes, split_axis=0, concat_axis=0, tiled=True)]
    ppermute x4, waiting for transfers between devices: 5.68 us -> 13.2 us  [swap_low(): return lax.ppermute(values, 'low', SWAP)]
    unnamed x108 -> x118, local copies, waits for them, and re-layouts: 9.53 us -> 14.8 us
    convert_element_type x6 -> x11, other arithmetic: 9.82 us -> 14.1 us  [add_low(): return (left.astype(F32) + right.astype(F32)).astype(BF16)]
  transfers between devices with their start and end apart: 64 -> 59, of which waited for: 19 -> 23; matrix products, arithmetic and copies ran while one was open for 9% -> 6% of each run, Pallas kernels for 36% -> 37%
where the time goes in v6:
time: 552 us; the launch traced here: 542 us
  Pallas kernels  272 us (49%)
  waiting for transfers between devices  135 us (24%)
  starting transfers between devices  63.5 us (12%)
  other arithmetic  43.1 us (8%)
  local copies, waits for them, and re-layouts  25.6 us (5%)
    pallas_call x14, Pallas kernels, run(): pl.pallas_call(kernel, grid_spec=pltpu.PrefetchScalarGridSpec(num_scalar_...  97.7 us
    pallas_call x4, Pallas kernels, attend_back(): pl.pallas_call(functools.partial(attend_back_kernel, tile, rows, padded),...  83.6 us
    pallas_call x1, Pallas kernels, feed(): pl.pallas_call(feed_kernel, grid_spec=pltpu.PrefetchScalarGridSpec(num_sc...  60.5 us
    ppermute x12, waiting for transfers between devices, exchange(): lax.ppermute(values, 'line', [(i, i ^ 1 << bit) for i in range(deep)])  32.3 us
    ppermute x8, waiting for transfers between devices, swap_half(): return lax.ppermute(values, 'half', SWAP)  32.2 us
    pallas_call x2, Pallas kernels, attend(): pl.pallas_call(kernel if kept is None else lambda ref, a, b, *rest: kerne...  30.6 us
    ppermute x4, starting transfers between devices, cross_over(): return lax.ppermute(values, ('core', 'half'), cross)  18.1 us
    unnamed x118, local copies, waits for them, and re-layouts  14.8 us
  transfers between devices with their start and end apart: 59, of which 23 were waited for; matrix products, arithmetic and copies ran while one was open for 6% of the time, Pallas kernels for 37%

profile of v6, /device:TPU:1, one launch (start us, length us, event | category | flops | bytes accessed | tf_op | source)
XLA Modules:
  0.0 541.9 jit_solution(9407311583311870598)
XLA Ops:
  0.7 4.5 collective-permute-start
  5.8 4.5 pack_qkv.1
  18.4 22.1 %collective-permute-done.2 = f32[6144]{0:T(1024)S(1)} collective-permute-done((f32[6144]{0:T(1024)S(1)}, f32[6144]{0:T(1024)S(1)}, u32[]{:S(2)}, u32[]{:S(2)}) %collective-permute-start.2) | collective-permute-done | bytes 24608 | tf_op jit(solution)/shard_map/ppermute | solution.py:1502
  49.2 13.1 %collective-permute-done.3.beside_ref = bf16[256,1536]{1,0:T(8,128)(2,1)} collective-permute-done((bf16[256,1536]{1,0:T(8,128)(2,1)}, bf16[256,1536]{1,0:T(8,128)(2,1)}, u32[]{:S(2)}, u32[]{:S(2)}) %collective-permute-start.3) | collective-permute-done | bytes 786464 | tf_op jit(solution)/shard_map/ppermute | solution.py:1508
  71.8 11.1 %project.1 = (bf16[1568,1536]{1,0:T(8,128)(2,1)}, bf16[1024,1536]{1,0:T(8,128)(2,1)}, bf16[1568,1024]{1,0:T(8,128)(2,1)}) custom-call(s32[5]{0:T(128)} %stack.132.s_ref, bf16[784,1024]{1,0:T(8,128)(2,1)} %get-tuple-element.234.mine_ref, bf16[784,1024]{1,0:T(8,128)(2,1)} %collective-permute-done.5.theirs_ref, bf16[512,1536]{1,0:T(8,128)(2,1)} %get-tuple-element.238.own_ref, ...), custom_call_target="tpu_custom_call" | custom-call | flops 4932501504 | bytes 12726272 | tf_op jit(solution)/shard_map/project/pallas_call | solution.py:399
  84.2 22.0 %attend.2 = (bf16[1568,512]{1,0:T(8,128)(2,1)}, f32[4,2,1664]{2,1,0:T(2,128)}) custom-call(bf16[1568,1536]{1,0:T(8,128)(2,1)} %get-tuple-element.242.qkv_ref.ref), custom_call_target="tpu_custom_call" | custom-call | flops 60423143424 | bytes 4816896 | tf_op jit(solution)/shard_map/attend/pallas_call | solution.py:101
  113.1 8.7 %attend.3 = (bf16[1568,512]{1,0:T(8,128)(2,1)}, f32[4,2,1664]{2,1,0:T(2,128)}) custom-call(bf16[1568,1536]{1,0:T(8,128)(2,1)} %get-tuple-element.242.qkv_ref.ref, bf16[1568,512]{1,0:T(8,128)(2,1)} %get-tuple-element.243.a, f32[4,2,1664]{2,1,0:T(2,128)} %copy.58.b), custom_call_target="tpu_custom_call", output_to_operand_aliasing={{0}: (1, {}), {1}: (2, {})} | custom-call | flops 20141047808 | bytes 1605632 | tf_op jit(solution)/shard_map/attend/pallas_call | solution.py:101
  126.1 10.5 %collective-permute-done.11.z_beside = bf16[512,1024]{1,0:T(8,128)(2,1)} collective-permute-done((bf16[512,1024]{1,0:T(8,128)(2,1)}, bf16[512,1024]{1,0:T(8,128)(2,1)}, u32[]{:S(2)}, u32[]{:S(2)}) %collective-permute-start.11) | collective-permute-done | bytes 1048608 | tf_op jit(solution)/shard_map/ppermute | solution.py:1511
  140.8 6.1 %second_norm.1 = (f32[784,1024]{1,0:T(8,128)}, bf16[784,1024]{1,0:T(8,128)(2,1)}) custom-call(s32[5]{0:T(128)} %stack.132.s_ref, bf16[1568,512]{1,0:T(8,128)(2,1)} %get-tuple-element.250.mixed_ref.out_ref, bf16[512,1024]{1,0:T(8,128)(2,1)} %get-tuple-element.251.w_ref, bf16[784,1024]{1,0:T(8,128)(2,1)} %get-tuple-element.233.x_ref, ...), custom_call_target="tpu_custom_call" | custom-call | flops 822083584 | bytes 11755520 | tf_op jit(solution)/shard_map/second_norm/pallas_call | solution.py:399
  152.8 60.5 %feed.1 = (bf16[784,1024]{1,0:T(8,128)(2,1)}, bf16[784,1024]{1,0:T(8,128)(2,1)}, bf16[784,1024]{1,0:T(8,128)(2,1)}, bf16[784,1024]{1,0:T(8,128)(2,1)}, bf16[512,...) custom-call(s32[5]{0:T(128)} %stack.132.s_ref, ...), custom_call_target="tpu_custom_call" | custom-call | flops 39460012032 | bytes 25690112 | tf_op jit(solution)/shard_map/feed/pallas_call | solution.py:357
  218.0 8.9 %second_back.1 = (bf16[784,1024]{1,0:T(8,128)(2,1)}, f32[8,1024]{1,0:T(8,128)}) custom-call(s32[5]{0:T(128)} %stack.132.s_ref, bf16[784,1024]{1,0:T(8,128)(2,1)} %get-tuple-element.264.g_ref, bf16[784,1024]{1,0:T(8,128)(2,1)} %collective-permute-done.15.r_ref, f32[784,1024]{1,0:T(8,128)} %get-tuple-element.272.mid_ref, bf16[784,1024]{1,0:T(8,128)(2,1)} %copy-done.1, ...), custom_call_target="tpu_custom_call" | custom-call | bytes 16064512 | tf_op jit(solution)/shard_map/second_back/pallas_call | solution.py:399
  230.4 7.0 %layer_rows.1 = bf16[784,1024]{1,0:T(8,128)(2,1)} custom-call(s32[5]{0:T(128)} %stack.132.s_ref, bf16[784,1024]{1,0:T(8,128)(2,1)} %get-tuple-element.275.o_ref, bf16[784,1024]{1,0:T(8,128)(2,1)} %copy-done.9, f32[784,1024]{1,0:T(8,128)} %get-tuple-element.272.mid_ref, f32[1,1024]{1,0:T(1,128)} %bitcast.120), custom_call_target="tpu_custom_call" | custom-call | bytes 12853248 | tf_op jit(solution)/shard_map/layer_rows/pallas_call | solution.py:399
  237.3 9.4 %mixed_back.1 = (bf16[1568,512]{1,0:T(8,128)(2,1)}, bf16[512,512]{1,0:T(8,128)(2,1)}, bf16[512,512]{1,0:T(8,128)(2,1)}) custom-call(s32[5]{0:T(128)} %stack.132.s_ref, bf16[784,1024]{1,0:T(8,128)(2,1)} %get-tuple-element.274.mine_ref.wide_ref, bf16[784,1024]{1,0:T(8,128)(2,1)} %collective-permute-done.16.theirs_ref, ...), custom_call_target="tpu_custom_call" | custom-call | flops 3288334336 | bytes 11730944 | tf_op jit(solution)/shard_map/mixed_back/pallas_call | solution.py:399
  246.7 20.9 %attend_back.4 = (bf16[1568,384]{1,0:T(8,128)(2,1)}, bf16[384,512]{1,0:T(8,128)(2,1)}, bf16[384,512]{1,0:T(8,128)(2,1)}, f32[8,384]{1,0:T(8,128)}) custom-call(s32[5]{0:T(128)} %stack.132.s_ref, bf16[1568,1536]{1,0:T(8,128)(2,1)} %get-tuple-element.242.qkv_ref.ref, bf16[1568,512]{1,0:T(8,128)(2,1)} %get-tuple-element.281.grad_ref, ...), custom_call_target="tpu_custom_call" | custom-call | flops 50352619520 | bytes 3211264 | tf_op jit(solution)/shard_map/attend_back/pallas_call | solution.py:190
  267.7 6.9 %collective-permute-done.19 = bf16[512,1024]{1,0:T(8,128)(2,1)} collective-permute-done((bf16[512,1024]{1,0:T(8,128)(2,1)}, bf16[512,1024]{1,0:T(8,128)(2,1)}, u32[]{:S(2)}, u32[]{:S(2)}) %collective-permute-start.19) | collective-permute-done | bytes 1048608 | tf_op jit(solution)/shard_map/ppermute | solution.py:1502
  285.1 20.9 %attend_back.5 = (bf16[1568,384]{1,0:T(8,128)(2,1)}, bf16[384,512]{1,0:T(8,128)(2,1)}, bf16[384,512]{1,0:T(8,128)(2,1)}, f32[8,384]{1,0:T(8,128)}) custom-call(s32[5]{0:T(128)} %stack.132.s_ref, bf16[1568,1536]{1,0:T(8,128)(2,1)} %get-tuple-element.242.qkv_ref.ref, bf16[1568,512]{1,0:T(8,128)(2,1)} %get-tuple-element.281.grad_ref, ...), custom_call_target="tpu_custom_call" | custom-call | flops 50352619520 | bytes 3211264 | tf_op jit(solution)/shard_map/attend_back/pallas_call | solution.py:190
  316.1 20.7 %attend_back.6 = (bf16[1568,384]{1,0:T(8,128)(2,1)}, bf16[384,512]{1,0:T(8,128)(2,1)}, bf16[384,512]{1,0:T(8,128)(2,1)}, f32[8,384]{1,0:T(8,128)}) custom-call(s32[5]{0:T(128)} %stack.132.s_ref, bf16[1568,1536]{1,0:T(8,128)(2,1)} %get-tuple-element.242.qkv_ref.ref, bf16[1568,512]{1,0:T(8,128)(2,1)} %get-tuple-element.281.grad_ref, ...), custom_call_target="tpu_custom_call" | custom-call | flops 50352619520 | bytes 3211264 | tf_op jit(solution)/shard_map/attend_back/pallas_call | solution.py:190
  336.8 6.7 %collective-permute-done.24 = bf16[1280,512]{1,0:T(8,128)(2,1)} collective-permute-done((bf16[1280,512]{1,0:T(8,128)(2,1)}, bf16[1280,512]{1,0:T(8,128)(2,1)}, u32[]{:S(2)}, u32[]{:S(2)}) %collective-permute-start.24) | collective-permute-done | bytes 1310752 | tf_op jit(solution)/shard_map/ppermute | solution.py:1443
  350.1 6.3 %collective-permute-start.25 = (bf16[784,1024]{1,0:T(8,128)(2,1)S(1)}, bf16[784,1024]{1,0:T(8,128)(2,1)}, u32[]{:S(2)}, u32[]{:S(2)}) collective-permute-start(bf16[784,1024]{1,0:T(8,128)(2,1)S(1)} %copy-done), channel_id=1, source_target_pairs={{1,2},{2,1},{5,6},{6,5},{9,10},{10,9},{13,14},{14,13},{17,18},{18,... | collective-permute-start | bytes 4816904 | tf_op jit(solution)/shard_map/ppermute | solution.py:1514
  359.0 21.0 %attend_back.7 = (bf16[1568,384]{1,0:T(8,128)(2,1)}, bf16[384,512]{1,0:T(8,128)(2,1)}, bf16[384,512]{1,0:T(8,128)(2,1)}, f32[8,384]{1,0:T(8,128)}) custom-call(s32[5]{0:T(128)} %stack.132.s_ref, bf16[1568,1536]{1,0:T(8,128)(2,1)} %get-tuple-element.242.qkv_ref.ref, bf16[1568,512]{1,0:T(8,128)(2,1)} %get-tuple-element.281.grad_ref, ...), custom_call_target="tpu_custom_call" | custom-call | flops 50352619520 | bytes 3211264 | tf_op jit(solution)/shard_map/attend_back/pallas_call | solution.py:190
  389.0 9.9 %first_grad.1 = (bf16[784,1024]{1,0:T(8,128)(2,1)}, bf16[784,1024]{1,0:T(8,128)(2,1)}) custom-call(s32[5]{0:T(128)} %stack.132.s_ref, bf16[1568,384]{1,0:T(8,128)(2,1)} %get-tuple-element.353.refs_0_, bf16[1568,384]{1,0:T(8,128)(2,1)} %get-tuple-element.354.refs_1_, bf16[1568,384]{1,0:T(8,128)(2,1)} %get-tuple-element.355.refs_2_, ...), custom_call_target="tpu_custom_call" | custom-call | flops 4932501504 | bytes 15925248 | tf_op jit(solution)/shard_map/first_grad/pallas_call | solution.py:399
  398.9 5.2 collective-permute-done.29
  404.1 8.3 %collective-permute-done.30 = bf16[256,1024]{1,0:T(8,128)(2,1)} collective-permute-done((bf16[256,1024]{1,0:T(8,128)(2,1)}, bf16[256,1024]{1,0:T(8,128)(2,1)}, u32[]{:S(2)}, u32[]{:S(2)}) %collective-permute-start.30) | collective-permute-done | bytes 524320 | tf_op jit(solution)/shard_map/ppermute | solution.py:1420
  428.3 8.4 %first_back.1 = (bf16[784,1024]{1,0:T(8,128)(2,1)}, f32[8,1024]{1,0:T(8,128)}) custom-call(s32[5]{0:T(128)} %stack.132.s_ref, bf16[784,1024]{1,0:T(8,128)(2,1)} %get-tuple-element.360.g_ref, bf16[784,1024]{1,0:T(8,128)(2,1)} %collective-permute-done.31.r_ref, bf16[784,1024]{1,0:T(8,128)(2,1)} %get-tuple-element.233.x_ref, ...), custom_call_target="tpu_custom_call" | custom-call | bytes 12853248 | tf_op jit(solution)/shard_map/first_back/pallas_call | solution.py:399
  437.5 10.7 %collective-permute-done.32 = bf16[160,512]{1,0:T(8,128)(2,1)} collective-permute-done((bf16[160,512]{1,0:T(8,128)(2,1)}, bf16[160,512]{1,0:T(8,128)(2,1)}, u32[]{:S(2)}, u32[]{:S(2)}) %collective-permute-start.32) | collective-permute-done | bytes 163872 | tf_op jit(solution)/shard_map/ppermute | solution.py:1394
  448.1 5.9 %collective-permute-done.33 = bf16[384,512]{1,0:T(8,128)(2,1)} collective-permute-done((bf16[384,512]{1,0:T(8,128)(2,1)}, bf16[384,512]{1,0:T(8,128)(2,1)}, u32[]{:S(2)}, u32[]{:S(2)}) %collective-permute-start.33) | collective-permute-done | bytes 393248 | tf_op jit(solution)/shard_map/ppermute | solution.py:1449
  466.1 4.9 collective-permute-done.38
  473.5 8.8 %collective-permute-done.41 = f32[6144]{0:T(1024)S(1)} collective-permute-done((f32[6144]{0:T(1024)S(1)}, f32[6144]{0:T(1024)S(1)}, u32[]{:S(2)}, u32[]{:S(2)}) %collective-permute-start.41) | collective-permute-done | bytes 24608 | tf_op jit(solution)/shard_map/ppermute | solution.py:1457
  486.1 4.6 collective-permute-done.48
  513.9 5.6 %collective-permute-done.56.refs_5_ = bf16[384,512]{1,0:T(8,128)(2,1)} collective-permute-done((bf16[384,512]{1,0:T(8,128)(2,1)S(1)}, bf16[384,512]{1,0:T(8,128)(2,1)}, u32[]{:S(2)}, u32[]{:S(2)}) %collective-permute-start.56) | collective-permute-done | bytes 393248 | tf_op jit(solution)/shard_map/ppermute | solution.py:1408
  521.7 10.5 %finish_feed.1 = (f32[512,4096]{1,0:T(8,128)}, f32[2,2,512,1024]{3,2,1,0:T(8,128)}) custom-call(s32[5]{0:T(128)} %stack.132.s_ref, bf16[512,1024]{1,0:T(8,128)(2,1)} %bitcast.19.refs_0_, bf16[512,1024]{1,0:T(8,128)(2,1)} %collective-permute-done.34.refs_1_, bf16[512,1024]{1,0:T(8,128)(2,1)} %collective-permute-done.35.refs_2_, bf16[512,1024]{1,0:T(8,128)(2,1)} %copy-done.14, ...), custom_call_target="tpu_custom_call" | custom-call | bytes 16777216 | tf_op jit(solution)/shard_map/finish_feed/pallas_call | solution.py:399
  534.2 7.1 %finish_attention.1 = (f32[512,1024]{1,0:T(8,128)}, f32[512,1024]{1,0:T(8,128)}, f32[512,1024]{1,0:T(8,128)}, f32[512,1024]{1,0:T(8,128)}) custom-call(s32[5]{0:T(128)} %stack.132.s_ref, bf16[640,512]{1,0:T(8,128)(2,1)} %bitcast.92, bf16[640,512]{1,0:T(8,128)(2,1)} %copy-done.20, bf16[640,512]{1,0:T(8,128)(2,1)} %collective-permute-done.45.refs_2_, ...), custom_call_target="tpu_custom_call" | custom-call | bytes 8388608 | tf_op jit(solution)/shard_map/finish_attention/pallas_call | solution.py:399
  (304 shorter events, 158.1 us)
Async XLA Ops:
  0.7 39.8 %collective-permute-start = (bf16[784,1024]{1,0:T(8,128)(2,1)}, bf16[784,1024]{1,0:T(8,128)(2,1)S(1)}, u32[]{:S(2)}, u32[]{:S(2)}) collective-permute-start(bf16[784,1024]{1,0:T(8,128)(2,1)} %bitcast.94), channel_id=1, source_target_pairs={{1,2},{2,1},{5,6},{6,5},{9,10},{10,9},{13,14},{14,13},{17,18},{18,... | collective-permute-start | bytes 4816904 | tf_op jit(solution)/shard_map/ppermute | solution.py:1514
  10.3 30.1 %collective-permute-start.1 = (bf16[256,1536]{1,0:T(8,128)(2,1)}, bf16[256,1536]{1,0:T(8,128)(2,1)}, u32[]{:S(2)}, u32[]{:S(2)}) collective-permute-start(bf16[256,1536]{1,0:T(8,128)(2,1)} %get-tuple-element.222), channel_id=1, source_target_pairs={{0,1},{1,0},{2,3},{3,2},{4,5},{5,4},{6,7},{7,6},{8,9},{9,8},{10,11... | collective-permute-start | bytes 2359304 | tf_op jit(solution)/shard_map/ppermute | solution.py:1502
  16.9 23.6 %collective-permute-start.2 = (f32[6144]{0:T(1024)S(1)}, f32[6144]{0:T(1024)S(1)}, u32[]{:S(2)}, u32[]{:S(2)}) collective-permute-start(f32[6144]{0:T(1024)S(1)} %constant_dynamic-update-slice_fusion.10), channel_id=1, source_target_pairs={{0,1},{1,0},{2,3},{3,2},{4,5},{5,4},{6,7},{7,6},{8,9},{9,8},{10,11... | collective-permute-start | bytes 73736 | tf_op jit(solution)/shard_map/ppermute | solution.py:1502
  40.5 25.0 %collective-permute-start.4 = (bf16[512,1024]{1,0:T(8,128)(2,1)}, bf16[512,1024]{1,0:T(8,128)(2,1)}, u32[]{:S(2)}, u32[]{:S(2)}) collective-permute-start(bf16[512,1024]{1,0:T(8,128)(2,1)} %pack_feed.2), channel_id=1, source_target_pairs={{0,1},{1,0},{2,3},{3,2},{4,5},{5,4},{6,7},{7,6},{8,9},{9,8},{10,11... | collective-permute-start | bytes 3145736 | tf_op jit(solution)/shard_map/ppermute | solution.py:1502
  42.4 19.8 %collective-permute-start.3 = (bf16[256,1536]{1,0:T(8,128)(2,1)}, bf16[256,1536]{1,0:T(8,128)(2,1)}, u32[]{:S(2)}, u32[]{:S(2)}) collective-permute-start(bf16[256,1536]{1,0:T(8,128)(2,1)} %collective-permute-done.1.piece_ref), channel_id=1, source_target_pairs={{0,4},{4,0},{1,5},{5,1},{2,6},{6,2},{3,7},{7,3},{8,12},{12,8},{9,1... | collective-permute-start | bytes 2359304 | tf_op jit(solution)/shard_map/ppermute | solution.py:1508
  68.7 57.4 %collective-permute-start.10 = (bf16[512,1024]{1,0:T(8,128)(2,1)}, bf16[512,1024]{1,0:T(8,128)(2,1)}, u32[]{:S(2)}, u32[]{:S(2)}) collective-permute-start(bf16[512,1024]{1,0:T(8,128)(2,1)} %collective-permute-done.4.x_piece), channel_id=1, source_target_pairs={{0,4},{4,0},{1,5},{5,1},{2,6},{6,2},{3,7},{7,3},{8,12},{12,8},{9,1... | collective-permute-start | bytes 3145736 | tf_op jit(solution)/shard_map/ppermute | solution.py:1508
  71.2 35.0 %collective-permute-start.8 = (bf16[512,1024]{1,0:T(8,128)(2,1)}, bf16[512,1024]{1,0:T(8,128)(2,1)}, u32[]{:S(2)}, u32[]{:S(2)}) collective-permute-start(bf16[512,1024]{1,0:T(8,128)(2,1)} %pack_feed.3), channel_id=1, source_target_pairs={{0,1},{1,0},{2,3},{3,2},{4,5},{5,4},{6,7},{7,6},{8,9},{9,8},{10,11... | collective-permute-start | bytes 3145736 | tf_op jit(solution)/shard_map/ppermute | solution.py:1502
  82.9 23.3 %collective-permute-start.7 = (bf16[128,1024]{1,0:T(8,128)(2,1)S(1)}, bf16[128,1024]{1,0:T(8,128)(2,1)}, u32[]{:S(2)}, u32[]{:S(2)}) collective-permute-start(bf16[128,1024]{1,0:T(8,128)(2,1)S(1)} %collective-permute-done.6.piece_ref), channel_id=1, source_target_pairs={{0,4},{4,0},{1,5},{5,1},{2,6},{6,2},{3,7},{7,3},{8,12},{12,8},{9,1... | collective-permute-start | bytes 786440 | tf_op jit(solution)/shard_map/ppermute | solution.py:1508
  107.7 28.9 %collective-permute-start.9 = (bf16[784,1024]{1,0:T(8,128)(2,1)S(1)}, bf16[784,1024]{1,0:T(8,128)(2,1)}, u32[]{:S(2)}, u32[]{:S(2)}) collective-permute-start(bf16[784,1024]{1,0:T(8,128)(2,1)S(1)} %bitcast.93), channel_id=1, source_target_pairs={{1,2},{2,1},{5,6},{6,5},{9,10},{10,9},{13,14},{14,13},{17,18},{18,... | collective-permute-start | bytes 4816904 | tf_op jit(solution)/shard_map/ppermute | solution.py:1514
  111.7 24.8 %collective-permute-start.11 = (bf16[512,1024]{1,0:T(8,128)(2,1)}, bf16[512,1024]{1,0:T(8,128)(2,1)}, u32[]{:S(2)}, u32[]{:S(2)}) collective-permute-start(bf16[512,1024]{1,0:T(8,128)(2,1)} %collective-permute-done.8.z_piece), channel_id=1, source_target_pairs={{0,8},{8,0},{16,24},{24,16},{1,9},{9,1},{17,25},{25,17},{2,10},{10... | collective-permute-start | bytes 3145736 | tf_op jit(solution)/shard_map/ppermute | solution.py:1511
  213.5 15.7 %collective-permute-start.17 = (bf16[784,1024]{1,0:T(8,128)(2,1)}, bf16[784,1024]{1,0:T(8,128)(2,1)S(1)}, u32[]{:S(2)}, u32[]{:S(2)}) collective-permute-start(bf16[784,1024]{1,0:T(8,128)(2,1)} %get-tuple-element.276), channel_id=1, source_target_pairs={{0,2},{2,0},{1,3},{3,1},{4,6},{6,4},{5,7},{7,5},{8,10},{10,8},{9,1... | collective-permute-start | bytes 4816904 | tf_op jit(solution)/shard_map/ppermute | solution.py:1505
  227.5 47.2 %collective-permute-start.20 = (bf16[1024,1024]{1,0:T(8,128)(2,1)}, bf16[1024,1024]{1,0:T(8,128)(2,1)}, u32[]{:S(2)}, u32[]{:S(2)}) collective-permute-start(bf16[1024,1024]{1,0:T(8,128)(2,1)} %get-tuple-element.293), channel_id=1, source_target_pairs={{0,4},{4,0},{1,5},{5,1},{2,6},{6,2},{3,7},{7,3},{8,12},{12,8},{9,1... | collective-permute-start | bytes 6291464 | tf_op jit(solution)/shard_map/ppermute | solution.py:1508
  227.7 39.9 %collective-permute-start.18 = (bf16[512,1024]{1,0:T(8,128)(2,1)}, bf16[512,1024]{1,0:T(8,128)(2,1)}, u32[]{:S(2)}, u32[]{:S(2)}) collective-permute-start(bf16[512,1024]{1,0:T(8,128)(2,1)} %get-tuple-element.291), channel_id=1, source_target_pairs={{0,1},{1,0},{2,3},{3,2},{4,5},{5,4},{6,7},{7,6},{8,9},{9,8},{10,11... | collective-permute-start | bytes 3145736 | tf_op jit(solution)/shard_map/ppermute | solution.py:1502
  227.7 46.8 %collective-permute-start.19 = (bf16[512,1024]{1,0:T(8,128)(2,1)}, bf16[512,1024]{1,0:T(8,128)(2,1)}, u32[]{:S(2)}, u32[]{:S(2)}) collective-permute-start(bf16[512,1024]{1,0:T(8,128)(2,1)} %get-tuple-element.292), channel_id=1, source_target_pairs={{0,1},{1,0},{2,3},{3,2},{4,5},{5,4},{6,7},{7,6},{8,9},{9,8},{10,11... | collective-permute-start | bytes 3145736 | tf_op jit(solution)/shard_map/ppermute | solution.py:1502
  282.1 26.7 %collective-permute-start.21 = (bf16[512,1024]{1,0:T(8,128)(2,1)}, bf16[512,1024]{1,0:T(8,128)(2,1)}, u32[]{:S(2)}, u32[]{:S(2)}) collective-permute-start(bf16[512,1024]{1,0:T(8,128)(2,1)} %get-tuple-element.301), channel_id=1, source_target_pairs={{0,4},{4,0},{1,5},{5,1},{2,6},{6,2},{3,7},{7,3},{8,12},{12,8},{9,1... | collective-permute-start | bytes 3145736 | tf_op jit(solution)/shard_map/ppermute | solution.py:1624
  284.8 23.9 %collective-permute-start.22 = (bf16[512,1024]{1,0:T(8,128)(2,1)}, bf16[512,1024]{1,0:T(8,128)(2,1)}, u32[]{:S(2)}, u32[]{:S(2)}) collective-permute-start(bf16[512,1024]{1,0:T(8,128)(2,1)} %get-tuple-element.302), channel_id=1, source_target_pairs={{0,1},{1,0},{2,3},{3,2},{4,5},{5,4},{6,7},{7,6},{8,9},{9,8},{10,11... | collective-permute-start | bytes 3145736 | tf_op jit(solution)/shard_map/ppermute | solution.py:1502
  313.5 23.3 %collective-permute-start.23 = (bf16[512,1024]{1,0:T(8,128)(2,1)}, bf16[512,1024]{1,0:T(8,128)(2,1)}, u32[]{:S(2)}, u32[]{:S(2)}) collective-permute-start(bf16[512,1024]{1,0:T(8,128)(2,1)} %get-tuple-element.318), channel_id=1, source_target_pairs={{0,8},{8,0},{16,24},{24,16},{1,9},{9,1},{17,25},{25,17},{2,10},{10... | collective-permute-start | bytes 3145736 | tf_op jit(solution)/shard_map/ppermute | solution.py:1420
  314.9 28.6 %collective-permute-start.24 = (bf16[1280,512]{1,0:T(8,128)(2,1)}, bf16[1280,512]{1,0:T(8,128)(2,1)}, u32[]{:S(2)}, u32[]{:S(2)}) collective-permute-start(bf16[1280,512]{1,0:T(8,128)(2,1)} %pad_maximum_fusion), channel_id=1, source_target_pairs={{0,1},{1,0},{2,3},{3,2},{4,5},{5,4},{6,7},{7,6},{8,9},{9,8},{10,11... | collective-permute-start | bytes 3932168 | tf_op jit(solution)/shard_map/ppermute | solution.py:1443
  350.1 33.0 %collective-permute-start.25 = (bf16[784,1024]{1,0:T(8,128)(2,1)S(1)}, bf16[784,1024]{1,0:T(8,128)(2,1)}, u32[]{:S(2)}, u32[]{:S(2)}) collective-permute-start(bf16[784,1024]{1,0:T(8,128)(2,1)S(1)} %copy-done), channel_id=1, source_target_pairs={{1,2},{2,1},{5,6},{6,5},{9,10},{10,9},{13,14},{14,13},{17,18},{18,... | collective-permute-start | bytes 4816904 | tf_op jit(solution)/shard_map/ppermute | solution.py:1514
  356.3 26.7 %collective-permute-start.27 = (bf16[640,512]{1,0:T(8,128)(2,1)}, bf16[640,512]{1,0:T(8,128)(2,1)}, u32[]{:S(2)}, u32[]{:S(2)}) collective-permute-start(bf16[640,512]{1,0:T(8,128)(2,1)} %get-tuple-element.332), channel_id=1, source_target_pairs={{0,4},{4,0},{1,5},{5,1},{2,6},{6,2},{3,7},{7,3},{8,12},{12,8},{9,1... | collective-permute-start | bytes 1966088 | tf_op jit(solution)/shard_map/ppermute | solution.py:1449
  356.7 26.3 %collective-permute-start.26 = (bf16[256,1024]{1,0:T(8,128)(2,1)}, bf16[256,1024]{1,0:T(8,128)(2,1)}, u32[]{:S(2)}, u32[]{:S(2)}) collective-permute-start(bf16[256,1024]{1,0:T(8,128)(2,1)} %get-tuple-element.330), channel_id=1, source_target_pairs={{0,16},{8,24},{16,0},{24,8},{1,17},{9,25},{17,1},{25,9},{2,18},{10... | collective-permute-start | bytes 1572872 | tf_op jit(solution)/shard_map/ppermute | solution.py:1420
  383.0 29.4 %collective-permute-start.28 = (bf16[768,512]{1,0:T(8,128)(2,1)}, bf16[768,512]{1,0:T(8,128)(2,1)}, u32[]{:S(2)}, u32[]{:S(2)}) collective-permute-start(bf16[768,512]{1,0:T(8,128)(2,1)} %pad_maximum_fusion.2), channel_id=1, source_target_pairs={{0,1},{1,0},{2,3},{3,2},{4,5},{5,4},{6,7},{7,6},{8,9},{9,8},{10,11... | collective-permute-start | bytes 2359304 | tf_op jit(solution)/shard_map/ppermute | solution.py:1443
  386.4 26.1 %collective-permute-start.30 = (bf16[256,1024]{1,0:T(8,128)(2,1)}, bf16[256,1024]{1,0:T(8,128)(2,1)}, u32[]{:S(2)}, u32[]{:S(2)}) collective-permute-start(bf16[256,1024]{1,0:T(8,128)(2,1)} %add_convert_fusion.9), channel_id=1, source_target_pairs={{0,16},{8,24},{16,0},{24,8},{1,17},{9,25},{17,1},{25,9},{2,18},{10... | collective-permute-start | bytes 1572872 | tf_op jit(solution)/shard_map/ppermute | solution.py:1420
  387.4 16.7 %collective-permute-start.29 = (bf16[320,512]{1,0:T(8,128)(2,1)}, bf16[320,512]{1,0:T(8,128)(2,1)S(1)}, u32[]{:S(2)}, u32[]{:S(2)}) collective-permute-start(bf16[320,512]{1,0:T(8,128)(2,1)} %get-tuple-element.352), channel_id=1, source_target_pairs={{0,8},{8,0},{16,24},{24,16},{1,9},{9,1},{17,25},{25,17},{2,10},{10... | collective-permute-start | bytes 983048 | tf_op jit(solution)/shard_map/ppermute | solution.py:1394
  420.5 33.6 %collective-permute-start.34 = (bf16[512,1024]{1,0:T(8,128)(2,1)}, bf16[512,1024]{1,0:T(8,128)(2,1)}, u32[]{:S(2)}, u32[]{:S(2)}) collective-permute-start(bf16[512,1024]{1,0:T(8,128)(2,1)} %bitcast.19.refs_0_), channel_id=1, source_target_pairs={{0,4},{4,0},{1,5},{5,1},{2,6},{6,2},{3,7},{7,3},{8,12},{12,8},{9,1... | collective-permute-start | bytes 3145736 | tf_op jit(solution)/shard_map/ppermute | solution.py:1434
  421.7 32.4 %collective-permute-start.35 = (bf16[512,1024]{1,0:T(8,128)(2,1)}, bf16[512,1024]{1,0:T(8,128)(2,1)}, u32[]{:S(2)}, u32[]{:S(2)}) collective-permute-start(bf16[512,1024]{1,0:T(8,128)(2,1)} %bitcast.19.refs_0_), channel_id=1, source_target_pairs={{0,8},{8,0},{16,24},{24,16},{1,9},{9,1},{17,25},{25,17},{2,10},{10... | collective-permute-start | bytes 3145736 | tf_op jit(solution)/shard_map/ppermute | solution.py:1420
  425.3 28.8 %collective-permute-start.33 = (bf16[384,512]{1,0:T(8,128)(2,1)}, bf16[384,512]{1,0:T(8,128)(2,1)}, u32[]{:S(2)}, u32[]{:S(2)}) collective-permute-start(bf16[384,512]{1,0:T(8,128)(2,1)} %get-tuple-element.366), channel_id=1, source_target_pairs={{0,4},{4,0},{1,5},{5,1},{2,6},{6,2},{3,7},{7,3},{8,12},{12,8},{9,1... | collective-permute-start | bytes 1179656 | tf_op jit(solution)/shard_map/ppermute | solution.py:1449
  426.2 22.0 %collective-permute-start.32 = (bf16[160,512]{1,0:T(8,128)(2,1)}, bf16[160,512]{1,0:T(8,128)(2,1)}, u32[]{:S(2)}, u32[]{:S(2)}) collective-permute-start(bf16[160,512]{1,0:T(8,128)(2,1)} %get-tuple-element.368), channel_id=1, source_target_pairs={{0,16},{8,24},{16,0},{24,8},{1,17},{9,25},{17,1},{25,9},{2,18},{10... | collective-permute-start | bytes 491528 | tf_op jit(solution)/shard_map/ppermute | solution.py:1394
  464.2 27.8 %collective-permute-start.47 = (bf16[512,1024]{1,0:T(8,128)(2,1)}, bf16[512,1024]{1,0:T(8,128)(2,1)S(1)}, u32[]{:S(2)}, u32[]{:S(2)}) collective-permute-start(bf16[512,1024]{1,0:T(8,128)(2,1)} %bitcast.19.refs_0_), channel_id=1, source_target_pairs={{0,2},{2,0},{1,3},{3,1},{4,6},{6,4},{5,7},{7,5},{8,10},{10,8},{9,1... | collective-permute-start | bytes 3145736 | tf_op jit(solution)/shard_map/ppermute | solution.py:1435
  464.8 34.5 %collective-permute-start.46 = (bf16[512,1024]{1,0:T(8,128)(2,1)}, bf16[512,1024]{1,0:T(8,128)(2,1)S(1)}, u32[]{:S(2)}, u32[]{:S(2)}) collective-permute-start(bf16[512,1024]{1,0:T(8,128)(2,1)} %collective-permute-done.35.refs_2_), channel_id=1, source_target_pairs={{0,4},{4,0},{1,5},{5,1},{2,6},{6,2},{3,7},{7,3},{8,12},{12,8},{9,1... | collective-permute-start | bytes 3145736 | tf_op jit(solution)/shard_map/ppermute | solution.py:1435
  485.0 18.9 %collective-permute-start.44 = (bf16[640,512]{1,0:T(8,128)(2,1)S(1)}, bf16[640,512]{1,0:T(8,128)(2,1)S(1)}, u32[]{:S(2)}, u32[]{:S(2)}) collective-permute-start(bf16[640,512]{1,0:T(8,128)(2,1)S(1)} %bitcast.90), channel_id=1, source_target_pairs={{0,4},{4,0},{1,5},{5,1},{2,6},{6,2},{3,7},{7,3},{8,12},{12,8},{9,1... | collective-permute-start | bytes 1966088 | tf_op jit(solution)/shard_map/ppermute | solution.py:1408
  492.0 28.3 %collective-permute-start.40 = (bf16[784,1024]{1,0:T(8,128)(2,1)S(1)}, bf16[784,1024]{1,0:T(8,128)(2,1)S(1)}, u32[]{:S(2)}, u32[]{:S(2)}) collective-permute-start(bf16[784,1024]{1,0:T(8,128)(2,1)S(1)} %copy-done.8), channel_id=1, source_target_pairs={{1,2},{2,1},{5,6},{6,5},{9,10},{10,9},{13,14},{14,13},{17,18},{18,... | collective-permute-start | bytes 4816904 | tf_op jit(solution)/shard_map/ppermute | solution.py:1514
  (74 other events, 540.4 us)

commit v7 on v6

--- a/solution.py
+++ b/solution.py
@@ -182,21 +182,21 @@
             send_ref[...] = grad
 
 
-def attend_back(scal, qkv, grad, out, lse, first, first_pair, last_pair, tile=256):
+def attend_back(scal, qkv, grad, out, lse, first, tile=256):
     rows, full = qkv.shape
     width = first.shape[1]
     padded = padded_rows(rows, tile)
-    count = last_pair - first_pair
+    count = 1
     return pl.pallas_call(
         functools.partial(attend_back_kernel, tile, rows, padded),
         grid_spec=pltpu.PrefetchScalarGridSpec(
             num_scalar_prefetch=1,
             grid=(count,),
             in_specs=[
-                pl.BlockSpec((rows, 3 * PAIR), lambda i, s: (0, i + first_pair)),
-                pl.BlockSpec((rows, PAIR), lambda i, s: (0, i + first_pair)),
-                pl.BlockSpec((rows, PAIR), lambda i, s: (0, i + first_pair)),
-                pl.BlockSpec((None, 2, lse.shape[2]), lambda i, s: (i + first_pair, 0, 0)),
+                pl.BlockSpec((rows, 3 * PAIR), lambda i, s: (0, s[5])),
+                pl.BlockSpec((rows, PAIR), lambda i, s: (0, s[5])),
+                pl.BlockSpec((rows, PAIR), lambda i, s: (0, s[5])),
+                pl.BlockSpec((None, 2, lse.shape[2]), lambda i, s: (s[5], 0, 0)),
                 pl.BlockSpec((rows, width), lambda i, s: (0, 0), pipeline_mode=pl.Buffered(1)),
             ],
             out_specs=[
@@ -1610,7 +1610,8 @@
 
     def back(pair):
         gate = order.pin(lse)
-        backs.append(attend_back(scal, qkv, grad_mixed, mixed, gate, first_all, pair, pair + 1))
+        named = jnp.concatenate([scal, jnp.full((1,), pair, jnp.int32)])
+        backs.append(attend_back(named, qkv, grad_mixed, mixed, gate, first_all))
         backs[-1] = order.pin(*backs[-1])
         order.fence(backs[-1][3])
 
@@ -1661,8 +1662,9 @@
     )
     first_own, first_part = order.pin(first_own, first_part)
     order.fence(first_part)
-    advance(order, late, early, ranges)
+    advance(order, late, early)
     first_part_in = swap_core(order.pin(first_part))
+    advance(order, ranges)
     tokens_out, sums_one = first_back(
         scal, first_own, order.pin(first_part_in), x, grad_low, gain_one
     )
@@ -1689,7 +1691,7 @@
     advance(order, vectors, late)
     advance(order, early, ranges, late)
     advance(order, ranges, vectors, early)
-    up_weight_grad, down_weight_grad = finish_feed(scal, feed_parts)
+    up_weight_grad, down_weight_grad = order.pin(*finish_feed(scal, feed_parts))
     advance(order, late)
     advance(order, late)
     (entries,) = vector_parts

time: 552 us -> 545 us (0.987)
  waiting for transfers between devices: 135 us -> 119 us
    ppermute x12, waiting for transfers between devices: 32.3 us -> 24.2 us  [exchange(): lax.ppermute(values, 'line', [(i, i ^ 1 << bit) for i in range(deep)])]
    unnamed x118 -> x114, local copies, waits for them, and re-layouts: 14.8 us -> 16.2 us
  transfers between devices with their start and end apart: 59 -> 59, of which waited for: 23 -> 23; matrix products, arithmetic and copies ran while one was open for 6% -> 8% of each run, Pallas kernels for 37% -> 37%
where the time goes in v7:
time: 545 us; the launch traced here: 535 us
  Pallas kernels  272 us (50%)
  waiting for transfers between devices  119 us (22%)
  starting transfers between devices  68.5 us (13%)
  other arithmetic  44.3 us (8%)
  local copies, waits for them, and re-layouts  29.4 us (5%)
    pallas_call x14, Pallas kernels, run(): pl.pallas_call(kernel, grid_spec=pltpu.PrefetchScalarGridSpec(num_scalar_...  97.5 us
    pallas_call x4, Pallas kernels, attend_back(): pl.pallas_call(functools.partial(attend_back_kernel, tile, rows, padded),...  83.7 us
    pallas_call x1, Pallas kernels, feed(): pl.pallas_call(feed_kernel, grid_spec=pltpu.PrefetchScalarGridSpec(num_sc...  60.5 us
    ppermute x8, waiting for transfers between devices, swap_half(): return lax.ppermute(values, 'half', SWAP)  32.1 us
    pallas_call x2, Pallas kernels, attend(): pl.pallas_call(kernel if kept is None else lambda ref, a, b, *rest: kerne...  30.6 us
    ppermute x12, waiting for transfers between devices, exchange(): lax.ppermute(values, 'line', [(i, i ^ 1 << bit) for i in range(deep)])  24.2 us
    ppermute x4, starting transfers between devices, cross_over(): return lax.ppermute(values, ('core', 'half'), cross)  18.1 us
    unnamed x114, local copies, waits for them, and re-layouts  16.2 us
  transfers between devices with their start and end apart: 59, of which 23 were waited for; matrix products, arithmetic and copies ran while one was open for 8% of the time, Pallas kernels for 37%

profile of v7, /device:TPU:1, one launch (start us, length us, event | category | flops | bytes accessed | tf_op | source)
XLA Modules:
  0.0 535.4 jit_solution(15208308208983318063)
XLA Ops:
  0.7 4.5 collective-permute-start
  5.9 4.5 pack_qkv.1
  18.5 22.0 %collective-permute-done.2 = f32[6144]{0:T(1024)S(1)} collective-permute-done((f32[6144]{0:T(1024)S(1)}, f32[6144]{0:T(1024)S(1)}, u32[]{:S(2)}, u32[]{:S(2)}) %collective-permute-start.2) | collective-permute-done | bytes 24608 | tf_op jit(solution)/shard_map/ppermute | solution.py:1502
  45.0 4.2 first_norm.1
  49.2 13.1 %collective-permute-done.3.beside_ref = bf16[256,1536]{1,0:T(8,128)(2,1)} collective-permute-done((bf16[256,1536]{1,0:T(8,128)(2,1)}, bf16[256,1536]{1,0:T(8,128)(2,1)}, u32[]{:S(2)}, u32[]{:S(2)}) %collective-permute-start.3) | collective-permute-done | bytes 786464 | tf_op jit(solution)/shard_map/ppermute | solution.py:1508
  71.8 11.1 %project.1 = (bf16[1568,1536]{1,0:T(8,128)(2,1)}, bf16[1024,1536]{1,0:T(8,128)(2,1)}, bf16[1568,1024]{1,0:T(8,128)(2,1)}) custom-call(s32[5]{0:T(128)} %stack.132.s_ref, bf16[784,1024]{1,0:T(8,128)(2,1)} %get-tuple-element.236.mine_ref, bf16[784,1024]{1,0:T(8,128)(2,1)} %collective-permute-done.5.theirs_ref, bf16[512,1536]{1,0:T(8,128)(2,1)} %get-tuple-element.240.own_ref, ...), custom_call_target="tpu_custom_call" | custom-call | flops 4932501504 | bytes 12726272 | tf_op jit(solution)/shard_map/project/pallas_call | solution.py:399
  84.2 22.0 %attend.2 = (bf16[1568,512]{1,0:T(8,128)(2,1)}, f32[4,2,1664]{2,1,0:T(2,128)}) custom-call(bf16[1568,1536]{1,0:T(8,128)(2,1)} %get-tuple-element.244.qkv_ref.ref), custom_call_target="tpu_custom_call" | custom-call | flops 60423143424 | bytes 4816896 | tf_op jit(solution)/shard_map/attend/pallas_call | solution.py:101
  113.1 8.7 %attend.3 = (bf16[1568,512]{1,0:T(8,128)(2,1)}, f32[4,2,1664]{2,1,0:T(2,128)}) custom-call(bf16[1568,1536]{1,0:T(8,128)(2,1)} %get-tuple-element.244.qkv_ref.ref, bf16[1568,512]{1,0:T(8,128)(2,1)} %get-tuple-element.245.a, f32[4,2,1664]{2,1,0:T(2,128)} %copy.58.b), custom_call_target="tpu_custom_call", output_to_operand_aliasing={{0}: (1, {}), {1}: (2, {})} | custom-call | flops 20141047808 | bytes 1605632 | tf_op jit(solution)/shard_map/attend/pallas_call | solution.py:101
  121.8 4.3 out_other.1
  126.1 10.5 %collective-permute-done.11.z_beside = bf16[512,1024]{1,0:T(8,128)(2,1)} collective-permute-done((bf16[512,1024]{1,0:T(8,128)(2,1)}, bf16[512,1024]{1,0:T(8,128)(2,1)}, u32[]{:S(2)}, u32[]{:S(2)}) %collective-permute-start.11) | collective-permute-done | bytes 1048608 | tf_op jit(solution)/shard_map/ppermute | solution.py:1511
  140.8 6.1 %second_norm.1 = (f32[784,1024]{1,0:T(8,128)}, bf16[784,1024]{1,0:T(8,128)(2,1)}) custom-call(s32[5]{0:T(128)} %stack.132.s_ref, bf16[1568,512]{1,0:T(8,128)(2,1)} %get-tuple-element.252.mixed_ref.out_ref, bf16[512,1024]{1,0:T(8,128)(2,1)} %get-tuple-element.253.w_ref, bf16[784,1024]{1,0:T(8,128)(2,1)} %get-tuple-element.235.x_ref, ...), custom_call_target="tpu_custom_call" | custom-call | flops 822083584 | bytes 11755520 | tf_op jit(solution)/shard_map/second_norm/pallas_call | solution.py:399
  152.8 60.5 %feed.1 = (bf16[784,1024]{1,0:T(8,128)(2,1)}, bf16[784,1024]{1,0:T(8,128)(2,1)}, bf16[784,1024]{1,0:T(8,128)(2,1)}, bf16[784,1024]{1,0:T(8,128)(2,1)}, bf16[512,...) custom-call(s32[5]{0:T(128)} %stack.132.s_ref, ...), custom_call_target="tpu_custom_call" | custom-call | flops 39460012032 | bytes 25690112 | tf_op jit(solution)/shard_map/feed/pallas_call | solution.py:357
  213.9 4.2 collective-permute-done.15.r_ref
  218.1 8.8 %second_back.1 = (bf16[784,1024]{1,0:T(8,128)(2,1)}, f32[8,1024]{1,0:T(8,128)}) custom-call(s32[5]{0:T(128)} %stack.132.s_ref, bf16[784,1024]{1,0:T(8,128)(2,1)} %get-tuple-element.266.g_ref, bf16[784,1024]{1,0:T(8,128)(2,1)} %collective-permute-done.15.r_ref, f32[784,1024]{1,0:T(8,128)} %get-tuple-element.274.mid_ref, bf16[784,1024]{1,0:T(8,128)(2,1)} %copy-done.1, ...), custom_call_target="tpu_custom_call" | custom-call | bytes 16064512 | tf_op jit(solution)/shard_map/second_back/pallas_call | solution.py:399
  232.9 7.0 %layer_rows.1 = bf16[784,1024]{1,0:T(8,128)(2,1)} custom-call(s32[5]{0:T(128)} %stack.132.s_ref, bf16[784,1024]{1,0:T(8,128)(2,1)} %get-tuple-element.277.o_ref, bf16[784,1024]{1,0:T(8,128)(2,1)} %copy-done.8, f32[784,1024]{1,0:T(8,128)} %get-tuple-element.274.mid_ref, f32[1,1024]{1,0:T(1,128)} %bitcast.120), custom_call_target="tpu_custom_call" | custom-call | bytes 12853248 | tf_op jit(solution)/shard_map/layer_rows/pallas_call | solution.py:399
  239.9 9.4 %mixed_back.1 = (bf16[1568,512]{1,0:T(8,128)(2,1)}, bf16[512,512]{1,0:T(8,128)(2,1)}, bf16[512,512]{1,0:T(8,128)(2,1)}) custom-call(s32[5]{0:T(128)} %stack.132.s_ref, bf16[784,1024]{1,0:T(8,128)(2,1)} %get-tuple-element.276.mine_ref.wide_ref, bf16[784,1024]{1,0:T(8,128)(2,1)} %collective-permute-done.16.theirs_ref, ...), custom_call_target="tpu_custom_call" | custom-call | flops 3288334336 | bytes 11730944 | tf_op jit(solution)/shard_map/mixed_back/pallas_call | solution.py:399
  249.3 21.0 %attend_back.4 = (bf16[1568,384]{1,0:T(8,128)(2,1)}, bf16[384,512]{1,0:T(8,128)(2,1)}, bf16[384,512]{1,0:T(8,128)(2,1)}, f32[8,384]{1,0:T(8,128)}) custom-call(s32[6]{0:T(128)} %concatenate.47.s_ref, bf16[1568,1536]{1,0:T(8,128)(2,1)} %get-tuple-element.244.qkv_ref.ref, bf16[1568,512]{1,0:T(8,128)(2,1)} %get-tuple-element.283.grad_ref, ...), custom_call_target="tpu_custom_call" | custom-call | flops 50352619520 | bytes 3211264 | tf_op jit(solution)/shard_map/attend_back/pallas_call | solution.py:190
  270.2 6.9 %collective-permute-done.19 = bf16[512,1024]{1,0:T(8,128)(2,1)} collective-permute-done((bf16[512,1024]{1,0:T(8,128)(2,1)}, bf16[512,1024]{1,0:T(8,128)(2,1)}, u32[]{:S(2)}, u32[]{:S(2)}) %collective-permute-start.19) | collective-permute-done | bytes 1048608 | tf_op jit(solution)/shard_map/ppermute | solution.py:1502
  287.5 20.9 %attend_back.5 = (bf16[1568,384]{1,0:T(8,128)(2,1)}, bf16[384,512]{1,0:T(8,128)(2,1)}, bf16[384,512]{1,0:T(8,128)(2,1)}, f32[8,384]{1,0:T(8,128)}) custom-call(s32[6]{0:T(128)} %concatenate.48.s_ref, bf16[1568,1536]{1,0:T(8,128)(2,1)} %get-tuple-element.244.qkv_ref.ref, bf16[1568,512]{1,0:T(8,128)(2,1)} %get-tuple-element.283.grad_ref, ...), custom_call_target="tpu_custom_call" | custom-call | flops 50352619520 | bytes 3211264 | tf_op jit(solution)/shard_map/attend_back/pallas_call | solution.py:190
  318.1 20.7 %attend_back.6 = (bf16[1568,384]{1,0:T(8,128)(2,1)}, bf16[384,512]{1,0:T(8,128)(2,1)}, bf16[384,512]{1,0:T(8,128)(2,1)}, f32[8,384]{1,0:T(8,128)}) custom-call(s32[6]{0:T(128)} %concatenate.51.s_ref, bf16[1568,1536]{1,0:T(8,128)(2,1)} %get-tuple-element.244.qkv_ref.ref, bf16[1568,512]{1,0:T(8,128)(2,1)} %get-tuple-element.283.grad_ref, ...), custom_call_target="tpu_custom_call" | custom-call | flops 50352619520 | bytes 3211264 | tf_op jit(solution)/shard_map/attend_back/pallas_call | solution.py:190
  338.9 6.5 %collective-permute-done.24 = bf16[1280,512]{1,0:T(8,128)(2,1)} collective-permute-done((bf16[1280,512]{1,0:T(8,128)(2,1)}, bf16[1280,512]{1,0:T(8,128)(2,1)}, u32[]{:S(2)}, u32[]{:S(2)}) %collective-permute-start.24) | collective-permute-done | bytes 1310752 | tf_op jit(solution)/shard_map/ppermute | solution.py:1443
  352.1 6.3 %collective-permute-start.25 = (bf16[784,1024]{1,0:T(8,128)(2,1)S(1)}, bf16[784,1024]{1,0:T(8,128)(2,1)}, u32[]{:S(2)}, u32[]{:S(2)}) collective-permute-start(bf16[784,1024]{1,0:T(8,128)(2,1)S(1)} %copy-done), channel_id=1, source_target_pairs={{1,2},{2,1},{5,6},{6,5},{9,10},{10,9},{13,14},{14,13},{17,18},{18,... | collective-permute-start | bytes 4816904 | tf_op jit(solution)/shard_map/ppermute | solution.py:1514
  361.1 21.0 %attend_back.7 = (bf16[1568,384]{1,0:T(8,128)(2,1)}, bf16[384,512]{1,0:T(8,128)(2,1)}, bf16[384,512]{1,0:T(8,128)(2,1)}, f32[8,384]{1,0:T(8,128)}) custom-call(s32[6]{0:T(128)} %concatenate.52.s_ref, bf16[1568,1536]{1,0:T(8,128)(2,1)} %get-tuple-element.244.qkv_ref.ref, bf16[1568,512]{1,0:T(8,128)(2,1)} %get-tuple-element.283.grad_ref, ...), custom_call_target="tpu_custom_call" | custom-call | flops 50352619520 | bytes 3211264 | tf_op jit(solution)/shard_map/attend_back/pallas_call | solution.py:190
  391.2 9.9 %first_grad.1 = (bf16[784,1024]{1,0:T(8,128)(2,1)}, bf16[784,1024]{1,0:T(8,128)(2,1)}) custom-call(s32[5]{0:T(128)} %stack.132.s_ref, bf16[1568,384]{1,0:T(8,128)(2,1)} %get-tuple-element.355.refs_0_, bf16[1568,384]{1,0:T(8,128)(2,1)} %get-tuple-element.356.refs_1_, bf16[1568,384]{1,0:T(8,128)(2,1)} %get-tuple-element.357.refs_2_, ...), custom_call_target="tpu_custom_call" | custom-call | flops 4932501504 | bytes 15925248 | tf_op jit(solution)/shard_map/first_grad/pallas_call | solution.py:399
  401.2 4.9 collective-permute-done.29
  425.6 8.4 %first_back.1 = (bf16[784,1024]{1,0:T(8,128)(2,1)}, f32[8,1024]{1,0:T(8,128)}) custom-call(s32[5]{0:T(128)} %stack.132.s_ref, bf16[784,1024]{1,0:T(8,128)(2,1)} %get-tuple-element.362.g_ref, bf16[784,1024]{1,0:T(8,128)(2,1)} %collective-permute-done.30.r_ref, bf16[784,1024]{1,0:T(8,128)(2,1)} %get-tuple-element.235.x_ref, ...), custom_call_target="tpu_custom_call" | custom-call | bytes 12853248 | tf_op jit(solution)/shard_map/first_back/pallas_call | solution.py:399
  434.8 10.7 %collective-permute-done.32 = bf16[160,512]{1,0:T(8,128)(2,1)} collective-permute-done((bf16[160,512]{1,0:T(8,128)(2,1)}, bf16[160,512]{1,0:T(8,128)(2,1)}, u32[]{:S(2)}, u32[]{:S(2)}) %collective-permute-start.32) | collective-permute-done | bytes 163872 | tf_op jit(solution)/shard_map/ppermute | solution.py:1394
  445.5 4.9 collective-permute-done.33
  471.1 8.6 %collective-permute-done.41 = f32[6144]{0:T(1024)S(1)} collective-permute-done((f32[6144]{0:T(1024)S(1)}, f32[6144]{0:T(1024)S(1)}, u32[]{:S(2)}, u32[]{:S(2)}) %collective-permute-start.41) | collective-permute-done | bytes 24608 | tf_op jit(solution)/shard_map/ppermute | solution.py:1457
  496.7 4.8 collective-permute-done.44.refs_1_
  512.5 10.4 %finish_feed.1 = (f32[512,4096]{1,0:T(8,128)}, f32[2,2,512,1024]{3,2,1,0:T(8,128)}) custom-call(s32[5]{0:T(128)} %stack.132.s_ref, bf16[512,1024]{1,0:T(8,128)(2,1)} %bitcast.19.refs_0_, bf16[512,1024]{1,0:T(8,128)(2,1)} %collective-permute-done.34.refs_1_, bf16[512,1024]{1,0:T(8,128)(2,1)} %collective-permute-done.35.refs_2_, bf16[512,1024]{1,0:T(8,128)(2,1)} %copy-done.15, ...), custom_call_target="tpu_custom_call" | custom-call | bytes 16777216 | tf_op jit(solution)/shard_map/finish_feed/pallas_call | solution.py:399
  527.8 7.1 %finish_attention.1 = (f32[512,1024]{1,0:T(8,128)}, f32[512,1024]{1,0:T(8,128)}, f32[512,1024]{1,0:T(8,128)}, f32[512,1024]{1,0:T(8,128)}) custom-call(s32[5]{0:T(128)} %stack.132.s_ref, bf16[640,512]{1,0:T(8,128)(2,1)} %bitcast.92, bf16[640,512]{1,0:T(8,128)(2,1)} %copy-done.18, bf16[640,512]{1,0:T(8,128)(2,1)} %copy-done.19, bf16[640,512]{1,0:T(8,128)(2,1)} %copy-done.20, ...), custom_call_target="tpu_custom_call" | custom-call | bytes 8388608 | tf_op jit(solution)/shard_map/finish_attention/pallas_call | solution.py:399
  (304 shorter events, 159.4 us)
Async XLA Ops:
  0.7 39.8 %collective-permute-start = (bf16[784,1024]{1,0:T(8,128)(2,1)}, bf16[784,1024]{1,0:T(8,128)(2,1)S(1)}, u32[]{:S(2)}, u32[]{:S(2)}) collective-permute-start(bf16[784,1024]{1,0:T(8,128)(2,1)} %bitcast.94), channel_id=1, source_target_pairs={{1,2},{2,1},{5,6},{6,5},{9,10},{10,9},{13,14},{14,13},{17,18},{18,... | collective-permute-start | bytes 4816904 | tf_op jit(solution)/shard_map/ppermute | solution.py:1514
  10.4 30.0 %collective-permute-start.1 = (bf16[256,1536]{1,0:T(8,128)(2,1)}, bf16[256,1536]{1,0:T(8,128)(2,1)}, u32[]{:S(2)}, u32[]{:S(2)}) collective-permute-start(bf16[256,1536]{1,0:T(8,128)(2,1)} %get-tuple-element.224), channel_id=1, source_target_pairs={{0,1},{1,0},{2,3},{3,2},{4,5},{5,4},{6,7},{7,6},{8,9},{9,8},{10,11... | collective-permute-start | bytes 2359304 | tf_op jit(solution)/shard_map/ppermute | solution.py:1502
  16.9 23.5 %collective-permute-start.2 = (f32[6144]{0:T(1024)S(1)}, f32[6144]{0:T(1024)S(1)}, u32[]{:S(2)}, u32[]{:S(2)}) collective-permute-start(f32[6144]{0:T(1024)S(1)} %constant_dynamic-update-slice_fusion.10), channel_id=1, source_target_pairs={{0,1},{1,0},{2,3},{3,2},{4,5},{5,4},{6,7},{7,6},{8,9},{9,8},{10,11... | collective-permute-start | bytes 73736 | tf_op jit(solution)/shard_map/ppermute | solution.py:1502
  40.5 25.0 %collective-permute-start.4 = (bf16[512,1024]{1,0:T(8,128)(2,1)}, bf16[512,1024]{1,0:T(8,128)(2,1)}, u32[]{:S(2)}, u32[]{:S(2)}) collective-permute-start(bf16[512,1024]{1,0:T(8,128)(2,1)} %pack_feed.2), channel_id=1, source_target_pairs={{0,1},{1,0},{2,3},{3,2},{4,5},{5,4},{6,7},{7,6},{8,9},{9,8},{10,11... | collective-permute-start | bytes 3145736 | tf_op jit(solution)/shard_map/ppermute | solution.py:1502
  42.4 19.8 %collective-permute-start.3 = (bf16[256,1536]{1,0:T(8,128)(2,1)}, bf16[256,1536]{1,0:T(8,128)(2,1)}, u32[]{:S(2)}, u32[]{:S(2)}) collective-permute-start(bf16[256,1536]{1,0:T(8,128)(2,1)} %collective-permute-done.1.piece_ref), channel_id=1, source_target_pairs={{0,4},{4,0},{1,5},{5,1},{2,6},{6,2},{3,7},{7,3},{8,12},{12,8},{9,1... | collective-permute-start | bytes 2359304 | tf_op jit(solution)/shard_map/ppermute | solution.py:1508
  68.7 57.4 %collective-permute-start.10 = (bf16[512,1024]{1,0:T(8,128)(2,1)}, bf16[512,1024]{1,0:T(8,128)(2,1)}, u32[]{:S(2)}, u32[]{:S(2)}) collective-permute-start(bf16[512,1024]{1,0:T(8,128)(2,1)} %collective-permute-done.4.x_piece), channel_id=1, source_target_pairs={{0,4},{4,0},{1,5},{5,1},{2,6},{6,2},{3,7},{7,3},{8,12},{12,8},{9,1... | collective-permute-start | bytes 3145736 | tf_op jit(solution)/shard_map/ppermute | solution.py:1508
  71.2 35.0 %collective-permute-start.8 = (bf16[512,1024]{1,0:T(8,128)(2,1)}, bf16[512,1024]{1,0:T(8,128)(2,1)}, u32[]{:S(2)}, u32[]{:S(2)}) collective-permute-start(bf16[512,1024]{1,0:T(8,128)(2,1)} %pack_feed.3), channel_id=1, source_target_pairs={{0,1},{1,0},{2,3},{3,2},{4,5},{5,4},{6,7},{7,6},{8,9},{9,8},{10,11... | collective-permute-start | bytes 3145736 | tf_op jit(solution)/shard_map/ppermute | solution.py:1502
  82.9 23.3 %collective-permute-start.7 = (bf16[128,1024]{1,0:T(8,128)(2,1)S(1)}, bf16[128,1024]{1,0:T(8,128)(2,1)}, u32[]{:S(2)}, u32[]{:S(2)}) collective-permute-start(bf16[128,1024]{1,0:T(8,128)(2,1)S(1)} %collective-permute-done.6.piece_ref), channel_id=1, source_target_pairs={{0,4},{4,0},{1,5},{5,1},{2,6},{6,2},{3,7},{7,3},{8,12},{12,8},{9,1... | collective-permute-start | bytes 786440 | tf_op jit(solution)/shard_map/ppermute | solution.py:1508
  107.7 28.9 %collective-permute-start.9 = (bf16[784,1024]{1,0:T(8,128)(2,1)S(1)}, bf16[784,1024]{1,0:T(8,128)(2,1)}, u32[]{:S(2)}, u32[]{:S(2)}) collective-permute-start(bf16[784,1024]{1,0:T(8,128)(2,1)S(1)} %bitcast.93), channel_id=1, source_target_pairs={{1,2},{2,1},{5,6},{6,5},{9,10},{10,9},{13,14},{14,13},{17,18},{18,... | collective-permute-start | bytes 4816904 | tf_op jit(solution)/shard_map/ppermute | solution.py:1514
  111.7 24.9 %collective-permute-start.11 = (bf16[512,1024]{1,0:T(8,128)(2,1)}, bf16[512,1024]{1,0:T(8,128)(2,1)}, u32[]{:S(2)}, u32[]{:S(2)}) collective-permute-start(bf16[512,1024]{1,0:T(8,128)(2,1)} %collective-permute-done.8.z_piece), channel_id=1, source_target_pairs={{0,8},{8,0},{16,24},{24,16},{1,9},{9,1},{17,25},{25,17},{2,10},{10... | collective-permute-start | bytes 3145736 | tf_op jit(solution)/shard_map/ppermute | solution.py:1511
  213.5 18.3 %collective-permute-start.17 = (bf16[784,1024]{1,0:T(8,128)(2,1)}, bf16[784,1024]{1,0:T(8,128)(2,1)S(1)}, u32[]{:S(2)}, u32[]{:S(2)}) collective-permute-start(bf16[784,1024]{1,0:T(8,128)(2,1)} %get-tuple-element.278), channel_id=1, source_target_pairs={{0,2},{2,0},{1,3},{3,1},{4,6},{6,4},{5,7},{7,5},{8,10},{10,8},{9,1... | collective-permute-start | bytes 4816904 | tf_op jit(solution)/shard_map/ppermute | solution.py:1505
  230.1 47.2 %collective-permute-start.20 = (bf16[1024,1024]{1,0:T(8,128)(2,1)}, bf16[1024,1024]{1,0:T(8,128)(2,1)}, u32[]{:S(2)}, u32[]{:S(2)}) collective-permute-start(bf16[1024,1024]{1,0:T(8,128)(2,1)} %get-tuple-element.295), channel_id=1, source_target_pairs={{0,4},{4,0},{1,5},{5,1},{2,6},{6,2},{3,7},{7,3},{8,12},{12,8},{9,1... | collective-permute-start | bytes 6291464 | tf_op jit(solution)/shard_map/ppermute | solution.py:1508
  230.3 39.9 %collective-permute-start.18 = (bf16[512,1024]{1,0:T(8,128)(2,1)}, bf16[512,1024]{1,0:T(8,128)(2,1)}, u32[]{:S(2)}, u32[]{:S(2)}) collective-permute-start(bf16[512,1024]{1,0:T(8,128)(2,1)} %get-tuple-element.293), channel_id=1, source_target_pairs={{0,1},{1,0},{2,3},{3,2},{4,5},{5,4},{6,7},{7,6},{8,9},{9,8},{10,11... | collective-permute-start | bytes 3145736 | tf_op jit(solution)/shard_map/ppermute | solution.py:1502
  230.3 46.8 %collective-permute-start.19 = (bf16[512,1024]{1,0:T(8,128)(2,1)}, bf16[512,1024]{1,0:T(8,128)(2,1)}, u32[]{:S(2)}, u32[]{:S(2)}) collective-permute-start(bf16[512,1024]{1,0:T(8,128)(2,1)} %get-tuple-element.294), channel_id=1, source_target_pairs={{0,1},{1,0},{2,3},{3,2},{4,5},{5,4},{6,7},{7,6},{8,9},{9,8},{10,11... | collective-permute-start | bytes 3145736 | tf_op jit(solution)/shard_map/ppermute | solution.py:1502
  284.5 26.6 %collective-permute-start.21 = (bf16[512,1024]{1,0:T(8,128)(2,1)}, bf16[512,1024]{1,0:T(8,128)(2,1)}, u32[]{:S(2)}, u32[]{:S(2)}) collective-permute-start(bf16[512,1024]{1,0:T(8,128)(2,1)} %get-tuple-element.303), channel_id=1, source_target_pairs={{0,4},{4,0},{1,5},{5,1},{2,6},{6,2},{3,7},{7,3},{8,12},{12,8},{9,1... | collective-permute-start | bytes 3145736 | tf_op jit(solution)/shard_map/ppermute | solution.py:1625
  287.2 23.9 %collective-permute-start.22 = (bf16[512,1024]{1,0:T(8,128)(2,1)}, bf16[512,1024]{1,0:T(8,128)(2,1)}, u32[]{:S(2)}, u32[]{:S(2)}) collective-permute-start(bf16[512,1024]{1,0:T(8,128)(2,1)} %get-tuple-element.304), channel_id=1, source_target_pairs={{0,1},{1,0},{2,3},{3,2},{4,5},{5,4},{6,7},{7,6},{8,9},{9,8},{10,11... | collective-permute-start | bytes 3145736 | tf_op jit(solution)/shard_map/ppermute | solution.py:1502
  315.7 23.2 %collective-permute-start.23 = (bf16[512,1024]{1,0:T(8,128)(2,1)}, bf16[512,1024]{1,0:T(8,128)(2,1)}, u32[]{:S(2)}, u32[]{:S(2)}) collective-permute-start(bf16[512,1024]{1,0:T(8,128)(2,1)} %get-tuple-element.320), channel_id=1, source_target_pairs={{0,8},{8,0},{16,24},{24,16},{1,9},{9,1},{17,25},{25,17},{2,10},{10... | collective-permute-start | bytes 3145736 | tf_op jit(solution)/shard_map/ppermute | solution.py:1420
  316.9 28.6 %collective-permute-start.24 = (bf16[1280,512]{1,0:T(8,128)(2,1)}, bf16[1280,512]{1,0:T(8,128)(2,1)}, u32[]{:S(2)}, u32[]{:S(2)}) collective-permute-start(bf16[1280,512]{1,0:T(8,128)(2,1)} %pad_maximum_fusion), channel_id=1, source_target_pairs={{0,1},{1,0},{2,3},{3,2},{4,5},{5,4},{6,7},{7,6},{8,9},{9,8},{10,11... | collective-permute-start | bytes 3932168 | tf_op jit(solution)/shard_map/ppermute | solution.py:1443
  352.1 33.0 %collective-permute-start.25 = (bf16[784,1024]{1,0:T(8,128)(2,1)S(1)}, bf16[784,1024]{1,0:T(8,128)(2,1)}, u32[]{:S(2)}, u32[]{:S(2)}) collective-permute-start(bf16[784,1024]{1,0:T(8,128)(2,1)S(1)} %copy-done), channel_id=1, source_target_pairs={{1,2},{2,1},{5,6},{6,5},{9,10},{10,9},{13,14},{14,13},{17,18},{18,... | collective-permute-start | bytes 4816904 | tf_op jit(solution)/shard_map/ppermute | solution.py:1514
  358.4 26.7 %collective-permute-start.27 = (bf16[640,512]{1,0:T(8,128)(2,1)}, bf16[640,512]{1,0:T(8,128)(2,1)}, u32[]{:S(2)}, u32[]{:S(2)}) collective-permute-start(bf16[640,512]{1,0:T(8,128)(2,1)} %get-tuple-element.334), channel_id=1, source_target_pairs={{0,4},{4,0},{1,5},{5,1},{2,6},{6,2},{3,7},{7,3},{8,12},{12,8},{9,1... | collective-permute-start | bytes 1966088 | tf_op jit(solution)/shard_map/ppermute | solution.py:1449
  358.8 26.3 %collective-permute-start.26 = (bf16[256,1024]{1,0:T(8,128)(2,1)}, bf16[256,1024]{1,0:T(8,128)(2,1)}, u32[]{:S(2)}, u32[]{:S(2)}) collective-permute-start(bf16[256,1024]{1,0:T(8,128)(2,1)} %get-tuple-element.332), channel_id=1, source_target_pairs={{0,16},{8,24},{16,0},{24,8},{1,17},{9,25},{17,1},{25,9},{2,18},{10... | collective-permute-start | bytes 1572872 | tf_op jit(solution)/shard_map/ppermute | solution.py:1420
  385.1 21.0 %collective-permute-start.28 = (bf16[768,512]{1,0:T(8,128)(2,1)}, bf16[768,512]{1,0:T(8,128)(2,1)}, u32[]{:S(2)}, u32[]{:S(2)}) collective-permute-start(bf16[768,512]{1,0:T(8,128)(2,1)} %pad_maximum_fusion.2), channel_id=1, source_target_pairs={{0,1},{1,0},{2,3},{3,2},{4,5},{5,4},{6,7},{7,6},{8,9},{9,8},{10,11... | collective-permute-start | bytes 2359304 | tf_op jit(solution)/shard_map/ppermute | solution.py:1443
  388.4 26.3 %collective-permute-start.31 = (bf16[256,1024]{1,0:T(8,128)(2,1)}, bf16[256,1024]{1,0:T(8,128)(2,1)}, u32[]{:S(2)}, u32[]{:S(2)}) collective-permute-start(bf16[256,1024]{1,0:T(8,128)(2,1)} %add_convert_fusion.9), channel_id=1, source_target_pairs={{0,16},{8,24},{16,0},{24,8},{1,17},{9,25},{17,1},{25,9},{2,18},{10... | collective-permute-start | bytes 1572872 | tf_op jit(solution)/shard_map/ppermute | solution.py:1420
  389.4 16.7 %collective-permute-start.29 = (bf16[320,512]{1,0:T(8,128)(2,1)}, bf16[320,512]{1,0:T(8,128)(2,1)S(1)}, u32[]{:S(2)}, u32[]{:S(2)}) collective-permute-start(bf16[320,512]{1,0:T(8,128)(2,1)} %get-tuple-element.354), channel_id=1, source_target_pairs={{0,8},{8,0},{16,24},{24,16},{1,9},{9,1},{17,25},{25,17},{2,10},{10... | collective-permute-start | bytes 983048 | tf_op jit(solution)/shard_map/ppermute | solution.py:1394
  417.5 33.0 %collective-permute-start.34 = (bf16[512,1024]{1,0:T(8,128)(2,1)}, bf16[512,1024]{1,0:T(8,128)(2,1)}, u32[]{:S(2)}, u32[]{:S(2)}) collective-permute-start(bf16[512,1024]{1,0:T(8,128)(2,1)} %bitcast.19.refs_0_), channel_id=1, source_target_pairs={{0,4},{4,0},{1,5},{5,1},{2,6},{6,2},{3,7},{7,3},{8,12},{12,8},{9,1... | collective-permute-start | bytes 3145736 | tf_op jit(solution)/shard_map/ppermute | solution.py:1434
  418.5 31.9 %collective-permute-start.35 = (bf16[512,1024]{1,0:T(8,128)(2,1)}, bf16[512,1024]{1,0:T(8,128)(2,1)}, u32[]{:S(2)}, u32[]{:S(2)}) collective-permute-start(bf16[512,1024]{1,0:T(8,128)(2,1)} %bitcast.19.refs_0_), channel_id=1, source_target_pairs={{0,8},{8,0},{16,24},{24,16},{1,9},{9,1},{17,25},{25,17},{2,10},{10... | collective-permute-start | bytes 3145736 | tf_op jit(solution)/shard_map/ppermute | solution.py:1420
  423.0 27.5 %collective-permute-start.33 = (bf16[384,512]{1,0:T(8,128)(2,1)}, bf16[384,512]{1,0:T(8,128)(2,1)}, u32[]{:S(2)}, u32[]{:S(2)}) collective-permute-start(bf16[384,512]{1,0:T(8,128)(2,1)} %get-tuple-element.367), channel_id=1, source_target_pairs={{0,4},{4,0},{1,5},{5,1},{2,6},{6,2},{3,7},{7,3},{8,12},{12,8},{9,1... | collective-permute-start | bytes 1179656 | tf_op jit(solution)/shard_map/ppermute | solution.py:1449
  423.9 21.6 %collective-permute-start.32 = (bf16[160,512]{1,0:T(8,128)(2,1)}, bf16[160,512]{1,0:T(8,128)(2,1)}, u32[]{:S(2)}, u32[]{:S(2)}) collective-permute-start(bf16[160,512]{1,0:T(8,128)(2,1)} %get-tuple-element.369), channel_id=1, source_target_pairs={{0,16},{8,24},{16,0},{24,8},{1,17},{9,25},{17,1},{25,9},{2,18},{10... | collective-permute-start | bytes 491528 | tf_op jit(solution)/shard_map/ppermute | solution.py:1394
  461.9 27.4 %collective-permute-start.47 = (bf16[512,1024]{1,0:T(8,128)(2,1)}, bf16[512,1024]{1,0:T(8,128)(2,1)S(1)}, u32[]{:S(2)}, u32[]{:S(2)}) collective-permute-start(bf16[512,1024]{1,0:T(8,128)(2,1)} %bitcast.19.refs_0_), channel_id=1, source_target_pairs={{0,2},{2,0},{1,3},{3,1},{4,6},{6,4},{5,7},{7,5},{8,10},{10,8},{9,1... | collective-permute-start | bytes 3145736 | tf_op jit(solution)/shard_map/ppermute | solution.py:1435
  462.5 34.1 %collective-permute-start.46 = (bf16[512,1024]{1,0:T(8,128)(2,1)}, bf16[512,1024]{1,0:T(8,128)(2,1)S(1)}, u32[]{:S(2)}, u32[]{:S(2)}) collective-permute-start(bf16[512,1024]{1,0:T(8,128)(2,1)} %collective-permute-done.35.refs_2_), channel_id=1, source_target_pairs={{0,4},{4,0},{1,5},{5,1},{2,6},{6,2},{3,7},{7,3},{8,12},{12,8},{9,1... | collective-permute-start | bytes 3145736 | tf_op jit(solution)/shard_map/ppermute | solution.py:1435
  482.3 19.2 %collective-permute-start.44 = (bf16[640,512]{1,0:T(8,128)(2,1)S(1)}, bf16[640,512]{1,0:T(8,128)(2,1)S(1)}, u32[]{:S(2)}, u32[]{:S(2)}) collective-permute-start(bf16[640,512]{1,0:T(8,128)(2,1)S(1)} %bitcast.90), channel_id=1, source_target_pairs={{0,4},{4,0},{1,5},{5,1},{2,6},{6,2},{3,7},{7,3},{8,12},{12,8},{9,1... | collective-permute-start | bytes 1966088 | tf_op jit(solution)/shard_map/ppermute | solution.py:1408
  489.3 33.7 %collective-permute-start.40 = (bf16[784,1024]{1,0:T(8,128)(2,1)}, bf16[784,1024]{1,0:T(8,128)(2,1)}, u32[]{:S(2)}, u32[]{:S(2)}) collective-permute-start(bf16[784,1024]{1,0:T(8,128)(2,1)} %get-tuple-element.398), channel_id=1, source_target_pairs={{1,2},{2,1},{5,6},{6,5},{9,10},{10,9},{13,14},{14,13},{17,18},{18,... | collective-permute-start | bytes 4816904 | tf_op jit(solution)/shard_map/ppermute | solution.py:1514
  (72 other events, 491.4 us)

commit v8 on v7

--- a/solution.py
+++ b/solution.py
@@ -1438,10 +1438,12 @@
     yield []
 
 
-def plane_steps(order, low, deep, send, keep, result):
+def plane_steps(order, low, deep, send, keep, result, more=()):
     send, keep = order.pin(send, keep)
-    (other,) = yield [lax.ppermute(send, "half", SWAP)]
+    other, *more_in = yield [lax.ppermute(send, "half", SWAP), *more[1:]]
     total = add_low(keep, other)
+    if more:
+        total = jnp.concatenate([total, add_low(more[0], more_in[0])], axis=0)
     size = total.shape[0] // 2
     parts = (total[:size], total[size:])
     even = low == 0
@@ -1595,14 +1597,12 @@
     order.fence(dx_part)
     dx_in = swap_core(dx_part)
     up_in, down_in, low_in = swap_half(up_send), swap_half(down_send), swap_low(low_send)
-    out_in = swap_core(out_part)
     grad_low, sums_two = second_back(
         scal, dx_own, order.pin(dx_in), middle, grad_out, gain_two
     )
     grad_low = order.pin(grad_low)
     grad_low_in = swap_core(grad_low)
-    layer = layer_rows(scal, out_own, order.pin(out_in), middle, full_dbias)
-    grad_low_in, layer = order.pin(grad_low_in, layer)
+    grad_low_in = order.pin(grad_low_in)
     grad_mixed, out_send, out_keep = mixed_back(scal, (grad_low, grad_low_in), out_set, mixed)
     grad_mixed = order.pin(grad_mixed)
 
@@ -1626,6 +1626,7 @@
     range_sum = add_low(low_keep, low_in).reshape(2, own_rows, width)
     half_send, half_keep = order.pin(pick(range_sum, 1 - half, 0), pick(range_sum, half, 0))
     half_in = swap_half(half_send)
+    out_half_in = swap_half(order.pin(out_send))
 
     back(1)
     one_in, half_in = order.pin(one_in, half_in)
@@ -1638,17 +1639,18 @@
     early = Steps(
         plane_steps(
             order, low, deep,
-            jnp.concatenate([backs[0][1], backs[1][1], out_send], axis=0),
-            jnp.concatenate([backs[0][2], backs[1][2], out_keep], axis=0), early_parts,
+            jnp.concatenate([backs[0][1], backs[1][1]], axis=0),
+            jnp.concatenate([backs[0][2], backs[1][2]], axis=0), early_parts,
+            more=(out_keep, out_half_in),
         )
     )
 
     back(2)
     advance(order, ranges, early)
-    layer_in = cross_over(order.pin(layer))
+    out_in = swap_core(order.pin(out_part))
 
     back(3)
-    layer_in = order.pin(layer_in)
+    out_in = order.pin(out_in)
     late = Steps(
         plane_steps(
             order, low, deep,
@@ -1670,6 +1672,7 @@
     )
     tokens_out, sums_one = order.pin(tokens_out, sums_one)
     order.fence(sums_one)
+    layer = order.pin(layer_rows(scal, out_own, out_in, after(middle, sums_one), full_dbias))
     advance(order, early, late, ranges)
 
     def place_entries(values, inner=1):
@@ -1687,6 +1690,7 @@
     advance(order, vectors)
     advance(order, vectors, early, late)
     tokens_in = cross_over(order.pin(tokens_out))
+    layer_in = cross_over(layer)
     advance(order, vectors, early, late)
     advance(order, vectors, late)
     advance(order, early, ranges, late)

time: 545 us -> 532 us (0.976)
  other arithmetic: 44.3 us -> 36.9 us
  waiting for transfers between devices: 119 us -> 113 us
  starting transfers between devices: 68.5 us -> 74.2 us
    ppermute x4, waiting for transfers between devices: 0.01 us -> 8.4 us  [cross_over(): return lax.ppermute(values, ('core', 'half'), cross)]
    ppermute x12, waiting for transfers between devices: 24.2 us -> 16 us  [exchange(): lax.ppermute(values, 'line', [(i, i ^ 1 << bit) for i in range(deep)])]
    ppermute x8 -> x9, waiting for transfers between devices: 32.1 us -> 40.3 us  [swap_half(): return lax.ppermute(values, 'half', SWAP)]
    ppermute x2, waiting for transfers between devices: 6.53 us -> 0.01 us  [plane_steps(): other, *more_in = (yield [lax.ppermute(send, 'half', SWAP), *more[1:]])]
    ppermute x12, starting transfers between devices: 12.9 us -> 19.4 us  [exchange(): lax.ppermute(values, 'line', [(i, i ^ 1 << bit) for i in range(deep)])]
    unnamed x114 -> x116, local copies, waits for them, and re-layouts: 16.2 us -> 11.7 us
    convert_element_type x11 -> x12, other arithmetic: 14.1 us -> 12.5 us  [add_low(): return (left.astype(F32) + right.astype(F32)).astype(BF16)]
  transfers between devices with their start and end apart: 59 -> 60, of which waited for: 23 -> 23; matrix products, arithmetic and copies ran while one was open for 8% -> 8% of each run, Pallas kernels for 37% -> 36%
where the time goes in v8:
time: 532 us; the launch traced here: 523 us
  Pallas kernels  273 us (51%)
  waiting for transfers between devices  113 us (21%)
  starting transfers between devices  74.2 us (14%)
  other arithmetic  36.9 us (7%)
  local copies, waits for them, and re-layouts  24.2 us (5%)
    pallas_call x14, Pallas kernels, run(): pl.pallas_call(kernel, grid_spec=pltpu.PrefetchScalarGridSpec(num_scalar_...  97.7 us
    pallas_call x4, Pallas kernels, attend_back(): pl.pallas_call(functools.partial(attend_back_kernel, tile, rows, padded),...  83.9 us
    pallas_call x1, Pallas kernels, feed(): pl.pallas_call(feed_kernel, grid_spec=pltpu.PrefetchScalarGridSpec(num_sc...  60.5 us
    ppermute x9, waiting for transfers between devices, swap_half(): return lax.ppermute(values, 'half', SWAP)  40.3 us
    pallas_call x2, Pallas kernels, attend(): pl.pallas_call(kernel if kept is None else lambda ref, a, b, *rest: kerne...  30.6 us
    ppermute x12, starting transfers between devices, exchange(): lax.ppermute(values, 'line', [(i, i ^ 1 << bit) for i in range(deep)])  19.4 us
    ppermute x4, starting transfers between devices, cross_over(): return lax.ppermute(values, ('core', 'half'), cross)  17.3 us
    ppermute x12, waiting for transfers between devices, exchange(): lax.ppermute(values, 'line', [(i, i ^ 1 << bit) for i in range(deep)])  16 us
  transfers between devices with their start and end apart: 60, of which 23 were waited for; matrix products, arithmetic and copies ran while one was open for 8% of the time, Pallas kernels for 36%

profile of v8, /device:TPU:1, one launch (start us, length us, event | category | flops | bytes accessed | tf_op | source)
XLA Modules:
  0.0 522.9 jit_solution(9800450196406768271)
XLA Ops:
  0.7 4.5 collective-permute-start
  5.8 4.5 pack_qkv.1
  18.4 22.1 %collective-permute-done.2 = f32[6144]{0:T(1024)S(1)} collective-permute-done((f32[6144]{0:T(1024)S(1)}, f32[6144]{0:T(1024)S(1)}, u32[]{:S(2)}, u32[]{:S(2)}) %collective-permute-start.2) | collective-permute-done | bytes 24608 | tf_op jit(solution)/shard_map/ppermute | solution.py:1504
  45.5 4.2 first_norm.1
  49.7 12.5 %collective-permute-done.3.beside_ref = bf16[256,1536]{1,0:T(8,128)(2,1)} collective-permute-done((bf16[256,1536]{1,0:T(8,128)(2,1)}, bf16[256,1536]{1,0:T(8,128)(2,1)}, u32[]{:S(2)}, u32[]{:S(2)}) %collective-permute-start.3) | collective-permute-done | bytes 786464 | tf_op jit(solution)/shard_map/ppermute | solution.py:1510
  71.8 11.1 %project.1 = (bf16[1568,1536]{1,0:T(8,128)(2,1)}, bf16[1024,1536]{1,0:T(8,128)(2,1)}, bf16[1568,1024]{1,0:T(8,128)(2,1)}) custom-call(s32[5]{0:T(128)} %stack.132.s_ref, bf16[784,1024]{1,0:T(8,128)(2,1)} %get-tuple-element.238.mine_ref, bf16[784,1024]{1,0:T(8,128)(2,1)} %collective-permute-done.5.theirs_ref, bf16[512,1536]{1,0:T(8,128)(2,1)} %get-tuple-element.242.own_ref, ...), custom_call_target="tpu_custom_call" | custom-call | flops 4932501504 | bytes 12726272 | tf_op jit(solution)/shard_map/project/pallas_call | solution.py:399
  84.2 22.0 %attend.2 = (bf16[1568,512]{1,0:T(8,128)(2,1)}, f32[4,2,1664]{2,1,0:T(2,128)}) custom-call(bf16[1568,1536]{1,0:T(8,128)(2,1)} %get-tuple-element.246.qkv_ref.ref), custom_call_target="tpu_custom_call" | custom-call | flops 60423143424 | bytes 4816896 | tf_op jit(solution)/shard_map/attend/pallas_call | solution.py:101
  107.7 4.1 collective-permute-start.9
  113.1 8.7 %attend.3 = (bf16[1568,512]{1,0:T(8,128)(2,1)}, f32[4,2,1664]{2,1,0:T(2,128)}) custom-call(bf16[1568,1536]{1,0:T(8,128)(2,1)} %get-tuple-element.246.qkv_ref.ref, bf16[1568,512]{1,0:T(8,128)(2,1)} %get-tuple-element.247.a, f32[4,2,1664]{2,1,0:T(2,128)} %copy.58.b), custom_call_target="tpu_custom_call", output_to_operand_aliasing={{0}: (1, {}), {1}: (2, {})} | custom-call | flops 20141047808 | bytes 1605632 | tf_op jit(solution)/shard_map/attend/pallas_call | solution.py:101
  121.8 4.3 out_other.1
  126.1 10.5 %collective-permute-done.11.z_beside = bf16[512,1024]{1,0:T(8,128)(2,1)} collective-permute-done((bf16[512,1024]{1,0:T(8,128)(2,1)}, bf16[512,1024]{1,0:T(8,128)(2,1)}, u32[]{:S(2)}, u32[]{:S(2)}) %collective-permute-start.11) | collective-permute-done | bytes 1048608 | tf_op jit(solution)/shard_map/ppermute | solution.py:1513
  140.8 6.1 %second_norm.1 = (f32[784,1024]{1,0:T(8,128)}, bf16[784,1024]{1,0:T(8,128)(2,1)}) custom-call(s32[5]{0:T(128)} %stack.132.s_ref, bf16[1568,512]{1,0:T(8,128)(2,1)} %get-tuple-element.254.mixed_ref.out_ref, bf16[512,1024]{1,0:T(8,128)(2,1)} %get-tuple-element.255.w_ref, bf16[784,1024]{1,0:T(8,128)(2,1)} %get-tuple-element.237.x_ref, ...), custom_call_target="tpu_custom_call" | custom-call | flops 822083584 | bytes 11755520 | tf_op jit(solution)/shard_map/second_norm/pallas_call | solution.py:399
  148.1 4.1 collective-permute-done.13.x_other
  152.8 60.5 %feed.1 = (bf16[784,1024]{1,0:T(8,128)(2,1)}, bf16[784,1024]{1,0:T(8,128)(2,1)}, bf16[784,1024]{1,0:T(8,128)(2,1)}, bf16[784,1024]{1,0:T(8,128)(2,1)}, bf16[512,...) custom-call(s32[5]{0:T(128)} %stack.132.s_ref, ...), custom_call_target="tpu_custom_call" | custom-call | flops 39460012032 | bytes 25690112 | tf_op jit(solution)/shard_map/feed/pallas_call | solution.py:357
  218.2 8.8 %second_back.1 = (bf16[784,1024]{1,0:T(8,128)(2,1)}, f32[8,1024]{1,0:T(8,128)}) custom-call(s32[5]{0:T(128)} %stack.132.s_ref, bf16[784,1024]{1,0:T(8,128)(2,1)} %get-tuple-element.275.g_ref, bf16[784,1024]{1,0:T(8,128)(2,1)} %copy-done.8, f32[784,1024]{1,0:T(8,128)} %get-tuple-element.379.mid_ref, bf16[784,1024]{1,0:T(8,128)(2,1)} %copy-done.1, ...), custom_call_target="tpu_custom_call" | custom-call | bytes 16064512 | tf_op jit(solution)/shard_map/second_back/pallas_call | solution.py:399
  231.2 9.4 %mixed_back.1 = (bf16[1568,512]{1,0:T(8,128)(2,1)}, bf16[512,512]{1,0:T(8,128)(2,1)}, bf16[512,512]{1,0:T(8,128)(2,1)}) custom-call(s32[5]{0:T(128)} %stack.132.s_ref, bf16[784,1024]{1,0:T(8,128)(2,1)} %get-tuple-element.280.mine_ref.wide_ref, bf16[784,1024]{1,0:T(8,128)(2,1)} %collective-permute-done.16.theirs_ref, ...), custom_call_target="tpu_custom_call" | custom-call | flops 3288334336 | bytes 11730944 | tf_op jit(solution)/shard_map/mixed_back/pallas_call | solution.py:399
  240.7 20.9 %attend_back.4 = (bf16[1568,384]{1,0:T(8,128)(2,1)}, bf16[384,512]{1,0:T(8,128)(2,1)}, bf16[384,512]{1,0:T(8,128)(2,1)}, f32[8,384]{1,0:T(8,128)}) custom-call(s32[6]{0:T(128)} %concatenate.50.s_ref, bf16[1568,1536]{1,0:T(8,128)(2,1)} %get-tuple-element.246.qkv_ref.ref, bf16[1568,512]{1,0:T(8,128)(2,1)} %get-tuple-element.283.grad_ref, ...), custom_call_target="tpu_custom_call" | custom-call | flops 50352619520 | bytes 3211264 | tf_op jit(solution)/shard_map/attend_back/pallas_call | solution.py:190
  261.6 15.0 %collective-permute-done.18 = bf16[512,1024]{1,0:T(8,128)(2,1)} collective-permute-done((bf16[512,1024]{1,0:T(8,128)(2,1)}, bf16[512,1024]{1,0:T(8,128)(2,1)}, u32[]{:S(2)}, u32[]{:S(2)}) %collective-permute-start.18) | collective-permute-done | bytes 1048608 | tf_op jit(solution)/shard_map/ppermute | solution.py:1504
  287.7 20.9 %attend_back.5 = (bf16[1568,384]{1,0:T(8,128)(2,1)}, bf16[384,512]{1,0:T(8,128)(2,1)}, bf16[384,512]{1,0:T(8,128)(2,1)}, f32[8,384]{1,0:T(8,128)}) custom-call(s32[6]{0:T(128)} %concatenate.51.s_ref, bf16[1568,1536]{1,0:T(8,128)(2,1)} %get-tuple-element.246.qkv_ref.ref, bf16[1568,512]{1,0:T(8,128)(2,1)} %get-tuple-element.283.grad_ref, ...), custom_call_target="tpu_custom_call" | custom-call | flops 50352619520 | bytes 3211264 | tf_op jit(solution)/shard_map/attend_back/pallas_call | solution.py:190
  311.9 3.9 broadcast_select_fusion.1
  317.4 21.0 %attend_back.6 = (bf16[1568,384]{1,0:T(8,128)(2,1)}, bf16[384,512]{1,0:T(8,128)(2,1)}, bf16[384,512]{1,0:T(8,128)(2,1)}, f32[8,384]{1,0:T(8,128)}) custom-call(s32[6]{0:T(128)} %concatenate.54.s_ref, bf16[1568,1536]{1,0:T(8,128)(2,1)} %get-tuple-element.246.qkv_ref.ref, bf16[1568,512]{1,0:T(8,128)(2,1)} %get-tuple-element.283.grad_ref, ...), custom_call_target="tpu_custom_call" | custom-call | flops 50352619520 | bytes 3211264 | tf_op jit(solution)/shard_map/attend_back/pallas_call | solution.py:190
  350.7 21.0 %attend_back.7 = (bf16[1568,384]{1,0:T(8,128)(2,1)}, bf16[384,512]{1,0:T(8,128)(2,1)}, bf16[384,512]{1,0:T(8,128)(2,1)}, f32[8,384]{1,0:T(8,128)}) custom-call(s32[6]{0:T(128)} %concatenate.56.s_ref, bf16[1568,1536]{1,0:T(8,128)(2,1)} %get-tuple-element.246.qkv_ref.ref, bf16[1568,512]{1,0:T(8,128)(2,1)} %get-tuple-element.283.grad_ref, ...), custom_call_target="tpu_custom_call" | custom-call | flops 50352619520 | bytes 3211264 | tf_op jit(solution)/shard_map/attend_back/pallas_call | solution.py:190
  381.4 9.9 %first_grad.1 = (bf16[784,1024]{1,0:T(8,128)(2,1)}, bf16[784,1024]{1,0:T(8,128)(2,1)}) custom-call(s32[5]{0:T(128)} %stack.132.s_ref, bf16[1568,384]{1,0:T(8,128)(2,1)} %get-tuple-element.357.refs_0_, bf16[1568,384]{1,0:T(8,128)(2,1)} %get-tuple-element.358.refs_1_, bf16[1568,384]{1,0:T(8,128)(2,1)} %get-tuple-element.359.refs_2_, ...), custom_call_target="tpu_custom_call" | custom-call | flops 4932501504 | bytes 15925248 | tf_op jit(solution)/shard_map/first_grad/pallas_call | solution.py:399
  391.3 3.8 collective-permute-done.29
  414.1 8.4 %first_back.1 = (bf16[784,1024]{1,0:T(8,128)(2,1)}, f32[8,1024]{1,0:T(8,128)}) custom-call(s32[5]{0:T(128)} %stack.132.s_ref, bf16[784,1024]{1,0:T(8,128)(2,1)} %get-tuple-element.364.g_ref, bf16[784,1024]{1,0:T(8,128)(2,1)} %collective-permute-done.30.r_ref, bf16[784,1024]{1,0:T(8,128)(2,1)} %get-tuple-element.237.x_ref, ...), custom_call_target="tpu_custom_call" | custom-call | bytes 12853248 | tf_op jit(solution)/shard_map/first_back/pallas_call | solution.py:399
  422.5 7.1 %layer_rows.1 = bf16[784,1024]{1,0:T(8,128)(2,1)} custom-call(s32[5]{0:T(128)} %stack.132.s_ref, bf16[784,1024]{1,0:T(8,128)(2,1)} %get-tuple-element.268.o_ref, bf16[784,1024]{1,0:T(8,128)(2,1)} %collective-permute-done.25.r_ref, f32[784,1024]{1,0:T(8,128)} %get-tuple-element.379.mid_ref, f32[1,1024]{1,0:T(1,128)} %bitcast.125), custom_call_target="tpu_custom_call" | custom-call | bytes 12853248 | tf_op jit(solution)/shard_map/layer_rows/pallas_call | solution.py:399
  454.8 8.4 %collective-permute-done.42 = f32[6144]{0:T(1024)S(1)} collective-permute-done((f32[6144]{0:T(1024)S(1)}, f32[6144]{0:T(1024)S(1)}, u32[]{:S(2)}, u32[]{:S(2)}) %collective-permute-start.42) | collective-permute-done | bytes 24608 | tf_op jit(solution)/shard_map/ppermute | solution.py:1459
  470.0 6.4 %collective-permute-start.32 = (bf16[784,1024]{1,0:T(8,128)(2,1)S(1)}, bf16[784,1024]{1,0:T(8,128)(2,1)S(1)}, u32[]{:S(2)}, u32[]{:S(2)}) collective-permute-start(bf16[784,1024]{1,0:T(8,128)(2,1)S(1)} %copy-done), channel_id=1, source_target_pairs={{1,2},{2,1},{5,6},{6,5},{9,10},{10,9},{13,14},{14,13},{17,18},{18,... | collective-permute-start | bytes 4816904 | tf_op jit(solution)/shard_map/ppermute | solution.py:1516
  477.2 4.5 collective-permute-done.51
  490.3 4.9 collective-permute-done.32
  497.5 10.4 %finish_feed.1 = (f32[512,4096]{1,0:T(8,128)}, f32[2,2,512,1024]{3,2,1,0:T(8,128)}) custom-call(s32[5]{0:T(128)} %stack.132.s_ref, bf16[512,1024]{1,0:T(8,128)(2,1)} %bitcast.93, bf16[512,1024]{1,0:T(8,128)(2,1)} %collective-permute-done.35.refs_1_, bf16[512,1024]{1,0:T(8,128)(2,1)} %collective-permute-done.36.refs_2_, bf16[512,1024]{1,0:T(8,128)(2,1)} %copy-done.13, ...), custom_call_target="tpu_custom_call" | custom-call | bytes 16777216 | tf_op jit(solution)/shard_map/finish_feed/pallas_call | solution.py:399
  515.3 7.1 %finish_attention.1 = (f32[512,1024]{1,0:T(8,128)}, f32[512,1024]{1,0:T(8,128)}, f32[512,1024]{1,0:T(8,128)}, f32[512,1024]{1,0:T(8,128)}) custom-call(s32[5]{0:T(128)} %stack.132.s_ref, bf16[640,512]{1,0:T(8,128)(2,1)} %bitcast.96, bf16[640,512]{1,0:T(8,128)(2,1)} %copy-done.19, bf16[640,512]{1,0:T(8,128)(2,1)} %copy-done.20, bf16[640,512]{1,0:T(8,128)(2,1)} %copy-done.21, ...), custom_call_target="tpu_custom_call" | custom-call | bytes 8388608 | tf_op jit(solution)/shard_map/finish_attention/pallas_call | solution.py:399
  (309 shorter events, 149.9 us)
Async XLA Ops:
  0.7 39.8 %collective-permute-start = (bf16[784,1024]{1,0:T(8,128)(2,1)}, bf16[784,1024]{1,0:T(8,128)(2,1)S(1)}, u32[]{:S(2)}, u32[]{:S(2)}) collective-permute-start(bf16[784,1024]{1,0:T(8,128)(2,1)} %bitcast.99), channel_id=1, source_target_pairs={{1,2},{2,1},{5,6},{6,5},{9,10},{10,9},{13,14},{14,13},{17,18},{18,... | collective-permute-start | bytes 4816904 | tf_op jit(solution)/shard_map/ppermute | solution.py:1516
  10.3 30.1 %collective-permute-start.1 = (bf16[256,1536]{1,0:T(8,128)(2,1)}, bf16[256,1536]{1,0:T(8,128)(2,1)}, u32[]{:S(2)}, u32[]{:S(2)}) collective-permute-start(bf16[256,1536]{1,0:T(8,128)(2,1)} %get-tuple-element.226), channel_id=1, source_target_pairs={{0,1},{1,0},{2,3},{3,2},{4,5},{5,4},{6,7},{7,6},{8,9},{9,8},{10,11... | collective-permute-start | bytes 2359304 | tf_op jit(solution)/shard_map/ppermute | solution.py:1504
  16.9 23.6 %collective-permute-start.2 = (f32[6144]{0:T(1024)S(1)}, f32[6144]{0:T(1024)S(1)}, u32[]{:S(2)}, u32[]{:S(2)}) collective-permute-start(f32[6144]{0:T(1024)S(1)} %constant_dynamic-update-slice_fusion.10), channel_id=1, source_target_pairs={{0,1},{1,0},{2,3},{3,2},{4,5},{5,4},{6,7},{7,6},{8,9},{9,8},{10,11... | collective-permute-start | bytes 73736 | tf_op jit(solution)/shard_map/ppermute | solution.py:1504
  40.5 25.0 %collective-permute-start.4 = (bf16[512,1024]{1,0:T(8,128)(2,1)}, bf16[512,1024]{1,0:T(8,128)(2,1)}, u32[]{:S(2)}, u32[]{:S(2)}) collective-permute-start(bf16[512,1024]{1,0:T(8,128)(2,1)} %pack_feed.2), channel_id=1, source_target_pairs={{0,1},{1,0},{2,3},{3,2},{4,5},{5,4},{6,7},{7,6},{8,9},{9,8},{10,11... | collective-permute-start | bytes 3145736 | tf_op jit(solution)/shard_map/ppermute | solution.py:1504
  42.4 19.8 %collective-permute-start.3 = (bf16[256,1536]{1,0:T(8,128)(2,1)}, bf16[256,1536]{1,0:T(8,128)(2,1)}, u32[]{:S(2)}, u32[]{:S(2)}) collective-permute-start(bf16[256,1536]{1,0:T(8,128)(2,1)} %collective-permute-done.1.piece_ref), channel_id=1, source_target_pairs={{0,4},{4,0},{1,5},{5,1},{2,6},{6,2},{3,7},{7,3},{8,12},{12,8},{9,1... | collective-permute-start | bytes 2359304 | tf_op jit(solution)/shard_map/ppermute | solution.py:1510
  68.7 57.4 %collective-permute-start.10 = (bf16[512,1024]{1,0:T(8,128)(2,1)}, bf16[512,1024]{1,0:T(8,128)(2,1)}, u32[]{:S(2)}, u32[]{:S(2)}) collective-permute-start(bf16[512,1024]{1,0:T(8,128)(2,1)} %collective-permute-done.4.x_piece), channel_id=1, source_target_pairs={{0,4},{4,0},{1,5},{5,1},{2,6},{6,2},{3,7},{7,3},{8,12},{12,8},{9,1... | collective-permute-start | bytes 3145736 | tf_op jit(solution)/shard_map/ppermute | solution.py:1510
  71.2 35.0 %collective-permute-start.8 = (bf16[512,1024]{1,0:T(8,128)(2,1)}, bf16[512,1024]{1,0:T(8,128)(2,1)}, u32[]{:S(2)}, u32[]{:S(2)}) collective-permute-start(bf16[512,1024]{1,0:T(8,128)(2,1)} %pack_feed.3), channel_id=1, source_target_pairs={{0,1},{1,0},{2,3},{3,2},{4,5},{5,4},{6,7},{7,6},{8,9},{9,8},{10,11... | collective-permute-start | bytes 3145736 | tf_op jit(solution)/shard_map/ppermute | solution.py:1504
  82.9 23.3 %collective-permute-start.7 = (bf16[128,1024]{1,0:T(8,128)(2,1)S(1)}, bf16[128,1024]{1,0:T(8,128)(2,1)}, u32[]{:S(2)}, u32[]{:S(2)}) collective-permute-start(bf16[128,1024]{1,0:T(8,128)(2,1)S(1)} %collective-permute-done.6.piece_ref), channel_id=1, source_target_pairs={{0,4},{4,0},{1,5},{5,1},{2,6},{6,2},{3,7},{7,3},{8,12},{12,8},{9,1... | collective-permute-start | bytes 786440 | tf_op jit(solution)/shard_map/ppermute | solution.py:1510
  107.7 28.9 %collective-permute-start.9 = (bf16[784,1024]{1,0:T(8,128)(2,1)S(1)}, bf16[784,1024]{1,0:T(8,128)(2,1)}, u32[]{:S(2)}, u32[]{:S(2)}) collective-permute-start(bf16[784,1024]{1,0:T(8,128)(2,1)S(1)} %bitcast.98), channel_id=1, source_target_pairs={{1,2},{2,1},{5,6},{6,5},{9,10},{10,9},{13,14},{14,13},{17,18},{18,... | collective-permute-start | bytes 4816904 | tf_op jit(solution)/shard_map/ppermute | solution.py:1516
  111.7 24.8 %collective-permute-start.11 = (bf16[512,1024]{1,0:T(8,128)(2,1)}, bf16[512,1024]{1,0:T(8,128)(2,1)}, u32[]{:S(2)}, u32[]{:S(2)}) collective-permute-start(bf16[512,1024]{1,0:T(8,128)(2,1)} %collective-permute-done.8.z_piece), channel_id=1, source_target_pairs={{0,8},{8,0},{16,24},{24,16},{1,9},{9,1},{17,25},{25,17},{2,10},{10... | collective-permute-start | bytes 3145736 | tf_op jit(solution)/shard_map/ppermute | solution.py:1513
  229.6 47.2 %collective-permute-start.19 = (bf16[1024,1024]{1,0:T(8,128)(2,1)}, bf16[1024,1024]{1,0:T(8,128)(2,1)}, u32[]{:S(2)}, u32[]{:S(2)}) collective-permute-start(bf16[1024,1024]{1,0:T(8,128)(2,1)} %get-tuple-element.296), channel_id=1, source_target_pairs={{0,4},{4,0},{1,5},{5,1},{2,6},{6,2},{3,7},{7,3},{8,12},{12,8},{9,1... | collective-permute-start | bytes 6291464 | tf_op jit(solution)/shard_map/ppermute | solution.py:1510
  229.8 31.8 %collective-permute-start.17 = (bf16[512,1024]{1,0:T(8,128)(2,1)}, bf16[512,1024]{1,0:T(8,128)(2,1)S(1)}, u32[]{:S(2)}, u32[]{:S(2)}) collective-permute-start(bf16[512,1024]{1,0:T(8,128)(2,1)} %get-tuple-element.294), channel_id=1, source_target_pairs={{0,1},{1,0},{2,3},{3,2},{4,5},{5,4},{6,7},{7,6},{8,9},{9,8},{10,11... | collective-permute-start | bytes 3145736 | tf_op jit(solution)/shard_map/ppermute | solution.py:1504
  229.8 46.8 %collective-permute-start.18 = (bf16[512,1024]{1,0:T(8,128)(2,1)}, bf16[512,1024]{1,0:T(8,128)(2,1)}, u32[]{:S(2)}, u32[]{:S(2)}) collective-permute-start(bf16[512,1024]{1,0:T(8,128)(2,1)} %get-tuple-element.295), channel_id=1, source_target_pairs={{0,1},{1,0},{2,3},{3,2},{4,5},{5,4},{6,7},{7,6},{8,9},{9,8},{10,11... | collective-permute-start | bytes 3145736 | tf_op jit(solution)/shard_map/ppermute | solution.py:1504
  283.6 28.3 %collective-permute-start.20 = (bf16[512,1024]{1,0:T(8,128)(2,1)}, bf16[512,1024]{1,0:T(8,128)(2,1)}, u32[]{:S(2)}, u32[]{:S(2)}) collective-permute-start(bf16[512,1024]{1,0:T(8,128)(2,1)} %get-tuple-element.304), channel_id=1, source_target_pairs={{0,4},{4,0},{1,5},{5,1},{2,6},{6,2},{3,7},{7,3},{8,12},{12,8},{9,1... | collective-permute-start | bytes 3145736 | tf_op jit(solution)/shard_map/ppermute | solution.py:1625
  286.2 25.6 %collective-permute-start.21 = (bf16[512,1024]{1,0:T(8,128)(2,1)}, bf16[512,1024]{1,0:T(8,128)(2,1)}, u32[]{:S(2)}, u32[]{:S(2)}) collective-permute-start(bf16[512,1024]{1,0:T(8,128)(2,1)} %get-tuple-element.305), channel_id=1, source_target_pairs={{0,1},{1,0},{2,3},{3,2},{4,5},{5,4},{6,7},{7,6},{8,9},{9,8},{10,11... | collective-permute-start | bytes 3145736 | tf_op jit(solution)/shard_map/ppermute | solution.py:1504
  286.6 51.9 %collective-permute-start.24 = (bf16[512,512]{1,0:T(8,128)(2,1)}, bf16[512,512]{1,0:T(8,128)(2,1)}, u32[]{:S(2)}, u32[]{:S(2)}) collective-permute-start(bf16[512,512]{1,0:T(8,128)(2,1)} %get-tuple-element.307), channel_id=1, source_target_pairs={{0,1},{1,0},{2,3},{3,2},{4,5},{5,4},{6,7},{7,6},{8,9},{9,8},{10,11... | collective-permute-start | bytes 1572872 | tf_op jit(solution)/shard_map/ppermute | solution.py:1504
  315.8 22.7 %collective-permute-start.22 = (bf16[512,1024]{1,0:T(8,128)(2,1)}, bf16[512,1024]{1,0:T(8,128)(2,1)}, u32[]{:S(2)}, u32[]{:S(2)}) collective-permute-start(bf16[512,1024]{1,0:T(8,128)(2,1)} %get-tuple-element.320), channel_id=1, source_target_pairs={{0,8},{8,0},{16,24},{24,16},{1,9},{9,1},{17,25},{25,17},{2,10},{10... | collective-permute-start | bytes 3145736 | tf_op jit(solution)/shard_map/ppermute | solution.py:1420
  317.1 21.4 %collective-permute-start.23 = (bf16[768,512]{1,0:T(8,128)(2,1)}, bf16[768,512]{1,0:T(8,128)(2,1)}, u32[]{:S(2)}, u32[]{:S(2)}) collective-permute-start(bf16[768,512]{1,0:T(8,128)(2,1)} %pad_maximum_fusion), channel_id=1, source_target_pairs={{0,1},{1,0},{2,3},{3,2},{4,5},{5,4},{6,7},{7,6},{8,9},{9,8},{10,11... | collective-permute-start | bytes 2359304 | tf_op jit(solution)/shard_map/ppermute | solution.py:1443
  344.9 29.1 %collective-permute-start.25 = (bf16[784,1024]{1,0:T(8,128)(2,1)}, bf16[784,1024]{1,0:T(8,128)(2,1)}, u32[]{:S(2)}, u32[]{:S(2)}) collective-permute-start(bf16[784,1024]{1,0:T(8,128)(2,1)} %get-tuple-element.337), channel_id=1, source_target_pairs={{0,2},{2,0},{1,3},{3,1},{4,6},{6,4},{5,7},{7,5},{8,10},{10,8},{9,1... | collective-permute-start | bytes 4816904 | tf_op jit(solution)/shard_map/ppermute | solution.py:1507
  348.1 26.9 %collective-permute-start.27 = (bf16[640,512]{1,0:T(8,128)(2,1)}, bf16[640,512]{1,0:T(8,128)(2,1)}, u32[]{:S(2)}, u32[]{:S(2)}) collective-permute-start(bf16[640,512]{1,0:T(8,128)(2,1)} %get-tuple-element.336), channel_id=1, source_target_pairs={{0,4},{4,0},{1,5},{5,1},{2,6},{6,2},{3,7},{7,3},{8,12},{12,8},{9,1... | collective-permute-start | bytes 1966088 | tf_op jit(solution)/shard_map/ppermute | solution.py:1451
  348.4 26.6 %collective-permute-start.26 = (bf16[256,1024]{1,0:T(8,128)(2,1)S(1)}, bf16[256,1024]{1,0:T(8,128)(2,1)}, u32[]{:S(2)}, u32[]{:S(2)}) collective-permute-start(bf16[256,1024]{1,0:T(8,128)(2,1)S(1)} %get-tuple-element.334), channel_id=1, source_target_pairs={{0,16},{8,24},{16,0},{24,8},{1,17},{9,25},{17,1},{25,9},{2,18},{10... | collective-permute-start | bytes 1572872 | tf_op jit(solution)/shard_map/ppermute | solution.py:1420
  374.0 21.1 %collective-permute-start.28 = (bf16[768,512]{1,0:T(8,128)(2,1)}, bf16[768,512]{1,0:T(8,128)(2,1)}, u32[]{:S(2)}, u32[]{:S(2)}) collective-permute-start(bf16[768,512]{1,0:T(8,128)(2,1)} %pad_maximum_fusion.2), channel_id=1, source_target_pairs={{0,1},{1,0},{2,3},{3,2},{4,5},{5,4},{6,7},{7,6},{8,9},{9,8},{10,11... | collective-permute-start | bytes 2359304 | tf_op jit(solution)/shard_map/ppermute | solution.py:1443
  377.5 25.7 %collective-permute-start.31 = (bf16[256,1024]{1,0:T(8,128)(2,1)S(1)}, bf16[256,1024]{1,0:T(8,128)(2,1)}, u32[]{:S(2)}, u32[]{:S(2)}) collective-permute-start(bf16[256,1024]{1,0:T(8,128)(2,1)S(1)} %add_convert_fusion.9), channel_id=1, source_target_pairs={{0,16},{8,24},{16,0},{24,8},{1,17},{9,25},{17,1},{25,9},{2,18},{10... | collective-permute-start | bytes 1572872 | tf_op jit(solution)/shard_map/ppermute | solution.py:1420
  404.7 32.2 %collective-permute-start.35 = (bf16[512,1024]{1,0:T(8,128)(2,1)S(1)}, bf16[512,1024]{1,0:T(8,128)(2,1)}, u32[]{:S(2)}, u32[]{:S(2)}) collective-permute-start(bf16[512,1024]{1,0:T(8,128)(2,1)S(1)} %bitcast.90), channel_id=1, source_target_pairs={{0,4},{4,0},{1,5},{5,1},{2,6},{6,2},{3,7},{7,3},{8,12},{12,8},{9,1... | collective-permute-start | bytes 3145736 | tf_op jit(solution)/shard_map/ppermute | solution.py:1434
  406.1 30.8 %collective-permute-start.36 = (bf16[512,1024]{1,0:T(8,128)(2,1)S(1)}, bf16[512,1024]{1,0:T(8,128)(2,1)}, u32[]{:S(2)}, u32[]{:S(2)}) collective-permute-start(bf16[512,1024]{1,0:T(8,128)(2,1)S(1)} %bitcast.91), channel_id=1, source_target_pairs={{0,8},{8,0},{16,24},{24,16},{1,9},{9,1},{17,25},{25,17},{2,10},{10... | collective-permute-start | bytes 3145736 | tf_op jit(solution)/shard_map/ppermute | solution.py:1420
  411.2 25.7 %collective-permute-start.34 = (bf16[384,512]{1,0:T(8,128)(2,1)}, bf16[384,512]{1,0:T(8,128)(2,1)S(1)}, u32[]{:S(2)}, u32[]{:S(2)}) collective-permute-start(bf16[384,512]{1,0:T(8,128)(2,1)} %get-tuple-element.369), channel_id=1, source_target_pairs={{0,4},{4,0},{1,5},{5,1},{2,6},{6,2},{3,7},{7,3},{8,12},{12,8},{9,1... | collective-permute-start | bytes 1179656 | tf_op jit(solution)/shard_map/ppermute | solution.py:1451
  412.0 21.5 %collective-permute-start.33 = (bf16[160,512]{1,0:T(8,128)(2,1)}, bf16[160,512]{1,0:T(8,128)(2,1)}, u32[]{:S(2)}, u32[]{:S(2)}) collective-permute-start(bf16[160,512]{1,0:T(8,128)(2,1)} %get-tuple-element.371), channel_id=1, source_target_pairs={{0,16},{8,24},{16,0},{24,8},{1,17},{9,25},{17,1},{25,9},{2,18},{10... | collective-permute-start | bytes 491528 | tf_op jit(solution)/shard_map/ppermute | solution.py:1394
  444.5 32.8 %collective-permute-start.48 = (bf16[512,1024]{1,0:T(8,128)(2,1)S(1)}, bf16[512,1024]{1,0:T(8,128)(2,1)S(1)}, u32[]{:S(2)}, u32[]{:S(2)}) collective-permute-start(bf16[512,1024]{1,0:T(8,128)(2,1)S(1)} %bitcast.92), channel_id=1, source_target_pairs={{0,2},{2,0},{1,3},{3,1},{4,6},{6,4},{5,7},{7,5},{8,10},{10,8},{9,1... | collective-permute-start | bytes 3145736 | tf_op jit(solution)/shard_map/ppermute | solution.py:1435
  445.2 36.5 %collective-permute-start.47 = (bf16[512,1024]{1,0:T(8,128)(2,1)}, bf16[512,1024]{1,0:T(8,128)(2,1)S(1)}, u32[]{:S(2)}, u32[]{:S(2)}) collective-permute-start(bf16[512,1024]{1,0:T(8,128)(2,1)} %collective-permute-done.36.refs_2_), channel_id=1, source_target_pairs={{0,4},{4,0},{1,5},{5,1},{2,6},{6,2},{3,7},{7,3},{8,12},{12,8},{9,1... | collective-permute-start | bytes 3145736 | tf_op jit(solution)/shard_map/ppermute | solution.py:1435
  464.7 19.5 %collective-permute-start.45 = (bf16[640,512]{1,0:T(8,128)(2,1)S(1)}, bf16[640,512]{1,0:T(8,128)(2,1)S(1)}, u32[]{:S(2)}, u32[]{:S(2)}) collective-permute-start(bf16[640,512]{1,0:T(8,128)(2,1)S(1)} %bitcast.94), channel_id=1, source_target_pairs={{0,4},{4,0},{1,5},{5,1},{2,6},{6,2},{3,7},{7,3},{8,12},{12,8},{9,1... | collective-permute-start | bytes 1966088 | tf_op jit(solution)/shard_map/ppermute | solution.py:1408
  470.0 25.2 %collective-permute-start.32 = (bf16[784,1024]{1,0:T(8,128)(2,1)S(1)}, bf16[784,1024]{1,0:T(8,128)(2,1)S(1)}, u32[]{:S(2)}, u32[]{:S(2)}) collective-permute-start(bf16[784,1024]{1,0:T(8,128)(2,1)S(1)} %copy-done), channel_id=1, source_target_pairs={{1,2},{2,1},{5,6},{6,5},{9,10},{10,9},{13,14},{14,13},{17,18},{18,... | collective-permute-start | bytes 4816904 | tf_op jit(solution)/shard_map/ppermute | solution.py:1516
  481.7 30.3 %collective-permute-start.41 = (bf16[784,1024]{1,0:T(8,128)(2,1)}, bf16[784,1024]{1,0:T(8,128)(2,1)S(1)}, u32[]{:S(2)}, u32[]{:S(2)}) collective-permute-start(bf16[784,1024]{1,0:T(8,128)(2,1)} %get-tuple-element.402), channel_id=1, source_target_pairs={{1,2},{2,1},{5,6},{6,5},{9,10},{10,9},{13,14},{14,13},{17,18},{18,... | collective-permute-start | bytes 4816904 | tf_op jit(solution)/shard_map/ppermute | solution.py:1516
  (74 other events, 601.4 us)

commit v9 on v8

--- a/solution.py
+++ b/solution.py
@@ -131,8 +131,11 @@
 def attend_back_kernel(
     tile, rows, padded, s_ref, qkv_ref, grad_ref, out_ref, lse_ref, first_ref, dqkv_ref, send_ref,
     keep_ref, sums_ref, q_t, g_t, k_t, delta, dq_t, dk_t, dv_t, all_t, scores, d_probs,
+    rows_in, sem,
 ):
     scale = HEAD_DIM**-0.5
+    fetch = pltpu.make_async_copy(first_ref, rows_in, sem)
+    fetch.start()
     q_t[:, :rows] = qkv_ref[:, :PAIR].T
     g_t[:, :rows] = grad_ref[...].T
     if padded > rows:
@@ -170,8 +173,9 @@
         dqkv_ref[:, lanes] = all_t[lanes, :].T
     sums_ref[...] = contract(jnp.ones((8, rows), BF16), all_t[...], 1, 1)
     own = first_ref.shape[1] // 2
+    fetch.wait()
     for h in range(2):
-        grad = contract(all_t[...], first_ref[:, h * own : (h + 1) * own], 1, 0).astype(BF16)
+        grad = contract(all_t[...], rows_in[:, h * own : (h + 1) * own], 1, 0).astype(BF16)
 
         @pl.when(s_ref[0] == h)
         def _():
@@ -197,7 +201,7 @@
                 pl.BlockSpec((rows, PAIR), lambda i, s: (0, s[5])),
                 pl.BlockSpec((rows, PAIR), lambda i, s: (0, s[5])),
                 pl.BlockSpec((None, 2, lse.shape[2]), lambda i, s: (s[5], 0, 0)),
-                pl.BlockSpec((rows, width), lambda i, s: (0, 0), pipeline_mode=pl.Buffered(1)),
+                pl.BlockSpec(memory_space=pl.ANY),
             ],
             out_specs=[
                 pl.BlockSpec((rows, 3 * PAIR), lambda i, s: (0, i)),
@@ -216,6 +220,8 @@
                 pltpu.VMEM((3 * PAIR, rows), BF16),
                 pltpu.VMEM((2, rows, tile), F32),
                 pltpu.VMEM((2, rows, tile), F32),
+                pltpu.VMEM((rows, width), BF16),
+                pltpu.SemaphoreType.DMA,
             ],
         ),
         out_shape=[

time: 532 us -> 530 us (level)
  no operation moved by 1% of the time
where the time goes in v9:
time: 530 us; the launch traced here: 521 us
  Pallas kernels  269 us (51%)
  waiting for transfers between devices  112 us (21%)
  starting transfers between devices  77.1 us (15%)
  other arithmetic  36.9 us (7%)
  local copies, waits for them, and re-layouts  24.1 us (5%)
    pallas_call x14, Pallas kernels, run(): pl.pallas_call(kernel, grid_spec=pltpu.PrefetchScalarGridSpec(num_scalar_...  97.7 us
    pallas_call x4, Pallas kernels, attend_back(): pl.pallas_call(functools.partial(attend_back_kernel, tile, rows, padded),...  80.1 us
    pallas_call x1, Pallas kernels, feed(): pl.pallas_call(feed_kernel, grid_spec=pltpu.PrefetchScalarGridSpec(num_sc...  60.5 us
    ppermute x9, waiting for transfers between devices, swap_half(): return lax.ppermute(values, 'half', SWAP)  41.2 us
    pallas_call x2, Pallas kernels, attend(): pl.pallas_call(kernel if kept is None else lambda ref, a, b, *rest: kerne...  30.6 us
    ppermute x12, starting transfers between devices, exchange(): lax.ppermute(values, 'line', [(i, i ^ 1 << bit) for i in range(deep)])  24.3 us
    ppermute x4, starting transfers between devices, cross_over(): return lax.ppermute(values, ('core', 'half'), cross)  15.9 us
    ppermute x12, waiting for transfers between devices, exchange(): lax.ppermute(values, 'line', [(i, i ^ 1 << bit) for i in range(deep)])  13.5 us
  transfers between devices with their start and end apart: 60, of which 23 were waited for; matrix products, arithmetic and copies ran while one was open for 8% of the time, Pallas kernels for 36%

profile of v9, /device:TPU:1, one launch (start us, length us, event | category | flops | bytes accessed | tf_op | source)
XLA Modules:
  0.0 521.1 jit_solution(15869808638395098156)
XLA Ops:
  0.7 4.5 collective-permute-start
  5.8 4.5 pack_qkv.1
  18.4 22.1 %collective-permute-done.2 = f32[6144]{0:T(1024)S(1)} collective-permute-done((f32[6144]{0:T(1024)S(1)}, f32[6144]{0:T(1024)S(1)}, u32[]{:S(2)}, u32[]{:S(2)}) %collective-permute-start.2) | collective-permute-done | bytes 24608 | tf_op jit(solution)/shard_map/ppermute | solution.py:1510
  45.5 4.2 first_norm.1
  49.7 12.5 %collective-permute-done.3.beside_ref = bf16[256,1536]{1,0:T(8,128)(2,1)} collective-permute-done((bf16[256,1536]{1,0:T(8,128)(2,1)}, bf16[256,1536]{1,0:T(8,128)(2,1)}, u32[]{:S(2)}, u32[]{:S(2)}) %collective-permute-start.3) | collective-permute-done | bytes 786464 | tf_op jit(solution)/shard_map/ppermute | solution.py:1516
  71.8 11.1 %project.1 = (bf16[1568,1536]{1,0:T(8,128)(2,1)}, bf16[1024,1536]{1,0:T(8,128)(2,1)}, bf16[1568,1024]{1,0:T(8,128)(2,1)}) custom-call(s32[5]{0:T(128)} %stack.132.s_ref, bf16[784,1024]{1,0:T(8,128)(2,1)} %get-tuple-element.238.mine_ref, bf16[784,1024]{1,0:T(8,128)(2,1)} %collective-permute-done.5.theirs_ref, bf16[512,1536]{1,0:T(8,128)(2,1)} %get-tuple-element.242.own_ref, ...), custom_call_target="tpu_custom_call" | custom-call | flops 4932501504 | bytes 12726272 | tf_op jit(solution)/shard_map/project/pallas_call | solution.py:405
  84.2 22.0 %attend.2 = (bf16[1568,512]{1,0:T(8,128)(2,1)}, f32[4,2,1664]{2,1,0:T(2,128)}) custom-call(bf16[1568,1536]{1,0:T(8,128)(2,1)} %get-tuple-element.246.qkv_ref.ref), custom_call_target="tpu_custom_call" | custom-call | flops 60423143424 | bytes 4816896 | tf_op jit(solution)/shard_map/attend/pallas_call | solution.py:101
  107.7 4.1 collective-permute-start.9
  113.1 8.7 %attend.3 = (bf16[1568,512]{1,0:T(8,128)(2,1)}, f32[4,2,1664]{2,1,0:T(2,128)}) custom-call(bf16[1568,1536]{1,0:T(8,128)(2,1)} %get-tuple-element.246.qkv_ref.ref, bf16[1568,512]{1,0:T(8,128)(2,1)} %get-tuple-element.247.a, f32[4,2,1664]{2,1,0:T(2,128)} %copy.58.b), custom_call_target="tpu_custom_call", output_to_operand_aliasing={{0}: (1, {}), {1}: (2, {})} | custom-call | flops 20141047808 | bytes 1605632 | tf_op jit(solution)/shard_map/attend/pallas_call | solution.py:101
  121.8 4.3 out_other.1
  126.1 10.5 %collective-permute-done.11.z_beside = bf16[512,1024]{1,0:T(8,128)(2,1)} collective-permute-done((bf16[512,1024]{1,0:T(8,128)(2,1)}, bf16[512,1024]{1,0:T(8,128)(2,1)}, u32[]{:S(2)}, u32[]{:S(2)}) %collective-permute-start.11) | collective-permute-done | bytes 1048608 | tf_op jit(solution)/shard_map/ppermute | solution.py:1519
  140.8 6.1 %second_norm.1 = (f32[784,1024]{1,0:T(8,128)}, bf16[784,1024]{1,0:T(8,128)(2,1)}) custom-call(s32[5]{0:T(128)} %stack.132.s_ref, bf16[1568,512]{1,0:T(8,128)(2,1)} %get-tuple-element.254.mixed_ref.out_ref, bf16[512,1024]{1,0:T(8,128)(2,1)} %get-tuple-element.255.w_ref, bf16[784,1024]{1,0:T(8,128)(2,1)} %get-tuple-element.237.x_ref, ...), custom_call_target="tpu_custom_call" | custom-call | flops 822083584 | bytes 11755520 | tf_op jit(solution)/shard_map/second_norm/pallas_call | solution.py:405
  148.1 4.1 collective-permute-done.13.x_other
  152.8 60.5 %feed.1 = (bf16[784,1024]{1,0:T(8,128)(2,1)}, bf16[784,1024]{1,0:T(8,128)(2,1)}, bf16[784,1024]{1,0:T(8,128)(2,1)}, bf16[784,1024]{1,0:T(8,128)(2,1)}, bf16[512,...) custom-call(s32[5]{0:T(128)} %stack.132.s_ref, ...), custom_call_target="tpu_custom_call" | custom-call | flops 39460012032 | bytes 25690112 | tf_op jit(solution)/shard_map/feed/pallas_call | solution.py:363
  218.2 8.8 %second_back.1 = (bf16[784,1024]{1,0:T(8,128)(2,1)}, f32[8,1024]{1,0:T(8,128)}) custom-call(s32[5]{0:T(128)} %stack.132.s_ref, bf16[784,1024]{1,0:T(8,128)(2,1)} %get-tuple-element.275.g_ref, bf16[784,1024]{1,0:T(8,128)(2,1)} %copy-done.8, f32[784,1024]{1,0:T(8,128)} %get-tuple-element.379.mid_ref, bf16[784,1024]{1,0:T(8,128)(2,1)} %copy-done.1, ...), custom_call_target="tpu_custom_call" | custom-call | bytes 16064512 | tf_op jit(solution)/shard_map/second_back/pallas_call | solution.py:405
  231.2 9.4 %mixed_back.1 = (bf16[1568,512]{1,0:T(8,128)(2,1)}, bf16[512,512]{1,0:T(8,128)(2,1)}, bf16[512,512]{1,0:T(8,128)(2,1)}) custom-call(s32[5]{0:T(128)} %stack.132.s_ref, bf16[784,1024]{1,0:T(8,128)(2,1)} %get-tuple-element.280.mine_ref.wide_ref, bf16[784,1024]{1,0:T(8,128)(2,1)} %collective-permute-done.16.theirs_ref, ...), custom_call_target="tpu_custom_call" | custom-call | flops 3288334336 | bytes 11730944 | tf_op jit(solution)/shard_map/mixed_back/pallas_call | solution.py:405
  240.7 20.0 %attend_back.4 = (bf16[1568,384]{1,0:T(8,128)(2,1)}, bf16[384,512]{1,0:T(8,128)(2,1)}, bf16[384,512]{1,0:T(8,128)(2,1)}, f32[8,384]{1,0:T(8,128)}) custom-call(s32[6]{0:T(128)} %concatenate.50.s_ref, bf16[1568,1536]{1,0:T(8,128)(2,1)} %get-tuple-element.246.qkv_ref.ref, bf16[1568,512]{1,0:T(8,128)(2,1)} %get-tuple-element.283.grad_ref, ...), custom_call_target="tpu_custom_call" | custom-call | flops 50352619520 | bytes 3211264 | tf_op jit(solution)/shard_map/attend_back/pallas_call | solution.py:194
  260.7 16.0 %collective-permute-done.18 = bf16[512,1024]{1,0:T(8,128)(2,1)} collective-permute-done((bf16[512,1024]{1,0:T(8,128)(2,1)}, bf16[512,1024]{1,0:T(8,128)(2,1)}, u32[]{:S(2)}, u32[]{:S(2)}) %collective-permute-start.18) | collective-permute-done | bytes 1048608 | tf_op jit(solution)/shard_map/ppermute | solution.py:1510
  287.7 20.0 %attend_back.5 = (bf16[1568,384]{1,0:T(8,128)(2,1)}, bf16[384,512]{1,0:T(8,128)(2,1)}, bf16[384,512]{1,0:T(8,128)(2,1)}, f32[8,384]{1,0:T(8,128)}) custom-call(s32[6]{0:T(128)} %concatenate.51.s_ref, bf16[1568,1536]{1,0:T(8,128)(2,1)} %get-tuple-element.246.qkv_ref.ref, bf16[1568,512]{1,0:T(8,128)(2,1)} %get-tuple-element.283.grad_ref, ...), custom_call_target="tpu_custom_call" | custom-call | flops 50352619520 | bytes 3211264 | tf_op jit(solution)/shard_map/attend_back/pallas_call | solution.py:194
  311.0 3.9 broadcast_select_fusion.1
  316.5 20.1 %attend_back.6 = (bf16[1568,384]{1,0:T(8,128)(2,1)}, bf16[384,512]{1,0:T(8,128)(2,1)}, bf16[384,512]{1,0:T(8,128)(2,1)}, f32[8,384]{1,0:T(8,128)}) custom-call(s32[6]{0:T(128)} %concatenate.54.s_ref, bf16[1568,1536]{1,0:T(8,128)(2,1)} %get-tuple-element.246.qkv_ref.ref, bf16[1568,512]{1,0:T(8,128)(2,1)} %get-tuple-element.283.grad_ref, ...), custom_call_target="tpu_custom_call" | custom-call | flops 50352619520 | bytes 3211264 | tf_op jit(solution)/shard_map/attend_back/pallas_call | solution.py:194
  349.8 20.1 %attend_back.7 = (bf16[1568,384]{1,0:T(8,128)(2,1)}, bf16[384,512]{1,0:T(8,128)(2,1)}, bf16[384,512]{1,0:T(8,128)(2,1)}, f32[8,384]{1,0:T(8,128)}) custom-call(s32[6]{0:T(128)} %concatenate.56.s_ref, bf16[1568,1536]{1,0:T(8,128)(2,1)} %get-tuple-element.246.qkv_ref.ref, bf16[1568,512]{1,0:T(8,128)(2,1)} %get-tuple-element.283.grad_ref, ...), custom_call_target="tpu_custom_call" | custom-call | flops 50352619520 | bytes 3211264 | tf_op jit(solution)/shard_map/attend_back/pallas_call | solution.py:194
  376.6 3.9 collective-permute-start.29
  380.5 9.9 %first_grad.1 = (bf16[784,1024]{1,0:T(8,128)(2,1)}, bf16[784,1024]{1,0:T(8,128)(2,1)}) custom-call(s32[5]{0:T(128)} %stack.132.s_ref, bf16[1568,384]{1,0:T(8,128)(2,1)} %get-tuple-element.357.refs_0_, bf16[1568,384]{1,0:T(8,128)(2,1)} %get-tuple-element.358.refs_1_, bf16[1568,384]{1,0:T(8,128)(2,1)} %get-tuple-element.359.refs_2_, ...), custom_call_target="tpu_custom_call" | custom-call | flops 4932501504 | bytes 15925248 | tf_op jit(solution)/shard_map/first_grad/pallas_call | solution.py:405
  413.2 8.4 %first_back.1 = (bf16[784,1024]{1,0:T(8,128)(2,1)}, f32[8,1024]{1,0:T(8,128)}) custom-call(s32[5]{0:T(128)} %stack.132.s_ref, bf16[784,1024]{1,0:T(8,128)(2,1)} %get-tuple-element.364.g_ref, bf16[784,1024]{1,0:T(8,128)(2,1)} %collective-permute-done.30.r_ref, bf16[784,1024]{1,0:T(8,128)(2,1)} %get-tuple-element.237.x_ref, ...), custom_call_target="tpu_custom_call" | custom-call | bytes 12853248 | tf_op jit(solution)/shard_map/first_back/pallas_call | solution.py:405
  421.5 7.1 %layer_rows.1 = bf16[784,1024]{1,0:T(8,128)(2,1)} custom-call(s32[5]{0:T(128)} %stack.132.s_ref, bf16[784,1024]{1,0:T(8,128)(2,1)} %get-tuple-element.268.o_ref, bf16[784,1024]{1,0:T(8,128)(2,1)} %collective-permute-done.25.r_ref, f32[784,1024]{1,0:T(8,128)} %get-tuple-element.379.mid_ref, f32[1,1024]{1,0:T(1,128)} %bitcast.125), custom_call_target="tpu_custom_call" | custom-call | bytes 12853248 | tf_op jit(solution)/shard_map/layer_rows/pallas_call | solution.py:405
  453.9 8.4 %collective-permute-done.42 = f32[6144]{0:T(1024)S(1)} collective-permute-done((f32[6144]{0:T(1024)S(1)}, f32[6144]{0:T(1024)S(1)}, u32[]{:S(2)}, u32[]{:S(2)}) %collective-permute-start.42) | collective-permute-done | bytes 24608 | tf_op jit(solution)/shard_map/ppermute | solution.py:1465
  469.0 5.4 %collective-permute-start.32 = (bf16[784,1024]{1,0:T(8,128)(2,1)S(1)}, bf16[784,1024]{1,0:T(8,128)(2,1)S(1)}, u32[]{:S(2)}, u32[]{:S(2)}) collective-permute-start(bf16[784,1024]{1,0:T(8,128)(2,1)S(1)} %copy-done), channel_id=1, source_target_pairs={{1,2},{2,1},{5,6},{6,5},{9,10},{10,9},{13,14},{14,13},{17,18},{18,... | collective-permute-start | bytes 4816904 | tf_op jit(solution)/shard_map/ppermute | solution.py:1522
  475.4 5.4 %collective-permute-done.51 = bf16[192,512]{1,0:T(8,128)(2,1)S(1)} collective-permute-done((bf16[192,512]{1,0:T(8,128)(2,1)S(1)}, bf16[192,512]{1,0:T(8,128)(2,1)S(1)}, u32[]{:S(2)}, u32[]{:S(2)}) %collective-permute-start.51) | collective-permute-done | bytes 196640 | tf_op jit(solution)/shard_map/ppermute | solution.py:1400
  488.5 4.9 collective-permute-done.32
  495.6 10.4 %finish_feed.1 = (f32[512,4096]{1,0:T(8,128)}, f32[2,2,512,1024]{3,2,1,0:T(8,128)}) custom-call(s32[5]{0:T(128)} %stack.132.s_ref, bf16[512,1024]{1,0:T(8,128)(2,1)} %bitcast.93, bf16[512,1024]{1,0:T(8,128)(2,1)} %collective-permute-done.35.refs_1_, bf16[512,1024]{1,0:T(8,128)(2,1)} %collective-permute-done.36.refs_2_, bf16[512,1024]{1,0:T(8,128)(2,1)} %copy-done.13, ...), custom_call_target="tpu_custom_call" | custom-call | bytes 16777216 | tf_op jit(solution)/shard_map/finish_feed/pallas_call | solution.py:405
  513.4 7.1 %finish_attention.1 = (f32[512,1024]{1,0:T(8,128)}, f32[512,1024]{1,0:T(8,128)}, f32[512,1024]{1,0:T(8,128)}, f32[512,1024]{1,0:T(8,128)}) custom-call(s32[5]{0:T(128)} %stack.132.s_ref, bf16[640,512]{1,0:T(8,128)(2,1)} %bitcast.96, bf16[640,512]{1,0:T(8,128)(2,1)} %copy-done.19, bf16[640,512]{1,0:T(8,128)(2,1)} %copy-done.20, bf16[640,512]{1,0:T(8,128)(2,1)} %copy-done.21, ...), custom_call_target="tpu_custom_call" | custom-call | bytes 8388608 | tf_op jit(solution)/shard_map/finish_attention/pallas_call | solution.py:405
  (309 shorter events, 150.7 us)
Async XLA Ops:
  0.7 39.8 %collective-permute-start = (bf16[784,1024]{1,0:T(8,128)(2,1)}, bf16[784,1024]{1,0:T(8,128)(2,1)S(1)}, u32[]{:S(2)}, u32[]{:S(2)}) collective-permute-start(bf16[784,1024]{1,0:T(8,128)(2,1)} %bitcast.99), channel_id=1, source_target_pairs={{1,2},{2,1},{5,6},{6,5},{9,10},{10,9},{13,14},{14,13},{17,18},{18,... | collective-permute-start | bytes 4816904 | tf_op jit(solution)/shard_map/ppermute | solution.py:1522
  10.3 30.1 %collective-permute-start.1 = (bf16[256,1536]{1,0:T(8,128)(2,1)}, bf16[256,1536]{1,0:T(8,128)(2,1)}, u32[]{:S(2)}, u32[]{:S(2)}) collective-permute-start(bf16[256,1536]{1,0:T(8,128)(2,1)} %get-tuple-element.226), channel_id=1, source_target_pairs={{0,1},{1,0},{2,3},{3,2},{4,5},{5,4},{6,7},{7,6},{8,9},{9,8},{10,11... | collective-permute-start | bytes 2359304 | tf_op jit(solution)/shard_map/ppermute | solution.py:1510
  16.9 23.6 %collective-permute-start.2 = (f32[6144]{0:T(1024)S(1)}, f32[6144]{0:T(1024)S(1)}, u32[]{:S(2)}, u32[]{:S(2)}) collective-permute-start(f32[6144]{0:T(1024)S(1)} %constant_dynamic-update-slice_fusion.10), channel_id=1, source_target_pairs={{0,1},{1,0},{2,3},{3,2},{4,5},{5,4},{6,7},{7,6},{8,9},{9,8},{10,11... | collective-permute-start | bytes 73736 | tf_op jit(solution)/shard_map/ppermute | solution.py:1510
  40.5 25.0 %collective-permute-start.4 = (bf16[512,1024]{1,0:T(8,128)(2,1)}, bf16[512,1024]{1,0:T(8,128)(2,1)}, u32[]{:S(2)}, u32[]{:S(2)}) collective-permute-start(bf16[512,1024]{1,0:T(8,128)(2,1)} %pack_feed.2), channel_id=1, source_target_pairs={{0,1},{1,0},{2,3},{3,2},{4,5},{5,4},{6,7},{7,6},{8,9},{9,8},{10,11... | collective-permute-start | bytes 3145736 | tf_op jit(solution)/shard_map/ppermute | solution.py:1510
  42.4 19.8 %collective-permute-start.3 = (bf16[256,1536]{1,0:T(8,128)(2,1)}, bf16[256,1536]{1,0:T(8,128)(2,1)}, u32[]{:S(2)}, u32[]{:S(2)}) collective-permute-start(bf16[256,1536]{1,0:T(8,128)(2,1)} %collective-permute-done.1.piece_ref), channel_id=1, source_target_pairs={{0,4},{4,0},{1,5},{5,1},{2,6},{6,2},{3,7},{7,3},{8,12},{12,8},{9,1... | collective-permute-start | bytes 2359304 | tf_op jit(solution)/shard_map/ppermute | solution.py:1516
  68.7 57.4 %collective-permute-start.10 = (bf16[512,1024]{1,0:T(8,128)(2,1)}, bf16[512,1024]{1,0:T(8,128)(2,1)}, u32[]{:S(2)}, u32[]{:S(2)}) collective-permute-start(bf16[512,1024]{1,0:T(8,128)(2,1)} %collective-permute-done.4.x_piece), channel_id=1, source_target_pairs={{0,4},{4,0},{1,5},{5,1},{2,6},{6,2},{3,7},{7,3},{8,12},{12,8},{9,1... | collective-permute-start | bytes 3145736 | tf_op jit(solution)/shard_map/ppermute | solution.py:1516
  71.2 35.0 %collective-permute-start.8 = (bf16[512,1024]{1,0:T(8,128)(2,1)}, bf16[512,1024]{1,0:T(8,128)(2,1)}, u32[]{:S(2)}, u32[]{:S(2)}) collective-permute-start(bf16[512,1024]{1,0:T(8,128)(2,1)} %pack_feed.3), channel_id=1, source_target_pairs={{0,1},{1,0},{2,3},{3,2},{4,5},{5,4},{6,7},{7,6},{8,9},{9,8},{10,11... | collective-permute-start | bytes 3145736 | tf_op jit(solution)/shard_map/ppermute | solution.py:1510
  82.9 23.3 %collective-permute-start.7 = (bf16[128,1024]{1,0:T(8,128)(2,1)S(1)}, bf16[128,1024]{1,0:T(8,128)(2,1)}, u32[]{:S(2)}, u32[]{:S(2)}) collective-permute-start(bf16[128,1024]{1,0:T(8,128)(2,1)S(1)} %collective-permute-done.6.piece_ref), channel_id=1, source_target_pairs={{0,4},{4,0},{1,5},{5,1},{2,6},{6,2},{3,7},{7,3},{8,12},{12,8},{9,1... | collective-permute-start | bytes 786440 | tf_op jit(solution)/shard_map/ppermute | solution.py:1516
  107.7 28.9 %collective-permute-start.9 = (bf16[784,1024]{1,0:T(8,128)(2,1)S(1)}, bf16[784,1024]{1,0:T(8,128)(2,1)}, u32[]{:S(2)}, u32[]{:S(2)}) collective-permute-start(bf16[784,1024]{1,0:T(8,128)(2,1)S(1)} %bitcast.98), channel_id=1, source_target_pairs={{1,2},{2,1},{5,6},{6,5},{9,10},{10,9},{13,14},{14,13},{17,18},{18,... | collective-permute-start | bytes 4816904 | tf_op jit(solution)/shard_map/ppermute | solution.py:1522
  111.7 24.8 %collective-permute-start.11 = (bf16[512,1024]{1,0:T(8,128)(2,1)}, bf16[512,1024]{1,0:T(8,128)(2,1)}, u32[]{:S(2)}, u32[]{:S(2)}) collective-permute-start(bf16[512,1024]{1,0:T(8,128)(2,1)} %collective-permute-done.8.z_piece), channel_id=1, source_target_pairs={{0,8},{8,0},{16,24},{24,16},{1,9},{9,1},{17,25},{25,17},{2,10},{10... | collective-permute-start | bytes 3145736 | tf_op jit(solution)/shard_map/ppermute | solution.py:1519
  229.6 47.2 %collective-permute-start.19 = (bf16[1024,1024]{1,0:T(8,128)(2,1)}, bf16[1024,1024]{1,0:T(8,128)(2,1)}, u32[]{:S(2)}, u32[]{:S(2)}) collective-permute-start(bf16[1024,1024]{1,0:T(8,128)(2,1)} %get-tuple-element.296), channel_id=1, source_target_pairs={{0,4},{4,0},{1,5},{5,1},{2,6},{6,2},{3,7},{7,3},{8,12},{12,8},{9,1... | collective-permute-start | bytes 6291464 | tf_op jit(solution)/shard_map/ppermute | solution.py:1516
  229.8 30.9 %collective-permute-start.17 = (bf16[512,1024]{1,0:T(8,128)(2,1)}, bf16[512,1024]{1,0:T(8,128)(2,1)S(1)}, u32[]{:S(2)}, u32[]{:S(2)}) collective-permute-start(bf16[512,1024]{1,0:T(8,128)(2,1)} %get-tuple-element.294), channel_id=1, source_target_pairs={{0,1},{1,0},{2,3},{3,2},{4,5},{5,4},{6,7},{7,6},{8,9},{9,8},{10,11... | collective-permute-start | bytes 3145736 | tf_op jit(solution)/shard_map/ppermute | solution.py:1510
  229.8 46.8 %collective-permute-start.18 = (bf16[512,1024]{1,0:T(8,128)(2,1)}, bf16[512,1024]{1,0:T(8,128)(2,1)}, u32[]{:S(2)}, u32[]{:S(2)}) collective-permute-start(bf16[512,1024]{1,0:T(8,128)(2,1)} %get-tuple-element.295), channel_id=1, source_target_pairs={{0,1},{1,0},{2,3},{3,2},{4,5},{5,4},{6,7},{7,6},{8,9},{9,8},{10,11... | collective-permute-start | bytes 3145736 | tf_op jit(solution)/shard_map/ppermute | solution.py:1510
  283.6 27.3 %collective-permute-start.20 = (bf16[512,1024]{1,0:T(8,128)(2,1)}, bf16[512,1024]{1,0:T(8,128)(2,1)}, u32[]{:S(2)}, u32[]{:S(2)}) collective-permute-start(bf16[512,1024]{1,0:T(8,128)(2,1)} %get-tuple-element.304), channel_id=1, source_target_pairs={{0,4},{4,0},{1,5},{5,1},{2,6},{6,2},{3,7},{7,3},{8,12},{12,8},{9,1... | collective-permute-start | bytes 3145736 | tf_op jit(solution)/shard_map/ppermute | solution.py:1631
  286.2 24.7 %collective-permute-start.21 = (bf16[512,1024]{1,0:T(8,128)(2,1)}, bf16[512,1024]{1,0:T(8,128)(2,1)}, u32[]{:S(2)}, u32[]{:S(2)}) collective-permute-start(bf16[512,1024]{1,0:T(8,128)(2,1)} %get-tuple-element.305), channel_id=1, source_target_pairs={{0,1},{1,0},{2,3},{3,2},{4,5},{5,4},{6,7},{7,6},{8,9},{9,8},{10,11... | collective-permute-start | bytes 3145736 | tf_op jit(solution)/shard_map/ppermute | solution.py:1510
  286.6 50.0 %collective-permute-start.24 = (bf16[512,512]{1,0:T(8,128)(2,1)}, bf16[512,512]{1,0:T(8,128)(2,1)}, u32[]{:S(2)}, u32[]{:S(2)}) collective-permute-start(bf16[512,512]{1,0:T(8,128)(2,1)} %get-tuple-element.307), channel_id=1, source_target_pairs={{0,1},{1,0},{2,3},{3,2},{4,5},{5,4},{6,7},{7,6},{8,9},{9,8},{10,11... | collective-permute-start | bytes 1572872 | tf_op jit(solution)/shard_map/ppermute | solution.py:1510
  314.9 22.6 %collective-permute-start.22 = (bf16[512,1024]{1,0:T(8,128)(2,1)}, bf16[512,1024]{1,0:T(8,128)(2,1)}, u32[]{:S(2)}, u32[]{:S(2)}) collective-permute-start(bf16[512,1024]{1,0:T(8,128)(2,1)} %get-tuple-element.320), channel_id=1, source_target_pairs={{0,8},{8,0},{16,24},{24,16},{1,9},{9,1},{17,25},{25,17},{2,10},{10... | collective-permute-start | bytes 3145736 | tf_op jit(solution)/shard_map/ppermute | solution.py:1426
  316.2 21.3 %collective-permute-start.23 = (bf16[768,512]{1,0:T(8,128)(2,1)}, bf16[768,512]{1,0:T(8,128)(2,1)}, u32[]{:S(2)}, u32[]{:S(2)}) collective-permute-start(bf16[768,512]{1,0:T(8,128)(2,1)} %pad_maximum_fusion), channel_id=1, source_target_pairs={{0,1},{1,0},{2,3},{3,2},{4,5},{5,4},{6,7},{7,6},{8,9},{9,8},{10,11... | collective-permute-start | bytes 2359304 | tf_op jit(solution)/shard_map/ppermute | solution.py:1449
  343.9 28.3 %collective-permute-start.25 = (bf16[784,1024]{1,0:T(8,128)(2,1)}, bf16[784,1024]{1,0:T(8,128)(2,1)}, u32[]{:S(2)}, u32[]{:S(2)}) collective-permute-start(bf16[784,1024]{1,0:T(8,128)(2,1)} %get-tuple-element.337), channel_id=1, source_target_pairs={{0,2},{2,0},{1,3},{3,1},{4,6},{6,4},{5,7},{7,5},{8,10},{10,8},{9,1... | collective-permute-start | bytes 4816904 | tf_op jit(solution)/shard_map/ppermute | solution.py:1513
  347.2 26.0 %collective-permute-start.27 = (bf16[640,512]{1,0:T(8,128)(2,1)}, bf16[640,512]{1,0:T(8,128)(2,1)}, u32[]{:S(2)}, u32[]{:S(2)}) collective-permute-start(bf16[640,512]{1,0:T(8,128)(2,1)} %get-tuple-element.336), channel_id=1, source_target_pairs={{0,4},{4,0},{1,5},{5,1},{2,6},{6,2},{3,7},{7,3},{8,12},{12,8},{9,1... | collective-permute-start | bytes 1966088 | tf_op jit(solution)/shard_map/ppermute | solution.py:1457
  347.5 25.6 %collective-permute-start.26 = (bf16[256,1024]{1,0:T(8,128)(2,1)S(1)}, bf16[256,1024]{1,0:T(8,128)(2,1)}, u32[]{:S(2)}, u32[]{:S(2)}) collective-permute-start(bf16[256,1024]{1,0:T(8,128)(2,1)S(1)} %get-tuple-element.334), channel_id=1, source_target_pairs={{0,16},{8,24},{16,0},{24,8},{1,17},{9,25},{17,1},{25,9},{2,18},{10... | collective-permute-start | bytes 1572872 | tf_op jit(solution)/shard_map/ppermute | solution.py:1426
  372.2 21.1 %collective-permute-start.28 = (bf16[768,512]{1,0:T(8,128)(2,1)}, bf16[768,512]{1,0:T(8,128)(2,1)}, u32[]{:S(2)}, u32[]{:S(2)}) collective-permute-start(bf16[768,512]{1,0:T(8,128)(2,1)} %pad_maximum_fusion.2), channel_id=1, source_target_pairs={{0,1},{1,0},{2,3},{3,2},{4,5},{5,4},{6,7},{7,6},{8,9},{9,8},{10,11... | collective-permute-start | bytes 2359304 | tf_op jit(solution)/shard_map/ppermute | solution.py:1449
  375.7 25.1 %collective-permute-start.31 = (bf16[256,1024]{1,0:T(8,128)(2,1)S(1)}, bf16[256,1024]{1,0:T(8,128)(2,1)}, u32[]{:S(2)}, u32[]{:S(2)}) collective-permute-start(bf16[256,1024]{1,0:T(8,128)(2,1)S(1)} %add_convert_fusion.9), channel_id=1, source_target_pairs={{0,16},{8,24},{16,0},{24,8},{1,17},{9,25},{17,1},{25,9},{2,18},{10... | collective-permute-start | bytes 1572872 | tf_op jit(solution)/shard_map/ppermute | solution.py:1426
  402.2 31.6 %collective-permute-start.35 = (bf16[512,1024]{1,0:T(8,128)(2,1)S(1)}, bf16[512,1024]{1,0:T(8,128)(2,1)}, u32[]{:S(2)}, u32[]{:S(2)}) collective-permute-start(bf16[512,1024]{1,0:T(8,128)(2,1)S(1)} %bitcast.90), channel_id=1, source_target_pairs={{0,4},{4,0},{1,5},{5,1},{2,6},{6,2},{3,7},{7,3},{8,12},{12,8},{9,1... | collective-permute-start | bytes 3145736 | tf_op jit(solution)/shard_map/ppermute | solution.py:1440
  403.6 30.3 %collective-permute-start.36 = (bf16[512,1024]{1,0:T(8,128)(2,1)S(1)}, bf16[512,1024]{1,0:T(8,128)(2,1)}, u32[]{:S(2)}, u32[]{:S(2)}) collective-permute-start(bf16[512,1024]{1,0:T(8,128)(2,1)S(1)} %bitcast.91), channel_id=1, source_target_pairs={{0,8},{8,0},{16,24},{24,16},{1,9},{9,1},{17,25},{25,17},{2,10},{10... | collective-permute-start | bytes 3145736 | tf_op jit(solution)/shard_map/ppermute | solution.py:1426
  409.3 24.5 %collective-permute-start.34 = (bf16[384,512]{1,0:T(8,128)(2,1)}, bf16[384,512]{1,0:T(8,128)(2,1)S(1)}, u32[]{:S(2)}, u32[]{:S(2)}) collective-permute-start(bf16[384,512]{1,0:T(8,128)(2,1)} %get-tuple-element.369), channel_id=1, source_target_pairs={{0,4},{4,0},{1,5},{5,1},{2,6},{6,2},{3,7},{7,3},{8,12},{12,8},{9,1... | collective-permute-start | bytes 1179656 | tf_op jit(solution)/shard_map/ppermute | solution.py:1457
  410.1 21.5 %collective-permute-start.33 = (bf16[160,512]{1,0:T(8,128)(2,1)}, bf16[160,512]{1,0:T(8,128)(2,1)}, u32[]{:S(2)}, u32[]{:S(2)}) collective-permute-start(bf16[160,512]{1,0:T(8,128)(2,1)} %get-tuple-element.371), channel_id=1, source_target_pairs={{0,16},{8,24},{16,0},{24,8},{1,17},{9,25},{17,1},{25,9},{2,18},{10... | collective-permute-start | bytes 491528 | tf_op jit(solution)/shard_map/ppermute | solution.py:1400
  442.6 32.8 %collective-permute-start.48 = (bf16[512,1024]{1,0:T(8,128)(2,1)S(1)}, bf16[512,1024]{1,0:T(8,128)(2,1)S(1)}, u32[]{:S(2)}, u32[]{:S(2)}) collective-permute-start(bf16[512,1024]{1,0:T(8,128)(2,1)S(1)} %bitcast.92), channel_id=1, source_target_pairs={{0,2},{2,0},{1,3},{3,1},{4,6},{6,4},{5,7},{7,5},{8,10},{10,8},{9,1... | collective-permute-start | bytes 3145736 | tf_op jit(solution)/shard_map/ppermute | solution.py:1441
  443.3 37.4 %collective-permute-start.47 = (bf16[512,1024]{1,0:T(8,128)(2,1)}, bf16[512,1024]{1,0:T(8,128)(2,1)S(1)}, u32[]{:S(2)}, u32[]{:S(2)}) collective-permute-start(bf16[512,1024]{1,0:T(8,128)(2,1)} %collective-permute-done.36.refs_2_), channel_id=1, source_target_pairs={{0,4},{4,0},{1,5},{5,1},{2,6},{6,2},{3,7},{7,3},{8,12},{12,8},{9,1... | collective-permute-start | bytes 3145736 | tf_op jit(solution)/shard_map/ppermute | solution.py:1441
  463.8 18.9 %collective-permute-start.45 = (bf16[640,512]{1,0:T(8,128)(2,1)S(1)}, bf16[640,512]{1,0:T(8,128)(2,1)S(1)}, u32[]{:S(2)}, u32[]{:S(2)}) collective-permute-start(bf16[640,512]{1,0:T(8,128)(2,1)S(1)} %bitcast.94), channel_id=1, source_target_pairs={{0,4},{4,0},{1,5},{5,1},{2,6},{6,2},{3,7},{7,3},{8,12},{12,8},{9,1... | collective-permute-start | bytes 1966088 | tf_op jit(solution)/shard_map/ppermute | solution.py:1414
  469.0 24.3 %collective-permute-start.32 = (bf16[784,1024]{1,0:T(8,128)(2,1)S(1)}, bf16[784,1024]{1,0:T(8,128)(2,1)S(1)}, u32[]{:S(2)}, u32[]{:S(2)}) collective-permute-start(bf16[784,1024]{1,0:T(8,128)(2,1)S(1)} %copy-done), channel_id=1, source_target_pairs={{1,2},{2,1},{5,6},{6,5},{9,10},{10,9},{13,14},{14,13},{17,18},{18,... | collective-permute-start | bytes 4816904 | tf_op jit(solution)/shard_map/ppermute | solution.py:1522
  480.8 29.4 %collective-permute-start.41 = (bf16[784,1024]{1,0:T(8,128)(2,1)}, bf16[784,1024]{1,0:T(8,128)(2,1)S(1)}, u32[]{:S(2)}, u32[]{:S(2)}) collective-permute-start(bf16[784,1024]{1,0:T(8,128)(2,1)} %get-tuple-element.402), channel_id=1, source_target_pairs={{1,2},{2,1},{5,6},{6,5},{9,10},{10,9},{13,14},{14,13},{17,18},{18,... | collective-permute-start | bytes 4816904 | tf_op jit(solution)/shard_map/ppermute | solution.py:1522
  (74 other events, 599.6 us)
